TPU v7x, 32 devices: a whole 2x2x4 slice. The times are simulated.
32 devices in a mesh: seq: 4 (over z_hi, core), expert: 4 (over y, x), tensor: 2 (over z_lo).
Axes of the slice: x: 2, y: 2, z: 4 (z_hi: 2, z_lo: 2; z = z_hi * 2 + z_lo), core: 2. Of those that a mesh axis runs over, the one named last changes fastest.
Arguments:
- q_rows: bfloat16 [4, 512, 4096], P('expert', 'seq', 'tensor'), may hold values from -6 to 6
- k_rows: bfloat16 [4, 512, 512], P('expert', 'seq', 'tensor'), may hold values from -6 to 6
- value_rows: bfloat16 [4, 512, 512], P('expert', 'seq', 'tensor'), may hold values from -6 to 6
- x_rows: bfloat16 [4, 512, 2048], P('expert', 'seq'), may hold values from -40 to 40
- out_weight: bfloat16 [4096, 2048], P('tensor', 'expert'), may hold values from -0.09375 to 0.09375
- norm_gain: float32 [2048], P('tensor'), may hold values from 0.1 to 1.9
- w_gate: bfloat16 [16, 2048, 768], P(('seq', 'expert'), None, 'tensor'), may hold values from -0.125 to 0.125
- w_up: bfloat16 [16, 2048, 768], P(('seq', 'expert'), None, 'tensor'), may hold values from -0.125 to 0.125
- w_down: bfloat16 [16, 768, 2048], P(('seq', 'expert'), 'tensor'), may hold values from -0.21875 to 0.21875
- expert_ids: int32 [4, 512, 8], P('expert', 'seq'), may hold values from 0 to 15, all different within a row; in each aligned block of 128 rows (0 to 127, 128 to 255, ..., all dimensions but the last counted through in order) at most 96 rows name the same one
- gate_weights: float32 [4, 512, 8], P('expert', 'seq'), may hold values from 0.02 to 0.4
Outputs:
- layer_out: bfloat16 [4, 512, 2048], P('expert', 'seq', 'tensor')
Inputs may be any that keep to these rules, and one draw needn't show every extreme that they name: `expert_ids`: in each token's row the 8 ids differ. Among the 128 tokens of one block of positions (the blocks laid session after session) no expert is named more than 96 times, a bound that some block reaches; every expert is named somewhere.
All inputs are finite; a program needn't handle non-finite values.
Results may differ from a plain program's by a relative error of at most 0.007.
Values may be sent and summed in bfloat16 or wider, within the bound.
No kernel may reach another device: no remote copies, remote signals or barrier semaphores. Data moves between devices by JAX's collectives and lax.ppermute only.
A program may use at most 128 MiB of HBM per device.

v0:
```python
import functools
import math

import jax
import jax.numpy as jnp
from jax import lax
from jax.experimental import pallas as pl
from jax.experimental.pallas import tpu as pltpu
from jax.sharding import PartitionSpec as P


HEAD_SIZE = 128
TOPK = 8
CHUNKS = 2
KERNEL_BYTES = 24 << 20


def dispatch_plan(
    q_rows,
    k_rows,
    value_rows,
    x_rows,
    out_weight,
    norm_gain,
    w_gate,
    w_up,
    w_down,
    expert_ids,
    gate_weights,
):
    rows_here = q_rows.shape[1]
    kv_heads = k_rows.shape[2] // HEAD_SIZE
    q_heads = q_rows.shape[2] // HEAD_SIZE
    group_width = q_heads // kv_heads
    queries = q_rows[0].reshape(rows_here, kv_heads, group_width, HEAD_SIZE)
    offset = lax.axis_index("seq") * rows_here
    query_pos = offset + jnp.arange(rows_here, dtype=jnp.int32)
    softmax_scale = 1.0 / math.sqrt(HEAD_SIZE)
    tensor_pos = lax.axis_index("tensor")
    tensor_count = lax.axis_size("tensor")
    pieces = (
        lax.all_gather(k_rows, "seq", axis=1, tiled=True),
        lax.all_gather(value_rows, "seq", axis=1, tiled=True),
    )
    running_max = jnp.full((kv_heads, group_width, rows_here), -1e30, jnp.float32)
    block_rows = pieces[0].shape[1]
    key_block = pieces[0][0].reshape(block_rows, kv_heads, HEAD_SIZE)
    value_block = pieces[1][0].reshape(block_rows, kv_heads, HEAD_SIZE)
    scores = (
        jnp.einsum("igrd,jgd->grij", queries, key_block, preferred_element_type=jnp.float32)
        * softmax_scale
    )
    key_pos = jnp.arange(block_rows, dtype=jnp.int32)
    allowed = key_pos[None, :] <= query_pos[:, None]
    scores = jnp.where(allowed, scores, jnp.float32(-1e30))
    new_max = jnp.maximum(running_max, jnp.max(scores, axis=-1))
    weights = jnp.where(allowed, jnp.exp(scores - new_max[..., None]), jnp.float32(0.0))
    running_sum = jnp.sum(weights, axis=-1)
    weighted = jnp.einsum(
        "grij,jgd->grid",
        weights.astype(jnp.bfloat16),
        value_block,
        preferred_element_type=jnp.float32,
    )
    running_max, running_sum, weighted = (new_max, running_sum, weighted)
    attn_rows = (
        (weighted / running_sum[..., None])
        .transpose(2, 0, 1, 3)
        .reshape(rows_here, q_heads * HEAD_SIZE)
        .astype(jnp.bfloat16)
    )
    head_terms = jnp.dot(
        attn_rows,
        lax.all_gather(out_weight, "expert", axis=1, tiled=True),
        preferred_element_type=jnp.float32,
    )
    width = x_rows.shape[2]
    half_width = width // tensor_count
    share_sum = lax.psum_scatter(
        head_terms.astype(jnp.bfloat16), "tensor", scatter_dimension=1, tiled=True
    ).astype(jnp.float32)
    mixed_half = (
        lax.dynamic_slice_in_dim(x_rows[0], tensor_pos * half_width, half_width, 1).astype(
            jnp.float32
        )
        + share_sum
    )
    power = lax.psum(jnp.sum(mixed_half * mixed_half, axis=1), "tensor")
    inverse = lax.rsqrt(power / width + 1e-06)
    normed = (mixed_half * inverse[:, None] * norm_gain[None, :]).astype(jnp.bfloat16)
    seq_count = lax.axis_size("seq")
    group_count = lax.axis_size("expert")
    experts = seq_count * group_count
    capacity = max(2, 3 * rows_here * TOPK // (2 * experts))
    routed = expert_ids[0].reshape(-1)
    assigned = routed.shape[0]
    member = (routed[:, None] == jnp.arange(experts, dtype=jnp.int32)[None, :]).astype(jnp.int32)
    earlier = jnp.cumsum(member, axis=0) - member
    slot_index = jnp.sum(earlier * member, axis=1)
    target = routed * capacity + slot_index
    owner_index = (
        jnp.full((experts * capacity,), assigned, jnp.int32)
        .at[target]
        .set(jnp.arange(assigned, dtype=jnp.int32))
    )
    filled = owner_index < assigned
    source = jnp.minimum(owner_index // TOPK, rows_here - 1)
    outgoing = jnp.where(filled[:, None], normed[source], jnp.zeros((), jnp.bfloat16)).reshape(
        experts, capacity, half_width
    )
    arrived = lax.all_to_all(outgoing, ("seq", "expert"), split_axis=0, concat_axis=0, tiled=True)
    slot_count = arrived.shape[1]
    whole_rows = lax.all_gather(arrived, "tensor", axis=2, tiled=True)
    flat_rows = whole_rows.reshape(-1, whole_rows.shape[2])
    gate_act = jnp.dot(flat_rows, w_gate[0], preferred_element_type=jnp.float32)
    up_act = jnp.dot(flat_rows, w_up[0], preferred_element_type=jnp.float32)
    hidden = (jax.nn.silu(gate_act) * up_act).astype(jnp.bfloat16)
    partial_value = jnp.dot(hidden, w_down[0], preferred_element_type=jnp.float32).reshape(
        arrived.shape[0], slot_count, whole_rows.shape[2]
    )
    returned = lax.all_to_all(
        lax.psum_scatter(
            partial_value.astype(jnp.bfloat16), "tensor", scatter_dimension=2, tiled=True
        ),
        ("seq", "expert"),
        split_axis=0,
        concat_axis=0,
        tiled=True,
    )
    came_back = returned.reshape(experts * capacity, half_width)
    picked = came_back[target].astype(jnp.float32)
    weights_flat = gate_weights[0].reshape(-1)
    blended = jnp.sum((picked * weights_flat[:, None]).reshape(rows_here, TOPK, half_width), axis=1)
    return (mixed_half + blended).astype(jnp.bfloat16)[None]


def bits_of(size):
    return [1 << n for n in range(size.bit_length() - 1)]


def swap(value, axis, bit):
    count = lax.axis_size(axis)
    return lax.ppermute(value, axis, [(i, i ^ bit) for i in range(count)])


def slot_order(bits):
    order = [0]
    for bit in bits:
        order = order + [place ^ bit for place in order]
    return order


def gather_slots(value, axis, bits):
    held = value[None]
    for bit in bits:
        held = jnp.concatenate([held, swap(held, axis, bit)], axis=0)
    return held


def add_rounded(kept, received):
    return (kept.astype(jnp.float32) + received.astype(jnp.float32)).astype(kept.dtype)


def scatter_slots(held, axis, bits):
    for bit in reversed(bits):
        half = held.shape[0] // 2
        held = add_rounded(held[:half], swap(held[half:], axis, bit))
    return held[0]


def expert_kernel(order, slots, near, start_row, has_received, *refs):
    refs = list(refs)
    place_ref, first_ref, second_ref, gain_ref, table_ref = refs[:5]
    del refs[:5]
    proj_ref = None if near else refs.pop(0)
    received_ref = refs.pop(0) if has_received else None
    w_in_ref, w_out_ref, out_ref, normed_ref = refs
    half_groups, halves, blocks, sessions, rows, piece = first_ref.shape
    half_width = out_ref.shape[-1]
    width = half_width * halves
    hidden_width = w_out_ref.shape[0]
    me, half_me, seq_me = place_ref[0], place_ref[1], place_ref[2]
    per_half = half_width // piece
    count = len(slots) * rows * blocks

    power = jnp.zeros((count, 1), jnp.float32)
    pieces = []
    for i in range(2 * half_groups):
        in_ref = first_ref if i < half_groups else second_ref
        for k in range(halves):
            tokens = jnp.concatenate(
                [
                    in_ref[i % half_groups, k, b, lax.bitwise_xor(me, order[r])]
                    for b in range(blocks)
                    for r in slots
                ],
                axis=0,
            )
            mixed = tokens.astype(jnp.float32)
            power = power + jnp.sum(mixed * mixed, axis=1, keepdims=True)
            pieces.append((i, k, tokens))
    inverse = lax.rsqrt(power * (1.0 / width) + 1e-06)
    for i, k, tokens in pieces:
        spot = lax.bitwise_xor(me, order[i]) * halves + lax.bitwise_xor(half_me, k)
        gain = gain_ref[pl.ds(spot, 1), :]
        normed_ref[:, pl.ds(pl.multiple_of(spot * piece, piece), piece)] = (
            tokens.astype(jnp.float32) * inverse * gain
        ).astype(jnp.bfloat16)
    both = jnp.dot(normed_ref[...], w_in_ref[...], preferred_element_type=jnp.float32)
    gate_act, up_act = both[:, :hidden_width], both[:, hidden_width:]
    hidden = (gate_act / (1.0 + jnp.exp(-gate_act)) * up_act).astype(jnp.bfloat16)

    diagonal = lax.broadcasted_iota(jnp.int32, (rows, rows), 0) == lax.broadcasted_iota(
        jnp.int32, (rows, rows), 1
    )
    scales = []
    for b in range(blocks):
        for r in slots:
            source = lax.bitwise_xor(seq_me, 2 * b + near) * sessions
            source = source + lax.bitwise_xor(me, order[r])
            line = table_ref[pl.ds(source, 1), :][:, start_row : start_row + rows]
            scales.append(
                jnp.sum(jnp.where(diagonal, line, 0.0), axis=1, keepdims=True)
            )
    scale = jnp.concatenate(scales, axis=0)
    for half in range(halves):
        k = lax.bitwise_xor(half_me, half)
        result = scale * jnp.dot(
            hidden,
            w_out_ref[:, half * half_width : (half + 1) * half_width],
            preferred_element_type=jnp.float32,
        )
        at = 0
        for b in range(blocks):
            for n, r in enumerate(slots):
                part = result[at : at + rows]
                at += rows
                if proj_ref is not None and b == 0:
                    proj = proj_ref[order[r], start_row : start_row + rows]
                    columns = []
                    for m in range(per_half):
                        mine = me * halves + half_me == half * per_half + m
                        columns.append(
                            part[:, m * piece : (m + 1) * piece]
                            + proj * mine.astype(jnp.float32)
                        )
                    part = jnp.concatenate(columns, axis=1)
                if received_ref is not None:
                    part = part + received_ref[n, k, b].astype(jnp.float32)
                out_ref[n, k, b] = part.astype(jnp.bfloat16)


def dense_plan(
    q_rows,
    k_rows,
    value_rows,
    x_rows,
    out_weight,
    norm_gain,
    w_gate,
    w_up,
    w_down,
    expert_ids,
    gate_weights,
):
    rows_here = q_rows.shape[1]
    width = x_rows.shape[2]
    seq_count, group_count = lax.axis_size("seq"), lax.axis_size("expert")
    tensor_count = lax.axis_size("tensor")
    experts = seq_count * group_count
    seq_pos, group_pos = lax.axis_index("seq"), lax.axis_index("expert")
    tensor_pos = lax.axis_index("tensor")
    seq_bits, group_bits = bits_of(seq_count), bits_of(group_count)
    tensor_bits = bits_of(tensor_count)
    half_width = width // tensor_count
    piece = width // (group_count * tensor_count)
    near, far = seq_bits[:1], seq_bits[1:]

    kv_width = k_rows.shape[2]
    kv_bits = far + near
    kv_all = gather_slots(
        jnp.concatenate([k_rows[0], value_rows[0]], axis=1), "seq", kv_bits
    ).reshape(seq_count * rows_here, 2 * kv_width)
    key_pos = (seq_pos ^ jnp.array(slot_order(kv_bits), jnp.int32))[:, None] * rows_here
    key_pos = (key_pos + jnp.arange(rows_here, dtype=jnp.int32)[None, :]).reshape(-1)

    x_slots = []
    for r in range(group_count):
        start = ((group_pos ^ r) * tensor_count + tensor_pos) * piece
        columns = lax.dynamic_slice_in_dim(x_rows[0], start, piece, 1)
        x_slots.append(swap(columns, "expert", r) if r else columns)
    gain_slots = gather_slots(norm_gain, "tensor", tensor_bits)
    gain = jnp.take(
        gain_slots,
        jnp.array(slot_order(tensor_bits), jnp.int32) ^ tensor_pos,
        axis=0,
    ).reshape(width // piece, piece)

    named = expert_ids[0][:, :, None] == jnp.arange(experts, dtype=jnp.int32)[None, None, :]
    table = jnp.sum(jnp.where(named, gate_weights[0][:, :, None], 0.0), axis=1).T
    table = lax.all_to_all(table, ("seq", "expert"), split_axis=0, concat_axis=0, tiled=True)
    w_in = jnp.concatenate([w_gate[0], w_up[0]], axis=1)
    kv_all, table, gain, w_in, *x_slots = lax.optimization_barrier(
        (kv_all, table, gain, w_in, *x_slots)
    )

    kv_heads = kv_width // HEAD_SIZE
    q_heads = q_rows.shape[2] // HEAD_SIZE
    group_width = q_heads // kv_heads
    queries = q_rows[0].reshape(rows_here, kv_heads, group_width, HEAD_SIZE)
    query_pos = seq_pos * rows_here + jnp.arange(rows_here, dtype=jnp.int32)
    block_rows = kv_all.shape[0]
    key_block = kv_all[:, :kv_width].reshape(block_rows, kv_heads, HEAD_SIZE)
    value_block = kv_all[:, kv_width:].reshape(block_rows, kv_heads, HEAD_SIZE)
    scores = jnp.einsum(
        "igrd,jgd->grij", queries, key_block, preferred_element_type=jnp.float32
    ) * (1.0 / math.sqrt(HEAD_SIZE))
    allowed = key_pos[None, :] <= query_pos[:, None]
    scores = jnp.where(allowed, scores, jnp.float32(-1e30))
    weights = jnp.where(
        allowed, jnp.exp(scores - jnp.max(scores, axis=-1, keepdims=True)), jnp.float32(0.0)
    )
    totals = jnp.sum(weights, axis=-1)
    weighted = jnp.einsum(
        "grij,jgd->grid",
        weights.astype(jnp.bfloat16),
        value_block,
        preferred_element_type=jnp.float32,
    )
    attn_rows = (
        (weighted / totals[..., None])
        .transpose(2, 0, 1, 3)
        .reshape(rows_here, q_heads * HEAD_SIZE)
        .astype(jnp.bfloat16)
    )

    paths = (group_bits, group_bits[::-1])
    depth = attn_rows.shape[1] // len(paths)
    gathered = []
    for n, path in enumerate(paths):
        held = [attn_rows[:, n * depth : (n + 1) * depth]]
        for bit in path:
            held = held + [swap(value, "expert", bit) for value in held]
        order = slot_order(path)
        gathered.append(
            jnp.concatenate([held[order.index(r)] for r in range(group_count)], axis=0)
        )

    def projected(k):
        columns = lax.dynamic_slice_in_dim(out_weight, (tensor_pos ^ k) * piece, piece, 1)
        return sum(
            jnp.dot(
                held, columns[n * depth : (n + 1) * depth], preferred_element_type=jnp.float32
            )
            for n, held in enumerate(gathered)
        )

    proj = projected(0)
    for k in range(1, tensor_count):
        away = projected(k).astype(jnp.bfloat16)
        proj = proj + swap(away, "tensor", k).astype(jnp.float32)
    proj = proj.reshape(group_count, rows_here, piece)
    mixed = (jnp.stack(x_slots).astype(jnp.float32) + proj).astype(jnp.bfloat16)
    by_session = jnp.take(
        mixed, jnp.arange(group_count, dtype=jnp.int32) ^ group_pos, axis=0
    )

    rows = rows_here // CHUNKS
    place = jnp.stack([group_pos, tensor_pos, seq_pos]).astype(jnp.int32)
    half_groups = group_count // 2
    near_bit = near[0]
    chunks = []
    for c in range(CHUNKS):
        path = paths[c % len(paths)]
        held = by_session[:, c * rows : (c + 1) * rows]
        held = gather_slots(held, "seq", far)
        held = gather_slots(held, "tensor", tensor_bits)
        first = gather_slots(held, "expert", path[:-1])
        second = swap(first, "expert", path[-1])
        parts = ((first, second), tuple(swap(v, "seq", near_bit) for v in (first, second)))
        chunks.append((c, path, parts))

    def experts_on(place, c, path, parts, slots, core, received):
        operands = [place, *parts[core], gain, table]
        if not core:
            operands.append(proj)
        if received is not None:
            operands.append(received)
        operands += [w_in, w_down[0]]
        blocks = seq_count // 2
        return pl.pallas_call(
            functools.partial(
                expert_kernel,
                tuple(slot_order(path)),
                tuple(slots),
                core,
                c * rows,
                received is not None,
            ),
            out_shape=jax.ShapeDtypeStruct(
                (len(slots), tensor_count, blocks, rows, half_width), jnp.bfloat16
            ),
            in_specs=[pl.BlockSpec(memory_space=pltpu.SMEM)]
            + [pl.BlockSpec(memory_space=pltpu.VMEM)] * (len(operands) - 1),
            out_specs=pl.BlockSpec(memory_space=pltpu.VMEM),
            scratch_shapes=[pltpu.VMEM((len(slots) * blocks * rows, width), jnp.bfloat16)],
            compiler_params=pltpu.CompilerParams(vmem_limit_bytes=KERNEL_BYTES),
        )(*operands)

    sent, kept = range(half_groups, group_count), range(half_groups)
    totals = []
    for slots in (sent, kept):
        away, outs = [], []
        for chunk in chunks:
            away.append(experts_on(place, *chunk, slots, 1, None))
        away = [swap(value, "seq", near_bit) for value in away]
        for chunk, got in zip(chunks, away):
            outs.append(experts_on(place, *chunk, slots, 0, got))
        place = lax.optimization_barrier((place, *outs))[0]
        totals.append(outs)
    finished = []
    for (c, path, _), away, held in zip(chunks, *totals):
        arrived = swap(away, "expert", path[-1])
        held = add_rounded(held, arrived)
        held = scatter_slots(held, "expert", path[:-1])
        held = scatter_slots(held, "tensor", tensor_bits)
        finished.append(scatter_slots(held, "seq", far))
    x_half = lax.dynamic_slice_in_dim(x_rows[0], tensor_pos * half_width, half_width, 1)
    summed = jnp.concatenate(finished, axis=0).astype(jnp.float32)
    return (x_half.astype(jnp.float32) + summed).astype(jnp.bfloat16)[None]


def per_device(*arrays):
    rows_here = arrays[0].shape[1]
    counts = [lax.axis_size(axis) for axis in ("seq", "expert", "tensor")]
    experts = counts[0] * counts[1]
    capacity = max(2, 3 * rows_here * TOPK // (2 * experts))
    dense = experts * rows_here <= 2 * experts * capacity
    regular = all(count > 1 and count & (count - 1) == 0 for count in counts)
    if dense and regular and rows_here % (16 * CHUNKS) == 0:
        return dense_plan(*arrays)
    return dispatch_plan(*arrays)


def solution(mesh):
    return jax.shard_map(
        per_device,
        mesh=mesh,
        in_specs=(
            P("expert", "seq", "tensor"),
            P("expert", "seq", "tensor"),
            P("expert", "seq", "tensor"),
            P("expert", "seq", None),
            P("tensor", "expert"),
            P("tensor"),
            P(("seq", "expert"), None, "tensor"),
            P(("seq", "expert"), None, "tensor"),
            P(("seq", "expert"), "tensor", None),
            P("expert", "seq", None),
            P("expert", "seq", None),
        ),
        out_specs=P("expert", "seq", "tensor"),
        check_vma=False,
    )
```

profile of v0, /device:TPU:0, one launch (start us, length us, event | category | flops | bytes accessed | tf_op | source)
XLA Modules:
  0.0 217.9 jit_solution(14136522223924916537)
XLA Ops:
  0.0 1.8 dynamic-slice_bitcast_fusion
  1.8 3.0 %collective-permute-start.3 = (bf16[128,256]{1,0:T(8,128)(2,1)}, bf16[128,256]{1,0:T(8,128)(2,1)S(1)}, u32[]{:S(2)}, u32[]{:S(2)}) collective-permute-start(bf16[128,256]{1,0:T(8,128)(2,1)} %get-tuple-element.28), channel_id=1, source_target_pairs={{0,2},{2,0},{4,6},{6,4},{1,3},{3,1},{5,7},{7,5},{8,10},{10,8},{12,... | collective-permute-start | bytes 196616 | tf_op jit(solution)/shard_map/ppermute | solution.py:143
  4.7 1.5 collective-permute-start.4
  6.3 2.1 collective-permute-start.2
  8.3 0.9 maximum_bitcast_fusion.4
  9.2 2.7 %collective-permute-start = (bf16[1,128,512]{2,1,0:T(8,128)(2,1)S(1)}, bf16[1,128,512]{2,1,0:T(8,128)(2,1)S(1)}, u32[]{:S(2)}, u32[]{:S(2)}) collective-permute-start(bf16[1,128,512]{2,1,0:T(8,128)(2,1)S(1)} %maximum_bitcast_fusion.4), channel_id=1, source_target_pairs={{0,16},{8,24},{16,0},{24,8},{1,17},{9,25},{17,1},{25,9},{2,18},{10... | collective-permute-start | bytes 393224 | tf_op jit(solution)/shard_map/ppermute | solution.py:143
  11.9 1.3 select_reduce_fusion
  13.2 3.8 %all-to-all-start = ((f32[16,1,128]{2,1,0:T(1,128)}), f32[16,1,128]{2,1,0:T(1,128)S(1)}, u32[]{:S(2)}, u32[]{:S(2)}) async-start(f32[16,1,128]{2,1,0:T(1,128)} %bitcast.11), calls=%async_computation | async-start | bytes 16384 | tf_op jit(solution)/shard_map/all_to_all | solution.py:301
  18.3 3.8 %pad_maximum_fusion.refs_5_.refs_7_ = bf16[2048,768]{1,0:T(8,128)(2,1)} fusion(bf16[2048,384]{1,0:T(8,128)(2,1)} %bitcast.136, bf16[2048,384]{1,0:T(8,128)(2,1)} %bitcast.137), kind=kLoop, calls=%fused_computation.6 | loop fusion | flops 6291456 | bytes 6291456 | tf_op jit(solution)/shard_map/concatenate | solution.py:302
  23.7 1.2 pad_clamp_fusion.1
  26.1 1.3 gather_fusion
  27.4 1.3 gather.11
  28.7 0.8 broadcast_select_fusion.1.refs_3_
  29.5 0.8 pad_maximum_fusion.5
  30.3 1.3 copy.39
  32.5 2.3 %fusion.41 = (f32[2,8,128]{2,1,0:T(8,128)S(1)}, bf16[2,8,128,512]{2,3,1,0:T(8,128)(2,1)S(1)}) fusion(f32[2,512,128,8]{2,1,3,0:T(8,128)S(1)} %fusion.26, pred[128,512]{0,1:T(8,128)(4,1)S(1)} %copy-done.9), kind=kOutput, calls=%fused_computation.94 | output fusion | flops 8389119 | bytes 6365184 | tf_op jit(solution)/shard_map/sub | solution.py:321
  35.3 1.7 collective-permute-start.10
  37.0 1.5 collective-permute-start.6
  39.0 4.8 %collective-permute-done.10 = bf16[128,1024]{0,1:T(8,128)(2,1)S(1)} collective-permute-done((bf16[128,1024]{0,1:T(8,128)(2,1)S(1)}, bf16[128,1024]{0,1:T(8,128)(2,1)S(1)}, u32[]{:S(2)}, u32[]{:S(2)}) %collective-permute-start.10) | collective-permute-done | bytes 262176 | tf_op jit(solution)/shard_map/ppermute | solution.py:143
  43.9 1.7 collective-permute-start.11
  45.6 1.5 collective-permute-start.7
  47.7 4.3 %collective-permute-done.9 = bf16[128,1024]{0,1:T(8,128)(2,1)} collective-permute-done((bf16[128,1024]{0,1:T(8,128)(2,1)S(1)}, bf16[128,1024]{0,1:T(8,128)(2,1)}, u32[]{:S(2)}, u32[]{:S(2)}) %collective-permute-start.9) | collective-permute-done | bytes 262176 | tf_op jit(solution)/shard_map/ppermute | solution.py:143
  51.9 4.8 %collective-permute-done.11 = bf16[128,1024]{0,1:T(8,128)(2,1)} collective-permute-done((bf16[128,1024]{0,1:T(8,128)(2,1)S(1)}, bf16[128,1024]{0,1:T(8,128)(2,1)}, u32[]{:S(2)}, u32[]{:S(2)}) %collective-permute-start.11) | collective-permute-done | bytes 262176 | tf_op jit(solution)/shard_map/ppermute | solution.py:143
  56.7 1.5 fusion.18
  58.8 2.2 %fusion.17 = bf16[512,256]{1,0:T(8,128)(2,1)} fusion(f32[512,256]{1,0:T(8,128)S(1)} %fusion.18, bf16[2048,512]{1,0:T(8,128)(2,1)S(1)} %copy-done, s32[]{:T(128)S(6)} %select_n.74, bf16[128,1024]{0,1:T(8,128)(2,1)} %collective-permute-done.8, bf16[128,1024]{0,1:T(8,128)(2,1)} %collective-permute-done.7, bf16[128,1024]{0,1:T(8,128)(2,1)S(1)} %collective-permute-done.6, ...), kind=kOutput, calls=%fused_computation.20 | convolution fusion | flops 272891904 | bytes 2359300 | tf_op jit(solution)/shard_map/dot_general | solution.py:352
  61.5 1.6 fusion.21
  63.1 5.2 %collective-permute-done.12 = bf16[512,256]{1,0:T(8,128)(2,1)} collective-permute-done((bf16[512,256]{1,0:T(8,128)(2,1)}, bf16[512,256]{1,0:T(8,128)(2,1)}, u32[]{:S(2)}, u32[]{:S(2)}) %collective-permute-start.12) | collective-permute-done | bytes 262176 | tf_op jit(solution)/shard_map/ppermute | solution.py:143
  68.3 1.6 fusion.16
  69.8 0.9 add_convert_fusion.5
  71.5 2.4 %collective-permute-start.13 = (bf16[1,4,64,256]{3,2,1,0:T(8,128)(2,1)S(1)}, bf16[1,4,64,256]{3,2,1,0:T(8,128)(2,1)S(1)}, u32[]{:S(2)}, u32[]{:S(2)}) collective-permute-start(bf16[1,4,64,256]{3,2,1,0:T(8,128)(2,1)S(1)} %get-tuple-element.31), channel_id=1, source_target_pairs={{0,16},{8,24},{16,0},{24,8},{1,17},{9,25},{17,1},{25,9},{2,18},{10... | collective-permute-start | bytes 393224 | tf_op jit(solution)/shard_map/ppermute | solution.py:143
  74.5 7.5 %collective-permute-done.13 = bf16[1,4,64,256]{3,2,1,0:T(8,128)(2,1)S(1)} collective-permute-done((bf16[1,4,64,256]{3,2,1,0:T(8,128)(2,1)S(1)}, bf16[1,4,64,256]{3,2,1,0:T(8,128)(2,1)S(1)}, u32[]{:S(2)}, u32[]{:S(2)}) %collective-permute-start.13) | collective-permute-done | bytes 131104 | tf_op jit(solution)/shard_map/ppermute | solution.py:143
  82.0 2.0 collective-permute-done.20
  84.2 7.0 %collective-permute-done.14 = bf16[1,2,4,64,256]{4,3,2,1,0:T(8,128)(2,1)S(1)} collective-permute-done((bf16[1,2,4,64,256]{4,3,2,1,0:T(8,128)(2,1)S(1)}, bf16[1,2,4,64,256]{4,3,2,1,0:T(8,128)(2,1)S(1)}, u32[]{:S(2)}, u32[]{:S(2)}) %collective-permute-start.14) | collective-permute-done | bytes 262176 | tf_op jit(solution)/shard_map/ppermute | solution.py:143
  91.3 2.1 collective-permute-start.15
  93.4 1.8 collective-permute-done.21
  95.3 1.0 collective-permute-start.22
  96.2 6.1 %collective-permute-done.15 = bf16[1,2,2,4,64,256]{5,4,3,2,1,0:T(8,128)(2,1)S(1)} collective-permute-done((bf16[1,2,2,4,64,256]{5,4,3,2,1,0:T(8,128)(2,1)S(1)}, bf16[1,2,2,4,64,256]{5,4,3,2,1,0:T(8,128)(2,1)S(1)}, u32[]{:S(2)}, u32[]{:S(2)}) %collective-permute-start.15) | collective-permute-done | bytes 524320 | tf_op jit(solution)/shard_map/ppermute | solution.py:143
  103.1 7.0 %collective-permute-done.22 = bf16[1,2,2,4,64,256]{5,4,3,2,1,0:T(8,128)(2,1)S(1)} collective-permute-done((bf16[1,2,2,4,64,256]{5,4,3,2,1,0:T(8,128)(2,1)S(1)}, bf16[1,2,2,4,64,256]{5,4,3,2,1,0:T(8,128)(2,1)S(1)}, u32[]{:S(2)}, u32[]{:S(2)}) %collective-permute-start.22) | collective-permute-done | bytes 524320 | tf_op jit(solution)/shard_map/ppermute | solution.py:143
  110.2 2.1 collective-permute-start.23
  112.3 17.8 %collective-permute-done.16.refs_2_ = bf16[2,2,2,4,64,256]{5,4,3,2,1,0:T(8,128)(2,1)S(1)} collective-permute-done((bf16[2,2,2,4,64,256]{5,4,3,2,1,0:T(8,128)(2,1)S(1)}, bf16[2,2,2,4,64,256]{5,4,3,2,1,0:T(8,128)(2,1)S(1)}, u32[]{:S(2)}, u32[]{:S(2)}) %collective-permute-start.16) | collective-permute-done | bytes 1048608 | tf_op jit(solution)/shard_map/ppermute | solution.py:143
  130.9 1.9 collective-permute-done.18.refs_2_
  132.8 3.4 %shard_map.127 = bf16[2,2,2,64,1024]{4,3,2,1,0:T(8,128)(2,1)S(1)} custom-call(s32[3]{0:T(128)S(1)} %pad_add_fusion.refs_0_, bf16[2,2,2,4,64,256]{5,4,3,2,1,0:T(8,128)(2,1)S(1)} %collective-permute-done.17.refs_1_, bf16[2,2,2,4,64,256]{5,4,3,2,1,0:T(8,128)(2,1)S(1)} %collective-permute-done.18.refs_2_, f32[8,256]{1,0:T(8,128)S(1)} %broadcast_select_fusion.1.refs_3_, ...), custom_call_target="tpu_custom_call" | custom-call | tf_op jit(solution)/shard_map/pallas_call | solution.py:391
  136.4 3.5 %shard_map.129 = bf16[2,2,2,64,1024]{4,3,2,1,0:T(8,128)(2,1)S(1)} custom-call(s32[3]{0:T(128)S(1)} %pad_add_fusion.refs_0_, bf16[2,2,2,4,64,256]{5,4,3,2,1,0:T(8,128)(2,1)S(1)} %collective-permute-done.24.refs_1_, bf16[2,2,2,4,64,256]{5,4,3,2,1,0:T(8,128)(2,1)S(1)} %collective-permute-done.25.refs_2_, f32[8,256]{1,0:T(8,128)S(1)} %broadcast_select_fusion.1.refs_3_, ...), custom_call_target="tpu_custom_call" | custom-call | tf_op jit(solution)/shard_map/pallas_call | solution.py:391
  140.4 3.4 %shard_map.128 = bf16[2,2,2,64,1024]{4,3,2,1,0:T(8,128)(2,1)S(1)} custom-call(s32[3]{0:T(128)S(1)} %pad_add_fusion.refs_0_, bf16[2,2,2,4,64,256]{5,4,3,2,1,0:T(8,128)(2,1)S(1)} %pad_maximum_fusion.3.refs_1_, bf16[2,2,2,4,64,256]{5,4,3,2,1,0:T(8,128)(2,1)S(1)} %collective-permute-done.16.refs_2_, f32[8,256]{1,0:T(8,128)S(1)} %broadcast_select_fusion.1.refs_3_, ...), custom_call_target="tpu_custom_call" | custom-call | tf_op jit(solution)/shard_map/pallas_call | solution.py:391
  143.8 3.4 %shard_map.130 = bf16[2,2,2,64,1024]{4,3,2,1,0:T(8,128)(2,1)S(1)} custom-call(s32[3]{0:T(128)S(1)} %pad_add_fusion.refs_0_, bf16[2,2,2,4,64,256]{5,4,3,2,1,0:T(8,128)(2,1)S(1)} %pad_maximum_fusion.4.refs_1_, bf16[2,2,2,4,64,256]{5,4,3,2,1,0:T(8,128)(2,1)S(1)} %collective-permute-done.23.refs_2_, f32[8,256]{1,0:T(8,128)S(1)} %broadcast_select_fusion.1.refs_3_, ...), custom_call_target="tpu_custom_call" | custom-call | tf_op jit(solution)/shard_map/pallas_call | solution.py:391
  147.2 3.4 %shard_map.131 = bf16[2,2,2,64,1024]{4,3,2,1,0:T(8,128)(2,1)S(1)} custom-call(s32[3]{0:T(128)S(1)} %pad_add_fusion.refs_0_, bf16[2,2,2,4,64,256]{5,4,3,2,1,0:T(8,128)(2,1)S(1)} %collective-permute-done.17.refs_1_, bf16[2,2,2,4,64,256]{5,4,3,2,1,0:T(8,128)(2,1)S(1)} %collective-permute-done.18.refs_2_, f32[8,256]{1,0:T(8,128)S(1)} %broadcast_select_fusion.1.refs_3_, ...), custom_call_target="tpu_custom_call" | custom-call | tf_op jit(solution)/shard_map/pallas_call | solution.py:391
  150.8 0.9 collective-permute-start.28
  151.7 3.4 %shard_map.133 = bf16[2,2,2,64,1024]{4,3,2,1,0:T(8,128)(2,1)S(1)} custom-call(s32[3]{0:T(128)S(1)} %pad_add_fusion.refs_0_, bf16[2,2,2,4,64,256]{5,4,3,2,1,0:T(8,128)(2,1)S(1)} %collective-permute-done.24.refs_1_, bf16[2,2,2,4,64,256]{5,4,3,2,1,0:T(8,128)(2,1)S(1)} %collective-permute-done.25.refs_2_, f32[8,256]{1,0:T(8,128)S(1)} %broadcast_select_fusion.1.refs_3_, ...), custom_call_target="tpu_custom_call" | custom-call | tf_op jit(solution)/shard_map/pallas_call | solution.py:391
  155.3 1.4 collective-permute-start.33
  156.7 3.4 %shard_map.132 = bf16[2,2,2,64,1024]{4,3,2,1,0:T(8,128)(2,1)S(1)} custom-call(s32[3]{0:T(128)S(1)} %pad_add_fusion.refs_0_, bf16[2,2,2,4,64,256]{5,4,3,2,1,0:T(8,128)(2,1)S(1)} %pad_maximum_fusion.3.refs_1_, bf16[2,2,2,4,64,256]{5,4,3,2,1,0:T(8,128)(2,1)S(1)} %collective-permute-done.16.refs_2_, f32[8,256]{1,0:T(8,128)S(1)} %broadcast_select_fusion.1.refs_3_, ...), custom_call_target="tpu_custom_call" | custom-call | tf_op jit(solution)/shard_map/pallas_call | solution.py:391
  160.1 16.2 %collective-permute-done.28 = bf16[2,2,2,64,1024]{4,3,2,1,0:T(8,128)(2,1)S(1)} collective-permute-done((bf16[2,2,2,64,1024]{4,3,2,1,0:T(8,128)(2,1)S(1)}, bf16[2,2,2,64,1024]{4,3,2,1,0:T(8,128)(2,1)S(1)}, u32[]{:S(2)}, u32[]{:S(2)}) %collective-permute-start.28) | collective-permute-done | bytes 1048608 | tf_op jit(solution)/shard_map/ppermute | solution.py:143
  176.9 0.9 slice.117
  177.8 2.0 collective-permute-start.29
  179.9 3.4 %shard_map.134 = bf16[2,2,2,64,1024]{4,3,2,1,0:T(8,128)(2,1)S(1)} custom-call(s32[3]{0:T(128)S(1)} %pad_add_fusion.refs_0_, bf16[2,2,2,4,64,256]{5,4,3,2,1,0:T(8,128)(2,1)S(1)} %pad_maximum_fusion.4.refs_1_, bf16[2,2,2,4,64,256]{5,4,3,2,1,0:T(8,128)(2,1)S(1)} %collective-permute-done.23.refs_2_, f32[8,256]{1,0:T(8,128)S(1)} %broadcast_select_fusion.1.refs_3_, ...), custom_call_target="tpu_custom_call" | custom-call | tf_op jit(solution)/shard_map/pallas_call | solution.py:391
  183.8 1.0 copy-done.5
  184.8 0.8 slice.123
  185.9 6.2 %collective-permute-done.29 = bf16[1,2,2,64,1024]{4,3,2,1,0:T(8,128)(2,1)} collective-permute-done((bf16[1,2,2,64,1024]{4,3,2,1,0:T(8,128)(2,1)}, bf16[1,2,2,64,1024]{4,3,2,1,0:T(8,128)(2,1)}, u32[]{:S(2)}, u32[]{:S(2)}) %collective-permute-start.29) | collective-permute-done | bytes 524320 | tf_op jit(solution)/shard_map/ppermute | solution.py:143
  192.1 1.2 add_convert_fusion.3
  193.4 5.5 %collective-permute-done.34 = bf16[1,2,2,64,1024]{4,3,2,1,0:T(8,128)(2,1)} collective-permute-done((bf16[1,2,2,64,1024]{4,3,2,1,0:T(8,128)(2,1)}, bf16[1,2,2,64,1024]{4,3,2,1,0:T(8,128)(2,1)}, u32[]{:S(2)}, u32[]{:S(2)}) %collective-permute-start.34) | collective-permute-done | bytes 524320 | tf_op jit(solution)/shard_map/ppermute | solution.py:143
  199.0 1.2 add_convert_fusion.2
  201.0 2.1 collective-permute-start.31
  203.1 6.6 %collective-permute-done.35 = bf16[1,2,64,1024]{3,2,1,0:T(8,128)(2,1)S(1)} collective-permute-done((bf16[1,2,64,1024]{3,2,1,0:T(8,128)(2,1)S(1)}, bf16[1,2,64,1024]{3,2,1,0:T(8,128)(2,1)S(1)}, u32[]{:S(2)}, u32[]{:S(2)}) %collective-permute-start.35) | collective-permute-done | bytes 262176 | tf_op jit(solution)/shard_map/ppermute | solution.py:143
  210.0 7.1 %collective-permute-done.36 = bf16[1,64,1024]{2,1,0:T(8,128)(2,1)S(1)} collective-permute-done((bf16[1,64,1024]{2,1,0:T(8,128)(2,1)S(1)}, bf16[1,64,1024]{2,1,0:T(8,128)(2,1)S(1)}, u32[]{:S(2)}, u32[]{:S(2)}) %collective-permute-start.36) | collective-permute-done | bytes 131104 | tf_op jit(solution)/shard_map/ppermute | solution.py:143
  217.2 0.8 add_convert_fusion.4
  (101 shorter events, 14.3 us)
Async XLA Ops:
  0.0 56.7 %copy-start = (bf16[2048,512]{1,0:T(8,128)(2,1)S(1)}, bf16[2048,512]{1,0:T(8,128)(2,1)}, u32[]{:S(2)}) copy-start(bf16[2048,512]{1,0:T(8,128)(2,1)} %param.17) | copy-start | bytes 6291460
  1.8 29.8 %collective-permute-start.3 = (bf16[128,256]{1,0:T(8,128)(2,1)}, bf16[128,256]{1,0:T(8,128)(2,1)S(1)}, u32[]{:S(2)}, u32[]{:S(2)}) collective-permute-start(bf16[128,256]{1,0:T(8,128)(2,1)} %get-tuple-element.28), channel_id=1, source_target_pairs={{0,2},{2,0},{4,6},{6,4},{1,3},{3,1},{5,7},{7,5},{8,10},{10,8},{12,... | collective-permute-start | bytes 196616 | tf_op jit(solution)/shard_map/ppermute | solution.py:143
  4.7 26.9 %collective-permute-start.4 = (bf16[128,256]{1,0:T(8,128)(2,1)}, bf16[128,256]{1,0:T(8,128)(2,1)}, u32[]{:S(2)}, u32[]{:S(2)}) collective-permute-start(bf16[128,256]{1,0:T(8,128)(2,1)} %get-tuple-element.30), channel_id=1, source_target_pairs={{0,4},{2,6},{4,0},{6,2},{1,5},{3,7},{5,1},{7,3},{8,12},{10,14},{12... | collective-permute-start | bytes 196616 | tf_op jit(solution)/shard_map/ppermute | solution.py:143
  6.3 25.4 %collective-permute-start.5 = (bf16[128,256]{1,0:T(8,128)(2,1)}, bf16[128,256]{1,0:T(8,128)(2,1)}, u32[]{:S(2)}, u32[]{:S(2)}) collective-permute-start(bf16[128,256]{1,0:T(8,128)(2,1)} %get-tuple-element.27), channel_id=1, source_target_pairs={{0,6},{2,4},{4,2},{6,0},{1,7},{3,5},{5,3},{7,1},{8,14},{10,12},{12... | collective-permute-start | bytes 196616 | tf_op jit(solution)/shard_map/ppermute | solution.py:143
  6.3 19.2 %collective-permute-start.2 = (f32[1,1024]{1,0:T(1,128)}, f32[1,1024]{1,0:T(1,128)}, u32[]{:S(2)}, u32[]{:S(2)}) collective-permute-start(f32[1,1024]{1,0:T(1,128)} %bitcast.148), channel_id=1, source_target_pairs={{0,1},{1,0},{2,3},{3,2},{4,5},{5,4},{6,7},{7,6},{8,9},{9,8},{10,11... | collective-permute-start | bytes 12296 | tf_op jit(solution)/shard_map/ppermute | solution.py:143
  9.2 15.7 %collective-permute-start = (bf16[1,128,512]{2,1,0:T(8,128)(2,1)S(1)}, bf16[1,128,512]{2,1,0:T(8,128)(2,1)S(1)}, u32[]{:S(2)}, u32[]{:S(2)}) collective-permute-start(bf16[1,128,512]{2,1,0:T(8,128)(2,1)S(1)} %maximum_bitcast_fusion.4), channel_id=1, source_target_pairs={{0,16},{8,24},{16,0},{24,8},{1,17},{9,25},{17,1},{25,9},{2,18},{10... | collective-permute-start | bytes 393224 | tf_op jit(solution)/shard_map/ppermute | solution.py:143
  13.2 18.4 %all-to-all-start = ((f32[16,1,128]{2,1,0:T(1,128)}), f32[16,1,128]{2,1,0:T(1,128)S(1)}, u32[]{:S(2)}, u32[]{:S(2)}) async-start(f32[16,1,128]{2,1,0:T(1,128)} %bitcast.11), calls=%async_computation | async-start | bytes 16384 | tf_op jit(solution)/shard_map/all_to_all | solution.py:301
  18.3 5.3 %copy-start.7 = (bf16[1,128,2048]{2,1,0:T(8,128)(2,1)S(1)}, bf16[1,128,2048]{2,1,0:T(8,128)(2,1)}, u32[]{:S(2)}) copy-start(bf16[1,128,2048]{2,1,0:T(8,128)(2,1)} %param.13) | copy-start | bytes 1572868
  25.0 4.5 %collective-permute-start.1 = (bf16[2,128,512]{2,1,0:T(8,128)(2,1)S(1)}, bf16[2,128,512]{2,1,0:T(8,128)(2,1)S(1)}, u32[]{:S(2)}, u32[]{:S(2)}) collective-permute-start(bf16[2,128,512]{2,1,0:T(8,128)(2,1)S(1)} %pad_maximum_fusion.6), channel_id=1, source_target_pairs={{0,8},{8,0},{16,24},{24,16},{1,9},{9,1},{17,25},{25,17},{2,10},{10... | collective-permute-start | bytes 786440 | tf_op jit(solution)/shard_map/ppermute | solution.py:143
  31.7 0.8 copy-start.9
  35.3 8.6 %collective-permute-start.10 = (bf16[128,1024]{0,1:T(8,128)(2,1)S(1)}, bf16[128,1024]{0,1:T(8,128)(2,1)S(1)}, u32[]{:S(2)}, u32[]{:S(2)}) collective-permute-start(bf16[128,1024]{0,1:T(8,128)(2,1)S(1)} %get-tuple-element.24), channel_id=1, source_target_pairs={{0,4},{2,6},{4,0},{6,2},{1,5},{3,7},{5,1},{7,3},{8,12},{10,14},{12... | collective-permute-start | bytes 786440 | tf_op jit(solution)/shard_map/ppermute | solution.py:143
  37.0 10.1 %collective-permute-start.6 = (bf16[128,1024]{0,1:T(8,128)(2,1)S(1)}, bf16[128,1024]{0,1:T(8,128)(2,1)S(1)}, u32[]{:S(2)}, u32[]{:S(2)}) collective-permute-start(bf16[128,1024]{0,1:T(8,128)(2,1)S(1)} %get-tuple-element.23), channel_id=1, source_target_pairs={{0,2},{2,0},{4,6},{6,4},{1,3},{3,1},{5,7},{7,5},{8,10},{10,8},{12,... | collective-permute-start | bytes 786440 | tf_op jit(solution)/shard_map/ppermute | solution.py:143
  38.5 13.4 %collective-permute-start.9 = (bf16[128,1024]{0,1:T(8,128)(2,1)S(1)}, bf16[128,1024]{0,1:T(8,128)(2,1)}, u32[]{:S(2)}, u32[]{:S(2)}) collective-permute-start(bf16[128,1024]{0,1:T(8,128)(2,1)S(1)} %get-tuple-element.24), channel_id=1, source_target_pairs={{0,2},{2,0},{4,6},{6,4},{1,3},{3,1},{5,7},{7,5},{8,10},{10,8},{12,... | collective-permute-start | bytes 786440 | tf_op jit(solution)/shard_map/ppermute | solution.py:143
  43.9 14.3 %copy-start.10 = (bf16[128,1024]{0,1:T(8,128)(2,1)}, bf16[128,1024]{0,1:T(8,128)(2,1)S(1)}, u32[]{:S(2)}) copy-start(bf16[128,1024]{0,1:T(8,128)(2,1)S(1)} %collective-permute-done.10) | copy-start | bytes 786436
  43.9 12.8 %collective-permute-start.11 = (bf16[128,1024]{0,1:T(8,128)(2,1)S(1)}, bf16[128,1024]{0,1:T(8,128)(2,1)}, u32[]{:S(2)}, u32[]{:S(2)}) collective-permute-start(bf16[128,1024]{0,1:T(8,128)(2,1)S(1)} %collective-permute-done.10), channel_id=1, source_target_pairs={{0,2},{2,0},{4,6},{6,4},{1,3},{3,1},{5,7},{7,5},{8,10},{10,8},{12,... | collective-permute-start | bytes 786440 | tf_op jit(solution)/shard_map/ppermute | solution.py:143
  45.6 12.6 %collective-permute-start.7 = (bf16[128,1024]{0,1:T(8,128)(2,1)S(1)}, bf16[128,1024]{0,1:T(8,128)(2,1)}, u32[]{:S(2)}, u32[]{:S(2)}) collective-permute-start(bf16[128,1024]{0,1:T(8,128)(2,1)S(1)} %get-tuple-element.23), channel_id=1, source_target_pairs={{0,4},{2,6},{4,0},{6,2},{1,5},{3,7},{5,1},{7,3},{8,12},{10,14},{12... | collective-permute-start | bytes 786440 | tf_op jit(solution)/shard_map/ppermute | solution.py:143
  47.1 11.7 %collective-permute-start.8 = (bf16[128,1024]{0,1:T(8,128)(2,1)S(1)}, bf16[128,1024]{0,1:T(8,128)(2,1)}, u32[]{:S(2)}, u32[]{:S(2)}) collective-permute-start(bf16[128,1024]{0,1:T(8,128)(2,1)S(1)} %collective-permute-done.6), channel_id=1, source_target_pairs={{0,4},{2,6},{4,0},{6,2},{1,5},{3,7},{5,1},{7,3},{8,12},{10,14},{12... | collective-permute-start | bytes 786440 | tf_op jit(solution)/shard_map/ppermute | solution.py:143
  61.0 7.2 %collective-permute-start.12 = (bf16[512,256]{1,0:T(8,128)(2,1)}, bf16[512,256]{1,0:T(8,128)(2,1)}, u32[]{:S(2)}, u32[]{:S(2)}) collective-permute-start(bf16[512,256]{1,0:T(8,128)(2,1)} %fusion.17), channel_id=1, source_target_pairs={{0,1},{1,0},{2,3},{3,2},{4,5},{5,4},{6,7},{7,6},{8,9},{9,8},{10,11... | collective-permute-start | bytes 786440 | tf_op jit(solution)/shard_map/ppermute | solution.py:143
  71.5 10.4 %collective-permute-start.13 = (bf16[1,4,64,256]{3,2,1,0:T(8,128)(2,1)S(1)}, bf16[1,4,64,256]{3,2,1,0:T(8,128)(2,1)S(1)}, u32[]{:S(2)}, u32[]{:S(2)}) collective-permute-start(bf16[1,4,64,256]{3,2,1,0:T(8,128)(2,1)S(1)} %get-tuple-element.31), channel_id=1, source_target_pairs={{0,16},{8,24},{16,0},{24,8},{1,17},{9,25},{17,1},{25,9},{2,18},{10... | collective-permute-start | bytes 393224 | tf_op jit(solution)/shard_map/ppermute | solution.py:143
  73.9 10.1 %collective-permute-start.20 = (bf16[1,4,64,256]{3,2,1,0:T(8,128)(2,1)S(1)}, bf16[1,4,64,256]{3,2,1,0:T(8,128)(2,1)S(1)}, u32[]{:S(2)}, u32[]{:S(2)}) collective-permute-start(bf16[1,4,64,256]{3,2,1,0:T(8,128)(2,1)S(1)} %get-tuple-element.32), channel_id=1, source_target_pairs={{0,16},{8,24},{16,0},{24,8},{1,17},{9,25},{17,1},{25,9},{2,18},{10... | collective-permute-start | bytes 393224 | tf_op jit(solution)/shard_map/ppermute | solution.py:143
  82.0 9.2 %collective-permute-start.14 = (bf16[1,2,4,64,256]{4,3,2,1,0:T(8,128)(2,1)S(1)}, bf16[1,2,4,64,256]{4,3,2,1,0:T(8,128)(2,1)S(1)}, u32[]{:S(2)}, u32[]{:S(2)}) collective-permute-start(bf16[1,2,4,64,256]{4,3,2,1,0:T(8,128)(2,1)S(1)} %maximum_bitcast_fusion.2), channel_id=1, source_target_pairs={{0,1},{1,0},{2,3},{3,2},{4,5},{5,4},{6,7},{7,6},{8,9},{9,8},{10,11... | collective-permute-start | bytes 786440 | tf_op jit(solution)/shard_map/ppermute | solution.py:143
  84.1 11.1 %collective-permute-start.21 = (bf16[1,2,4,64,256]{4,3,2,1,0:T(8,128)(2,1)S(1)}, bf16[1,2,4,64,256]{4,3,2,1,0:T(8,128)(2,1)S(1)}, u32[]{:S(2)}, u32[]{:S(2)}) collective-permute-start(bf16[1,2,4,64,256]{4,3,2,1,0:T(8,128)(2,1)S(1)} %maximum_bitcast_fusion.3), channel_id=1, source_target_pairs={{0,1},{1,0},{2,3},{3,2},{4,5},{5,4},{6,7},{7,6},{8,9},{9,8},{10,11... | collective-permute-start | bytes 786440 | tf_op jit(solution)/shard_map/ppermute | solution.py:143
  91.3 11.1 %collective-permute-start.15 = (bf16[1,2,2,4,64,256]{5,4,3,2,1,0:T(8,128)(2,1)S(1)}, bf16[1,2,2,4,64,256]{5,4,3,2,1,0:T(8,128)(2,1)S(1)}, u32[]{:S(2)}, u32[]{:S(2)}) collective-permute-start(bf16[1,2,2,4,64,256]{5,4,3,2,1,0:T(8,128)(2,1)S(1)} %maximum_bitcast_fusion), channel_id=1, source_target_pairs={{0,2},{2,0},{4,6},{6,4},{1,3},{3,1},{5,7},{7,5},{8,10},{10,8},{12,... | collective-permute-start | bytes 1572872 | tf_op jit(solution)/shard_map/ppermute | solution.py:143
  95.2 37.6 %copy-start.2 = (bf16[1,384,2048]{2,1,0:T(8,128)(2,1)S(1)}, bf16[1,384,2048]{2,1,0:T(8,128)(2,1)}, u32[]{:S(2)}) copy-start(bf16[1,384,2048]{2,1,0:T(8,128)(2,1)} %param.21) | copy-start | bytes 4718596
  95.3 37.5 %copy-start.1 = (bf16[2048,768]{1,0:T(8,128)(2,1)S(1)}, bf16[2048,768]{1,0:T(8,128)(2,1)}, u32[]{:S(2)}) copy-start(bf16[2048,768]{1,0:T(8,128)(2,1)} %pad_maximum_fusion.refs_5_.refs_7_) | copy-start | bytes 9437188
  95.3 14.9 %collective-permute-start.22 = (bf16[1,2,2,4,64,256]{5,4,3,2,1,0:T(8,128)(2,1)S(1)}, bf16[1,2,2,4,64,256]{5,4,3,2,1,0:T(8,128)(2,1)S(1)}, u32[]{:S(2)}, u32[]{:S(2)}) collective-permute-start(bf16[1,2,2,4,64,256]{5,4,3,2,1,0:T(8,128)(2,1)S(1)} %maximum_bitcast_fusion.1), channel_id=1, source_target_pairs={{0,4},{2,6},{4,0},{6,2},{1,5},{3,7},{5,1},{7,3},{8,12},{10,14},{12... | collective-permute-start | bytes 1572872 | tf_op jit(solution)/shard_map/ppermute | solution.py:143
  102.4 27.7 %collective-permute-start.16 = (bf16[2,2,2,4,64,256]{5,4,3,2,1,0:T(8,128)(2,1)S(1)}, bf16[2,2,2,4,64,256]{5,4,3,2,1,0:T(8,128)(2,1)S(1)}, u32[]{:S(2)}, u32[]{:S(2)}) collective-permute-start(bf16[2,2,2,4,64,256]{5,4,3,2,1,0:T(8,128)(2,1)S(1)} %pad_maximum_fusion.3.refs_1_), channel_id=1, source_target_pairs={{0,4},{2,6},{4,0},{6,2},{1,5},{3,7},{5,1},{7,3},{8,12},{10,14},{12... | collective-permute-start | bytes 3145736 | tf_op jit(solution)/shard_map/ppermute | solution.py:143
  110.2 20.6 %collective-permute-start.23 = (bf16[2,2,2,4,64,256]{5,4,3,2,1,0:T(8,128)(2,1)S(1)}, bf16[2,2,2,4,64,256]{5,4,3,2,1,0:T(8,128)(2,1)S(1)}, u32[]{:S(2)}, u32[]{:S(2)}) collective-permute-start(bf16[2,2,2,4,64,256]{5,4,3,2,1,0:T(8,128)(2,1)S(1)} %pad_maximum_fusion.4.refs_1_), channel_id=1, source_target_pairs={{0,2},{2,0},{4,6},{6,4},{1,3},{3,1},{5,7},{7,5},{8,10},{10,8},{12,... | collective-permute-start | bytes 3145736 | tf_op jit(solution)/shard_map/ppermute | solution.py:143
  112.3 18.5 %collective-permute-start.17 = (bf16[2,2,2,4,64,256]{5,4,3,2,1,0:T(8,128)(2,1)S(1)}, bf16[2,2,2,4,64,256]{5,4,3,2,1,0:T(8,128)(2,1)S(1)}, u32[]{:S(2)}, u32[]{:S(2)}) collective-permute-start(bf16[2,2,2,4,64,256]{5,4,3,2,1,0:T(8,128)(2,1)S(1)} %pad_maximum_fusion.3.refs_1_), channel_id=1, source_target_pairs={{0,8},{8,0},{16,24},{24,16},{1,9},{9,1},{17,25},{25,17},{2,10},{10... | collective-permute-start | bytes 3145736 | tf_op jit(solution)/shard_map/ppermute | solution.py:143
  130.1 2.7 %collective-permute-start.18 = (bf16[2,2,2,4,64,256]{5,4,3,2,1,0:T(8,128)(2,1)S(1)}, bf16[2,2,2,4,64,256]{5,4,3,2,1,0:T(8,128)(2,1)S(1)}, u32[]{:S(2)}, u32[]{:S(2)}) collective-permute-start(bf16[2,2,2,4,64,256]{5,4,3,2,1,0:T(8,128)(2,1)S(1)} %collective-permute-done.16.refs_2_), channel_id=1, source_target_pairs={{0,8},{8,0},{16,24},{24,16},{1,9},{9,1},{17,25},{25,17},{2,10},{10... | collective-permute-start | bytes 3145736 | tf_op jit(solution)/shard_map/ppermute | solution.py:143
  130.1 6.3 %collective-permute-start.24 = (bf16[2,2,2,4,64,256]{5,4,3,2,1,0:T(8,128)(2,1)S(1)}, bf16[2,2,2,4,64,256]{5,4,3,2,1,0:T(8,128)(2,1)S(1)}, u32[]{:S(2)}, u32[]{:S(2)}) collective-permute-start(bf16[2,2,2,4,64,256]{5,4,3,2,1,0:T(8,128)(2,1)S(1)} %pad_maximum_fusion.4.refs_1_), channel_id=1, source_target_pairs={{0,8},{8,0},{16,24},{24,16},{1,9},{9,1},{17,25},{25,17},{2,10},{10... | collective-permute-start | bytes 3145736 | tf_op jit(solution)/shard_map/ppermute | solution.py:143
  130.8 5.6 %collective-permute-start.25 = (bf16[2,2,2,4,64,256]{5,4,3,2,1,0:T(8,128)(2,1)S(1)}, bf16[2,2,2,4,64,256]{5,4,3,2,1,0:T(8,128)(2,1)S(1)}, u32[]{:S(2)}, u32[]{:S(2)}) collective-permute-start(bf16[2,2,2,4,64,256]{5,4,3,2,1,0:T(8,128)(2,1)S(1)} %collective-permute-done.23.refs_2_), channel_id=1, source_target_pairs={{0,8},{8,0},{16,24},{24,16},{1,9},{9,1},{17,25},{25,17},{2,10},{10... | collective-permute-start | bytes 3145736 | tf_op jit(solution)/shard_map/ppermute | solution.py:143
  136.2 4.2 %collective-permute-start.19 = (bf16[2,2,2,64,1024]{4,3,2,1,0:T(8,128)(2,1)S(1)}, bf16[2,2,2,64,1024]{4,3,2,1,0:T(8,128)(2,1)S(1)}, u32[]{:S(2)}, u32[]{:S(2)}) collective-permute-start(bf16[2,2,2,64,1024]{4,3,2,1,0:T(8,128)(2,1)S(1)} %shard_map.127), channel_id=1, source_target_pairs={{0,8},{8,0},{16,24},{24,16},{1,9},{9,1},{17,25},{25,17},{2,10},{10... | collective-permute-start | bytes 3145736 | tf_op jit(solution)/shard_map/ppermute | solution.py:143
  139.9 3.9 %collective-permute-start.26 = (bf16[2,2,2,64,1024]{4,3,2,1,0:T(8,128)(2,1)S(1)}, bf16[2,2,2,64,1024]{4,3,2,1,0:T(8,128)(2,1)S(1)}, u32[]{:S(2)}, u32[]{:S(2)}) collective-permute-start(bf16[2,2,2,64,1024]{4,3,2,1,0:T(8,128)(2,1)S(1)} %shard_map.129), channel_id=1, source_target_pairs={{0,8},{8,0},{16,24},{24,16},{1,9},{9,1},{17,25},{25,17},{2,10},{10... | collective-permute-start | bytes 3145736 | tf_op jit(solution)/shard_map/ppermute | solution.py:143
  150.6 6.1 %collective-permute-start.27 = (bf16[2,2,2,64,1024]{4,3,2,1,0:T(8,128)(2,1)S(1)}, bf16[2,2,2,64,1024]{4,3,2,1,0:T(8,128)(2,1)S(1)}, u32[]{:S(2)}, u32[]{:S(2)}) collective-permute-start(bf16[2,2,2,64,1024]{4,3,2,1,0:T(8,128)(2,1)S(1)} %shard_map.131), channel_id=1, source_target_pairs={{0,8},{8,0},{16,24},{24,16},{1,9},{9,1},{17,25},{25,17},{2,10},{10... | collective-permute-start | bytes 3145736 | tf_op jit(solution)/shard_map/ppermute | solution.py:143
  150.8 25.4 %collective-permute-start.28 = (bf16[2,2,2,64,1024]{4,3,2,1,0:T(8,128)(2,1)S(1)}, bf16[2,2,2,64,1024]{4,3,2,1,0:T(8,128)(2,1)S(1)}, u32[]{:S(2)}, u32[]{:S(2)}) collective-permute-start(bf16[2,2,2,64,1024]{4,3,2,1,0:T(8,128)(2,1)S(1)} %shard_map.128), channel_id=1, source_target_pairs={{0,4},{2,6},{4,0},{6,2},{1,5},{3,7},{5,1},{7,3},{8,12},{10,14},{12... | collective-permute-start | bytes 3145736 | tf_op jit(solution)/shard_map/ppermute | solution.py:143
  155.1 24.8 %collective-permute-start.32 = (bf16[2,2,2,64,1024]{4,3,2,1,0:T(8,128)(2,1)S(1)}, bf16[2,2,2,64,1024]{4,3,2,1,0:T(8,128)(2,1)S(1)}, u32[]{:S(2)}, u32[]{:S(2)}) collective-permute-start(bf16[2,2,2,64,1024]{4,3,2,1,0:T(8,128)(2,1)S(1)} %shard_map.133), channel_id=1, source_target_pairs={{0,8},{8,0},{16,24},{24,16},{1,9},{9,1},{17,25},{25,17},{2,10},{10... | collective-permute-start | bytes 3145736 | tf_op jit(solution)/shard_map/ppermute | solution.py:143
  155.3 28.1 %collective-permute-start.33 = (bf16[2,2,2,64,1024]{4,3,2,1,0:T(8,128)(2,1)S(1)}, bf16[2,2,2,64,1024]{4,3,2,1,0:T(8,128)(2,1)S(1)}, u32[]{:S(2)}, u32[]{:S(2)}) collective-permute-start(bf16[2,2,2,64,1024]{4,3,2,1,0:T(8,128)(2,1)S(1)} %shard_map.130), channel_id=1, source_target_pairs={{0,2},{2,0},{4,6},{6,4},{1,3},{3,1},{5,7},{7,5},{8,10},{10,8},{12,... | collective-permute-start | bytes 3145736 | tf_op jit(solution)/shard_map/ppermute | solution.py:143
  176.9 6.4 %copy-start.3 = (bf16[2,2,2,64,1024]{4,3,2,1,0:T(8,128)(2,1)}, bf16[2,2,2,64,1024]{4,3,2,1,0:T(8,128)(2,1)S(1)}, u32[]{:S(2)}) copy-start(bf16[2,2,2,64,1024]{4,3,2,1,0:T(8,128)(2,1)S(1)} %add_convert_fusion.1) | copy-start | bytes 3145732
  177.8 14.2 %collective-permute-start.29 = (bf16[1,2,2,64,1024]{4,3,2,1,0:T(8,128)(2,1)}, bf16[1,2,2,64,1024]{4,3,2,1,0:T(8,128)(2,1)}, u32[]{:S(2)}, u32[]{:S(2)}) collective-permute-start(bf16[1,2,2,64,1024]{4,3,2,1,0:T(8,128)(2,1)} %slice.117), channel_id=1, source_target_pairs={{0,2},{2,0},{4,6},{6,4},{1,3},{3,1},{5,7},{7,5},{8,10},{10,8},{12,... | collective-permute-start | bytes 1572872 | tf_op jit(solution)/shard_map/ppermute | solution.py:143
  183.3 8.8 %copy-start.4 = (bf16[2,2,2,64,1024]{4,3,2,1,0:T(8,128)(2,1)S(1)}, bf16[2,2,2,64,1024]{4,3,2,1,0:T(8,128)(2,1)}, u32[]{:S(2)}) copy-start(bf16[2,2,2,64,1024]{4,3,2,1,0:T(8,128)(2,1)} %copy-done.3) | copy-start | bytes 3145732
  183.8 1.0 copy-start.5
  185.6 13.4 %collective-permute-start.34 = (bf16[1,2,2,64,1024]{4,3,2,1,0:T(8,128)(2,1)}, bf16[1,2,2,64,1024]{4,3,2,1,0:T(8,128)(2,1)}, u32[]{:S(2)}, u32[]{:S(2)}) collective-permute-start(bf16[1,2,2,64,1024]{4,3,2,1,0:T(8,128)(2,1)} %slice.123), channel_id=1, source_target_pairs={{0,4},{2,6},{4,0},{6,2},{1,5},{3,7},{5,1},{7,3},{8,12},{10,14},{12... | collective-permute-start | bytes 1572872 | tf_op jit(solution)/shard_map/ppermute | solution.py:143
  185.9 13.1 %copy-start.6 = (bf16[2,2,2,64,1024]{4,3,2,1,0:T(8,128)(2,1)S(1)}, bf16[2,2,2,64,1024]{4,3,2,1,0:T(8,128)(2,1)}, u32[]{:S(2)}) copy-start(bf16[2,2,2,64,1024]{4,3,2,1,0:T(8,128)(2,1)} %copy-done.5) | copy-start | bytes 3145732
  193.4 23.8 %copy-start.8 = (bf16[1,128,2048]{2,1,0:T(8,128)(2,1)S(1)}, bf16[1,128,2048]{2,1,0:T(8,128)(2,1)}, u32[]{:S(2)}) copy-start(bf16[1,128,2048]{2,1,0:T(8,128)(2,1)} %param.16) | copy-start | bytes 1572868
  193.4 7.5 %collective-permute-start.30 = (bf16[1,2,64,1024]{3,2,1,0:T(8,128)(2,1)S(1)}, bf16[1,2,64,1024]{3,2,1,0:T(8,128)(2,1)S(1)}, u32[]{:S(2)}, u32[]{:S(2)}) collective-permute-start(bf16[1,2,64,1024]{3,2,1,0:T(8,128)(2,1)S(1)} %slice_bitcast_fusion.2), channel_id=1, source_target_pairs={{0,1},{1,0},{2,3},{3,2},{4,5},{5,4},{6,7},{7,6},{8,9},{9,8},{10,11... | collective-permute-start | bytes 786440 | tf_op jit(solution)/shard_map/ppermute | solution.py:143
  200.3 9.5 %collective-permute-start.35 = (bf16[1,2,64,1024]{3,2,1,0:T(8,128)(2,1)S(1)}, bf16[1,2,64,1024]{3,2,1,0:T(8,128)(2,1)S(1)}, u32[]{:S(2)}, u32[]{:S(2)}) collective-permute-start(bf16[1,2,64,1024]{3,2,1,0:T(8,128)(2,1)S(1)} %slice_bitcast_fusion), channel_id=1, source_target_pairs={{0,1},{1,0},{2,3},{3,2},{4,5},{5,4},{6,7},{7,6},{8,9},{9,8},{10,11... | collective-permute-start | bytes 786440 | tf_op jit(solution)/shard_map/ppermute | solution.py:143
  201.0 9.0 %collective-permute-start.31 = (bf16[1,64,1024]{2,1,0:T(8,128)(2,1)S(1)}, bf16[1,64,1024]{2,1,0:T(8,128)(2,1)S(1)}, u32[]{:S(2)}, u32[]{:S(2)}) collective-permute-start(bf16[1,64,1024]{2,1,0:T(8,128)(2,1)S(1)} %slice_bitcast_fusion.6), channel_id=1, source_target_pairs={{0,16},{8,24},{16,0},{24,8},{1,17},{9,25},{17,1},{25,9},{2,18},{10... | collective-permute-start | bytes 393224 | tf_op jit(solution)/shard_map/ppermute | solution.py:143
  209.8 7.3 %collective-permute-start.36 = (bf16[1,64,1024]{2,1,0:T(8,128)(2,1)S(1)}, bf16[1,64,1024]{2,1,0:T(8,128)(2,1)S(1)}, u32[]{:S(2)}, u32[]{:S(2)}) collective-permute-start(bf16[1,64,1024]{2,1,0:T(8,128)(2,1)S(1)} %slice_bitcast_fusion.4), channel_id=1, source_target_pairs={{0,16},{8,24},{16,0},{24,8},{1,17},{9,25},{17,1},{25,9},{2,18},{10... | collective-permute-start | bytes 393224 | tf_op jit(solution)/shard_map/ppermute | solution.py:143
where the time goes:
time: 219 us; the launch traced here: 218 us
  waiting for transfers between devices  113 us (52%)
  starting transfers between devices  39 us (18%)
  Pallas kernels  27.4 us (13%)
  other arithmetic  19.9 us (9%)
  local copies, waits for them, and re-layouts  9.97 us (5%)
  matrix products  8.15 us (4%)
    ppermute x37, waiting for transfers between devices, swap(): return lax.ppermute(value, axis, [(i, i ^ bit) for i in range(count)])  113 us
    ppermute x37, starting transfers between devices, swap(): return lax.ppermute(value, axis, [(i, i ^ bit) for i in range(count)])  35.2 us
    pallas_call x8, Pallas kernels, experts_on(): pl.pallas_call(functools.partial(expert_kernel, tuple(slot_order(path)),...  27.4 us
    dot_general x4, matrix products, projected(): jnp.dot(held, columns[n * depth:(n + 1) * depth], preferred_element_type=...  6.92 us
  transfers between devices with their start and end apart: 38, of which 20 were waited for; matrix products, arithmetic and copies ran while one was open for 12% of the time, Pallas kernels for 9%

commit v1 on v0

--- a/solution.py
+++ b/solution.py
@@ -11,8 +11,8 @@
 
 HEAD_SIZE = 128
 TOPK = 8
-CHUNKS = 2
-KERNEL_BYTES = 24 << 20
+CHUNKS = 4
+KERNEL_BYTES = 20 << 20
 
 
 def dispatch_plan(
@@ -157,42 +157,65 @@
     return held
 
 
-def add_rounded(kept, received):
-    return (kept.astype(jnp.float32) + received.astype(jnp.float32)).astype(kept.dtype)
-
-
-def scatter_slots(held, axis, bits):
+def gather_parts(value, axis, bits):
+    held = [value]
+    for bit in bits:
+        arrived = []
+        for part in held:
+            arrived.append(swap(part, axis, bit))
+        held = held + arrived
+    return held
+
+
+def total(terms):
+    if len(terms) == 1:
+        return terms[0]
+    return sum(term.astype(jnp.float32) for term in terms).astype(terms[0].dtype)
+
+
+def return_parts(parts, axis, bits):
+    held = [[part] for part in parts]
     for bit in reversed(bits):
-        half = held.shape[0] // 2
-        held = add_rounded(held[:half], swap(held[half:], axis, bit))
+        half = len(held) // 2
+        arrived = [None] * half
+        for i in reversed(range(half)):
+            arrived[i] = swap(total(held[half + i]), axis, bit)
+        held = [terms + [extra] for terms, extra in zip(held, arrived)]
     return held[0]
 
 
-def expert_kernel(order, slots, near, start_row, has_received, *refs):
+def return_rows(terms, axis, bits):
+    for bit in reversed(bits):
+        half = terms[0].shape[0] // 2
+        arrived = swap(total([term[half:] for term in terms]), axis, bit)
+        terms = [term[:half] for term in terms] + [arrived]
+    return [term[0] for term in terms]
+
+
+def expert_kernel(order, near, start_row, *refs):
+    groups = len(order)
     refs = list(refs)
-    place_ref, first_ref, second_ref, gain_ref, table_ref = refs[:5]
-    del refs[:5]
-    proj_ref = None if near else refs.pop(0)
-    received_ref = refs.pop(0) if has_received else None
-    w_in_ref, w_out_ref, out_ref, normed_ref = refs
-    half_groups, halves, blocks, sessions, rows, piece = first_ref.shape
-    half_width = out_ref.shape[-1]
+    place_ref, gain_ref, table_ref, w_in_ref, w_out_ref = refs[:5]
+    in_refs, refs = refs[5 : 5 + groups], refs[5 + groups :]
+    proj_ref, received_ref = (None, None) if near else (refs.pop(0), refs.pop(0))
+    normed_ref = refs.pop()
+    halves, blocks, sessions, rows, piece = in_refs[0].shape
+    half_width = refs[0].shape[-1]
     width = half_width * halves
     hidden_width = w_out_ref.shape[0]
     me, half_me, seq_me = place_ref[0], place_ref[1], place_ref[2]
     per_half = half_width // piece
-    count = len(slots) * rows * blocks
+    count = groups * rows * blocks
 
     power = jnp.zeros((count, 1), jnp.float32)
     pieces = []
-    for i in range(2 * half_groups):
-        in_ref = first_ref if i < half_groups else second_ref
+    for i, in_ref in enumerate(in_refs):
         for k in range(halves):
             tokens = jnp.concatenate(
                 [
-                    in_ref[i % half_groups, k, b, lax.bitwise_xor(me, order[r])]
+                    in_ref[k, b, lax.bitwise_xor(me, order[r])]
                     for b in range(blocks)
-                    for r in slots
+                    for r in range(groups)
                 ],
                 axis=0,
             )
@@ -215,7 +238,7 @@
     )
     scales = []
     for b in range(blocks):
-        for r in slots:
+        for r in range(groups):
             source = lax.bitwise_xor(seq_me, 2 * b + near) * sessions
             source = source + lax.bitwise_xor(me, order[r])
             line = table_ref[pl.ds(source, 1), :][:, start_row : start_row + rows]
@@ -232,7 +255,7 @@
         )
         at = 0
         for b in range(blocks):
-            for n, r in enumerate(slots):
+            for r in range(groups):
                 part = result[at : at + rows]
                 at += rows
                 if proj_ref is not None and b == 0:
@@ -246,8 +269,12 @@
                         )
                     part = jnp.concatenate(columns, axis=1)
                 if received_ref is not None:
-                    part = part + received_ref[n, k, b].astype(jnp.float32)
-                out_ref[n, k, b] = part.astype(jnp.bfloat16)
+                    part = part + received_ref[r, k, b].astype(jnp.float32)
+                part = part.astype(jnp.bfloat16)
+                if near:
+                    refs[0][r, k, b] = part
+                else:
+                    refs[r][k, b] = part
 
 
 def dense_plan(
@@ -278,9 +305,10 @@
 
     kv_width = k_rows.shape[2]
     kv_bits = far + near
-    kv_all = gather_slots(
-        jnp.concatenate([k_rows[0], value_rows[0]], axis=1), "seq", kv_bits
-    ).reshape(seq_count * rows_here, 2 * kv_width)
+    kv_all = jnp.concatenate(
+        gather_parts(jnp.concatenate([k_rows[0], value_rows[0]], axis=1), "seq", kv_bits),
+        axis=0,
+    )
     key_pos = (seq_pos ^ jnp.array(slot_order(kv_bits), jnp.int32))[:, None] * rows_here
     key_pos = (key_pos + jnp.arange(rows_here, dtype=jnp.int32)[None, :]).reshape(-1)
 
@@ -289,20 +317,7 @@
         start = ((group_pos ^ r) * tensor_count + tensor_pos) * piece
         columns = lax.dynamic_slice_in_dim(x_rows[0], start, piece, 1)
         x_slots.append(swap(columns, "expert", r) if r else columns)
-    gain_slots = gather_slots(norm_gain, "tensor", tensor_bits)
-    gain = jnp.take(
-        gain_slots,
-        jnp.array(slot_order(tensor_bits), jnp.int32) ^ tensor_pos,
-        axis=0,
-    ).reshape(width // piece, piece)
-
-    named = expert_ids[0][:, :, None] == jnp.arange(experts, dtype=jnp.int32)[None, None, :]
-    table = jnp.sum(jnp.where(named, gate_weights[0][:, :, None], 0.0), axis=1).T
-    table = lax.all_to_all(table, ("seq", "expert"), split_axis=0, concat_axis=0, tiled=True)
-    w_in = jnp.concatenate([w_gate[0], w_up[0]], axis=1)
-    kv_all, table, gain, w_in, *x_slots = lax.optimization_barrier(
-        (kv_all, table, gain, w_in, *x_slots)
-    )
+    kv_all, *x_slots = lax.optimization_barrier((kv_all, *x_slots))
 
     kv_heads = kv_width // HEAD_SIZE
     q_heads = q_rows.shape[2] // HEAD_SIZE
@@ -334,13 +349,22 @@
         .astype(jnp.bfloat16)
     )
 
+    attn_rows, expert_ids, gate_weights, norm_gain, w_gate, w_up = lax.optimization_barrier(
+        (attn_rows, expert_ids, gate_weights, norm_gain, w_gate, w_up)
+    )
+    gain_slots = gather_slots(norm_gain, "tensor", tensor_bits)
+    gain_at = jnp.array(slot_order(tensor_bits), jnp.int32) ^ tensor_pos
+    gain = gain_slots.at[gain_at].get(mode="promise_in_bounds").reshape(width // piece, piece)
+    named = expert_ids[0][:, :, None] == jnp.arange(experts, dtype=jnp.int32)[None, None, :]
+    table = jnp.sum(jnp.where(named, gate_weights[0][:, :, None], 0.0), axis=1).T
+    table = lax.all_to_all(table, ("seq", "expert"), split_axis=0, concat_axis=0, tiled=True)
+    w_in = jnp.concatenate([w_gate[0], w_up[0]], axis=1)
+
     paths = (group_bits, group_bits[::-1])
     depth = attn_rows.shape[1] // len(paths)
     gathered = []
     for n, path in enumerate(paths):
-        held = [attn_rows[:, n * depth : (n + 1) * depth]]
-        for bit in path:
-            held = held + [swap(value, "expert", bit) for value in held]
+        held = gather_parts(attn_rows[:, n * depth : (n + 1) * depth], "expert", path)
         order = slot_order(path)
         gathered.append(
             jnp.concatenate([held[order.index(r)] for r in range(group_count)], axis=0)
@@ -361,72 +385,56 @@
         proj = proj + swap(away, "tensor", k).astype(jnp.float32)
     proj = proj.reshape(group_count, rows_here, piece)
     mixed = (jnp.stack(x_slots).astype(jnp.float32) + proj).astype(jnp.bfloat16)
-    by_session = jnp.take(
-        mixed, jnp.arange(group_count, dtype=jnp.int32) ^ group_pos, axis=0
-    )
+    session_at = jnp.arange(group_count, dtype=jnp.int32) ^ group_pos
+    by_session = mixed.at[session_at].get(mode="promise_in_bounds")
+    by_session, gain, table, w_in = lax.optimization_barrier((by_session, gain, table, w_in))
 
     rows = rows_here // CHUNKS
+    blocks = seq_count // 2
     place = jnp.stack([group_pos, tensor_pos, seq_pos]).astype(jnp.int32)
-    half_groups = group_count // 2
-    near_bit = near[0]
     chunks = []
     for c in range(CHUNKS):
         path = paths[c % len(paths)]
         held = by_session[:, c * rows : (c + 1) * rows]
         held = gather_slots(held, "seq", far)
         held = gather_slots(held, "tensor", tensor_bits)
-        first = gather_slots(held, "expert", path[:-1])
-        second = swap(first, "expert", path[-1])
-        parts = ((first, second), tuple(swap(v, "seq", near_bit) for v in (first, second)))
-        chunks.append((c, path, parts))
-
-    def experts_on(place, c, path, parts, slots, core, received):
-        operands = [place, *parts[core], gain, table]
-        if not core:
-            operands.append(proj)
-        if received is not None:
-            operands.append(received)
-        operands += [w_in, w_down[0]]
-        blocks = seq_count // 2
+        own = gather_parts(held, "expert", path)
+        other = []
+        for part in own:
+            other.append(swap(part, "seq", near[0]))
+        chunks.append((c, path, own, other))
+
+    def experts_on(c, path, parts, received):
+        order = tuple(slot_order(path))
+        operands = [place, gain, table, w_in, w_down[0], *parts]
+        shape = (tensor_count, blocks, rows, half_width)
+        if received is None:
+            shapes = [jax.ShapeDtypeStruct((group_count, *shape), jnp.bfloat16)]
+        else:
+            operands += [proj, received]
+            shapes = [jax.ShapeDtypeStruct(shape, jnp.bfloat16)] * group_count
+        near_order = near[0] if received is None else 0
         return pl.pallas_call(
-            functools.partial(
-                expert_kernel,
-                tuple(slot_order(path)),
-                tuple(slots),
-                core,
-                c * rows,
-                received is not None,
-            ),
-            out_shape=jax.ShapeDtypeStruct(
-                (len(slots), tensor_count, blocks, rows, half_width), jnp.bfloat16
-            ),
+            functools.partial(expert_kernel, order, near_order, c * rows),
+            out_shape=shapes,
             in_specs=[pl.BlockSpec(memory_space=pltpu.SMEM)]
             + [pl.BlockSpec(memory_space=pltpu.VMEM)] * (len(operands) - 1),
-            out_specs=pl.BlockSpec(memory_space=pltpu.VMEM),
-            scratch_shapes=[pltpu.VMEM((len(slots) * blocks * rows, width), jnp.bfloat16)],
+            out_specs=[pl.BlockSpec(memory_space=pltpu.VMEM)] * len(shapes),
+            scratch_shapes=[pltpu.VMEM((group_count * blocks * rows, width), jnp.bfloat16)],
             compiler_params=pltpu.CompilerParams(vmem_limit_bytes=KERNEL_BYTES),
         )(*operands)
 
-    sent, kept = range(half_groups, group_count), range(half_groups)
-    totals = []
-    for slots in (sent, kept):
-        away, outs = [], []
-        for chunk in chunks:
-            away.append(experts_on(place, *chunk, slots, 1, None))
-        away = [swap(value, "seq", near_bit) for value in away]
-        for chunk, got in zip(chunks, away):
-            outs.append(experts_on(place, *chunk, slots, 0, got))
-        place = lax.optimization_barrier((place, *outs))[0]
-        totals.append(outs)
     finished = []
-    for (c, path, _), away, held in zip(chunks, *totals):
-        arrived = swap(away, "expert", path[-1])
-        held = add_rounded(held, arrived)
-        held = scatter_slots(held, "expert", path[:-1])
-        held = scatter_slots(held, "tensor", tensor_bits)
-        finished.append(scatter_slots(held, "seq", far))
+    for c, path, own, other in chunks:
+        (away,) = experts_on(c, path, other, None)
+        away = swap(away, "seq", near[0])
+        parts = experts_on(c, path, own, away)
+        terms = return_parts(parts, "expert", path)
+        terms = return_rows(terms, "tensor", tensor_bits)
+        terms = return_rows(terms, "seq", far)
+        finished.append(sum(term.astype(jnp.float32) for term in terms))
     x_half = lax.dynamic_slice_in_dim(x_rows[0], tensor_pos * half_width, half_width, 1)
-    summed = jnp.concatenate(finished, axis=0).astype(jnp.float32)
+    summed = jnp.concatenate(finished, axis=0)
     return (x_half.astype(jnp.float32) + summed).astype(jnp.bfloat16)[None]
 
 

time: 219 us -> 206 us (0.941)
  waiting for transfers between devices: 113 us -> 65.2 us
  starting transfers between devices: 39 us -> 70 us
  other arithmetic: 19.9 us -> 9.54 us
  local copies, waits for them, and re-layouts: 9.97 us -> 20 us
  Pallas kernels: 27.4 us -> 31.9 us
    ppermute x37 -> x74, waiting for transfers between devices: 113 us -> 65.2 us  [swap(): return lax.ppermute(value, axis, [(i, i ^ bit) for i in range(count)])]
    ppermute x37 -> x74, starting transfers between devices: 35.2 us -> 66.4 us  [swap(): return lax.ppermute(value, axis, [(i, i ^ bit) for i in range(count)])]
    unnamed x23 -> x67, local copies, waits for them, and re-layouts: 1.23 us -> 17.2 us
    pallas_call x8, Pallas kernels: 27.4 us -> 31.9 us  [experts_on(): pl.pallas_call(functools.partial(expert_kernel, order, near_order, c * ro...]
  transfers between devices with their start and end apart: 38 -> 75, of which waited for: 20 -> 29; matrix products, arithmetic and copies ran while one was open for 12% -> 8% of each run, Pallas kernels for 9% -> 15%
where the time goes in v1:
time: 206 us
  starting transfers between devices  70 us (34%)
  waiting for transfers between devices  65.2 us (32%)
  Pallas kernels  31.9 us (15%)
  local copies, waits for them, and re-layouts  20 us (10%)
  other arithmetic  9.54 us (5%)
  matrix products  8.35 us (4%)
    ppermute x74, starting transfers between devices, swap(): return lax.ppermute(value, axis, [(i, i ^ bit) for i in range(count)])  66.4 us
    ppermute x74, waiting for transfers between devices, swap(): return lax.ppermute(value, axis, [(i, i ^ bit) for i in range(count)])  65.2 us
    pallas_call x8, Pallas kernels, experts_on(): pl.pallas_call(functools.partial(expert_kernel, order, near_order, c * ro...  31.9 us
    unnamed x67, local copies, waits for them, and re-layouts  17.2 us
    dot_general x4, matrix products, projected(): jnp.dot(held, columns[n * depth:(n + 1) * depth], preferred_element_type=...  7.13 us
  transfers between devices with their start and end apart: 75, of which 29 were waited for; matrix products, arithmetic and copies ran while one was open for 8% of the time, Pallas kernels for 15%

profile of v1, /device:TPU:0, one launch (start us, length us, event | category | flops | bytes accessed | tf_op | source)
XLA Modules:
  0.0 205.7 jit_solution(7403599391553409110)
XLA Ops:
  2.1 4.1 %collective-permute-start = (bf16[128,512]{0,1:T(8,128)(2,1)S(1)}, bf16[128,512]{0,1:T(8,128)(2,1)S(1)}, u32[]{:S(2)}, u32[]{:S(2)}) collective-permute-start(bf16[128,512]{0,1:T(8,128)(2,1)S(1)} %pad_maximum_fusion.12), channel_id=1, source_target_pairs={{0,16},{8,24},{16,0},{24,8},{1,17},{9,25},{17,1},{25,9},{2,18},{10... | collective-permute-start | bytes 393224 | tf_op jit(solution)/shard_map/ppermute | solution.py:143
  6.2 1.6 dynamic-slice_bitcast_fusion
  7.8 1.5 collective-permute-start.3
  9.3 1.5 collective-permute-start.4
  13.4 1.2 collective-permute-done.2
  14.7 1.3 collective-permute-done.5
  16.8 2.3 %fusion.42 = (f32[2,8,128]{2,1,0:T(8,128)S(1)}, bf16[2,8,128,512]{2,3,1,0:T(8,128)(2,1)S(1)}) fusion(f32[2,512,128,8]{2,1,3,0:T(8,128)S(1)} %fusion.25, pred[128,512]{0,1:T(8,128)(4,1)S(1)} %broadcast_compare_fusion), kind=kOutput, calls=%fused_computation.93 | output fusion | flops 8389119 | bytes 6365184 | tf_op jit(solution)/shard_map/sub | solution.py:336
  20.2 1.2 collective-permute-start.6
  22.3 4.6 %collective-permute-done.10 = bf16[128,1024]{0,1:T(8,128)(2,1)} collective-permute-done((bf16[128,1024]{0,1:T(8,128)(2,1)S(1)}, bf16[128,1024]{0,1:T(8,128)(2,1)}, u32[]{:S(2)}, u32[]{:S(2)}) %collective-permute-start.10) | collective-permute-done | bytes 262176 | tf_op jit(solution)/shard_map/ppermute | solution.py:143
  26.9 1.5 collective-permute-start.11
  28.4 1.5 collective-permute-start.7
  31.5 3.7 %all-to-all-start = ((f32[16,1,128]{2,1,0:T(1,128)}), f32[16,1,128]{2,1,0:T(1,128)S(1)}, u32[]{:S(2)}, u32[]{:S(2)}) async-start(f32[16,1,128]{2,1,0:T(1,128)} %bitcast.30), calls=%async_computation | async-start | bytes 16384 | tf_op jit(solution)/shard_map/all_to_all | solution.py:360
  35.2 1.9 collective-permute-start.13
  37.1 2.2 %collective-permute-done.11 = bf16[128,1024]{0,1:T(8,128)(2,1)} collective-permute-done((bf16[128,1024]{0,1:T(8,128)(2,1)}, bf16[128,1024]{0,1:T(8,128)(2,1)}, u32[]{:S(2)}, u32[]{:S(2)}) %collective-permute-start.11) | collective-permute-done | bytes 262176 | tf_op jit(solution)/shard_map/ppermute | solution.py:143
  39.4 1.6 fusion.18
  41.2 2.4 %fusion.17 = bf16[512,256]{1,0:T(8,128)(2,1)} fusion(f32[512,256]{1,0:T(8,128)S(1)} %fusion.18, bf16[2048,512]{1,0:T(8,128)(2,1)S(1)} %copy-done, s32[]{:T(128)S(6)} %select_n.53, bf16[128,1024]{0,1:T(8,128)(2,1)} %collective-permute-done.8, bf16[128,1024]{0,1:T(8,128)(2,1)} %collective-permute-done.7, bf16[128,1024]{0,1:T(8,128)(2,1)S(1)} %collective-permute-done.6, ...), kind=kOutput, calls=%fused_computation.18 | convolution fusion | flops 272891904 | bytes 2359300 | tf_op jit(solution)/shard_map/dot_general | solution.py:376
  43.5 1.6 collective-permute-start.12
  45.1 1.9 pad_maximum_fusion.refs_3_
  47.6 1.6 fusion.21
  49.2 1.5 collective-permute-done.12
  50.7 1.6 fusion.16
  53.0 1.9 collective-permute-start.14
  55.9 1.8 collective-permute-start.44
  58.9 3.2 %collective-permute-done.14 = bf16[1,4,32,256]{3,2,1,0:T(8,128)(2,1)S(1)} collective-permute-done((bf16[1,4,32,256]{3,2,1,0:T(8,128)(2,1)S(1)}, bf16[1,4,32,256]{3,2,1,0:T(8,128)(2,1)S(1)}, u32[]{:S(2)}, u32[]{:S(2)}) %collective-permute-start.14) | collective-permute-done | bytes 65568 | tf_op jit(solution)/shard_map/ppermute | solution.py:143
  62.1 2.5 %collective-permute-done.29 = bf16[1,4,32,256]{3,2,1,0:T(8,128)(2,1)S(1)} collective-permute-done((bf16[1,4,32,256]{3,2,1,0:T(8,128)(2,1)S(1)}, bf16[1,4,32,256]{3,2,1,0:T(8,128)(2,1)S(1)}, u32[]{:S(2)}, u32[]{:S(2)}) %collective-permute-start.29) | collective-permute-done | bytes 65568 | tf_op jit(solution)/shard_map/ppermute | solution.py:143
  65.3 1.5 collective-permute-start.45
  66.8 1.6 collective-permute-done.15
  68.4 2.4 %collective-permute-start.16 = (bf16[2,2,4,32,256]{4,3,2,1,0:T(8,128)(2,1)S(1)}, bf16[2,2,4,32,256]{4,3,2,1,0:T(8,128)(2,1)S(1)}, u32[]{:S(2)}, u32[]{:S(2)}) collective-permute-start(bf16[2,2,4,32,256]{4,3,2,1,0:T(8,128)(2,1)S(1)} %pad_maximum_fusion.4.refs_5_), channel_id=1, source_target_pairs={{0,2},{2,0},{4,6},{6,4},{1,3},{3,1},{5,7},{7,5},{8,10},{10,8},{12,... | collective-permute-start | bytes 786440 | tf_op jit(solution)/shard_map/ppermute | solution.py:143
  71.7 1.3 collective-permute-start.31
  73.1 5.6 %collective-permute-done.60 = bf16[1,2,4,32,256]{4,3,2,1,0:T(8,128)(2,1)S(1)} collective-permute-done((bf16[1,2,4,32,256]{4,3,2,1,0:T(8,128)(2,1)S(1)}, bf16[1,2,4,32,256]{4,3,2,1,0:T(8,128)(2,1)S(1)}, u32[]{:S(2)}, u32[]{:S(2)}) %collective-permute-start.60) | collective-permute-done | bytes 131104 | tf_op jit(solution)/shard_map/ppermute | solution.py:143
  78.7 1.4 collective-permute-start.32
  82.8 5.0 %collective-permute-done.32.refs_7_ = bf16[2,2,4,32,256]{4,3,2,1,0:T(8,128)(2,1)S(1)} collective-permute-done((bf16[2,2,4,32,256]{4,3,2,1,0:T(8,128)(2,1)S(1)}, bf16[2,2,4,32,256]{4,3,2,1,0:T(8,128)(2,1)S(1)}, u32[]{:S(2)}, u32[]{:S(2)}) %collective-permute-start.32) | collective-permute-done | bytes 262176 | tf_op jit(solution)/shard_map/ppermute | solution.py:143
  89.8 3.7 %collective-permute-done.46.refs_6_ = bf16[2,2,4,32,256]{4,3,2,1,0:T(8,128)(2,1)S(1)} collective-permute-done((bf16[2,2,4,32,256]{4,3,2,1,0:T(8,128)(2,1)S(1)}, bf16[2,2,4,32,256]{4,3,2,1,0:T(8,128)(2,1)S(1)}, u32[]{:S(2)}, u32[]{:S(2)}) %collective-permute-start.46) | collective-permute-done | bytes 262176 | tf_op jit(solution)/shard_map/ppermute | solution.py:143
  94.9 2.6 %collective-permute-done.62.refs_7_ = bf16[2,2,4,32,256]{4,3,2,1,0:T(8,128)(2,1)S(1)} collective-permute-done((bf16[2,2,4,32,256]{4,3,2,1,0:T(8,128)(2,1)S(1)}, bf16[2,2,4,32,256]{4,3,2,1,0:T(8,128)(2,1)S(1)}, u32[]{:S(2)}, u32[]{:S(2)}) %collective-permute-start.62) | collective-permute-done | bytes 262176 | tf_op jit(solution)/shard_map/ppermute | solution.py:143
  97.5 1.4 collective-permute-start.33
  98.9 3.3 %collective-permute-done.18.refs_8_ = bf16[2,2,4,32,256]{4,3,2,1,0:T(8,128)(2,1)S(1)} collective-permute-done((bf16[2,2,4,32,256]{4,3,2,1,0:T(8,128)(2,1)S(1)}, bf16[2,2,4,32,256]{4,3,2,1,0:T(8,128)(2,1)S(1)}, u32[]{:S(2)}, u32[]{:S(2)}) %collective-permute-start.18) | collective-permute-done | bytes 262176 | tf_op jit(solution)/shard_map/ppermute | solution.py:143
  104.9 1.4 collective-permute-start.63
  106.6 4.4 %collective-permute-done.48.refs_8_ = bf16[2,2,4,32,256]{4,3,2,1,0:T(8,128)(2,1)S(1)} collective-permute-done((bf16[2,2,4,32,256]{4,3,2,1,0:T(8,128)(2,1)S(1)}, bf16[2,2,4,32,256]{4,3,2,1,0:T(8,128)(2,1)S(1)}, u32[]{:S(2)}, u32[]{:S(2)}) %collective-permute-start.48) | collective-permute-done | bytes 262176 | tf_op jit(solution)/shard_map/ppermute | solution.py:143
  115.6 1.4 copy-done.3
  117.0 3.3 %shard_map.127 = bf16[4,2,2,32,1024]{4,3,2,1,0:T(8,128)(2,1)S(1)} custom-call(s32[3]{0:T(128)S(1)} %pad_add_fusion.refs_0_, f32[8,256]{1,0:T(8,128)S(1)} %reshape.568.refs_1_, f32[16,128]{1,0:T(8,128)S(1)} %bitcast.115, bf16[2048,768]{1,0:T(8,128)(2,1)S(1)} %copy-done.1, bf16[384,2048]{1,0:T(8,128)(2,1)S(1)} %bitcast.102, ...), custom_call_target="tpu_custom_call" | custom-call | tf_op jit(solution)/shard_map/pallas_call | solution.py:417
  120.5 3.3 %shard_map.129 = bf16[4,2,2,32,1024]{4,3,2,1,0:T(8,128)(2,1)S(1)} custom-call(s32[3]{0:T(128)S(1)} %pad_add_fusion.refs_0_, f32[8,256]{1,0:T(8,128)S(1)} %reshape.568.refs_1_, f32[16,128]{1,0:T(8,128)S(1)} %bitcast.116, bf16[2048,768]{1,0:T(8,128)(2,1)S(1)} %copy-done.1, bf16[384,2048]{1,0:T(8,128)(2,1)S(1)} %bitcast.103, ...), custom_call_target="tpu_custom_call" | custom-call | tf_op jit(solution)/shard_map/pallas_call | solution.py:417
  124.4 4.6 %shard_map.131 = bf16[4,2,2,32,1024]{4,3,2,1,0:T(8,128)(2,1)} custom-call(s32[3]{0:T(128)S(1)} %pad_add_fusion.refs_0_, f32[8,256]{1,0:T(8,128)S(1)} %reshape.568.refs_1_, f32[16,128]{1,0:T(8,128)S(1)} %bitcast.117, bf16[2048,768]{1,0:T(8,128)(2,1)S(1)} %copy-done.1, bf16[384,2048]{1,0:T(8,128)(2,1)S(1)} %bitcast.104, ...), custom_call_target="tpu_custom_call" | custom-call | tf_op jit(solution)/shard_map/pallas_call | solution.py:417
  129.0 4.3 %shard_map.133 = bf16[4,2,2,32,1024]{4,3,2,1,0:T(8,128)(2,1)} custom-call(s32[3]{0:T(128)S(1)} %pad_add_fusion.refs_0_, f32[8,256]{1,0:T(8,128)S(1)} %reshape.568.refs_1_, f32[16,128]{1,0:T(8,128)S(1)} %bitcast.118, bf16[2048,768]{1,0:T(8,128)(2,1)S(1)} %copy-done.1, bf16[384,2048]{1,0:T(8,128)(2,1)S(1)} %bitcast.105, ...), custom_call_target="tpu_custom_call" | custom-call | tf_op jit(solution)/shard_map/pallas_call | solution.py:417
  133.8 4.1 %shard_map.128 = (bf16[2,2,32,1024]{3,2,1,0:T(8,128)(2,1)S(1)}, bf16[2,2,32,1024]{3,2,1,0:T(8,128)(2,1)S(1)}, bf16[2,2,32,1024]{3,2,1,0:T(8,128)(2,1)S(1)}, bf16[2,2,32,1024]{3,2,1,0:T(8,128)(2,1)}) custom-call(s32[3]{0:T(128)S(1)} %pad_add_fusion.refs_0_, f32[8,256]{1,0:T(8,128)S(1)} %reshape.568.refs_1_, f32[16,128]{1,0:T(8,128)S(1)} %bitcast.119, ...), custom_call_target="tpu_custom_call" | custom-call | tf_op jit(solution)/shard_map/pallas_call | solution.py:417
  138.9 4.0 %shard_map.130 = (bf16[2,2,32,1024]{3,2,1,0:T(8,128)(2,1)S(1)}, bf16[2,2,32,1024]{3,2,1,0:T(8,128)(2,1)S(1)}, bf16[2,2,32,1024]{3,2,1,0:T(8,128)(2,1)S(1)}, bf16[2,2,32,1024]{3,2,1,0:T(8,128)(2,1)}) custom-call(s32[3]{0:T(128)S(1)} %pad_add_fusion.refs_0_, f32[8,256]{1,0:T(8,128)S(1)} %reshape.568.refs_1_, f32[16,128]{1,0:T(8,128)S(1)} %bitcast.120, ...), custom_call_target="tpu_custom_call" | custom-call | tf_op jit(solution)/shard_map/pallas_call | solution.py:417
  145.0 1.4 collective-permute-start.40
  148.1 1.9 copy-done.2
  150.0 1.4 copy-done.5
  154.3 4.1 %shard_map.132 = (bf16[2,2,32,1024]{3,2,1,0:T(8,128)(2,1)S(1)}, bf16[2,2,32,1024]{3,2,1,0:T(8,128)(2,1)S(1)}, bf16[2,2,32,1024]{3,2,1,0:T(8,128)(2,1)S(1)}, bf16[2,2,32,1024]{3,2,1,0:T(8,128)(2,1)S(1)}) custom-call(s32[3]{0:T(128)S(1)} %pad_add_fusion.refs_0_, f32[8,256]{1,0:T(8,128)S(1)} %reshape.568.refs_1_, f32[16,128]{1,0:T(8,128)S(1)} %bitcast.121, ...), custom_call_target="tpu_custom_call" | custom-call | tf_op jit(solution)/shard_map/pallas_call | solution.py:417
  159.4 4.0 %shard_map.134 = (bf16[2,2,32,1024]{3,2,1,0:T(8,128)(2,1)S(1)}, bf16[2,2,32,1024]{3,2,1,0:T(8,128)(2,1)S(1)}, bf16[2,2,32,1024]{3,2,1,0:T(8,128)(2,1)S(1)}, bf16[2,2,32,1024]{3,2,1,0:T(8,128)(2,1)S(1)}) custom-call(s32[3]{0:T(128)S(1)} %pad_add_fusion.refs_0_, f32[8,256]{1,0:T(8,128)S(1)} %reshape.568.refs_1_, f32[16,128]{1,0:T(8,128)S(1)} %bitcast.122, ...), custom_call_target="tpu_custom_call" | custom-call | tf_op jit(solution)/shard_map/pallas_call | solution.py:417
  165.7 1.5 collective-permute-start.70
  168.9 6.0 %collective-permute-done.70 = bf16[2,2,32,1024]{3,2,1,0:T(8,128)(2,1)S(1)} collective-permute-done((bf16[2,2,32,1024]{3,2,1,0:T(8,128)(2,1)S(1)}, bf16[2,2,32,1024]{3,2,1,0:T(8,128)(2,1)S(1)}, u32[]{:S(2)}, u32[]{:S(2)}) %collective-permute-start.70) | collective-permute-done | bytes 262176 | tf_op jit(solution)/shard_map/ppermute | solution.py:143
  176.0 1.5 collective-permute-start.69
  177.5 3.1 %collective-permute-done.26 = bf16[2,2,32,1024]{3,2,1,0:T(8,128)(2,1)S(1)} collective-permute-done((bf16[2,2,32,1024]{3,2,1,0:T(8,128)(2,1)S(1)}, bf16[2,2,32,1024]{3,2,1,0:T(8,128)(2,1)S(1)}, u32[]{:S(2)}, u32[]{:S(2)}) %collective-permute-start.26) | collective-permute-done | bytes 262176 | tf_op jit(solution)/shard_map/ppermute | solution.py:143
  180.5 1.4 collective-permute-start.56
  184.3 1.3 collective-permute-start.42
  185.5 3.6 %collective-permute-done.56 = bf16[2,2,32,1024]{3,2,1,0:T(8,128)(2,1)S(1)} collective-permute-done((bf16[2,2,32,1024]{3,2,1,0:T(8,128)(2,1)S(1)}, bf16[2,2,32,1024]{3,2,1,0:T(8,128)(2,1)S(1)}, u32[]{:S(2)}, u32[]{:S(2)}) %collective-permute-start.56) | collective-permute-done | bytes 262176 | tf_op jit(solution)/shard_map/ppermute | solution.py:143
  190.2 1.2 collective-permute-start.72
  191.5 2.3 %collective-permute-start.28 = (bf16[1,32,1024]{2,1,0:T(8,128)(2,1)S(1)}, bf16[1,32,1024]{2,1,0:T(8,128)(2,1)S(1)}, u32[]{:S(2)}, u32[]{:S(2)}) collective-permute-start(bf16[1,32,1024]{2,1,0:T(8,128)(2,1)S(1)} %fusion.27), channel_id=1, source_target_pairs={{0,16},{8,24},{16,0},{24,8},{1,17},{9,25},{17,1},{25,9},{2,18},{10... | collective-permute-start | bytes 196616 | tf_op jit(solution)/shard_map/ppermute | solution.py:143
  194.6 1.5 collective-permute-done.57
  196.1 1.8 collective-permute-start.58
  198.9 1.8 collective-permute-start.73
  200.8 1.7 collective-permute-done.43
  203.3 1.6 collective-permute-done.73
  (215 shorter events, 49.6 us)
Async XLA Ops:
  2.1 11.1 %collective-permute-start = (bf16[128,512]{0,1:T(8,128)(2,1)S(1)}, bf16[128,512]{0,1:T(8,128)(2,1)S(1)}, u32[]{:S(2)}, u32[]{:S(2)}) collective-permute-start(bf16[128,512]{0,1:T(8,128)(2,1)S(1)} %pad_maximum_fusion.12), channel_id=1, source_target_pairs={{0,16},{8,24},{16,0},{24,8},{1,17},{9,25},{17,1},{25,9},{2,18},{10... | collective-permute-start | bytes 393224 | tf_op jit(solution)/shard_map/ppermute | solution.py:143
  6.2 7.2 %collective-permute-start.1 = (bf16[128,512]{0,1:T(8,128)(2,1)S(1)}, bf16[128,512]{0,1:T(8,128)(2,1)S(1)}, u32[]{:S(2)}, u32[]{:S(2)}) collective-permute-start(bf16[128,512]{0,1:T(8,128)(2,1)S(1)} %pad_maximum_fusion.12), channel_id=1, source_target_pairs={{0,8},{8,0},{16,24},{24,16},{1,9},{9,1},{17,25},{25,17},{2,10},{10... | collective-permute-start | bytes 393224 | tf_op jit(solution)/shard_map/ppermute | solution.py:143
  7.8 6.9 %collective-permute-start.3 = (bf16[128,256]{1,0:T(8,128)(2,1)}, bf16[128,256]{1,0:T(8,128)(2,1)S(1)}, u32[]{:S(2)}, u32[]{:S(2)}) collective-permute-start(bf16[128,256]{1,0:T(8,128)(2,1)} %get-tuple-element.72), channel_id=1, source_target_pairs={{0,2},{2,0},{4,6},{6,4},{1,3},{3,1},{5,7},{7,5},{8,10},{10,8},{12,... | collective-permute-start | bytes 196616 | tf_op jit(solution)/shard_map/ppermute | solution.py:143
  19.6 7.3 %collective-permute-start.10 = (bf16[128,1024]{0,1:T(8,128)(2,1)S(1)}, bf16[128,1024]{0,1:T(8,128)(2,1)}, u32[]{:S(2)}, u32[]{:S(2)}) collective-permute-start(bf16[128,1024]{0,1:T(8,128)(2,1)S(1)} %get-tuple-element.68), channel_id=1, source_target_pairs={{0,4},{2,6},{4,0},{6,2},{1,5},{3,7},{5,1},{7,3},{8,12},{10,14},{12... | collective-permute-start | bytes 786440 | tf_op jit(solution)/shard_map/ppermute | solution.py:143
  20.2 9.7 %collective-permute-start.6 = (bf16[128,1024]{0,1:T(8,128)(2,1)S(1)}, bf16[128,1024]{0,1:T(8,128)(2,1)S(1)}, u32[]{:S(2)}, u32[]{:S(2)}) collective-permute-start(bf16[128,1024]{0,1:T(8,128)(2,1)S(1)} %get-tuple-element.67), channel_id=1, source_target_pairs={{0,2},{2,0},{4,6},{6,4},{1,3},{3,1},{5,7},{7,5},{8,10},{10,8},{12,... | collective-permute-start | bytes 786440 | tf_op jit(solution)/shard_map/ppermute | solution.py:143
  21.4 15.7 %collective-permute-start.9 = (bf16[128,1024]{0,1:T(8,128)(2,1)S(1)}, bf16[128,1024]{0,1:T(8,128)(2,1)}, u32[]{:S(2)}, u32[]{:S(2)}) collective-permute-start(bf16[128,1024]{0,1:T(8,128)(2,1)S(1)} %get-tuple-element.68), channel_id=1, source_target_pairs={{0,2},{2,0},{4,6},{6,4},{1,3},{3,1},{5,7},{7,5},{8,10},{10,8},{12,... | collective-permute-start | bytes 786440 | tf_op jit(solution)/shard_map/ppermute | solution.py:143
  26.9 12.5 %collective-permute-start.11 = (bf16[128,1024]{0,1:T(8,128)(2,1)}, bf16[128,1024]{0,1:T(8,128)(2,1)}, u32[]{:S(2)}, u32[]{:S(2)}) collective-permute-start(bf16[128,1024]{0,1:T(8,128)(2,1)} %collective-permute-done.10), channel_id=1, source_target_pairs={{0,2},{2,0},{4,6},{6,4},{1,3},{3,1},{5,7},{7,5},{8,10},{10,8},{12,... | collective-permute-start | bytes 786440 | tf_op jit(solution)/shard_map/ppermute | solution.py:143
  28.4 12.6 %collective-permute-start.7 = (bf16[128,1024]{0,1:T(8,128)(2,1)S(1)}, bf16[128,1024]{0,1:T(8,128)(2,1)}, u32[]{:S(2)}, u32[]{:S(2)}) collective-permute-start(bf16[128,1024]{0,1:T(8,128)(2,1)S(1)} %get-tuple-element.67), channel_id=1, source_target_pairs={{0,4},{2,6},{4,0},{6,2},{1,5},{3,7},{5,1},{7,3},{8,12},{10,14},{12... | collective-permute-start | bytes 786440 | tf_op jit(solution)/shard_map/ppermute | solution.py:143
  29.9 11.3 %collective-permute-start.8 = (bf16[128,1024]{0,1:T(8,128)(2,1)S(1)}, bf16[128,1024]{0,1:T(8,128)(2,1)}, u32[]{:S(2)}, u32[]{:S(2)}) collective-permute-start(bf16[128,1024]{0,1:T(8,128)(2,1)S(1)} %collective-permute-done.6), channel_id=1, source_target_pairs={{0,4},{2,6},{4,0},{6,2},{1,5},{3,7},{5,1},{7,3},{8,12},{10,14},{12... | collective-permute-start | bytes 786440 | tf_op jit(solution)/shard_map/ppermute | solution.py:143
  31.5 21.4 %all-to-all-start = ((f32[16,1,128]{2,1,0:T(1,128)}), f32[16,1,128]{2,1,0:T(1,128)S(1)}, u32[]{:S(2)}, u32[]{:S(2)}) async-start(f32[16,1,128]{2,1,0:T(1,128)} %bitcast.30), calls=%async_computation | async-start | bytes 16384 | tf_op jit(solution)/shard_map/all_to_all | solution.py:360
  35.2 11.8 %collective-permute-start.13 = (f32[1,1024]{1,0:T(1,128)S(1)}, f32[1,1024]{1,0:T(1,128)S(1)}, u32[]{:S(2)}, u32[]{:S(2)}) collective-permute-start(f32[1,1024]{1,0:T(1,128)S(1)} %bitcast.140), channel_id=1, source_target_pairs={{0,1},{1,0},{2,3},{3,2},{4,5},{5,4},{6,7},{7,6},{8,9},{9,8},{10,11... | collective-permute-start | bytes 12296 | tf_op jit(solution)/shard_map/ppermute | solution.py:143
  43.5 7.1 %collective-permute-start.12 = (bf16[512,256]{1,0:T(8,128)(2,1)}, bf16[512,256]{1,0:T(8,128)(2,1)}, u32[]{:S(2)}, u32[]{:S(2)}) collective-permute-start(bf16[512,256]{1,0:T(8,128)(2,1)} %fusion.17), channel_id=1, source_target_pairs={{0,1},{1,0},{2,3},{3,2},{4,5},{5,4},{6,7},{7,6},{8,9},{9,8},{10,11... | collective-permute-start | bytes 786440 | tf_op jit(solution)/shard_map/ppermute | solution.py:143
  53.0 9.1 %collective-permute-start.14 = (bf16[1,4,32,256]{3,2,1,0:T(8,128)(2,1)S(1)}, bf16[1,4,32,256]{3,2,1,0:T(8,128)(2,1)S(1)}, u32[]{:S(2)}, u32[]{:S(2)}) collective-permute-start(bf16[1,4,32,256]{3,2,1,0:T(8,128)(2,1)S(1)} %get-tuple-element.75), channel_id=1, source_target_pairs={{0,16},{8,24},{16,0},{24,8},{1,17},{9,25},{17,1},{25,9},{2,18},{10... | collective-permute-start | bytes 196616 | tf_op jit(solution)/shard_map/ppermute | solution.py:143
  54.9 9.7 %collective-permute-start.29 = (bf16[1,4,32,256]{3,2,1,0:T(8,128)(2,1)S(1)}, bf16[1,4,32,256]{3,2,1,0:T(8,128)(2,1)S(1)}, u32[]{:S(2)}, u32[]{:S(2)}) collective-permute-start(bf16[1,4,32,256]{3,2,1,0:T(8,128)(2,1)S(1)} %get-tuple-element.78), channel_id=1, source_target_pairs={{0,16},{8,24},{16,0},{24,8},{1,17},{9,25},{17,1},{25,9},{2,18},{10... | collective-permute-start | bytes 196616 | tf_op jit(solution)/shard_map/ppermute | solution.py:143
  55.9 9.3 %collective-permute-start.44 = (bf16[1,4,32,256]{3,2,1,0:T(8,128)(2,1)S(1)}, bf16[1,4,32,256]{3,2,1,0:T(8,128)(2,1)S(1)}, u32[]{:S(2)}, u32[]{:S(2)}) collective-permute-start(bf16[1,4,32,256]{3,2,1,0:T(8,128)(2,1)S(1)} %get-tuple-element.77), channel_id=1, source_target_pairs={{0,16},{8,24},{16,0},{24,8},{1,17},{9,25},{17,1},{25,9},{2,18},{10... | collective-permute-start | bytes 196616 | tf_op jit(solution)/shard_map/ppermute | solution.py:143
  57.8 13.9 %collective-permute-start.59 = (bf16[1,4,32,256]{3,2,1,0:T(8,128)(2,1)S(1)}, bf16[1,4,32,256]{3,2,1,0:T(8,128)(2,1)S(1)}, u32[]{:S(2)}, u32[]{:S(2)}) collective-permute-start(bf16[1,4,32,256]{3,2,1,0:T(8,128)(2,1)S(1)} %get-tuple-element.76), channel_id=1, source_target_pairs={{0,16},{8,24},{16,0},{24,8},{1,17},{9,25},{17,1},{25,9},{2,18},{10... | collective-permute-start | bytes 196616 | tf_op jit(solution)/shard_map/ppermute | solution.py:143
  64.6 7.0 %collective-permute-start.30 = (bf16[1,2,4,32,256]{4,3,2,1,0:T(8,128)(2,1)S(1)}, bf16[1,2,4,32,256]{4,3,2,1,0:T(8,128)(2,1)S(1)}, u32[]{:S(2)}, u32[]{:S(2)}) collective-permute-start(bf16[1,2,4,32,256]{4,3,2,1,0:T(8,128)(2,1)S(1)} %maximum_bitcast_fusion.1), channel_id=1, source_target_pairs={{0,1},{1,0},{2,3},{3,2},{4,5},{5,4},{6,7},{7,6},{8,9},{9,8},{10,11... | collective-permute-start | bytes 393224 | tf_op jit(solution)/shard_map/ppermute | solution.py:143
  65.3 7.7 %collective-permute-start.45 = (bf16[1,2,4,32,256]{4,3,2,1,0:T(8,128)(2,1)S(1)}, bf16[1,2,4,32,256]{4,3,2,1,0:T(8,128)(2,1)S(1)}, u32[]{:S(2)}, u32[]{:S(2)}) collective-permute-start(bf16[1,2,4,32,256]{4,3,2,1,0:T(8,128)(2,1)S(1)} %maximum_bitcast_fusion.2), channel_id=1, source_target_pairs={{0,1},{1,0},{2,3},{3,2},{4,5},{5,4},{6,7},{7,6},{8,9},{9,8},{10,11... | collective-permute-start | bytes 393224 | tf_op jit(solution)/shard_map/ppermute | solution.py:143
  68.4 11.7 %collective-permute-start.16 = (bf16[2,2,4,32,256]{4,3,2,1,0:T(8,128)(2,1)S(1)}, bf16[2,2,4,32,256]{4,3,2,1,0:T(8,128)(2,1)S(1)}, u32[]{:S(2)}, u32[]{:S(2)}) collective-permute-start(bf16[2,2,4,32,256]{4,3,2,1,0:T(8,128)(2,1)S(1)} %pad_maximum_fusion.4.refs_5_), channel_id=1, source_target_pairs={{0,2},{2,0},{4,6},{6,4},{1,3},{3,1},{5,7},{7,5},{8,10},{10,8},{12,... | collective-permute-start | bytes 786440 | tf_op jit(solution)/shard_map/ppermute | solution.py:143
  70.8 9.4 %collective-permute-start.17 = (bf16[2,2,4,32,256]{4,3,2,1,0:T(8,128)(2,1)S(1)}, bf16[2,2,4,32,256]{4,3,2,1,0:T(8,128)(2,1)S(1)}, u32[]{:S(2)}, u32[]{:S(2)}) collective-permute-start(bf16[2,2,4,32,256]{4,3,2,1,0:T(8,128)(2,1)S(1)} %pad_maximum_fusion.4.refs_5_), channel_id=1, source_target_pairs={{0,4},{2,6},{4,0},{6,2},{1,5},{3,7},{5,1},{7,3},{8,12},{10,14},{12... | collective-permute-start | bytes 786440 | tf_op jit(solution)/shard_map/ppermute | solution.py:143
  71.6 9.3 %collective-permute-start.19 = (bf16[2,2,4,32,256]{4,3,2,1,0:T(8,128)(2,1)S(1)}, bf16[2,2,4,32,256]{4,3,2,1,0:T(8,128)(2,1)S(1)}, u32[]{:S(2)}, u32[]{:S(2)}) collective-permute-start(bf16[2,2,4,32,256]{4,3,2,1,0:T(8,128)(2,1)S(1)} %pad_maximum_fusion.4.refs_5_), channel_id=1, source_target_pairs={{0,8},{8,0},{16,24},{24,16},{1,9},{9,1},{17,25},{25,17},{2,10},{10... | collective-permute-start | bytes 786440 | tf_op jit(solution)/shard_map/ppermute | solution.py:143
  71.7 11.2 %collective-permute-start.31 = (bf16[2,2,4,32,256]{4,3,2,1,0:T(8,128)(2,1)S(1)}, bf16[2,2,4,32,256]{4,3,2,1,0:T(8,128)(2,1)S(1)}, u32[]{:S(2)}, u32[]{:S(2)}) collective-permute-start(bf16[2,2,4,32,256]{4,3,2,1,0:T(8,128)(2,1)S(1)} %pad_maximum_fusion.5.refs_5_), channel_id=1, source_target_pairs={{0,4},{2,6},{4,0},{6,2},{1,5},{3,7},{5,1},{7,3},{8,12},{10,14},{12... | collective-permute-start | bytes 786440 | tf_op jit(solution)/shard_map/ppermute | solution.py:143
  78.7 9.2 %collective-permute-start.32 = (bf16[2,2,4,32,256]{4,3,2,1,0:T(8,128)(2,1)S(1)}, bf16[2,2,4,32,256]{4,3,2,1,0:T(8,128)(2,1)S(1)}, u32[]{:S(2)}, u32[]{:S(2)}) collective-permute-start(bf16[2,2,4,32,256]{4,3,2,1,0:T(8,128)(2,1)S(1)} %pad_maximum_fusion.5.refs_5_), channel_id=1, source_target_pairs={{0,2},{2,0},{4,6},{6,4},{1,3},{3,1},{5,7},{7,5},{8,10},{10,8},{12,... | collective-permute-start | bytes 786440 | tf_op jit(solution)/shard_map/ppermute | solution.py:143
  80.1 8.5 %collective-permute-start.34 = (bf16[2,2,4,32,256]{4,3,2,1,0:T(8,128)(2,1)S(1)}, bf16[2,2,4,32,256]{4,3,2,1,0:T(8,128)(2,1)S(1)}, u32[]{:S(2)}, u32[]{:S(2)}) collective-permute-start(bf16[2,2,4,32,256]{4,3,2,1,0:T(8,128)(2,1)S(1)} %pad_maximum_fusion.5.refs_5_), channel_id=1, source_target_pairs={{0,8},{8,0},{16,24},{24,16},{1,9},{9,1},{17,25},{25,17},{2,10},{10... | collective-permute-start | bytes 786440 | tf_op jit(solution)/shard_map/ppermute | solution.py:143
  80.2 13.3 %collective-permute-start.46 = (bf16[2,2,4,32,256]{4,3,2,1,0:T(8,128)(2,1)S(1)}, bf16[2,2,4,32,256]{4,3,2,1,0:T(8,128)(2,1)S(1)}, u32[]{:S(2)}, u32[]{:S(2)}) collective-permute-start(bf16[2,2,4,32,256]{4,3,2,1,0:T(8,128)(2,1)S(1)} %pad_maximum_fusion.6.refs_5_), channel_id=1, source_target_pairs={{0,2},{2,0},{4,6},{6,4},{1,3},{3,1},{5,7},{7,5},{8,10},{10,8},{12,... | collective-permute-start | bytes 786440 | tf_op jit(solution)/shard_map/ppermute | solution.py:143
  80.9 12.6 %collective-permute-start.47 = (bf16[2,2,4,32,256]{4,3,2,1,0:T(8,128)(2,1)S(1)}, bf16[2,2,4,32,256]{4,3,2,1,0:T(8,128)(2,1)S(1)}, u32[]{:S(2)}, u32[]{:S(2)}) collective-permute-start(bf16[2,2,4,32,256]{4,3,2,1,0:T(8,128)(2,1)S(1)} %pad_maximum_fusion.6.refs_5_), channel_id=1, source_target_pairs={{0,4},{2,6},{4,0},{6,2},{1,5},{3,7},{5,1},{7,3},{8,12},{10,14},{12... | collective-permute-start | bytes 786440 | tf_op jit(solution)/shard_map/ppermute | solution.py:143
  82.8 11.5 %collective-permute-start.49 = (bf16[2,2,4,32,256]{4,3,2,1,0:T(8,128)(2,1)S(1)}, bf16[2,2,4,32,256]{4,3,2,1,0:T(8,128)(2,1)S(1)}, u32[]{:S(2)}, u32[]{:S(2)}) collective-permute-start(bf16[2,2,4,32,256]{4,3,2,1,0:T(8,128)(2,1)S(1)} %pad_maximum_fusion.6.refs_5_), channel_id=1, source_target_pairs={{0,8},{8,0},{16,24},{24,16},{1,9},{9,1},{17,25},{25,17},{2,10},{10... | collective-permute-start | bytes 786440 | tf_op jit(solution)/shard_map/ppermute | solution.py:143
  87.9 7.0 %collective-permute-start.61 = (bf16[2,2,4,32,256]{4,3,2,1,0:T(8,128)(2,1)S(1)}, bf16[2,2,4,32,256]{4,3,2,1,0:T(8,128)(2,1)S(1)}, u32[]{:S(2)}, u32[]{:S(2)}) collective-permute-start(bf16[2,2,4,32,256]{4,3,2,1,0:T(8,128)(2,1)S(1)} %pad_maximum_fusion.7.refs_5_), channel_id=1, source_target_pairs={{0,4},{2,6},{4,0},{6,2},{1,5},{3,7},{5,1},{7,3},{8,12},{10,14},{12... | collective-permute-start | bytes 786440 | tf_op jit(solution)/shard_map/ppermute | solution.py:143
  88.6 8.8 %collective-permute-start.62 = (bf16[2,2,4,32,256]{4,3,2,1,0:T(8,128)(2,1)S(1)}, bf16[2,2,4,32,256]{4,3,2,1,0:T(8,128)(2,1)S(1)}, u32[]{:S(2)}, u32[]{:S(2)}) collective-permute-start(bf16[2,2,4,32,256]{4,3,2,1,0:T(8,128)(2,1)S(1)} %pad_maximum_fusion.7.refs_5_), channel_id=1, source_target_pairs={{0,2},{2,0},{4,6},{6,4},{1,3},{3,1},{5,7},{7,5},{8,10},{10,8},{12,... | collective-permute-start | bytes 786440 | tf_op jit(solution)/shard_map/ppermute | solution.py:143
  93.5 8.7 %collective-permute-start.18 = (bf16[2,2,4,32,256]{4,3,2,1,0:T(8,128)(2,1)S(1)}, bf16[2,2,4,32,256]{4,3,2,1,0:T(8,128)(2,1)S(1)}, u32[]{:S(2)}, u32[]{:S(2)}) collective-permute-start(bf16[2,2,4,32,256]{4,3,2,1,0:T(8,128)(2,1)S(1)} %collective-permute-done.16.refs_6_), channel_id=1, source_target_pairs={{0,4},{2,6},{4,0},{6,2},{1,5},{3,7},{5,1},{7,3},{8,12},{10,14},{12... | collective-permute-start | bytes 786440 | tf_op jit(solution)/shard_map/ppermute | solution.py:143
  94.3 7.9 %collective-permute-start.20 = (bf16[2,2,4,32,256]{4,3,2,1,0:T(8,128)(2,1)S(1)}, bf16[2,2,4,32,256]{4,3,2,1,0:T(8,128)(2,1)S(1)}, u32[]{:S(2)}, u32[]{:S(2)}) collective-permute-start(bf16[2,2,4,32,256]{4,3,2,1,0:T(8,128)(2,1)S(1)} %collective-permute-done.16.refs_6_), channel_id=1, source_target_pairs={{0,8},{8,0},{16,24},{24,16},{1,9},{9,1},{17,25},{25,17},{2,10},{10... | collective-permute-start | bytes 786440 | tf_op jit(solution)/shard_map/ppermute | solution.py:143
  94.9 8.1 %collective-permute-start.21 = (bf16[2,2,4,32,256]{4,3,2,1,0:T(8,128)(2,1)S(1)}, bf16[2,2,4,32,256]{4,3,2,1,0:T(8,128)(2,1)S(1)}, u32[]{:S(2)}, u32[]{:S(2)}) collective-permute-start(bf16[2,2,4,32,256]{4,3,2,1,0:T(8,128)(2,1)S(1)} %collective-permute-done.17.refs_7_), channel_id=1, source_target_pairs={{0,8},{8,0},{16,24},{24,16},{1,9},{9,1},{17,25},{25,17},{2,10},{10... | collective-permute-start | bytes 786440 | tf_op jit(solution)/shard_map/ppermute | solution.py:143
  102.2 8.7 %collective-permute-start.48 = (bf16[2,2,4,32,256]{4,3,2,1,0:T(8,128)(2,1)S(1)}, bf16[2,2,4,32,256]{4,3,2,1,0:T(8,128)(2,1)S(1)}, u32[]{:S(2)}, u32[]{:S(2)}) collective-permute-start(bf16[2,2,4,32,256]{4,3,2,1,0:T(8,128)(2,1)S(1)} %collective-permute-done.46.refs_6_), channel_id=1, source_target_pairs={{0,4},{2,6},{4,0},{6,2},{1,5},{3,7},{5,1},{7,3},{8,12},{10,14},{12... | collective-permute-start | bytes 786440 | tf_op jit(solution)/shard_map/ppermute | solution.py:143
  103.0 7.9 %collective-permute-start.50 = (bf16[2,2,4,32,256]{4,3,2,1,0:T(8,128)(2,1)S(1)}, bf16[2,2,4,32,256]{4,3,2,1,0:T(8,128)(2,1)S(1)}, u32[]{:S(2)}, u32[]{:S(2)}) collective-permute-start(bf16[2,2,4,32,256]{4,3,2,1,0:T(8,128)(2,1)S(1)} %collective-permute-done.46.refs_6_), channel_id=1, source_target_pairs={{0,8},{8,0},{16,24},{24,16},{1,9},{9,1},{17,25},{25,17},{2,10},{10... | collective-permute-start | bytes 786440 | tf_op jit(solution)/shard_map/ppermute | solution.py:143
  104.2 8.0 %collective-permute-start.51 = (bf16[2,2,4,32,256]{4,3,2,1,0:T(8,128)(2,1)S(1)}, bf16[2,2,4,32,256]{4,3,2,1,0:T(8,128)(2,1)S(1)}, u32[]{:S(2)}, u32[]{:S(2)}) collective-permute-start(bf16[2,2,4,32,256]{4,3,2,1,0:T(8,128)(2,1)S(1)} %collective-permute-done.47.refs_7_), channel_id=1, source_target_pairs={{0,8},{8,0},{16,24},{24,16},{1,9},{9,1},{17,25},{25,17},{2,10},{10... | collective-permute-start | bytes 786440 | tf_op jit(solution)/shard_map/ppermute | solution.py:143
  104.9 8.7 %collective-permute-start.63 = (bf16[2,2,4,32,256]{4,3,2,1,0:T(8,128)(2,1)S(1)}, bf16[2,2,4,32,256]{4,3,2,1,0:T(8,128)(2,1)S(1)}, u32[]{:S(2)}, u32[]{:S(2)}) collective-permute-start(bf16[2,2,4,32,256]{4,3,2,1,0:T(8,128)(2,1)S(1)} %collective-permute-done.61.refs_6_), channel_id=1, source_target_pairs={{0,2},{2,0},{4,6},{6,4},{1,3},{3,1},{5,7},{7,5},{8,10},{10,8},{12,... | collective-permute-start | bytes 786440 | tf_op jit(solution)/shard_map/ppermute | solution.py:143
  106.3 8.0 %collective-permute-start.22 = (bf16[2,2,4,32,256]{4,3,2,1,0:T(8,128)(2,1)S(1)}, bf16[2,2,4,32,256]{4,3,2,1,0:T(8,128)(2,1)S(1)}, u32[]{:S(2)}, u32[]{:S(2)}) collective-permute-start(bf16[2,2,4,32,256]{4,3,2,1,0:T(8,128)(2,1)S(1)} %collective-permute-done.18.refs_8_), channel_id=1, source_target_pairs={{0,8},{8,0},{16,24},{24,16},{1,9},{9,1},{17,25},{25,17},{2,10},{10... | collective-permute-start | bytes 786440 | tf_op jit(solution)/shard_map/ppermute | solution.py:143
  110.9 9.4 %collective-permute-start.37 = (bf16[2,2,4,32,256]{4,3,2,1,0:T(8,128)(2,1)S(1)}, bf16[2,2,4,32,256]{4,3,2,1,0:T(8,128)(2,1)S(1)}, u32[]{:S(2)}, u32[]{:S(2)}) collective-permute-start(bf16[2,2,4,32,256]{4,3,2,1,0:T(8,128)(2,1)S(1)} %collective-permute-done.33.refs_8_), channel_id=1, source_target_pairs={{0,8},{8,0},{16,24},{24,16},{1,9},{9,1},{17,25},{25,17},{2,10},{10... | collective-permute-start | bytes 786440 | tf_op jit(solution)/shard_map/ppermute | solution.py:143
  110.9 12.9 %collective-permute-start.52 = (bf16[2,2,4,32,256]{4,3,2,1,0:T(8,128)(2,1)S(1)}, bf16[2,2,4,32,256]{4,3,2,1,0:T(8,128)(2,1)S(1)}, u32[]{:S(2)}, u32[]{:S(2)}) collective-permute-start(bf16[2,2,4,32,256]{4,3,2,1,0:T(8,128)(2,1)S(1)} %collective-permute-done.48.refs_8_), channel_id=1, source_target_pairs={{0,8},{8,0},{16,24},{24,16},{1,9},{9,1},{17,25},{25,17},{2,10},{10... | collective-permute-start | bytes 786440 | tf_op jit(solution)/shard_map/ppermute | solution.py:143
  112.2 16.7 %collective-permute-start.65 = (bf16[2,2,4,32,256]{4,3,2,1,0:T(8,128)(2,1)S(1)}, bf16[2,2,4,32,256]{4,3,2,1,0:T(8,128)(2,1)S(1)}, u32[]{:S(2)}, u32[]{:S(2)}) collective-permute-start(bf16[2,2,4,32,256]{4,3,2,1,0:T(8,128)(2,1)S(1)} %collective-permute-done.61.refs_6_), channel_id=1, source_target_pairs={{0,8},{8,0},{16,24},{24,16},{1,9},{9,1},{17,25},{25,17},{2,10},{10... | collective-permute-start | bytes 786440 | tf_op jit(solution)/shard_map/ppermute | solution.py:143
  113.7 15.3 %collective-permute-start.66 = (bf16[2,2,4,32,256]{4,3,2,1,0:T(8,128)(2,1)S(1)}, bf16[2,2,4,32,256]{4,3,2,1,0:T(8,128)(2,1)S(1)}, u32[]{:S(2)}, u32[]{:S(2)}) collective-permute-start(bf16[2,2,4,32,256]{4,3,2,1,0:T(8,128)(2,1)S(1)} %collective-permute-done.62.refs_7_), channel_id=1, source_target_pairs={{0,8},{8,0},{16,24},{24,16},{1,9},{9,1},{17,25},{25,17},{2,10},{10... | collective-permute-start | bytes 786440 | tf_op jit(solution)/shard_map/ppermute | solution.py:143
  114.4 14.6 %collective-permute-start.67 = (bf16[2,2,4,32,256]{4,3,2,1,0:T(8,128)(2,1)S(1)}, bf16[2,2,4,32,256]{4,3,2,1,0:T(8,128)(2,1)S(1)}, u32[]{:S(2)}, u32[]{:S(2)}) collective-permute-start(bf16[2,2,4,32,256]{4,3,2,1,0:T(8,128)(2,1)S(1)} %collective-permute-done.63.refs_8_), channel_id=1, source_target_pairs={{0,8},{8,0},{16,24},{24,16},{1,9},{9,1},{17,25},{25,17},{2,10},{10... | collective-permute-start | bytes 786440 | tf_op jit(solution)/shard_map/ppermute | solution.py:143
  120.4 13.4 %collective-permute-start.23 = (bf16[4,2,2,32,1024]{4,3,2,1,0:T(8,128)(2,1)S(1)}, bf16[4,2,2,32,1024]{4,3,2,1,0:T(8,128)(2,1)S(1)}, u32[]{:S(2)}, u32[]{:S(2)}) collective-permute-start(bf16[4,2,2,32,1024]{4,3,2,1,0:T(8,128)(2,1)S(1)} %shard_map.127), channel_id=1, source_target_pairs={{0,8},{8,0},{16,24},{24,16},{1,9},{9,1},{17,25},{25,17},{2,10},{10... | collective-permute-start | bytes 3145736 | tf_op jit(solution)/shard_map/ppermute | solution.py:143
  123.8 15.1 %collective-permute-start.38 = (bf16[4,2,2,32,1024]{4,3,2,1,0:T(8,128)(2,1)S(1)}, bf16[4,2,2,32,1024]{4,3,2,1,0:T(8,128)(2,1)S(1)}, u32[]{:S(2)}, u32[]{:S(2)}) collective-permute-start(bf16[4,2,2,32,1024]{4,3,2,1,0:T(8,128)(2,1)S(1)} %shard_map.129), channel_id=1, source_target_pairs={{0,8},{8,0},{16,24},{24,16},{1,9},{9,1},{17,25},{25,17},{2,10},{10... | collective-permute-start | bytes 3145736 | tf_op jit(solution)/shard_map/ppermute | solution.py:143
  129.0 18.5 %collective-permute-start.53 = (bf16[4,2,2,32,1024]{4,3,2,1,0:T(8,128)(2,1)}, bf16[4,2,2,32,1024]{4,3,2,1,0:T(8,128)(2,1)}, u32[]{:S(2)}, u32[]{:S(2)}) collective-permute-start(bf16[4,2,2,32,1024]{4,3,2,1,0:T(8,128)(2,1)} %shard_map.131), channel_id=1, source_target_pairs={{0,8},{8,0},{16,24},{24,16},{1,9},{9,1},{17,25},{25,17},{2,10},{10... | collective-permute-start | bytes 3145736 | tf_op jit(solution)/shard_map/ppermute | solution.py:143
  133.3 25.1 %collective-permute-start.68 = (bf16[4,2,2,32,1024]{4,3,2,1,0:T(8,128)(2,1)}, bf16[4,2,2,32,1024]{4,3,2,1,0:T(8,128)(2,1)}, u32[]{:S(2)}, u32[]{:S(2)}) collective-permute-start(bf16[4,2,2,32,1024]{4,3,2,1,0:T(8,128)(2,1)} %shard_map.133), channel_id=1, source_target_pairs={{0,8},{8,0},{16,24},{24,16},{1,9},{9,1},{17,25},{25,17},{2,10},{10... | collective-permute-start | bytes 3145736 | tf_op jit(solution)/shard_map/ppermute | solution.py:143
  137.9 25.6 %collective-permute-start.25 = (bf16[2,2,32,1024]{3,2,1,0:T(8,128)(2,1)}, bf16[2,2,32,1024]{3,2,1,0:T(8,128)(2,1)}, u32[]{:S(2)}, u32[]{:S(2)}) collective-permute-start(bf16[2,2,32,1024]{3,2,1,0:T(8,128)(2,1)} %get-tuple-element.54), channel_id=1, source_target_pairs={{0,4},{2,6},{4,0},{6,2},{1,5},{3,7},{5,1},{7,3},{8,12},{10,14},{12... | collective-permute-start | bytes 786440 | tf_op jit(solution)/shard_map/ppermute | solution.py:143
  145.0 20.7 %collective-permute-start.40 = (bf16[2,2,32,1024]{3,2,1,0:T(8,128)(2,1)}, bf16[2,2,32,1024]{3,2,1,0:T(8,128)(2,1)}, u32[]{:S(2)}, u32[]{:S(2)}) collective-permute-start(bf16[2,2,32,1024]{3,2,1,0:T(8,128)(2,1)} %get-tuple-element.58), channel_id=1, source_target_pairs={{0,2},{2,0},{4,6},{6,4},{1,3},{3,1},{5,7},{7,5},{8,10},{10,8},{12,... | collective-permute-start | bytes 786440 | tf_op jit(solution)/shard_map/ppermute | solution.py:143
  146.5 29.5 %collective-permute-start.24 = (bf16[2,2,32,1024]{3,2,1,0:T(8,128)(2,1)}, bf16[2,2,32,1024]{3,2,1,0:T(8,128)(2,1)S(1)}, u32[]{:S(2)}, u32[]{:S(2)}) collective-permute-start(bf16[2,2,32,1024]{3,2,1,0:T(8,128)(2,1)} %copy-done.24), channel_id=1, source_target_pairs={{0,4},{2,6},{4,0},{6,2},{1,5},{3,7},{5,1},{7,3},{8,12},{10,14},{12... | collective-permute-start | bytes 786440 | tf_op jit(solution)/shard_map/ppermute | solution.py:143
  147.5 34.5 %collective-permute-start.39 = (bf16[2,2,32,1024]{3,2,1,0:T(8,128)(2,1)}, bf16[2,2,32,1024]{3,2,1,0:T(8,128)(2,1)S(1)}, u32[]{:S(2)}, u32[]{:S(2)}) collective-permute-start(bf16[2,2,32,1024]{3,2,1,0:T(8,128)(2,1)} %copy-done.25), channel_id=1, source_target_pairs={{0,2},{2,0},{4,6},{6,4},{1,3},{3,1},{5,7},{7,5},{8,10},{10,8},{12,... | collective-permute-start | bytes 786440 | tf_op jit(solution)/shard_map/ppermute | solution.py:143
  158.4 9.8 %collective-permute-start.55 = (bf16[2,2,32,1024]{3,2,1,0:T(8,128)(2,1)S(1)}, bf16[2,2,32,1024]{3,2,1,0:T(8,128)(2,1)S(1)}, u32[]{:S(2)}, u32[]{:S(2)}) collective-permute-start(bf16[2,2,32,1024]{3,2,1,0:T(8,128)(2,1)S(1)} %get-tuple-element.62), channel_id=1, source_target_pairs={{0,4},{2,6},{4,0},{6,2},{1,5},{3,7},{5,1},{7,3},{8,12},{10,14},{12... | collective-permute-start | bytes 786440 | tf_op jit(solution)/shard_map/ppermute | solution.py:143
  163.5 20.7 %collective-permute-start.54 = (bf16[2,2,32,1024]{3,2,1,0:T(8,128)(2,1)S(1)}, bf16[2,2,32,1024]{3,2,1,0:T(8,128)(2,1)S(1)}, u32[]{:S(2)}, u32[]{:S(2)}) collective-permute-start(bf16[2,2,32,1024]{3,2,1,0:T(8,128)(2,1)S(1)} %get-tuple-element.60), channel_id=1, source_target_pairs={{0,4},{2,6},{4,0},{6,2},{1,5},{3,7},{5,1},{7,3},{8,12},{10,14},{12... | collective-permute-start | bytes 786440 | tf_op jit(solution)/shard_map/ppermute | solution.py:143
  165.7 9.2 %collective-permute-start.70 = (bf16[2,2,32,1024]{3,2,1,0:T(8,128)(2,1)S(1)}, bf16[2,2,32,1024]{3,2,1,0:T(8,128)(2,1)S(1)}, u32[]{:S(2)}, u32[]{:S(2)}) collective-permute-start(bf16[2,2,32,1024]{3,2,1,0:T(8,128)(2,1)S(1)} %get-tuple-element.66), channel_id=1, source_target_pairs={{0,2},{2,0},{4,6},{6,4},{1,3},{3,1},{5,7},{7,5},{8,10},{10,8},{12,... | collective-permute-start | bytes 786440 | tf_op jit(solution)/shard_map/ppermute | solution.py:143
  168.2 12.4 %collective-permute-start.26 = (bf16[2,2,32,1024]{3,2,1,0:T(8,128)(2,1)S(1)}, bf16[2,2,32,1024]{3,2,1,0:T(8,128)(2,1)S(1)}, u32[]{:S(2)}, u32[]{:S(2)}) collective-permute-start(bf16[2,2,32,1024]{3,2,1,0:T(8,128)(2,1)S(1)} %add_convert_fusion.3), channel_id=1, source_target_pairs={{0,2},{2,0},{4,6},{6,4},{1,3},{3,1},{5,7},{7,5},{8,10},{10,8},{12,... | collective-permute-start | bytes 786440 | tf_op jit(solution)/shard_map/ppermute | solution.py:143
  174.9 8.4 %collective-permute-start.41 = (bf16[2,2,32,1024]{3,2,1,0:T(8,128)(2,1)S(1)}, bf16[2,2,32,1024]{3,2,1,0:T(8,128)(2,1)S(1)}, u32[]{:S(2)}, u32[]{:S(2)}) collective-permute-start(bf16[2,2,32,1024]{3,2,1,0:T(8,128)(2,1)S(1)} %add_convert_fusion.2), channel_id=1, source_target_pairs={{0,4},{2,6},{4,0},{6,2},{1,5},{3,7},{5,1},{7,3},{8,12},{10,14},{12... | collective-permute-start | bytes 786440 | tf_op jit(solution)/shard_map/ppermute | solution.py:143
  176.0 14.2 %collective-permute-start.69 = (bf16[2,2,32,1024]{3,2,1,0:T(8,128)(2,1)S(1)}, bf16[2,2,32,1024]{3,2,1,0:T(8,128)(2,1)S(1)}, u32[]{:S(2)}, u32[]{:S(2)}) collective-permute-start(bf16[2,2,32,1024]{3,2,1,0:T(8,128)(2,1)S(1)} %get-tuple-element.64), channel_id=1, source_target_pairs={{0,2},{2,0},{4,6},{6,4},{1,3},{3,1},{5,7},{7,5},{8,10},{10,8},{12,... | collective-permute-start | bytes 786440 | tf_op jit(solution)/shard_map/ppermute | solution.py:143
  180.5 8.6 %collective-permute-start.56 = (bf16[2,2,32,1024]{3,2,1,0:T(8,128)(2,1)S(1)}, bf16[2,2,32,1024]{3,2,1,0:T(8,128)(2,1)S(1)}, u32[]{:S(2)}, u32[]{:S(2)}) collective-permute-start(bf16[2,2,32,1024]{3,2,1,0:T(8,128)(2,1)S(1)} %add_convert_fusion.1), channel_id=1, source_target_pairs={{0,2},{2,0},{4,6},{6,4},{1,3},{3,1},{5,7},{7,5},{8,10},{10,8},{12,... | collective-permute-start | bytes 786440 | tf_op jit(solution)/shard_map/ppermute | solution.py:143
  182.0 8.1 %collective-permute-start.71 = (bf16[2,2,32,1024]{3,2,1,0:T(8,128)(2,1)S(1)}, bf16[2,2,32,1024]{3,2,1,0:T(8,128)(2,1)S(1)}, u32[]{:S(2)}, u32[]{:S(2)}) collective-permute-start(bf16[2,2,32,1024]{3,2,1,0:T(8,128)(2,1)S(1)} %add_convert_fusion), channel_id=1, source_target_pairs={{0,4},{2,6},{4,0},{6,2},{1,5},{3,7},{5,1},{7,3},{8,12},{10,14},{12... | collective-permute-start | bytes 786440 | tf_op jit(solution)/shard_map/ppermute | solution.py:143
  183.4 8.1 %collective-permute-start.27 = (bf16[1,2,32,1024]{3,2,1,0:T(8,128)(2,1)S(1)}, bf16[1,2,32,1024]{3,2,1,0:T(8,128)(2,1)S(1)}, u32[]{:S(2)}, u32[]{:S(2)}) collective-permute-start(bf16[1,2,32,1024]{3,2,1,0:T(8,128)(2,1)S(1)} %add_convert_fusion.8), channel_id=1, source_target_pairs={{0,1},{1,0},{2,3},{3,2},{4,5},{5,4},{6,7},{7,6},{8,9},{9,8},{10,11... | collective-permute-start | bytes 393224 | tf_op jit(solution)/shard_map/ppermute | solution.py:143
  184.3 9.5 %collective-permute-start.42 = (bf16[1,2,32,1024]{3,2,1,0:T(8,128)(2,1)S(1)}, bf16[1,2,32,1024]{3,2,1,0:T(8,128)(2,1)S(1)}, u32[]{:S(2)}, u32[]{:S(2)}) collective-permute-start(bf16[1,2,32,1024]{3,2,1,0:T(8,128)(2,1)S(1)} %add_convert_fusion.7), channel_id=1, source_target_pairs={{0,1},{1,0},{2,3},{3,2},{4,5},{5,4},{6,7},{7,6},{8,9},{9,8},{10,11... | collective-permute-start | bytes 393224 | tf_op jit(solution)/shard_map/ppermute | solution.py:143
  190.2 8.7 %collective-permute-start.72 = (bf16[1,2,32,1024]{3,2,1,0:T(8,128)(2,1)S(1)}, bf16[1,2,32,1024]{3,2,1,0:T(8,128)(2,1)S(1)}, u32[]{:S(2)}, u32[]{:S(2)}) collective-permute-start(bf16[1,2,32,1024]{3,2,1,0:T(8,128)(2,1)S(1)} %add_convert_fusion.5), channel_id=1, source_target_pairs={{0,1},{1,0},{2,3},{3,2},{4,5},{5,4},{6,7},{7,6},{8,9},{9,8},{10,11... | collective-permute-start | bytes 393224 | tf_op jit(solution)/shard_map/ppermute | solution.py:143
  191.5 9.3 %collective-permute-start.28 = (bf16[1,32,1024]{2,1,0:T(8,128)(2,1)S(1)}, bf16[1,32,1024]{2,1,0:T(8,128)(2,1)S(1)}, u32[]{:S(2)}, u32[]{:S(2)}) collective-permute-start(bf16[1,32,1024]{2,1,0:T(8,128)(2,1)S(1)} %fusion.27), channel_id=1, source_target_pairs={{0,16},{8,24},{16,0},{24,8},{1,17},{9,25},{17,1},{25,9},{2,18},{10... | collective-permute-start | bytes 196616 | tf_op jit(solution)/shard_map/ppermute | solution.py:143
  193.8 8.7 %collective-permute-start.43 = (bf16[1,32,1024]{2,1,0:T(8,128)(2,1)S(1)}, bf16[1,32,1024]{2,1,0:T(8,128)(2,1)S(1)}, u32[]{:S(2)}, u32[]{:S(2)}) collective-permute-start(bf16[1,32,1024]{2,1,0:T(8,128)(2,1)S(1)} %fusion.28), channel_id=1, source_target_pairs={{0,16},{8,24},{16,0},{24,8},{1,17},{9,25},{17,1},{25,9},{2,18},{10... | collective-permute-start | bytes 196616 | tf_op jit(solution)/shard_map/ppermute | solution.py:143
  196.1 7.1 %collective-permute-start.58 = (bf16[1,32,1024]{2,1,0:T(8,128)(2,1)S(1)}, bf16[1,32,1024]{2,1,0:T(8,128)(2,1)S(1)}, u32[]{:S(2)}, u32[]{:S(2)}) collective-permute-start(bf16[1,32,1024]{2,1,0:T(8,128)(2,1)S(1)} %fusion.29), channel_id=1, source_target_pairs={{0,16},{8,24},{16,0},{24,8},{1,17},{9,25},{17,1},{25,9},{2,18},{10... | collective-permute-start | bytes 196616 | tf_op jit(solution)/shard_map/ppermute | solution.py:143
  (43 other events, 317.1 us)

commit v2 on v1

--- a/solution.py
+++ b/solution.py
@@ -12,7 +12,7 @@
 HEAD_SIZE = 128
 TOPK = 8
 CHUNKS = 4
-KERNEL_BYTES = 20 << 20
+KERNEL_BYTES = 6 << 20
 
 
 def dispatch_plan(
@@ -277,6 +277,80 @@
                     refs[r][k, b] = part
 
 
+def attention_kernel(head, order, place_ref, q_ref, *refs):
+    slots = len(order)
+    k_refs, v_refs, out_ref = refs[:slots], refs[slots : 2 * slots], refs[-1]
+    rows = q_ref.shape[0]
+    columns = slice(head * HEAD_SIZE, (head + 1) * HEAD_SIZE)
+    keys = jnp.concatenate([ref[:, columns] for ref in k_refs], axis=0)
+    values = jnp.concatenate([ref[:, columns] for ref in v_refs], axis=0)
+    down = lax.broadcasted_iota(jnp.int32, (rows, rows), 0)
+    across = lax.broadcasted_iota(jnp.int32, (rows, rows), 1)
+    seq_me = place_ref[2]
+    allowed = jnp.concatenate(
+        [
+            (lax.bitwise_xor(seq_me, place) - seq_me) * rows + across <= down
+            for place in order
+        ],
+        axis=1,
+    )
+    for n in range(out_ref.shape[1] // HEAD_SIZE):
+        start = head * out_ref.shape[1] + n * HEAD_SIZE
+        scores = lax.dot_general(
+            q_ref[:, start : start + HEAD_SIZE],
+            keys,
+            (((1,), (1,)), ((), ())),
+            preferred_element_type=jnp.float32,
+        ) * (1.0 / math.sqrt(HEAD_SIZE))
+        scores = jnp.where(allowed, scores, jnp.float32(-1e30))
+        weights = jnp.exp(scores - jnp.max(scores, axis=1, keepdims=True))
+        weights = jnp.where(allowed, weights, jnp.float32(0.0))
+        mixed = jnp.dot(
+            weights.astype(jnp.bfloat16), values, preferred_element_type=jnp.float32
+        )
+        mixed = mixed / jnp.sum(weights, axis=1, keepdims=True)
+        out_ref[:, n * HEAD_SIZE : (n + 1) * HEAD_SIZE] = mixed.astype(jnp.bfloat16)
+
+
+def project_kernel(away, place_ref, w_ref, *refs):
+    out_ref, joined_ref = refs[-2:]
+    sessions, rows, piece = out_ref.shape
+    depth = refs[0].shape[1]
+    for n, ref in enumerate(refs[:-2]):
+        half, r = divmod(n, sessions)
+        joined_ref[r * rows : (r + 1) * rows, half * depth : (half + 1) * depth] = ref[...]
+    start = pl.multiple_of(lax.bitwise_xor(place_ref[1], away) * piece, piece)
+    result = jnp.dot(
+        joined_ref[...], w_ref[:, pl.ds(start, piece)], preferred_element_type=jnp.float32
+    )
+    out_ref[...] = result.reshape(sessions, rows, piece).astype(out_ref.dtype)
+
+
+def mix_kernel(sessions, place_ref, *refs):
+    x_refs, refs = refs[:sessions], refs[sessions:]
+    terms, (proj_ref, *chunk_refs) = refs[: -1 - CHUNKS], refs[-1 - CHUNKS :]
+    rows = chunk_refs[0].shape[1]
+    me = place_ref[0]
+    for r in range(sessions):
+        proj = sum(ref[r].astype(jnp.float32) for ref in terms)
+        proj_ref[r] = proj
+        mixed = (x_refs[r][...].astype(jnp.float32) + proj).astype(jnp.bfloat16)
+        for c, chunk_ref in enumerate(chunk_refs):
+            chunk_ref[lax.bitwise_xor(me, r)] = mixed[c * rows : (c + 1) * rows]
+
+
+def local_kernel(kernel, outs, operands, scratch=(), limit=12 << 20):
+    return pl.pallas_call(
+        kernel,
+        out_shape=outs,
+        in_specs=[pl.BlockSpec(memory_space=pltpu.SMEM)]
+        + [pl.BlockSpec(memory_space=pltpu.VMEM)] * (len(operands) - 1),
+        out_specs=[pl.BlockSpec(memory_space=pltpu.VMEM)] * len(outs),
+        scratch_shapes=scratch,
+        compiler_params=pltpu.CompilerParams(vmem_limit_bytes=limit),
+    )(*operands)
+
+
 def dense_plan(
     q_rows,
     k_rows,
@@ -303,54 +377,30 @@
     piece = width // (group_count * tensor_count)
     near, far = seq_bits[:1], seq_bits[1:]
 
-    kv_width = k_rows.shape[2]
+    place = jnp.stack([group_pos, tensor_pos, seq_pos]).astype(jnp.int32)
+
     kv_bits = far + near
-    kv_all = jnp.concatenate(
-        gather_parts(jnp.concatenate([k_rows[0], value_rows[0]], axis=1), "seq", kv_bits),
-        axis=0,
-    )
-    key_pos = (seq_pos ^ jnp.array(slot_order(kv_bits), jnp.int32))[:, None] * rows_here
-    key_pos = (key_pos + jnp.arange(rows_here, dtype=jnp.int32)[None, :]).reshape(-1)
+    keys = gather_parts(k_rows[0], "seq", kv_bits)
+    values = gather_parts(value_rows[0], "seq", kv_bits)
 
     x_slots = []
     for r in range(group_count):
         start = ((group_pos ^ r) * tensor_count + tensor_pos) * piece
         columns = lax.dynamic_slice_in_dim(x_rows[0], start, piece, 1)
         x_slots.append(swap(columns, "expert", r) if r else columns)
-    kv_all, *x_slots = lax.optimization_barrier((kv_all, *x_slots))
-
-    kv_heads = kv_width // HEAD_SIZE
-    q_heads = q_rows.shape[2] // HEAD_SIZE
-    group_width = q_heads // kv_heads
-    queries = q_rows[0].reshape(rows_here, kv_heads, group_width, HEAD_SIZE)
-    query_pos = seq_pos * rows_here + jnp.arange(rows_here, dtype=jnp.int32)
-    block_rows = kv_all.shape[0]
-    key_block = kv_all[:, :kv_width].reshape(block_rows, kv_heads, HEAD_SIZE)
-    value_block = kv_all[:, kv_width:].reshape(block_rows, kv_heads, HEAD_SIZE)
-    scores = jnp.einsum(
-        "igrd,jgd->grij", queries, key_block, preferred_element_type=jnp.float32
-    ) * (1.0 / math.sqrt(HEAD_SIZE))
-    allowed = key_pos[None, :] <= query_pos[:, None]
-    scores = jnp.where(allowed, scores, jnp.float32(-1e30))
-    weights = jnp.where(
-        allowed, jnp.exp(scores - jnp.max(scores, axis=-1, keepdims=True)), jnp.float32(0.0)
-    )
-    totals = jnp.sum(weights, axis=-1)
-    weighted = jnp.einsum(
-        "grij,jgd->grid",
-        weights.astype(jnp.bfloat16),
-        value_block,
-        preferred_element_type=jnp.float32,
-    )
-    attn_rows = (
-        (weighted / totals[..., None])
-        .transpose(2, 0, 1, 3)
-        .reshape(rows_here, q_heads * HEAD_SIZE)
-        .astype(jnp.bfloat16)
-    )
-
-    attn_rows, expert_ids, gate_weights, norm_gain, w_gate, w_up = lax.optimization_barrier(
-        (attn_rows, expert_ids, gate_weights, norm_gain, w_gate, w_up)
+
+    kv_heads = k_rows.shape[2] // HEAD_SIZE
+    depth = q_rows.shape[2] // kv_heads
+    attended = []
+    for head in range(kv_heads):
+        attended += local_kernel(
+            functools.partial(attention_kernel, head, tuple(slot_order(kv_bits))),
+            [jax.ShapeDtypeStruct((rows_here, depth), jnp.bfloat16)],
+            [place, q_rows[0], *keys, *values],
+        )
+
+    expert_ids, gate_weights, norm_gain, w_gate, w_up, _ = lax.optimization_barrier(
+        (expert_ids, gate_weights, norm_gain, w_gate, w_up, attended[0])
     )
     gain_slots = gather_slots(norm_gain, "tensor", tensor_bits)
     gain_at = jnp.array(slot_order(tensor_bits), jnp.int32) ^ tensor_pos
@@ -361,41 +411,43 @@
     w_in = jnp.concatenate([w_gate[0], w_up[0]], axis=1)
 
     paths = (group_bits, group_bits[::-1])
-    depth = attn_rows.shape[1] // len(paths)
     gathered = []
-    for n, path in enumerate(paths):
-        held = gather_parts(attn_rows[:, n * depth : (n + 1) * depth], "expert", path)
+    for n, rows_of in enumerate(attended):
+        path = paths[n % len(paths)]
+        held = gather_parts(rows_of, "expert", path)
         order = slot_order(path)
-        gathered.append(
-            jnp.concatenate([held[order.index(r)] for r in range(group_count)], axis=0)
-        )
-
-    def projected(k):
-        columns = lax.dynamic_slice_in_dim(out_weight, (tensor_pos ^ k) * piece, piece, 1)
-        return sum(
-            jnp.dot(
-                held, columns[n * depth : (n + 1) * depth], preferred_element_type=jnp.float32
-            )
-            for n, held in enumerate(gathered)
-        )
-
-    proj = projected(0)
+        gathered += [held[order.index(r)] for r in range(group_count)]
+
+    def projected(k, kind):
+        shape = (group_count, rows_here, piece)
+        return local_kernel(
+            functools.partial(project_kernel, k),
+            [jax.ShapeDtypeStruct(shape, kind)],
+            [place, out_weight, *gathered],
+            [pltpu.VMEM((group_count * rows_here, out_weight.shape[0]), jnp.bfloat16)],
+        )[0]
+
+    terms = []
     for k in range(1, tensor_count):
-        away = projected(k).astype(jnp.bfloat16)
-        proj = proj + swap(away, "tensor", k).astype(jnp.float32)
-    proj = proj.reshape(group_count, rows_here, piece)
-    mixed = (jnp.stack(x_slots).astype(jnp.float32) + proj).astype(jnp.bfloat16)
-    session_at = jnp.arange(group_count, dtype=jnp.int32) ^ group_pos
-    by_session = mixed.at[session_at].get(mode="promise_in_bounds")
-    by_session, gain, table, w_in = lax.optimization_barrier((by_session, gain, table, w_in))
-
+        away = projected(k, jnp.bfloat16)
+        terms.append(swap(away, "tensor", k))
+    terms.append(projected(0, jnp.float32))
     rows = rows_here // CHUNKS
+    part = jax.ShapeDtypeStruct((group_count, rows, piece), jnp.bfloat16)
+    proj, *by_session = local_kernel(
+        functools.partial(mix_kernel, group_count),
+        [jax.ShapeDtypeStruct((group_count, rows_here, piece), jnp.float32)] + [part] * CHUNKS,
+        [place, *x_slots, *terms],
+    )
+    gain, table, w_in, *by_session = lax.optimization_barrier(
+        (gain, table, w_in, *by_session)
+    )
+
     blocks = seq_count // 2
-    place = jnp.stack([group_pos, tensor_pos, seq_pos]).astype(jnp.int32)
     chunks = []
     for c in range(CHUNKS):
         path = paths[c % len(paths)]
-        held = by_session[:, c * rows : (c + 1) * rows]
+        held = by_session[c]
         held = gather_slots(held, "seq", far)
         held = gather_slots(held, "tensor", tensor_bits)
         own = gather_parts(held, "expert", path)
@@ -414,15 +466,13 @@
             operands += [proj, received]
             shapes = [jax.ShapeDtypeStruct(shape, jnp.bfloat16)] * group_count
         near_order = near[0] if received is None else 0
-        return pl.pallas_call(
+        return local_kernel(
             functools.partial(expert_kernel, order, near_order, c * rows),
-            out_shape=shapes,
-            in_specs=[pl.BlockSpec(memory_space=pltpu.SMEM)]
-            + [pl.BlockSpec(memory_space=pltpu.VMEM)] * (len(operands) - 1),
-            out_specs=[pl.BlockSpec(memory_space=pltpu.VMEM)] * len(shapes),
-            scratch_shapes=[pltpu.VMEM((group_count * blocks * rows, width), jnp.bfloat16)],
-            compiler_params=pltpu.CompilerParams(vmem_limit_bytes=KERNEL_BYTES),
-        )(*operands)
+            shapes,
+            operands,
+            [pltpu.VMEM((group_count * blocks * rows, width), jnp.bfloat16)],
+            KERNEL_BYTES,
+        )
 
     finished = []
     for c, path, own, other in chunks:

time: 206 us -> 209 us (1.015)
  Pallas kernels: 31.9 us -> 43.5 us
  matrix products: 8.35 us -> 0 us
  other arithmetic: 9.54 us -> 4.59 us
  starting transfers between devices: 70 us -> 74.4 us
  local copies, waits for them, and re-layouts: 20 us -> 22.9 us
  waiting for transfers between devices: 65.2 us -> 62.7 us
    pallas_call x8 -> x13, Pallas kernels: 31.9 us -> 43.5 us  [local_kernel(): pl.pallas_call(kernel, out_shape=outs, in_specs=[pl.BlockSpec(memory_spac...]
    dot_general x6 -> x0, matrix products: 8.35 us -> none  [the longest x4 7.13 us: projected(): jnp.dot(held, columns[n * depth:(n + 1) * depth], preferred_element_type=...]
    ppermute x74 -> x77, starting transfers between devices: 66.4 us -> 70.1 us  [swap(): return lax.ppermute(value, axis, [(i, i ^ bit) for i in range(count)])]
    unnamed x67 -> x96, local copies, waits for them, and re-layouts: 17.2 us -> 20.7 us
    ppermute x74 -> x77, waiting for transfers between devices: 65.2 us -> 62.7 us  [swap(): return lax.ppermute(value, axis, [(i, i ^ bit) for i in range(count)])]
    sub x1 -> x0, other arithmetic: 2.28 us -> none  [dense_plan(): scores - jnp.max(scores, axis=-1, keepdims=True)]
  transfers between devices with their start and end apart: 75 -> 78, of which waited for: 29 -> 23; matrix products, arithmetic and copies ran while one was open for 8% -> 3% of each run, Pallas kernels for 15% -> 19%
where the time goes in v2:
time: 209 us
  starting transfers between devices  74.4 us (36%)
  waiting for transfers between devices  62.7 us (30%)
  Pallas kernels  43.5 us (21%)
  local copies, waits for them, and re-layouts  22.9 us (11%)
  other arithmetic  4.59 us (2%)
    ppermute x77, starting transfers between devices, swap(): return lax.ppermute(value, axis, [(i, i ^ bit) for i in range(count)])  70.1 us
    ppermute x77, waiting for transfers between devices, swap(): return lax.ppermute(value, axis, [(i, i ^ bit) for i in range(count)])  62.7 us
    pallas_call x13, Pallas kernels, local_kernel(): pl.pallas_call(kernel, out_shape=outs, in_specs=[pl.BlockSpec(memory_spac...  43.5 us
    unnamed x96, local copies, waits for them, and re-layouts  20.7 us
    all_to_all x1, starting transfers between devices, dense_plan(): lax.all_to_all(table, ('seq', 'expert'), split_axis=0, concat_axis=0, til...  4.23 us
  transfers between devices with their start and end apart: 78, of which 23 were waited for; matrix products, arithmetic and copies ran while one was open for 3% of the time, Pallas kernels for 19%

profile of v2, /device:TPU:0, one launch (start us, length us, event | category | flops | bytes accessed | tf_op | source)
XLA Modules:
  0.0 208.6 jit_solution(17545723188184776409)
XLA Ops:
  0.0 4.1 %collective-permute-start = (bf16[128,256]{1,0:T(8,128)(2,1)}, bf16[128,256]{1,0:T(8,128)(2,1)S(1)}, u32[]{:S(2)}, u32[]{:S(2)}) collective-permute-start(bf16[128,256]{1,0:T(8,128)(2,1)} %bitcast.72), channel_id=1, source_target_pairs={{0,16},{8,24},{16,0},{24,8},{1,17},{9,25},{17,1},{25,9},{2,18},{10... | collective-permute-start | bytes 196616 | tf_op jit(solution)/shard_map/ppermute | solution.py:143
  4.6 3.3 %collective-permute-done.refs_1_ = bf16[128,256]{1,0:T(8,128)(2,1)S(1)} collective-permute-done((bf16[128,256]{1,0:T(8,128)(2,1)}, bf16[128,256]{1,0:T(8,128)(2,1)S(1)}, u32[]{:S(2)}, u32[]{:S(2)}) %collective-permute-start) | collective-permute-done | bytes 65568 | tf_op jit(solution)/shard_map/ppermute | solution.py:143
  8.0 2.8 %collective-permute-done.3.refs_5_ = bf16[128,256]{1,0:T(8,128)(2,1)S(1)} collective-permute-done((bf16[128,256]{1,0:T(8,128)(2,1)}, bf16[128,256]{1,0:T(8,128)(2,1)S(1)}, u32[]{:S(2)}, u32[]{:S(2)}) %collective-permute-start.3) | collective-permute-done | bytes 65568 | tf_op jit(solution)/shard_map/ppermute | solution.py:143
  10.8 1.2 collective-permute-done.5.refs_7_
  14.7 2.9 %shard_map.118.refs_0_ = bf16[128,1024]{1,0:T(8,128)(2,1)S(1)} custom-call(s32[3]{0:T(128)S(1)} %pad_add_fusion.place_ref.refs_0_, bf16[128,2048]{1,0:T(8,128)(2,1)S(1)} %bitcast.62, bf16[128,256]{1,0:T(8,128)(2,1)S(1)} %bitcast.74, bf16[128,256]{1,0:T(8,128)(2,1)S(1)} %collective-permute-done.refs_1_, bf16[128,256]{1,0:T(8,128)(2,1)S(1)} %collective-permute-done.1.refs_2_, ...), custom_call_target="tpu_custom_call" | custom-call | tf_op jit(solution)/shard_map/pallas_call | solution.py:343
  17.6 1.8 collective-permute-start.10
  19.4 2.9 %shard_map.119.refs_4_ = bf16[128,1024]{1,0:T(8,128)(2,1)S(1)} custom-call(s32[3]{0:T(128)S(1)} %pad_add_fusion.place_ref.refs_0_, bf16[128,2048]{1,0:T(8,128)(2,1)S(1)} %bitcast.63, bf16[128,256]{1,0:T(8,128)(2,1)S(1)} %bitcast.75, bf16[128,256]{1,0:T(8,128)(2,1)S(1)} %collective-permute-done.refs_1_, bf16[128,256]{1,0:T(8,128)(2,1)S(1)} %collective-permute-done.1.refs_2_, ...), custom_call_target="tpu_custom_call" | custom-call | tf_op jit(solution)/shard_map/pallas_call | solution.py:343
  22.3 1.6 collective-permute-start.14
  23.9 1.6 dynamic-slice_bitcast_fusion
  26.3 1.7 collective-permute-start.13
  28.0 1.5 collective-permute-start.12
  29.5 2.0 collective-permute-done.14.refs_6_
  32.5 4.2 %all-to-all-start = ((f32[16,1,128]{2,1,0:T(1,128)}), f32[16,1,128]{2,1,0:T(1,128)S(1)}, u32[]{:S(2)}, u32[]{:S(2)}) async-start(f32[16,1,128]{2,1,0:T(1,128)} %bitcast.11), calls=%async_computation | async-start | bytes 16384 | tf_op jit(solution)/shard_map/all_to_all | solution.py:410
  37.2 1.5 collective-permute-start.8
  38.7 1.4 collective-permute-start.9
  40.1 3.2 %collective-permute-done.12.refs_3_ = bf16[128,1024]{1,0:T(8,128)(2,1)} collective-permute-done((bf16[128,1024]{1,0:T(8,128)(2,1)S(1)}, bf16[128,1024]{1,0:T(8,128)(2,1)}, u32[]{:S(2)}, u32[]{:S(2)}) %collective-permute-start.12) | collective-permute-done | bytes 262176 | tf_op jit(solution)/shard_map/ppermute | solution.py:143
  43.3 2.5 %shard_map.120 = bf16[4,128,256]{2,1,0:T(8,128)(2,1)} custom-call(s32[3]{0:T(128)S(1)} %pad_add_fusion.place_ref.refs_0_, bf16[2048,512]{1,0:T(8,128)(2,1)S(1)} %copy-done.2, bf16[128,1024]{1,0:T(8,128)(2,1)S(1)} %shard_map.118.refs_0_, bf16[128,1024]{1,0:T(8,128)(2,1)S(1)} %collective-permute-done.10.refs_1_, ...), custom_call_target="tpu_custom_call" | custom-call | tf_op jit(solution)/shard_map/pallas_call | solution.py:343
  45.8 2.0 collective-permute-start.16
  48.8 1.6 copy-done.3
  54.1 1.9 shard_map.121.refs_5_
  56.1 1.2 shard_map.122
  58.4 2.6 %collective-permute-start.32 = (bf16[1,4,32,256]{3,2,1,0:T(8,128)(2,1)S(1)}, bf16[1,4,32,256]{3,2,1,0:T(8,128)(2,1)S(1)}, u32[]{:S(2)}, u32[]{:S(2)}) collective-permute-start(bf16[1,4,32,256]{3,2,1,0:T(8,128)(2,1)S(1)} %bitcast.84), channel_id=1, source_target_pairs={{0,16},{8,24},{16,0},{24,8},{1,17},{9,25},{17,1},{25,9},{2,18},{10... | collective-permute-start | bytes 196616 | tf_op jit(solution)/shard_map/ppermute | solution.py:143
  61.3 2.6 %collective-permute-start.62 = (bf16[1,4,32,256]{3,2,1,0:T(8,128)(2,1)S(1)}, bf16[1,4,32,256]{3,2,1,0:T(8,128)(2,1)S(1)}, u32[]{:S(2)}, u32[]{:S(2)}) collective-permute-start(bf16[1,4,32,256]{3,2,1,0:T(8,128)(2,1)S(1)} %bitcast.80), channel_id=1, source_target_pairs={{0,16},{8,24},{16,0},{24,8},{1,17},{9,25},{17,1},{25,9},{2,18},{10... | collective-permute-start | bytes 196616 | tf_op jit(solution)/shard_map/ppermute | solution.py:143
  63.9 4.6 %collective-permute-done.17 = bf16[1,4,32,256]{3,2,1,0:T(8,128)(2,1)S(1)} collective-permute-done((bf16[1,4,32,256]{3,2,1,0:T(8,128)(2,1)S(1)}, bf16[1,4,32,256]{3,2,1,0:T(8,128)(2,1)S(1)}, u32[]{:S(2)}, u32[]{:S(2)}) %collective-permute-start.17) | collective-permute-done | bytes 65568 | tf_op jit(solution)/shard_map/ppermute | solution.py:143
  69.4 1.3 collective-permute-start.33
  71.6 3.0 %collective-permute-done.18 = bf16[1,2,4,32,256]{4,3,2,1,0:T(8,128)(2,1)S(1)} collective-permute-done((bf16[1,2,4,32,256]{4,3,2,1,0:T(8,128)(2,1)S(1)}, bf16[1,2,4,32,256]{4,3,2,1,0:T(8,128)(2,1)S(1)}, u32[]{:S(2)}, u32[]{:S(2)}) %collective-permute-start.18) | collective-permute-done | bytes 131104 | tf_op jit(solution)/shard_map/ppermute | solution.py:143
  74.7 2.0 collective-permute-start.20
  77.4 5.4 %collective-permute-done.63 = bf16[1,2,4,32,256]{4,3,2,1,0:T(8,128)(2,1)S(1)} collective-permute-done((bf16[1,2,4,32,256]{4,3,2,1,0:T(8,128)(2,1)S(1)}, bf16[1,2,4,32,256]{4,3,2,1,0:T(8,128)(2,1)S(1)}, u32[]{:S(2)}, u32[]{:S(2)}) %collective-permute-start.63) | collective-permute-done | bytes 131104 | tf_op jit(solution)/shard_map/ppermute | solution.py:143
  82.9 1.7 collective-permute-start.35
  84.7 1.2 collective-permute-start.49
  86.8 5.2 %collective-permute-done.35.refs_7_ = bf16[2,2,4,32,256]{4,3,2,1,0:T(8,128)(2,1)S(1)} collective-permute-done((bf16[2,2,4,32,256]{4,3,2,1,0:T(8,128)(2,1)S(1)}, bf16[2,2,4,32,256]{4,3,2,1,0:T(8,128)(2,1)S(1)}, u32[]{:S(2)}, u32[]{:S(2)}) %collective-permute-start.35) | collective-permute-done | bytes 262176 | tf_op jit(solution)/shard_map/ppermute | solution.py:143
  92.0 1.7 collective-permute-start.64
  94.1 3.5 %collective-permute-done.49.refs_6_ = bf16[2,2,4,32,256]{4,3,2,1,0:T(8,128)(2,1)S(1)} collective-permute-done((bf16[2,2,4,32,256]{4,3,2,1,0:T(8,128)(2,1)S(1)}, bf16[2,2,4,32,256]{4,3,2,1,0:T(8,128)(2,1)S(1)}, u32[]{:S(2)}, u32[]{:S(2)}) %collective-permute-start.49) | collective-permute-done | bytes 262176 | tf_op jit(solution)/shard_map/ppermute | solution.py:143
  98.4 1.7 collective-permute-start.21
  101.7 1.7 collective-permute-start.36
  103.4 3.7 %collective-permute-done.21.refs_8_ = bf16[2,2,4,32,256]{4,3,2,1,0:T(8,128)(2,1)S(1)} collective-permute-done((bf16[2,2,4,32,256]{4,3,2,1,0:T(8,128)(2,1)S(1)}, bf16[2,2,4,32,256]{4,3,2,1,0:T(8,128)(2,1)S(1)}, u32[]{:S(2)}, u32[]{:S(2)}) %collective-permute-start.21) | collective-permute-done | bytes 262176 | tf_op jit(solution)/shard_map/ppermute | solution.py:143
  107.1 1.7 collective-permute-start.51
  111.0 1.1 collective-permute-start.66
  112.1 3.7 %collective-permute-done.51.refs_8_ = bf16[2,2,4,32,256]{4,3,2,1,0:T(8,128)(2,1)S(1)} collective-permute-done((bf16[2,2,4,32,256]{4,3,2,1,0:T(8,128)(2,1)S(1)}, bf16[2,2,4,32,256]{4,3,2,1,0:T(8,128)(2,1)S(1)}, u32[]{:S(2)}, u32[]{:S(2)}) %collective-permute-start.51) | collective-permute-done | bytes 262176 | tf_op jit(solution)/shard_map/ppermute | solution.py:143
  116.3 3.4 %shard_map.123 = bf16[4,2,2,32,1024]{4,3,2,1,0:T(8,128)(2,1)S(1)} custom-call(s32[3]{0:T(128)S(1)} %pad_add_fusion.place_ref.refs_0_, f32[8,256]{1,0:T(8,128)S(1)} %reshape.516.refs_1_, f32[16,128]{1,0:T(8,128)S(1)} %bitcast.64, bf16[2048,768]{1,0:T(8,128)(2,1)S(1)} %pad_maximum_fusion.refs_3_, bf16[384,2048]{1,0:T(8,128)(2,1)S(1)} %bitcast.54, ...), custom_call_target="tpu_custom_call" | custom-call | tf_op jit(solution)/shard_map/pallas_call | solution.py:343
  122.2 3.3 %shard_map.125 = bf16[4,2,2,32,1024]{4,3,2,1,0:T(8,128)(2,1)S(1)} custom-call(s32[3]{0:T(128)S(1)} %pad_add_fusion.place_ref.refs_0_, f32[8,256]{1,0:T(8,128)S(1)} %reshape.516.refs_1_, f32[16,128]{1,0:T(8,128)S(1)} %bitcast.65, bf16[2048,768]{1,0:T(8,128)(2,1)S(1)} %pad_maximum_fusion.refs_3_, bf16[384,2048]{1,0:T(8,128)(2,1)S(1)} %bitcast.55, ...), custom_call_target="tpu_custom_call" | custom-call | tf_op jit(solution)/shard_map/pallas_call | solution.py:343
  125.8 4.4 %shard_map.127 = bf16[4,2,2,32,1024]{4,3,2,1,0:T(8,128)(2,1)} custom-call(s32[3]{0:T(128)S(1)} %pad_add_fusion.place_ref.refs_0_, f32[8,256]{1,0:T(8,128)S(1)} %reshape.516.refs_1_, f32[16,128]{1,0:T(8,128)S(1)} %bitcast.66, bf16[2048,768]{1,0:T(8,128)(2,1)S(1)} %pad_maximum_fusion.refs_3_, bf16[384,2048]{1,0:T(8,128)(2,1)S(1)} %bitcast.56, ...), custom_call_target="tpu_custom_call" | custom-call | tf_op jit(solution)/shard_map/pallas_call | solution.py:343
  130.6 4.5 %shard_map.129 = bf16[4,2,2,32,1024]{4,3,2,1,0:T(8,128)(2,1)} custom-call(s32[3]{0:T(128)S(1)} %pad_add_fusion.place_ref.refs_0_, f32[8,256]{1,0:T(8,128)S(1)} %reshape.516.refs_1_, f32[16,128]{1,0:T(8,128)S(1)} %bitcast.67, bf16[2048,768]{1,0:T(8,128)(2,1)S(1)} %pad_maximum_fusion.refs_3_, bf16[384,2048]{1,0:T(8,128)(2,1)S(1)} %bitcast.57, ...), custom_call_target="tpu_custom_call" | custom-call | tf_op jit(solution)/shard_map/pallas_call | solution.py:343
  135.2 4.1 %shard_map.124 = (bf16[2,2,32,1024]{3,2,1,0:T(8,128)(2,1)S(1)}, bf16[2,2,32,1024]{3,2,1,0:T(8,128)(2,1)S(1)}, bf16[2,2,32,1024]{3,2,1,0:T(8,128)(2,1)S(1)}, bf16[2,2,32,1024]{3,2,1,0:T(8,128)(2,1)}) custom-call(s32[3]{0:T(128)S(1)} %pad_add_fusion.place_ref.refs_0_, f32[8,256]{1,0:T(8,128)S(1)} %reshape.516.refs_1_, f32[16,128]{1,0:T(8,128)S(1)} %bitcast.68, ...), custom_call_target="tpu_custom_call" | custom-call | tf_op jit(solution)/shard_map/pallas_call | solution.py:343
  140.0 1.7 collective-permute-start.28
  141.7 4.1 %shard_map.126 = (bf16[2,2,32,1024]{3,2,1,0:T(8,128)(2,1)S(1)}, bf16[2,2,32,1024]{3,2,1,0:T(8,128)(2,1)S(1)}, bf16[2,2,32,1024]{3,2,1,0:T(8,128)(2,1)S(1)}, bf16[2,2,32,1024]{3,2,1,0:T(8,128)(2,1)}) custom-call(s32[3]{0:T(128)S(1)} %pad_add_fusion.place_ref.refs_0_, f32[8,256]{1,0:T(8,128)S(1)} %reshape.516.refs_1_, f32[16,128]{1,0:T(8,128)S(1)} %bitcast.69, ...), custom_call_target="tpu_custom_call" | custom-call | tf_op jit(solution)/shard_map/pallas_call | solution.py:343
  148.4 1.6 collective-permute-start.27
  150.3 1.4 copy-done.1
  155.7 4.2 %shard_map.128 = (bf16[2,2,32,1024]{3,2,1,0:T(8,128)(2,1)S(1)}, bf16[2,2,32,1024]{3,2,1,0:T(8,128)(2,1)S(1)}, bf16[2,2,32,1024]{3,2,1,0:T(8,128)(2,1)S(1)}, bf16[2,2,32,1024]{3,2,1,0:T(8,128)(2,1)S(1)}) custom-call(s32[3]{0:T(128)S(1)} %pad_add_fusion.place_ref.refs_0_, f32[8,256]{1,0:T(8,128)S(1)} %reshape.516.refs_1_, f32[16,128]{1,0:T(8,128)S(1)} %bitcast.70, ...), custom_call_target="tpu_custom_call" | custom-call | tf_op jit(solution)/shard_map/pallas_call | solution.py:343
  159.9 1.8 collective-permute-start.58
  161.7 4.1 %shard_map.130 = (bf16[2,2,32,1024]{3,2,1,0:T(8,128)(2,1)S(1)}, bf16[2,2,32,1024]{3,2,1,0:T(8,128)(2,1)S(1)}, bf16[2,2,32,1024]{3,2,1,0:T(8,128)(2,1)S(1)}, bf16[2,2,32,1024]{3,2,1,0:T(8,128)(2,1)S(1)}) custom-call(s32[3]{0:T(128)S(1)} %pad_add_fusion.place_ref.refs_0_, f32[8,256]{1,0:T(8,128)S(1)} %reshape.516.refs_1_, f32[16,128]{1,0:T(8,128)S(1)} %bitcast.71, ...), custom_call_target="tpu_custom_call" | custom-call | tf_op jit(solution)/shard_map/pallas_call | solution.py:343
  167.2 1.8 collective-permute-start.73
  170.6 5.9 %collective-permute-done.73 = bf16[2,2,32,1024]{3,2,1,0:T(8,128)(2,1)S(1)} collective-permute-done((bf16[2,2,32,1024]{3,2,1,0:T(8,128)(2,1)S(1)}, bf16[2,2,32,1024]{3,2,1,0:T(8,128)(2,1)S(1)}, u32[]{:S(2)}, u32[]{:S(2)}) %collective-permute-start.73) | collective-permute-done | bytes 262176 | tf_op jit(solution)/shard_map/ppermute | solution.py:143
  176.4 1.7 collective-permute-start.44
  178.7 3.4 %collective-permute-done.29 = bf16[2,2,32,1024]{3,2,1,0:T(8,128)(2,1)S(1)} collective-permute-done((bf16[2,2,32,1024]{3,2,1,0:T(8,128)(2,1)S(1)}, bf16[2,2,32,1024]{3,2,1,0:T(8,128)(2,1)S(1)}, u32[]{:S(2)}, u32[]{:S(2)}) %collective-permute-start.29) | collective-permute-done | bytes 262176 | tf_op jit(solution)/shard_map/ppermute | solution.py:143
  182.1 1.7 collective-permute-start.59
  184.7 1.8 collective-permute-start.45
  186.5 4.7 %collective-permute-done.59 = bf16[2,2,32,1024]{3,2,1,0:T(8,128)(2,1)S(1)} collective-permute-done((bf16[2,2,32,1024]{3,2,1,0:T(8,128)(2,1)S(1)}, bf16[2,2,32,1024]{3,2,1,0:T(8,128)(2,1)S(1)}, u32[]{:S(2)}, u32[]{:S(2)}) %collective-permute-start.59) | collective-permute-done | bytes 262176 | tf_op jit(solution)/shard_map/ppermute | solution.py:143
  191.6 1.8 collective-permute-start.75
  193.4 3.1 %collective-permute-start.31 = (bf16[1,32,1024]{2,1,0:T(8,128)(2,1)S(1)}, bf16[1,32,1024]{2,1,0:T(8,128)(2,1)S(1)}, u32[]{:S(2)}, u32[]{:S(2)}) collective-permute-start(bf16[1,32,1024]{2,1,0:T(8,128)(2,1)S(1)} %fusion.1), channel_id=1, source_target_pairs={{0,16},{8,24},{16,0},{24,8},{1,17},{9,25},{17,1},{25,9},{2,18},{10... | collective-permute-start | bytes 196616 | tf_op jit(solution)/shard_map/ppermute | solution.py:143
  196.9 3.8 %collective-permute-start.61 = (bf16[1,32,1024]{2,1,0:T(8,128)(2,1)S(1)}, bf16[1,32,1024]{2,1,0:T(8,128)(2,1)S(1)}, u32[]{:S(2)}, u32[]{:S(2)}) collective-permute-start(bf16[1,32,1024]{2,1,0:T(8,128)(2,1)S(1)} %fusion.3), channel_id=1, source_target_pairs={{0,16},{8,24},{16,0},{24,8},{1,17},{9,25},{17,1},{25,9},{2,18},{10... | collective-permute-start | bytes 196616 | tf_op jit(solution)/shard_map/ppermute | solution.py:143
  200.8 2.7 %collective-permute-start.76 = (bf16[1,32,1024]{2,1,0:T(8,128)(2,1)S(1)}, bf16[1,32,1024]{2,1,0:T(8,128)(2,1)S(1)}, u32[]{:S(2)}, u32[]{:S(2)}) collective-permute-start(bf16[1,32,1024]{2,1,0:T(8,128)(2,1)S(1)} %fusion.4), channel_id=1, source_target_pairs={{0,16},{8,24},{16,0},{24,8},{1,17},{9,25},{17,1},{25,9},{2,18},{10... | collective-permute-start | bytes 196616 | tf_op jit(solution)/shard_map/ppermute | solution.py:143
  203.6 1.9 collective-permute-done.46
  206.4 1.4 collective-permute-done.76
  (235 shorter events, 38.4 us)
Async XLA Ops:
  0.0 8.0 %collective-permute-start = (bf16[128,256]{1,0:T(8,128)(2,1)}, bf16[128,256]{1,0:T(8,128)(2,1)S(1)}, u32[]{:S(2)}, u32[]{:S(2)}) collective-permute-start(bf16[128,256]{1,0:T(8,128)(2,1)} %bitcast.72), channel_id=1, source_target_pairs={{0,16},{8,24},{16,0},{24,8},{1,17},{9,25},{17,1},{25,9},{2,18},{10... | collective-permute-start | bytes 196616 | tf_op jit(solution)/shard_map/ppermute | solution.py:143
  17.6 10.4 %collective-permute-start.10 = (bf16[128,1024]{1,0:T(8,128)(2,1)S(1)}, bf16[128,1024]{1,0:T(8,128)(2,1)S(1)}, u32[]{:S(2)}, u32[]{:S(2)}) collective-permute-start(bf16[128,1024]{1,0:T(8,128)(2,1)S(1)} %shard_map.118.refs_0_), channel_id=1, source_target_pairs={{0,2},{2,0},{4,6},{6,4},{1,3},{3,1},{5,7},{7,5},{8,10},{10,8},{12,... | collective-permute-start | bytes 786440 | tf_op jit(solution)/shard_map/ppermute | solution.py:143
  22.3 9.2 %collective-permute-start.14 = (bf16[128,1024]{1,0:T(8,128)(2,1)S(1)}, bf16[128,1024]{1,0:T(8,128)(2,1)S(1)}, u32[]{:S(2)}, u32[]{:S(2)}) collective-permute-start(bf16[128,1024]{1,0:T(8,128)(2,1)S(1)} %shard_map.119.refs_4_), channel_id=1, source_target_pairs={{0,4},{2,6},{4,0},{6,2},{1,5},{3,7},{5,1},{7,3},{8,12},{10,14},{12... | collective-permute-start | bytes 786440 | tf_op jit(solution)/shard_map/ppermute | solution.py:143
  25.5 30.5 %collective-permute-start.7 = (bf16[128,256]{1,0:T(8,128)(2,1)}, bf16[128,256]{1,0:T(8,128)(2,1)}, u32[]{:S(2)}, u32[]{:S(2)}) collective-permute-start(bf16[128,256]{1,0:T(8,128)(2,1)} %get-tuple-element.72), channel_id=1, source_target_pairs={{0,2},{2,0},{4,6},{6,4},{1,3},{3,1},{5,7},{7,5},{8,10},{10,8},{12,... | collective-permute-start | bytes 196616 | tf_op jit(solution)/shard_map/ppermute | solution.py:143
  26.0 11.2 %collective-permute-start.11 = (bf16[128,1024]{1,0:T(8,128)(2,1)S(1)}, bf16[128,1024]{1,0:T(8,128)(2,1)S(1)}, u32[]{:S(2)}, u32[]{:S(2)}) collective-permute-start(bf16[128,1024]{1,0:T(8,128)(2,1)S(1)} %shard_map.118.refs_0_), channel_id=1, source_target_pairs={{0,4},{2,6},{4,0},{6,2},{1,5},{3,7},{5,1},{7,3},{8,12},{10,14},{12... | collective-permute-start | bytes 786440 | tf_op jit(solution)/shard_map/ppermute | solution.py:143
  26.3 12.4 %collective-permute-start.13 = (bf16[128,1024]{1,0:T(8,128)(2,1)S(1)}, bf16[128,1024]{1,0:T(8,128)(2,1)}, u32[]{:S(2)}, u32[]{:S(2)}) collective-permute-start(bf16[128,1024]{1,0:T(8,128)(2,1)S(1)} %shard_map.119.refs_4_), channel_id=1, source_target_pairs={{0,2},{2,0},{4,6},{6,4},{1,3},{3,1},{5,7},{7,5},{8,10},{10,8},{12,... | collective-permute-start | bytes 786440 | tf_op jit(solution)/shard_map/ppermute | solution.py:143
  28.0 15.2 %collective-permute-start.12 = (bf16[128,1024]{1,0:T(8,128)(2,1)S(1)}, bf16[128,1024]{1,0:T(8,128)(2,1)}, u32[]{:S(2)}, u32[]{:S(2)}) collective-permute-start(bf16[128,1024]{1,0:T(8,128)(2,1)S(1)} %collective-permute-done.10.refs_1_), channel_id=1, source_target_pairs={{0,4},{2,6},{4,0},{6,2},{1,5},{3,7},{5,1},{7,3},{8,12},{10,14},{12... | collective-permute-start | bytes 786440 | tf_op jit(solution)/shard_map/ppermute | solution.py:143
  31.5 11.7 %collective-permute-start.15 = (bf16[128,1024]{1,0:T(8,128)(2,1)S(1)}, bf16[128,1024]{1,0:T(8,128)(2,1)}, u32[]{:S(2)}, u32[]{:S(2)}) collective-permute-start(bf16[128,1024]{1,0:T(8,128)(2,1)S(1)} %collective-permute-done.14.refs_6_), channel_id=1, source_target_pairs={{0,2},{2,0},{4,6},{6,4},{1,3},{3,1},{5,7},{7,5},{8,10},{10,8},{12,... | collective-permute-start | bytes 786440 | tf_op jit(solution)/shard_map/ppermute | solution.py:143
  32.5 25.5 %all-to-all-start = ((f32[16,1,128]{2,1,0:T(1,128)}), f32[16,1,128]{2,1,0:T(1,128)S(1)}, u32[]{:S(2)}, u32[]{:S(2)}) async-start(f32[16,1,128]{2,1,0:T(1,128)} %bitcast.11), calls=%async_computation | async-start | bytes 16384 | tf_op jit(solution)/shard_map/all_to_all | solution.py:410
  37.2 18.9 %collective-permute-start.8 = (bf16[128,256]{1,0:T(8,128)(2,1)}, bf16[128,256]{1,0:T(8,128)(2,1)}, u32[]{:S(2)}, u32[]{:S(2)}) collective-permute-start(bf16[128,256]{1,0:T(8,128)(2,1)} %get-tuple-element.74), channel_id=1, source_target_pairs={{0,4},{2,6},{4,0},{6,2},{1,5},{3,7},{5,1},{7,3},{8,12},{10,14},{12... | collective-permute-start | bytes 196616 | tf_op jit(solution)/shard_map/ppermute | solution.py:143
  38.7 17.4 %collective-permute-start.9 = (bf16[128,256]{1,0:T(8,128)(2,1)}, bf16[128,256]{1,0:T(8,128)(2,1)}, u32[]{:S(2)}, u32[]{:S(2)}) collective-permute-start(bf16[128,256]{1,0:T(8,128)(2,1)} %get-tuple-element.71), channel_id=1, source_target_pairs={{0,6},{2,4},{4,2},{6,0},{1,7},{3,5},{5,3},{7,1},{8,14},{10,12},{12... | collective-permute-start | bytes 196616 | tf_op jit(solution)/shard_map/ppermute | solution.py:143
  45.8 10.2 %collective-permute-start.16 = (bf16[4,128,256]{2,1,0:T(8,128)(2,1)}, bf16[4,128,256]{2,1,0:T(8,128)(2,1)}, u32[]{:S(2)}, u32[]{:S(2)}) collective-permute-start(bf16[4,128,256]{2,1,0:T(8,128)(2,1)} %shard_map.120), channel_id=1, source_target_pairs={{0,1},{1,0},{2,3},{3,2},{4,5},{5,4},{6,7},{7,6},{8,9},{9,8},{10,11... | collective-permute-start | bytes 786440 | tf_op jit(solution)/shard_map/ppermute | solution.py:143
  58.0 10.4 %collective-permute-start.17 = (bf16[1,4,32,256]{3,2,1,0:T(8,128)(2,1)S(1)}, bf16[1,4,32,256]{3,2,1,0:T(8,128)(2,1)S(1)}, u32[]{:S(2)}, u32[]{:S(2)}) collective-permute-start(bf16[1,4,32,256]{3,2,1,0:T(8,128)(2,1)S(1)} %bitcast.86), channel_id=1, source_target_pairs={{0,16},{8,24},{16,0},{24,8},{1,17},{9,25},{17,1},{25,9},{2,18},{10... | collective-permute-start | bytes 196616 | tf_op jit(solution)/shard_map/ppermute | solution.py:143
  58.4 11.0 %collective-permute-start.32 = (bf16[1,4,32,256]{3,2,1,0:T(8,128)(2,1)S(1)}, bf16[1,4,32,256]{3,2,1,0:T(8,128)(2,1)S(1)}, u32[]{:S(2)}, u32[]{:S(2)}) collective-permute-start(bf16[1,4,32,256]{3,2,1,0:T(8,128)(2,1)S(1)} %bitcast.84), channel_id=1, source_target_pairs={{0,16},{8,24},{16,0},{24,8},{1,17},{9,25},{17,1},{25,9},{2,18},{10... | collective-permute-start | bytes 196616 | tf_op jit(solution)/shard_map/ppermute | solution.py:143
  61.0 9.7 %collective-permute-start.47 = (bf16[1,4,32,256]{3,2,1,0:T(8,128)(2,1)S(1)}, bf16[1,4,32,256]{3,2,1,0:T(8,128)(2,1)S(1)}, u32[]{:S(2)}, u32[]{:S(2)}) collective-permute-start(bf16[1,4,32,256]{3,2,1,0:T(8,128)(2,1)S(1)} %bitcast.82), channel_id=1, source_target_pairs={{0,16},{8,24},{16,0},{24,8},{1,17},{9,25},{17,1},{25,9},{2,18},{10... | collective-permute-start | bytes 196616 | tf_op jit(solution)/shard_map/ppermute | solution.py:143
  61.3 15.5 %collective-permute-start.62 = (bf16[1,4,32,256]{3,2,1,0:T(8,128)(2,1)S(1)}, bf16[1,4,32,256]{3,2,1,0:T(8,128)(2,1)S(1)}, u32[]{:S(2)}, u32[]{:S(2)}) collective-permute-start(bf16[1,4,32,256]{3,2,1,0:T(8,128)(2,1)S(1)} %bitcast.80), channel_id=1, source_target_pairs={{0,16},{8,24},{16,0},{24,8},{1,17},{9,25},{17,1},{25,9},{2,18},{10... | collective-permute-start | bytes 196616 | tf_op jit(solution)/shard_map/ppermute | solution.py:143
  69.4 7.3 %collective-permute-start.33 = (bf16[1,2,4,32,256]{4,3,2,1,0:T(8,128)(2,1)S(1)}, bf16[1,2,4,32,256]{4,3,2,1,0:T(8,128)(2,1)S(1)}, u32[]{:S(2)}, u32[]{:S(2)}) collective-permute-start(bf16[1,2,4,32,256]{4,3,2,1,0:T(8,128)(2,1)S(1)} %maximum_bitcast_fusion.1), channel_id=1, source_target_pairs={{0,1},{1,0},{2,3},{3,2},{4,5},{5,4},{6,7},{7,6},{8,9},{9,8},{10,11... | collective-permute-start | bytes 393224 | tf_op jit(solution)/shard_map/ppermute | solution.py:143
  74.6 10.0 %collective-permute-start.19 = (bf16[2,2,4,32,256]{4,3,2,1,0:T(8,128)(2,1)S(1)}, bf16[2,2,4,32,256]{4,3,2,1,0:T(8,128)(2,1)S(1)}, u32[]{:S(2)}, u32[]{:S(2)}) collective-permute-start(bf16[2,2,4,32,256]{4,3,2,1,0:T(8,128)(2,1)S(1)} %pad_maximum_fusion.1.refs_5_), channel_id=1, source_target_pairs={{0,2},{2,0},{4,6},{6,4},{1,3},{3,1},{5,7},{7,5},{8,10},{10,8},{12,... | collective-permute-start | bytes 786440 | tf_op jit(solution)/shard_map/ppermute | solution.py:143
  74.7 10.0 %collective-permute-start.20 = (bf16[2,2,4,32,256]{4,3,2,1,0:T(8,128)(2,1)S(1)}, bf16[2,2,4,32,256]{4,3,2,1,0:T(8,128)(2,1)S(1)}, u32[]{:S(2)}, u32[]{:S(2)}) collective-permute-start(bf16[2,2,4,32,256]{4,3,2,1,0:T(8,128)(2,1)S(1)} %pad_maximum_fusion.1.refs_5_), channel_id=1, source_target_pairs={{0,4},{2,6},{4,0},{6,2},{1,5},{3,7},{5,1},{7,3},{8,12},{10,14},{12... | collective-permute-start | bytes 786440 | tf_op jit(solution)/shard_map/ppermute | solution.py:143
  76.7 9.2 %collective-permute-start.22 = (bf16[2,2,4,32,256]{4,3,2,1,0:T(8,128)(2,1)S(1)}, bf16[2,2,4,32,256]{4,3,2,1,0:T(8,128)(2,1)S(1)}, u32[]{:S(2)}, u32[]{:S(2)}) collective-permute-start(bf16[2,2,4,32,256]{4,3,2,1,0:T(8,128)(2,1)S(1)} %pad_maximum_fusion.1.refs_5_), channel_id=1, source_target_pairs={{0,8},{8,0},{16,24},{24,16},{1,9},{9,1},{17,25},{25,17},{2,10},{10... | collective-permute-start | bytes 786440 | tf_op jit(solution)/shard_map/ppermute | solution.py:143
  76.8 10.0 %collective-permute-start.34 = (bf16[2,2,4,32,256]{4,3,2,1,0:T(8,128)(2,1)S(1)}, bf16[2,2,4,32,256]{4,3,2,1,0:T(8,128)(2,1)S(1)}, u32[]{:S(2)}, u32[]{:S(2)}) collective-permute-start(bf16[2,2,4,32,256]{4,3,2,1,0:T(8,128)(2,1)S(1)} %pad_maximum_fusion.2.refs_5_), channel_id=1, source_target_pairs={{0,4},{2,6},{4,0},{6,2},{1,5},{3,7},{5,1},{7,3},{8,12},{10,14},{12... | collective-permute-start | bytes 786440 | tf_op jit(solution)/shard_map/ppermute | solution.py:143
  82.9 9.2 %collective-permute-start.35 = (bf16[2,2,4,32,256]{4,3,2,1,0:T(8,128)(2,1)S(1)}, bf16[2,2,4,32,256]{4,3,2,1,0:T(8,128)(2,1)S(1)}, u32[]{:S(2)}, u32[]{:S(2)}) collective-permute-start(bf16[2,2,4,32,256]{4,3,2,1,0:T(8,128)(2,1)S(1)} %pad_maximum_fusion.2.refs_5_), channel_id=1, source_target_pairs={{0,2},{2,0},{4,6},{6,4},{1,3},{3,1},{5,7},{7,5},{8,10},{10,8},{12,... | collective-permute-start | bytes 786440 | tf_op jit(solution)/shard_map/ppermute | solution.py:143
  84.6 9.1 %collective-permute-start.37 = (bf16[2,2,4,32,256]{4,3,2,1,0:T(8,128)(2,1)S(1)}, bf16[2,2,4,32,256]{4,3,2,1,0:T(8,128)(2,1)S(1)}, u32[]{:S(2)}, u32[]{:S(2)}) collective-permute-start(bf16[2,2,4,32,256]{4,3,2,1,0:T(8,128)(2,1)S(1)} %pad_maximum_fusion.2.refs_5_), channel_id=1, source_target_pairs={{0,8},{8,0},{16,24},{24,16},{1,9},{9,1},{17,25},{25,17},{2,10},{10... | collective-permute-start | bytes 786440 | tf_op jit(solution)/shard_map/ppermute | solution.py:143
  84.7 12.9 %collective-permute-start.49 = (bf16[2,2,4,32,256]{4,3,2,1,0:T(8,128)(2,1)S(1)}, bf16[2,2,4,32,256]{4,3,2,1,0:T(8,128)(2,1)S(1)}, u32[]{:S(2)}, u32[]{:S(2)}) collective-permute-start(bf16[2,2,4,32,256]{4,3,2,1,0:T(8,128)(2,1)S(1)} %pad_maximum_fusion.3.refs_5_), channel_id=1, source_target_pairs={{0,2},{2,0},{4,6},{6,4},{1,3},{3,1},{5,7},{7,5},{8,10},{10,8},{12,... | collective-permute-start | bytes 786440 | tf_op jit(solution)/shard_map/ppermute | solution.py:143
  85.9 12.5 %collective-permute-start.50 = (bf16[2,2,4,32,256]{4,3,2,1,0:T(8,128)(2,1)S(1)}, bf16[2,2,4,32,256]{4,3,2,1,0:T(8,128)(2,1)S(1)}, u32[]{:S(2)}, u32[]{:S(2)}) collective-permute-start(bf16[2,2,4,32,256]{4,3,2,1,0:T(8,128)(2,1)S(1)} %pad_maximum_fusion.3.refs_5_), channel_id=1, source_target_pairs={{0,4},{2,6},{4,0},{6,2},{1,5},{3,7},{5,1},{7,3},{8,12},{10,14},{12... | collective-permute-start | bytes 786440 | tf_op jit(solution)/shard_map/ppermute | solution.py:143
  86.8 13.3 %collective-permute-start.52 = (bf16[2,2,4,32,256]{4,3,2,1,0:T(8,128)(2,1)S(1)}, bf16[2,2,4,32,256]{4,3,2,1,0:T(8,128)(2,1)S(1)}, u32[]{:S(2)}, u32[]{:S(2)}) collective-permute-start(bf16[2,2,4,32,256]{4,3,2,1,0:T(8,128)(2,1)S(1)} %pad_maximum_fusion.3.refs_5_), channel_id=1, source_target_pairs={{0,8},{8,0},{16,24},{24,16},{1,9},{9,1},{17,25},{25,17},{2,10},{10... | collective-permute-start | bytes 786440 | tf_op jit(solution)/shard_map/ppermute | solution.py:143
  92.0 8.3 %collective-permute-start.64 = (bf16[2,2,4,32,256]{4,3,2,1,0:T(8,128)(2,1)S(1)}, bf16[2,2,4,32,256]{4,3,2,1,0:T(8,128)(2,1)S(1)}, u32[]{:S(2)}, u32[]{:S(2)}) collective-permute-start(bf16[2,2,4,32,256]{4,3,2,1,0:T(8,128)(2,1)S(1)} %pad_maximum_fusion.4.refs_5_), channel_id=1, source_target_pairs={{0,4},{2,6},{4,0},{6,2},{1,5},{3,7},{5,1},{7,3},{8,12},{10,14},{12... | collective-permute-start | bytes 786440 | tf_op jit(solution)/shard_map/ppermute | solution.py:143
  93.8 7.9 %collective-permute-start.65 = (bf16[2,2,4,32,256]{4,3,2,1,0:T(8,128)(2,1)S(1)}, bf16[2,2,4,32,256]{4,3,2,1,0:T(8,128)(2,1)S(1)}, u32[]{:S(2)}, u32[]{:S(2)}) collective-permute-start(bf16[2,2,4,32,256]{4,3,2,1,0:T(8,128)(2,1)S(1)} %pad_maximum_fusion.4.refs_5_), channel_id=1, source_target_pairs={{0,2},{2,0},{4,6},{6,4},{1,3},{3,1},{5,7},{7,5},{8,10},{10,8},{12,... | collective-permute-start | bytes 786440 | tf_op jit(solution)/shard_map/ppermute | solution.py:143
  98.4 8.7 %collective-permute-start.21 = (bf16[2,2,4,32,256]{4,3,2,1,0:T(8,128)(2,1)S(1)}, bf16[2,2,4,32,256]{4,3,2,1,0:T(8,128)(2,1)S(1)}, u32[]{:S(2)}, u32[]{:S(2)}) collective-permute-start(bf16[2,2,4,32,256]{4,3,2,1,0:T(8,128)(2,1)S(1)} %collective-permute-done.19.refs_6_), channel_id=1, source_target_pairs={{0,4},{2,6},{4,0},{6,2},{1,5},{3,7},{5,1},{7,3},{8,12},{10,14},{12... | collective-permute-start | bytes 786440 | tf_op jit(solution)/shard_map/ppermute | solution.py:143
  100.1 7.0 %collective-permute-start.23 = (bf16[2,2,4,32,256]{4,3,2,1,0:T(8,128)(2,1)S(1)}, bf16[2,2,4,32,256]{4,3,2,1,0:T(8,128)(2,1)S(1)}, u32[]{:S(2)}, u32[]{:S(2)}) collective-permute-start(bf16[2,2,4,32,256]{4,3,2,1,0:T(8,128)(2,1)S(1)} %collective-permute-done.19.refs_6_), channel_id=1, source_target_pairs={{0,8},{8,0},{16,24},{24,16},{1,9},{9,1},{17,25},{25,17},{2,10},{10... | collective-permute-start | bytes 786440 | tf_op jit(solution)/shard_map/ppermute | solution.py:143
  100.3 8.5 %collective-permute-start.24 = (bf16[2,2,4,32,256]{4,3,2,1,0:T(8,128)(2,1)S(1)}, bf16[2,2,4,32,256]{4,3,2,1,0:T(8,128)(2,1)S(1)}, u32[]{:S(2)}, u32[]{:S(2)}) collective-permute-start(bf16[2,2,4,32,256]{4,3,2,1,0:T(8,128)(2,1)S(1)} %collective-permute-done.20.refs_7_), channel_id=1, source_target_pairs={{0,8},{8,0},{16,24},{24,16},{1,9},{9,1},{17,25},{25,17},{2,10},{10... | collective-permute-start | bytes 786440 | tf_op jit(solution)/shard_map/ppermute | solution.py:143
  101.7 7.4 %collective-permute-start.36 = (bf16[2,2,4,32,256]{4,3,2,1,0:T(8,128)(2,1)S(1)}, bf16[2,2,4,32,256]{4,3,2,1,0:T(8,128)(2,1)S(1)}, u32[]{:S(2)}, u32[]{:S(2)}) collective-permute-start(bf16[2,2,4,32,256]{4,3,2,1,0:T(8,128)(2,1)S(1)} %collective-permute-done.34.refs_6_), channel_id=1, source_target_pairs={{0,2},{2,0},{4,6},{6,4},{1,3},{3,1},{5,7},{7,5},{8,10},{10,8},{12,... | collective-permute-start | bytes 786440 | tf_op jit(solution)/shard_map/ppermute | solution.py:143
  107.1 8.7 %collective-permute-start.51 = (bf16[2,2,4,32,256]{4,3,2,1,0:T(8,128)(2,1)S(1)}, bf16[2,2,4,32,256]{4,3,2,1,0:T(8,128)(2,1)S(1)}, u32[]{:S(2)}, u32[]{:S(2)}) collective-permute-start(bf16[2,2,4,32,256]{4,3,2,1,0:T(8,128)(2,1)S(1)} %collective-permute-done.49.refs_6_), channel_id=1, source_target_pairs={{0,4},{2,6},{4,0},{6,2},{1,5},{3,7},{5,1},{7,3},{8,12},{10,14},{12... | collective-permute-start | bytes 786440 | tf_op jit(solution)/shard_map/ppermute | solution.py:143
  108.8 7.0 %collective-permute-start.25 = (bf16[2,2,4,32,256]{4,3,2,1,0:T(8,128)(2,1)S(1)}, bf16[2,2,4,32,256]{4,3,2,1,0:T(8,128)(2,1)S(1)}, u32[]{:S(2)}, u32[]{:S(2)}) collective-permute-start(bf16[2,2,4,32,256]{4,3,2,1,0:T(8,128)(2,1)S(1)} %collective-permute-done.21.refs_8_), channel_id=1, source_target_pairs={{0,8},{8,0},{16,24},{24,16},{1,9},{9,1},{17,25},{25,17},{2,10},{10... | collective-permute-start | bytes 786440 | tf_op jit(solution)/shard_map/ppermute | solution.py:143
  109.0 10.7 %collective-permute-start.53 = (bf16[2,2,4,32,256]{4,3,2,1,0:T(8,128)(2,1)S(1)}, bf16[2,2,4,32,256]{4,3,2,1,0:T(8,128)(2,1)S(1)}, u32[]{:S(2)}, u32[]{:S(2)}) collective-permute-start(bf16[2,2,4,32,256]{4,3,2,1,0:T(8,128)(2,1)S(1)} %collective-permute-done.49.refs_6_), channel_id=1, source_target_pairs={{0,8},{8,0},{16,24},{24,16},{1,9},{9,1},{17,25},{25,17},{2,10},{10... | collective-permute-start | bytes 786440 | tf_op jit(solution)/shard_map/ppermute | solution.py:143
  110.1 10.5 %collective-permute-start.54 = (bf16[2,2,4,32,256]{4,3,2,1,0:T(8,128)(2,1)S(1)}, bf16[2,2,4,32,256]{4,3,2,1,0:T(8,128)(2,1)S(1)}, u32[]{:S(2)}, u32[]{:S(2)}) collective-permute-start(bf16[2,2,4,32,256]{4,3,2,1,0:T(8,128)(2,1)S(1)} %collective-permute-done.50.refs_7_), channel_id=1, source_target_pairs={{0,8},{8,0},{16,24},{24,16},{1,9},{9,1},{17,25},{25,17},{2,10},{10... | collective-permute-start | bytes 786440 | tf_op jit(solution)/shard_map/ppermute | solution.py:143
  111.0 10.7 %collective-permute-start.66 = (bf16[2,2,4,32,256]{4,3,2,1,0:T(8,128)(2,1)S(1)}, bf16[2,2,4,32,256]{4,3,2,1,0:T(8,128)(2,1)S(1)}, u32[]{:S(2)}, u32[]{:S(2)}) collective-permute-start(bf16[2,2,4,32,256]{4,3,2,1,0:T(8,128)(2,1)S(1)} %collective-permute-done.64.refs_6_), channel_id=1, source_target_pairs={{0,2},{2,0},{4,6},{6,4},{1,3},{3,1},{5,7},{7,5},{8,10},{10,8},{12,... | collective-permute-start | bytes 786440 | tf_op jit(solution)/shard_map/ppermute | solution.py:143
  115.8 9.8 %collective-permute-start.55 = (bf16[2,2,4,32,256]{4,3,2,1,0:T(8,128)(2,1)S(1)}, bf16[2,2,4,32,256]{4,3,2,1,0:T(8,128)(2,1)S(1)}, u32[]{:S(2)}, u32[]{:S(2)}) collective-permute-start(bf16[2,2,4,32,256]{4,3,2,1,0:T(8,128)(2,1)S(1)} %collective-permute-done.51.refs_8_), channel_id=1, source_target_pairs={{0,8},{8,0},{16,24},{24,16},{1,9},{9,1},{17,25},{25,17},{2,10},{10... | collective-permute-start | bytes 786440 | tf_op jit(solution)/shard_map/ppermute | solution.py:143
  119.7 10.4 %collective-permute-start.68 = (bf16[2,2,4,32,256]{4,3,2,1,0:T(8,128)(2,1)S(1)}, bf16[2,2,4,32,256]{4,3,2,1,0:T(8,128)(2,1)S(1)}, u32[]{:S(2)}, u32[]{:S(2)}) collective-permute-start(bf16[2,2,4,32,256]{4,3,2,1,0:T(8,128)(2,1)S(1)} %collective-permute-done.64.refs_6_), channel_id=1, source_target_pairs={{0,8},{8,0},{16,24},{24,16},{1,9},{9,1},{17,25},{25,17},{2,10},{10... | collective-permute-start | bytes 786440 | tf_op jit(solution)/shard_map/ppermute | solution.py:143
  120.6 10.0 %collective-permute-start.69 = (bf16[2,2,4,32,256]{4,3,2,1,0:T(8,128)(2,1)S(1)}, bf16[2,2,4,32,256]{4,3,2,1,0:T(8,128)(2,1)S(1)}, u32[]{:S(2)}, u32[]{:S(2)}) collective-permute-start(bf16[2,2,4,32,256]{4,3,2,1,0:T(8,128)(2,1)S(1)} %collective-permute-done.65.refs_7_), channel_id=1, source_target_pairs={{0,8},{8,0},{16,24},{24,16},{1,9},{9,1},{17,25},{25,17},{2,10},{10... | collective-permute-start | bytes 786440 | tf_op jit(solution)/shard_map/ppermute | solution.py:143
  121.7 8.8 %collective-permute-start.70 = (bf16[2,2,4,32,256]{4,3,2,1,0:T(8,128)(2,1)S(1)}, bf16[2,2,4,32,256]{4,3,2,1,0:T(8,128)(2,1)S(1)}, u32[]{:S(2)}, u32[]{:S(2)}) collective-permute-start(bf16[2,2,4,32,256]{4,3,2,1,0:T(8,128)(2,1)S(1)} %collective-permute-done.66.refs_8_), channel_id=1, source_target_pairs={{0,8},{8,0},{16,24},{24,16},{1,9},{9,1},{17,25},{25,17},{2,10},{10... | collective-permute-start | bytes 786440 | tf_op jit(solution)/shard_map/ppermute | solution.py:143
  121.8 13.4 %collective-permute-start.26 = (bf16[4,2,2,32,1024]{4,3,2,1,0:T(8,128)(2,1)S(1)}, bf16[4,2,2,32,1024]{4,3,2,1,0:T(8,128)(2,1)S(1)}, u32[]{:S(2)}, u32[]{:S(2)}) collective-permute-start(bf16[4,2,2,32,1024]{4,3,2,1,0:T(8,128)(2,1)S(1)} %shard_map.123), channel_id=1, source_target_pairs={{0,8},{8,0},{16,24},{24,16},{1,9},{9,1},{17,25},{25,17},{2,10},{10... | collective-permute-start | bytes 3145736 | tf_op jit(solution)/shard_map/ppermute | solution.py:143
  125.6 16.1 %collective-permute-start.41 = (bf16[4,2,2,32,1024]{4,3,2,1,0:T(8,128)(2,1)S(1)}, bf16[4,2,2,32,1024]{4,3,2,1,0:T(8,128)(2,1)S(1)}, u32[]{:S(2)}, u32[]{:S(2)}) collective-permute-start(bf16[4,2,2,32,1024]{4,3,2,1,0:T(8,128)(2,1)S(1)} %shard_map.125), channel_id=1, source_target_pairs={{0,8},{8,0},{16,24},{24,16},{1,9},{9,1},{17,25},{25,17},{2,10},{10... | collective-permute-start | bytes 3145736 | tf_op jit(solution)/shard_map/ppermute | solution.py:143
  130.1 19.9 %collective-permute-start.56 = (bf16[4,2,2,32,1024]{4,3,2,1,0:T(8,128)(2,1)}, bf16[4,2,2,32,1024]{4,3,2,1,0:T(8,128)(2,1)}, u32[]{:S(2)}, u32[]{:S(2)}) collective-permute-start(bf16[4,2,2,32,1024]{4,3,2,1,0:T(8,128)(2,1)} %shard_map.127), channel_id=1, source_target_pairs={{0,8},{8,0},{16,24},{24,16},{1,9},{9,1},{17,25},{25,17},{2,10},{10... | collective-permute-start | bytes 3145736 | tf_op jit(solution)/shard_map/ppermute | solution.py:143
  135.1 24.7 %collective-permute-start.71 = (bf16[4,2,2,32,1024]{4,3,2,1,0:T(8,128)(2,1)}, bf16[4,2,2,32,1024]{4,3,2,1,0:T(8,128)(2,1)}, u32[]{:S(2)}, u32[]{:S(2)}) collective-permute-start(bf16[4,2,2,32,1024]{4,3,2,1,0:T(8,128)(2,1)} %shard_map.129), channel_id=1, source_target_pairs={{0,8},{8,0},{16,24},{24,16},{1,9},{9,1},{17,25},{25,17},{2,10},{10... | collective-permute-start | bytes 3145736 | tf_op jit(solution)/shard_map/ppermute | solution.py:143
  140.0 25.8 %collective-permute-start.28 = (bf16[2,2,32,1024]{3,2,1,0:T(8,128)(2,1)}, bf16[2,2,32,1024]{3,2,1,0:T(8,128)(2,1)}, u32[]{:S(2)}, u32[]{:S(2)}) collective-permute-start(bf16[2,2,32,1024]{3,2,1,0:T(8,128)(2,1)} %get-tuple-element.55), channel_id=1, source_target_pairs={{0,4},{2,6},{4,0},{6,2},{1,5},{3,7},{5,1},{7,3},{8,12},{10,14},{12... | collective-permute-start | bytes 786440 | tf_op jit(solution)/shard_map/ppermute | solution.py:143
  148.0 19.2 %collective-permute-start.43 = (bf16[2,2,32,1024]{3,2,1,0:T(8,128)(2,1)}, bf16[2,2,32,1024]{3,2,1,0:T(8,128)(2,1)}, u32[]{:S(2)}, u32[]{:S(2)}) collective-permute-start(bf16[2,2,32,1024]{3,2,1,0:T(8,128)(2,1)} %get-tuple-element.60), channel_id=1, source_target_pairs={{0,2},{2,0},{4,6},{6,4},{1,3},{3,1},{5,7},{7,5},{8,10},{10,8},{12,... | collective-permute-start | bytes 786440 | tf_op jit(solution)/shard_map/ppermute | solution.py:143
  148.4 29.8 %collective-permute-start.27 = (bf16[2,2,32,1024]{3,2,1,0:T(8,128)(2,1)}, bf16[2,2,32,1024]{3,2,1,0:T(8,128)(2,1)S(1)}, u32[]{:S(2)}, u32[]{:S(2)}) collective-permute-start(bf16[2,2,32,1024]{3,2,1,0:T(8,128)(2,1)} %copy-done.40), channel_id=1, source_target_pairs={{0,4},{2,6},{4,0},{6,2},{1,5},{3,7},{5,1},{7,3},{8,12},{10,14},{12... | collective-permute-start | bytes 786440 | tf_op jit(solution)/shard_map/ppermute | solution.py:143
  150.0 33.8 %collective-permute-start.42 = (bf16[2,2,32,1024]{3,2,1,0:T(8,128)(2,1)}, bf16[2,2,32,1024]{3,2,1,0:T(8,128)(2,1)S(1)}, u32[]{:S(2)}, u32[]{:S(2)}) collective-permute-start(bf16[2,2,32,1024]{3,2,1,0:T(8,128)(2,1)} %copy-done.41), channel_id=1, source_target_pairs={{0,2},{2,0},{4,6},{6,4},{1,3},{3,1},{5,7},{7,5},{8,10},{10,8},{12,... | collective-permute-start | bytes 786440 | tf_op jit(solution)/shard_map/ppermute | solution.py:143
  159.9 10.1 %collective-permute-start.58 = (bf16[2,2,32,1024]{3,2,1,0:T(8,128)(2,1)S(1)}, bf16[2,2,32,1024]{3,2,1,0:T(8,128)(2,1)S(1)}, u32[]{:S(2)}, u32[]{:S(2)}) collective-permute-start(bf16[2,2,32,1024]{3,2,1,0:T(8,128)(2,1)S(1)} %get-tuple-element.65), channel_id=1, source_target_pairs={{0,4},{2,6},{4,0},{6,2},{1,5},{3,7},{5,1},{7,3},{8,12},{10,14},{12... | collective-permute-start | bytes 786440 | tf_op jit(solution)/shard_map/ppermute | solution.py:143
  165.8 18.9 %collective-permute-start.57 = (bf16[2,2,32,1024]{3,2,1,0:T(8,128)(2,1)S(1)}, bf16[2,2,32,1024]{3,2,1,0:T(8,128)(2,1)S(1)}, u32[]{:S(2)}, u32[]{:S(2)}) collective-permute-start(bf16[2,2,32,1024]{3,2,1,0:T(8,128)(2,1)S(1)} %get-tuple-element.63), channel_id=1, source_target_pairs={{0,4},{2,6},{4,0},{6,2},{1,5},{3,7},{5,1},{7,3},{8,12},{10,14},{12... | collective-permute-start | bytes 786440 | tf_op jit(solution)/shard_map/ppermute | solution.py:143
  167.2 9.2 %collective-permute-start.73 = (bf16[2,2,32,1024]{3,2,1,0:T(8,128)(2,1)S(1)}, bf16[2,2,32,1024]{3,2,1,0:T(8,128)(2,1)S(1)}, u32[]{:S(2)}, u32[]{:S(2)}) collective-permute-start(bf16[2,2,32,1024]{3,2,1,0:T(8,128)(2,1)S(1)} %get-tuple-element.70), channel_id=1, source_target_pairs={{0,2},{2,0},{4,6},{6,4},{1,3},{3,1},{5,7},{7,5},{8,10},{10,8},{12,... | collective-permute-start | bytes 786440 | tf_op jit(solution)/shard_map/ppermute | solution.py:143
  170.0 12.0 %collective-permute-start.29 = (bf16[2,2,32,1024]{3,2,1,0:T(8,128)(2,1)S(1)}, bf16[2,2,32,1024]{3,2,1,0:T(8,128)(2,1)S(1)}, u32[]{:S(2)}, u32[]{:S(2)}) collective-permute-start(bf16[2,2,32,1024]{3,2,1,0:T(8,128)(2,1)S(1)} %add_convert_fusion.3), channel_id=1, source_target_pairs={{0,2},{2,0},{4,6},{6,4},{1,3},{3,1},{5,7},{7,5},{8,10},{10,8},{12,... | collective-permute-start | bytes 786440 | tf_op jit(solution)/shard_map/ppermute | solution.py:143
  176.4 7.9 %collective-permute-start.44 = (bf16[2,2,32,1024]{3,2,1,0:T(8,128)(2,1)S(1)}, bf16[2,2,32,1024]{3,2,1,0:T(8,128)(2,1)S(1)}, u32[]{:S(2)}, u32[]{:S(2)}) collective-permute-start(bf16[2,2,32,1024]{3,2,1,0:T(8,128)(2,1)S(1)} %add_convert_fusion.2), channel_id=1, source_target_pairs={{0,4},{2,6},{4,0},{6,2},{1,5},{3,7},{5,1},{7,3},{8,12},{10,14},{12... | collective-permute-start | bytes 786440 | tf_op jit(solution)/shard_map/ppermute | solution.py:143
  178.2 13.3 %collective-permute-start.72 = (bf16[2,2,32,1024]{3,2,1,0:T(8,128)(2,1)S(1)}, bf16[2,2,32,1024]{3,2,1,0:T(8,128)(2,1)S(1)}, u32[]{:S(2)}, u32[]{:S(2)}) collective-permute-start(bf16[2,2,32,1024]{3,2,1,0:T(8,128)(2,1)S(1)} %get-tuple-element.68), channel_id=1, source_target_pairs={{0,2},{2,0},{4,6},{6,4},{1,3},{3,1},{5,7},{7,5},{8,10},{10,8},{12,... | collective-permute-start | bytes 786440 | tf_op jit(solution)/shard_map/ppermute | solution.py:143
  182.1 9.1 %collective-permute-start.59 = (bf16[2,2,32,1024]{3,2,1,0:T(8,128)(2,1)S(1)}, bf16[2,2,32,1024]{3,2,1,0:T(8,128)(2,1)S(1)}, u32[]{:S(2)}, u32[]{:S(2)}) collective-permute-start(bf16[2,2,32,1024]{3,2,1,0:T(8,128)(2,1)S(1)} %add_convert_fusion.1), channel_id=1, source_target_pairs={{0,2},{2,0},{4,6},{6,4},{1,3},{3,1},{5,7},{7,5},{8,10},{10,8},{12,... | collective-permute-start | bytes 786440 | tf_op jit(solution)/shard_map/ppermute | solution.py:143
  183.8 7.7 %collective-permute-start.74 = (bf16[2,2,32,1024]{3,2,1,0:T(8,128)(2,1)S(1)}, bf16[2,2,32,1024]{3,2,1,0:T(8,128)(2,1)S(1)}, u32[]{:S(2)}, u32[]{:S(2)}) collective-permute-start(bf16[2,2,32,1024]{3,2,1,0:T(8,128)(2,1)S(1)} %add_convert_fusion), channel_id=1, source_target_pairs={{0,4},{2,6},{4,0},{6,2},{1,5},{3,7},{5,1},{7,3},{8,12},{10,14},{12... | collective-permute-start | bytes 786440 | tf_op jit(solution)/shard_map/ppermute | solution.py:143
  184.3 9.1 %collective-permute-start.30 = (bf16[1,2,32,1024]{3,2,1,0:T(8,128)(2,1)S(1)}, bf16[1,2,32,1024]{3,2,1,0:T(8,128)(2,1)S(1)}, u32[]{:S(2)}, u32[]{:S(2)}) collective-permute-start(bf16[1,2,32,1024]{3,2,1,0:T(8,128)(2,1)S(1)} %add_convert_fusion.7), channel_id=1, source_target_pairs={{0,1},{1,0},{2,3},{3,2},{4,5},{5,4},{6,7},{7,6},{8,9},{9,8},{10,11... | collective-permute-start | bytes 393224 | tf_op jit(solution)/shard_map/ppermute | solution.py:143
  184.7 11.9 %collective-permute-start.45 = (bf16[1,2,32,1024]{3,2,1,0:T(8,128)(2,1)S(1)}, bf16[1,2,32,1024]{3,2,1,0:T(8,128)(2,1)S(1)}, u32[]{:S(2)}, u32[]{:S(2)}) collective-permute-start(bf16[1,2,32,1024]{3,2,1,0:T(8,128)(2,1)S(1)} %add_convert_fusion.6), channel_id=1, source_target_pairs={{0,1},{1,0},{2,3},{3,2},{4,5},{5,4},{6,7},{7,6},{8,9},{9,8},{10,11... | collective-permute-start | bytes 393224 | tf_op jit(solution)/shard_map/ppermute | solution.py:143
  191.6 9.2 %collective-permute-start.75 = (bf16[1,2,32,1024]{3,2,1,0:T(8,128)(2,1)S(1)}, bf16[1,2,32,1024]{3,2,1,0:T(8,128)(2,1)S(1)}, u32[]{:S(2)}, u32[]{:S(2)}) collective-permute-start(bf16[1,2,32,1024]{3,2,1,0:T(8,128)(2,1)S(1)} %add_convert_fusion.4), channel_id=1, source_target_pairs={{0,1},{1,0},{2,3},{3,2},{4,5},{5,4},{6,7},{7,6},{8,9},{9,8},{10,11... | collective-permute-start | bytes 393224 | tf_op jit(solution)/shard_map/ppermute | solution.py:143
  193.4 10.1 %collective-permute-start.31 = (bf16[1,32,1024]{2,1,0:T(8,128)(2,1)S(1)}, bf16[1,32,1024]{2,1,0:T(8,128)(2,1)S(1)}, u32[]{:S(2)}, u32[]{:S(2)}) collective-permute-start(bf16[1,32,1024]{2,1,0:T(8,128)(2,1)S(1)} %fusion.1), channel_id=1, source_target_pairs={{0,16},{8,24},{16,0},{24,8},{1,17},{9,25},{17,1},{25,9},{2,18},{10... | collective-permute-start | bytes 196616 | tf_op jit(solution)/shard_map/ppermute | solution.py:143
  196.6 8.9 %collective-permute-start.46 = (bf16[1,32,1024]{2,1,0:T(8,128)(2,1)S(1)}, bf16[1,32,1024]{2,1,0:T(8,128)(2,1)S(1)}, u32[]{:S(2)}, u32[]{:S(2)}) collective-permute-start(bf16[1,32,1024]{2,1,0:T(8,128)(2,1)S(1)} %fusion.2), channel_id=1, source_target_pairs={{0,16},{8,24},{16,0},{24,8},{1,17},{9,25},{17,1},{25,9},{2,18},{10... | collective-permute-start | bytes 196616 | tf_op jit(solution)/shard_map/ppermute | solution.py:143
  196.9 9.4 %collective-permute-start.61 = (bf16[1,32,1024]{2,1,0:T(8,128)(2,1)S(1)}, bf16[1,32,1024]{2,1,0:T(8,128)(2,1)S(1)}, u32[]{:S(2)}, u32[]{:S(2)}) collective-permute-start(bf16[1,32,1024]{2,1,0:T(8,128)(2,1)S(1)} %fusion.3), channel_id=1, source_target_pairs={{0,16},{8,24},{16,0},{24,8},{1,17},{9,25},{17,1},{25,9},{2,18},{10... | collective-permute-start | bytes 196616 | tf_op jit(solution)/shard_map/ppermute | solution.py:143
  200.8 7.0 %collective-permute-start.76 = (bf16[1,32,1024]{2,1,0:T(8,128)(2,1)S(1)}, bf16[1,32,1024]{2,1,0:T(8,128)(2,1)S(1)}, u32[]{:S(2)}, u32[]{:S(2)}) collective-permute-start(bf16[1,32,1024]{2,1,0:T(8,128)(2,1)S(1)} %fusion.4), channel_id=1, source_target_pairs={{0,16},{8,24},{16,0},{24,8},{1,17},{9,25},{17,1},{25,9},{2,18},{10... | collective-permute-start | bytes 196616 | tf_op jit(solution)/shard_map/ppermute | solution.py:143
  (62 other events, 493.2 us)

commit v3 on v2

--- a/solution.py
+++ b/solution.py
@@ -11,6 +11,7 @@
 
 HEAD_SIZE = 128
 TOPK = 8
+LANES = 128
 CHUNKS = 4
 KERNEL_BYTES = 6 << 20
 
@@ -195,17 +196,20 @@
 def expert_kernel(order, near, start_row, *refs):
     groups = len(order)
     refs = list(refs)
-    place_ref, gain_ref, table_ref, w_in_ref, w_out_ref = refs[:5]
-    in_refs, refs = refs[5 : 5 + groups], refs[5 + groups :]
+    place_ref, table_ref, w_in_ref, w_out_ref = refs[:4]
+    in_refs, refs = refs[4 : 4 + groups], refs[4 + groups :]
+    halves, blocks, sessions, rows, piece = in_refs[0].shape
+    gain_refs, refs = refs[:halves], refs[halves:]
     proj_ref, received_ref = (None, None) if near else (refs.pop(0), refs.pop(0))
-    normed_ref = refs.pop()
-    halves, blocks, sessions, rows, piece = in_refs[0].shape
+    normed_ref, gain_ref = refs.pop(-2), refs.pop()
     half_width = refs[0].shape[-1]
     width = half_width * halves
     hidden_width = w_out_ref.shape[0]
     me, half_me, seq_me = place_ref[0], place_ref[1], place_ref[2]
     per_half = half_width // piece
     count = groups * rows * blocks
+    for k, ref in enumerate(gain_refs):
+        gain_ref[k * per_half : (k + 1) * per_half] = ref[...]
 
     power = jnp.zeros((count, 1), jnp.float32)
     pieces = []
@@ -225,7 +229,8 @@
     inverse = lax.rsqrt(power * (1.0 / width) + 1e-06)
     for i, k, tokens in pieces:
         spot = lax.bitwise_xor(me, order[i]) * halves + lax.bitwise_xor(half_me, k)
-        gain = gain_ref[pl.ds(spot, 1), :]
+        away = lax.bitwise_xor(lax.div(spot, per_half), half_me)
+        gain = gain_ref[pl.ds(away * per_half + lax.rem(spot, per_half), 1), :]
         normed_ref[:, pl.ds(pl.multiple_of(spot * piece, piece), piece)] = (
             tokens.astype(jnp.float32) * inverse * gain
         ).astype(jnp.bfloat16)
@@ -294,22 +299,47 @@
         ],
         axis=1,
     )
-    for n in range(out_ref.shape[1] // HEAD_SIZE):
-        start = head * out_ref.shape[1] + n * HEAD_SIZE
+    heads = out_ref.shape[1] // HEAD_SIZE
+    batch = max(1, heads // 2)
+    allowed = jnp.concatenate([allowed] * batch, axis=0)
+    for first in range(0, heads, batch):
+        start = head * heads + first
+        queries = jnp.concatenate(
+            [
+                q_ref[:, (start + n) * HEAD_SIZE : (start + n + 1) * HEAD_SIZE]
+                for n in range(batch)
+            ],
+            axis=0,
+        )
         scores = lax.dot_general(
-            q_ref[:, start : start + HEAD_SIZE],
-            keys,
-            (((1,), (1,)), ((), ())),
-            preferred_element_type=jnp.float32,
+            queries, keys, (((1,), (1,)), ((), ())), preferred_element_type=jnp.float32
         ) * (1.0 / math.sqrt(HEAD_SIZE))
         scores = jnp.where(allowed, scores, jnp.float32(-1e30))
         weights = jnp.exp(scores - jnp.max(scores, axis=1, keepdims=True))
-        weights = jnp.where(allowed, weights, jnp.float32(0.0))
         mixed = jnp.dot(
             weights.astype(jnp.bfloat16), values, preferred_element_type=jnp.float32
         )
-        mixed = mixed / jnp.sum(weights, axis=1, keepdims=True)
-        out_ref[:, n * HEAD_SIZE : (n + 1) * HEAD_SIZE] = mixed.astype(jnp.bfloat16)
+        mixed = (mixed / jnp.sum(weights, axis=1, keepdims=True)).astype(jnp.bfloat16)
+        for n in range(batch):
+            out_ref[:, (first + n) * HEAD_SIZE : (first + n + 1) * HEAD_SIZE] = mixed[
+                n * rows : (n + 1) * rows
+            ]
+
+
+def side_kernel(place_ref, x_ref, ids_ref, weights_ref, table_ref, half_ref, *piece_refs):
+    me, half_me = place_ref[0], place_ref[1]
+    width, half_width, piece = (ref.shape[1] for ref in (x_ref, half_ref, piece_refs[0]))
+    halves = width // half_width
+    start = pl.multiple_of(half_me * half_width, half_width)
+    half_ref[...] = x_ref[:, pl.ds(start, half_width)]
+    for r, piece_ref in enumerate(piece_refs):
+        spot = lax.bitwise_xor(me, r) * halves + half_me
+        piece_ref[...] = x_ref[:, pl.ds(pl.multiple_of(spot * piece, piece), piece)]
+    number = lax.broadcasted_iota(jnp.int32, (x_ref.shape[0], LANES), 1)
+    table = jnp.zeros(number.shape, jnp.float32)
+    for k in range(ids_ref.shape[1]):
+        table += jnp.where(ids_ref[:, k : k + 1] == number, weights_ref[:, k : k + 1], 0.0)
+    table_ref[...] = table.T[: table_ref.shape[0]]
 
 
 def project_kernel(away, place_ref, w_ref, *refs):
@@ -339,7 +369,7 @@
             chunk_ref[lax.bitwise_xor(me, r)] = mixed[c * rows : (c + 1) * rows]
 
 
-def local_kernel(kernel, outs, operands, scratch=(), limit=12 << 20):
+def local_kernel(kernel, outs, operands, scratch=(), limit=8 << 20):
     return pl.pallas_call(
         kernel,
         out_shape=outs,
@@ -383,11 +413,21 @@
     keys = gather_parts(k_rows[0], "seq", kv_bits)
     values = gather_parts(value_rows[0], "seq", kv_bits)
 
-    x_slots = []
-    for r in range(group_count):
-        start = ((group_pos ^ r) * tensor_count + tensor_pos) * piece
-        columns = lax.dynamic_slice_in_dim(x_rows[0], start, piece, 1)
-        x_slots.append(swap(columns, "expert", r) if r else columns)
+    piece_type = jax.ShapeDtypeStruct((rows_here, piece), x_rows.dtype)
+    table, x_half, *x_slots = local_kernel(
+        side_kernel,
+        [
+            jax.ShapeDtypeStruct((experts, rows_here), jnp.float32),
+            jax.ShapeDtypeStruct((rows_here, half_width), x_rows.dtype),
+        ]
+        + [piece_type] * group_count,
+        [place, x_rows[0], expert_ids[0], gate_weights[0]],
+    )
+    for r in range(1, group_count):
+        x_slots[r] = swap(x_slots[r], "expert", r)
+    table = lax.all_to_all(table, ("seq", "expert"), split_axis=0, concat_axis=0, tiled=True)
+    gain = norm_gain.reshape(half_width // piece, piece)
+    place, table, gain = lax.optimization_barrier((place, table, gain))
 
     kv_heads = k_rows.shape[2] // HEAD_SIZE
     depth = q_rows.shape[2] // kv_heads
@@ -399,15 +439,8 @@
             [place, q_rows[0], *keys, *values],
         )
 
-    expert_ids, gate_weights, norm_gain, w_gate, w_up, _ = lax.optimization_barrier(
-        (expert_ids, gate_weights, norm_gain, w_gate, w_up, attended[0])
-    )
-    gain_slots = gather_slots(norm_gain, "tensor", tensor_bits)
-    gain_at = jnp.array(slot_order(tensor_bits), jnp.int32) ^ tensor_pos
-    gain = gain_slots.at[gain_at].get(mode="promise_in_bounds").reshape(width // piece, piece)
-    named = expert_ids[0][:, :, None] == jnp.arange(experts, dtype=jnp.int32)[None, None, :]
-    table = jnp.sum(jnp.where(named, gate_weights[0][:, :, None], 0.0), axis=1).T
-    table = lax.all_to_all(table, ("seq", "expert"), split_axis=0, concat_axis=0, tiled=True)
+    w_gate, w_up, gain, _ = lax.optimization_barrier((w_gate, w_up, gain, attended[0]))
+    gains = gather_parts(gain, "tensor", tensor_bits)
     w_in = jnp.concatenate([w_gate[0], w_up[0]], axis=1)
 
     paths = (group_bits, group_bits[::-1])
@@ -439,9 +472,8 @@
         [jax.ShapeDtypeStruct((group_count, rows_here, piece), jnp.float32)] + [part] * CHUNKS,
         [place, *x_slots, *terms],
     )
-    gain, table, w_in, *by_session = lax.optimization_barrier(
-        (gain, table, w_in, *by_session)
-    )
+    w_in, *rest = lax.optimization_barrier((w_in, *gains, *by_session))
+    gains, by_session = rest[:tensor_count], rest[tensor_count:]
 
     blocks = seq_count // 2
     chunks = []
@@ -458,7 +490,7 @@
 
     def experts_on(c, path, parts, received):
         order = tuple(slot_order(path))
-        operands = [place, gain, table, w_in, w_down[0], *parts]
+        operands = [place, table, w_in, w_down[0], *parts, *gains]
         shape = (tensor_count, blocks, rows, half_width)
         if received is None:
             shapes = [jax.ShapeDtypeStruct((group_count, *shape), jnp.bfloat16)]
@@ -470,7 +502,10 @@
             functools.partial(expert_kernel, order, near_order, c * rows),
             shapes,
             operands,
-            [pltpu.VMEM((group_count * blocks * rows, width), jnp.bfloat16)],
+            [
+                pltpu.VMEM((group_count * blocks * rows, width), jnp.bfloat16),
+                pltpu.VMEM((width // piece, piece), jnp.float32),
+            ],
             KERNEL_BYTES,
         )
 
@@ -483,7 +518,6 @@
         terms = return_rows(terms, "tensor", tensor_bits)
         terms = return_rows(terms, "seq", far)
         finished.append(sum(term.astype(jnp.float32) for term in terms))
-    x_half = lax.dynamic_slice_in_dim(x_rows[0], tensor_pos * half_width, half_width, 1)
     summed = jnp.concatenate(finished, axis=0)
     return (x_half.astype(jnp.float32) + summed).astype(jnp.bfloat16)[None]
 
@@ -495,7 +529,8 @@
     capacity = max(2, 3 * rows_here * TOPK // (2 * experts))
     dense = experts * rows_here <= 2 * experts * capacity
     regular = all(count > 1 and count & (count - 1) == 0 for count in counts)
-    if dense and regular and rows_here % (16 * CHUNKS) == 0:
+    fits = experts <= LANES and rows_here % (16 * CHUNKS) == 0
+    if dense and regular and fits:
         return dense_plan(*arrays)
     return dispatch_plan(*arrays)
 

time: 209 us -> 196 us (0.938)
  waiting for transfers between devices: 62.7 us -> 89.9 us
  local copies, waits for them, and re-layouts: 22.9 us -> 6.05 us
  starting transfers between devices: 74.4 us -> 61.9 us
  Pallas kernels: 43.5 us -> 35.6 us
  other arithmetic: 4.59 us -> 2.05 us
    ppermute x77, waiting for transfers between devices: 62.7 us -> 84.3 us  [swap(): return lax.ppermute(value, axis, [(i, i ^ bit) for i in range(count)])]
    unnamed x96 -> x18, local copies, waits for them, and re-layouts: 20.7 us -> 5.35 us
    ppermute x77, starting transfers between devices: 70.1 us -> 57.7 us  [swap(): return lax.ppermute(value, axis, [(i, i ^ bit) for i in range(count)])]
    pallas_call x13 -> x14, Pallas kernels: 43.5 us -> 35.6 us  [local_kernel(): pl.pallas_call(kernel, out_shape=outs, in_specs=[pl.BlockSpec(memory_spac...]
    all_to_all x1, waiting for transfers between devices: 0.01 us -> 5.62 us  [dense_plan(): lax.all_to_all(table, ('seq', 'expert'), split_axis=0, concat_axis=0, til...]
  transfers between devices with their start and end apart: 78 -> 78, of which waited for: 23 -> 33; matrix products, arithmetic and copies ran while one was open for 3% -> 2% of each run, Pallas kernels for 19% -> 17%
where the time goes in v3:
time: 196 us
  waiting for transfers between devices  89.9 us (46%)
  starting transfers between devices  61.9 us (32%)
  Pallas kernels  35.6 us (18%)
  local copies, waits for them, and re-layouts  6.05 us (3%)
  other arithmetic  2.05 us (1%)
    ppermute x77, waiting for transfers between devices, swap(): return lax.ppermute(value, axis, [(i, i ^ bit) for i in range(count)])  84.3 us
    ppermute x77, starting transfers between devices, swap(): return lax.ppermute(value, axis, [(i, i ^ bit) for i in range(count)])  57.7 us
    pallas_call x14, Pallas kernels, local_kernel(): pl.pallas_call(kernel, out_shape=outs, in_specs=[pl.BlockSpec(memory_spac...  35.6 us
    all_to_all x1, waiting for transfers between devices, dense_plan(): lax.all_to_all(table, ('seq', 'expert'), split_axis=0, concat_axis=0, til...  5.62 us
    unnamed x18, local copies, waits for them, and re-layouts  5.35 us
    all_to_all x1, starting transfers between devices, dense_plan(): lax.all_to_all(table, ('seq', 'expert'), split_axis=0, concat_axis=0, til...  4.15 us
  transfers between devices with their start and end apart: 78, of which 33 were waited for; matrix products, arithmetic and copies ran while one was open for 2% of the time, Pallas kernels for 17%

profile of v3, /device:TPU:0, one launch (start us, length us, event | category | flops | bytes accessed | tf_op | source)
XLA Modules:
  0.0 196.0 jit_solution(7500270414497485726)
XLA Ops:
  0.0 4.1 %collective-permute-start = (bf16[128,256]{1,0:T(8,128)(2,1)}, bf16[128,256]{1,0:T(8,128)(2,1)S(1)}, u32[]{:S(2)}, u32[]{:S(2)}) collective-permute-start(bf16[128,256]{1,0:T(8,128)(2,1)} %bitcast.77), channel_id=1, source_target_pairs={{0,16},{8,24},{16,0},{24,8},{1,17},{9,25},{17,1},{25,9},{2,18},{10... | collective-permute-start | bytes 196616 | tf_op jit(solution)/shard_map/ppermute | solution.py:144
  4.6 3.3 %collective-permute-done.refs_1_ = bf16[128,256]{1,0:T(8,128)(2,1)S(1)} collective-permute-done((bf16[128,256]{1,0:T(8,128)(2,1)}, bf16[128,256]{1,0:T(8,128)(2,1)S(1)}, u32[]{:S(2)}, u32[]{:S(2)}) %collective-permute-start) | collective-permute-done | bytes 65568 | tf_op jit(solution)/shard_map/ppermute | solution.py:144
  8.0 2.8 %collective-permute-done.3.refs_5_ = bf16[128,256]{1,0:T(8,128)(2,1)S(1)} collective-permute-done((bf16[128,256]{1,0:T(8,128)(2,1)}, bf16[128,256]{1,0:T(8,128)(2,1)S(1)}, u32[]{:S(2)}, u32[]{:S(2)}) %collective-permute-start.3) | collective-permute-done | bytes 65568 | tf_op jit(solution)/shard_map/ppermute | solution.py:144
  12.4 1.0 copy-done.3
  13.4 1.5 shard_map.109
  15.0 4.2 %all-to-all-start = ((f32[16,1,128]{2,1,0:T(1,128)}), f32[16,1,128]{2,1,0:T(1,128)S(1)}, u32[]{:S(2)}, u32[]{:S(2)}) async-start(f32[16,1,128]{2,1,0:T(1,128)} %bitcast.7), calls=%async_computation | async-start | bytes 16384 | tf_op jit(solution)/shard_map/all_to_all | solution.py:428
  19.8 5.6 %all-to-all-done = f32[16,1,128]{2,1,0:T(1,128)S(1)} async-done(((f32[16,1,128]{2,1,0:T(1,128)}), f32[16,1,128]{2,1,0:T(1,128)S(1)}, u32[]{:S(2)}, u32[]{:S(2)}) %all-to-all-start) | async-done | bytes 8224 | tf_op jit(solution)/shard_map/all_to_all | solution.py:428
  25.5 1.0 copy-done.2
  28.2 1.7 shard_map.110.refs_0_
  30.6 1.7 shard_map.111.refs_4_
  33.0 1.5 collective-permute-start.11
  34.4 1.5 collective-permute-start.13
  35.9 3.3 %collective-permute-done.10.refs_1_ = bf16[128,1024]{1,0:T(8,128)(2,1)S(1)} collective-permute-done((bf16[128,1024]{1,0:T(8,128)(2,1)S(1)}, bf16[128,1024]{1,0:T(8,128)(2,1)S(1)}, u32[]{:S(2)}, u32[]{:S(2)}) %collective-permute-start.10) | collective-permute-done | bytes 262176 | tf_op jit(solution)/shard_map/ppermute | solution.py:144
  39.8 1.8 collective-permute-done.14.refs_6_
  41.6 1.5 collective-permute-start.15
  43.6 3.6 %collective-permute-done.11.refs_2_ = bf16[128,1024]{1,0:T(8,128)(2,1)S(1)} collective-permute-done((bf16[128,1024]{1,0:T(8,128)(2,1)S(1)}, bf16[128,1024]{1,0:T(8,128)(2,1)S(1)}, u32[]{:S(2)}, u32[]{:S(2)}) %collective-permute-start.11) | collective-permute-done | bytes 262176 | tf_op jit(solution)/shard_map/ppermute | solution.py:144
  47.8 2.4 %collective-permute-start.9 = (bf16[128,256]{1,0:T(8,128)(2,1)S(1)}, bf16[128,256]{1,0:T(8,128)(2,1)S(1)}, u32[]{:S(2)}, u32[]{:S(2)}) collective-permute-start(bf16[128,256]{1,0:T(8,128)(2,1)S(1)} %get-tuple-element.56), channel_id=1, source_target_pairs={{0,6},{2,4},{4,2},{6,0},{1,7},{3,5},{5,3},{7,1},{8,14},{10,12},{12... | collective-permute-start | bytes 196616 | tf_op jit(solution)/shard_map/ppermute | solution.py:144
  50.1 3.4 %collective-permute-done.12.refs_3_ = bf16[128,1024]{1,0:T(8,128)(2,1)S(1)} collective-permute-done((bf16[128,1024]{1,0:T(8,128)(2,1)S(1)}, bf16[128,1024]{1,0:T(8,128)(2,1)S(1)}, u32[]{:S(2)}, u32[]{:S(2)}) %collective-permute-start.12) | collective-permute-done | bytes 262176 | tf_op jit(solution)/shard_map/ppermute | solution.py:144
  53.5 3.2 %collective-permute-start.6 = (f32[4,256]{1,0:T(4,128)S(1)}, f32[4,256]{1,0:T(4,128)S(1)}, u32[]{:S(2)}, u32[]{:S(2)}) collective-permute-start(f32[4,256]{1,0:T(4,128)S(1)} %reshape.377.refs_8_), channel_id=1, source_target_pairs={{0,1},{1,0},{2,3},{3,2},{4,5},{5,4},{6,7},{7,6},{8,9},{9,8},{10,11... | collective-permute-start | bytes 12296 | tf_op jit(solution)/shard_map/ppermute | solution.py:144
  56.7 1.3 shard_map.112
  58.3 1.3 shard_map.113.refs_5_
  59.6 4.8 %collective-permute-done.16.refs_4_ = bf16[4,128,256]{2,1,0:T(8,128)(2,1)S(1)} collective-permute-done((bf16[4,128,256]{2,1,0:T(8,128)(2,1)S(1)}, bf16[4,128,256]{2,1,0:T(8,128)(2,1)S(1)}, u32[]{:S(2)}, u32[]{:S(2)}) %collective-permute-start.16) | collective-permute-done | bytes 262176 | tf_op jit(solution)/shard_map/ppermute | solution.py:144
  65.9 2.2 %collective-permute-start.32 = (bf16[1,4,32,256]{3,2,1,0:T(8,128)(2,1)S(1)}, bf16[1,4,32,256]{3,2,1,0:T(8,128)(2,1)S(1)}, u32[]{:S(2)}, u32[]{:S(2)}) collective-permute-start(bf16[1,4,32,256]{3,2,1,0:T(8,128)(2,1)S(1)} %bitcast.91), channel_id=1, source_target_pairs={{0,16},{8,24},{16,0},{24,8},{1,17},{9,25},{17,1},{25,9},{2,18},{10... | collective-permute-start | bytes 196616 | tf_op jit(solution)/shard_map/ppermute | solution.py:144
  68.8 2.2 %collective-permute-start.62 = (bf16[1,4,32,256]{3,2,1,0:T(8,128)(2,1)S(1)}, bf16[1,4,32,256]{3,2,1,0:T(8,128)(2,1)S(1)}, u32[]{:S(2)}, u32[]{:S(2)}) collective-permute-start(bf16[1,4,32,256]{3,2,1,0:T(8,128)(2,1)S(1)} %bitcast.87), channel_id=1, source_target_pairs={{0,16},{8,24},{16,0},{24,8},{1,17},{9,25},{17,1},{25,9},{2,18},{10... | collective-permute-start | bytes 196616 | tf_op jit(solution)/shard_map/ppermute | solution.py:144
  71.0 1.1 collective-permute-done.17
  72.2 1.2 collective-permute-done.32
  75.6 2.8 %collective-permute-done.18 = bf16[1,2,4,32,256]{4,3,2,1,0:T(8,128)(2,1)S(1)} collective-permute-done((bf16[1,2,4,32,256]{4,3,2,1,0:T(8,128)(2,1)S(1)}, bf16[1,2,4,32,256]{4,3,2,1,0:T(8,128)(2,1)S(1)}, u32[]{:S(2)}, u32[]{:S(2)}) %collective-permute-start.18) | collective-permute-done | bytes 131104 | tf_op jit(solution)/shard_map/ppermute | solution.py:144
  78.5 1.5 collective-permute-start.19
  80.5 1.7 collective-permute-start.34
  82.2 5.6 %collective-permute-done.63 = bf16[1,2,4,32,256]{4,3,2,1,0:T(8,128)(2,1)S(1)} collective-permute-done((bf16[1,2,4,32,256]{4,3,2,1,0:T(8,128)(2,1)S(1)}, bf16[1,2,4,32,256]{4,3,2,1,0:T(8,128)(2,1)S(1)}, u32[]{:S(2)}, u32[]{:S(2)}) %collective-permute-start.63) | collective-permute-done | bytes 131104 | tf_op jit(solution)/shard_map/ppermute | solution.py:144
  89.1 1.0 collective-permute-start.49
  90.5 1.5 collective-permute-done.34.refs_5_
  92.0 5.0 %collective-permute-done.35.refs_6_ = bf16[2,2,4,32,256]{4,3,2,1,0:T(8,128)(2,1)S(1)} collective-permute-done((bf16[2,2,4,32,256]{4,3,2,1,0:T(8,128)(2,1)S(1)}, bf16[2,2,4,32,256]{4,3,2,1,0:T(8,128)(2,1)S(1)}, u32[]{:S(2)}, u32[]{:S(2)}) %collective-permute-start.35) | collective-permute-done | bytes 262176 | tf_op jit(solution)/shard_map/ppermute | solution.py:144
  98.3 4.3 %collective-permute-done.49.refs_5_ = bf16[2,2,4,32,256]{4,3,2,1,0:T(8,128)(2,1)S(1)} collective-permute-done((bf16[2,2,4,32,256]{4,3,2,1,0:T(8,128)(2,1)S(1)}, bf16[2,2,4,32,256]{4,3,2,1,0:T(8,128)(2,1)S(1)}, u32[]{:S(2)}, u32[]{:S(2)}) %collective-permute-start.49) | collective-permute-done | bytes 262176 | tf_op jit(solution)/shard_map/ppermute | solution.py:144
  104.1 2.6 %collective-permute-done.65.refs_6_ = bf16[2,2,4,32,256]{4,3,2,1,0:T(8,128)(2,1)S(1)} collective-permute-done((bf16[2,2,4,32,256]{4,3,2,1,0:T(8,128)(2,1)S(1)}, bf16[2,2,4,32,256]{4,3,2,1,0:T(8,128)(2,1)S(1)}, u32[]{:S(2)}, u32[]{:S(2)}) %collective-permute-start.65) | collective-permute-done | bytes 262176 | tf_op jit(solution)/shard_map/ppermute | solution.py:144
  107.2 4.1 %collective-permute-done.21.refs_7_ = bf16[2,2,4,32,256]{4,3,2,1,0:T(8,128)(2,1)S(1)} collective-permute-done((bf16[2,2,4,32,256]{4,3,2,1,0:T(8,128)(2,1)S(1)}, bf16[2,2,4,32,256]{4,3,2,1,0:T(8,128)(2,1)S(1)}, u32[]{:S(2)}, u32[]{:S(2)}) %collective-permute-start.21) | collective-permute-done | bytes 262176 | tf_op jit(solution)/shard_map/ppermute | solution.py:144
  112.0 1.3 collective-permute-done.36.refs_7_
  114.5 5.6 %collective-permute-done.51.refs_7_ = bf16[2,2,4,32,256]{4,3,2,1,0:T(8,128)(2,1)S(1)} collective-permute-done((bf16[2,2,4,32,256]{4,3,2,1,0:T(8,128)(2,1)S(1)}, bf16[2,2,4,32,256]{4,3,2,1,0:T(8,128)(2,1)S(1)}, u32[]{:S(2)}, u32[]{:S(2)}) %collective-permute-start.51) | collective-permute-done | bytes 262176 | tf_op jit(solution)/shard_map/ppermute | solution.py:144
  120.6 3.4 %shard_map.115 = bf16[4,2,2,32,1024]{4,3,2,1,0:T(8,128)(2,1)S(1)} custom-call(s32[3]{0:T(128)S(1)} %pad_add_fusion.place_ref.refs_0_, f32[16,128]{1,0:T(8,128)S(1)} %bitcast.68, bf16[2048,768]{1,0:T(8,128)(2,1)S(1)} %pad_maximum_fusion.refs_2_, bf16[384,2048]{1,0:T(8,128)(2,1)S(1)} %bitcast.58, ...), custom_call_target="tpu_custom_call" | custom-call | tf_op jit(solution)/shard_map/pallas_call | solution.py:373
  125.1 3.4 %shard_map.117 = bf16[4,2,2,32,1024]{4,3,2,1,0:T(8,128)(2,1)S(1)} custom-call(s32[3]{0:T(128)S(1)} %pad_add_fusion.place_ref.refs_0_, f32[16,128]{1,0:T(8,128)S(1)} %bitcast.69, bf16[2048,768]{1,0:T(8,128)(2,1)S(1)} %pad_maximum_fusion.refs_2_, bf16[384,2048]{1,0:T(8,128)(2,1)S(1)} %bitcast.59, ...), custom_call_target="tpu_custom_call" | custom-call | tf_op jit(solution)/shard_map/pallas_call | solution.py:373
  128.8 3.4 %shard_map.119 = bf16[4,2,2,32,1024]{4,3,2,1,0:T(8,128)(2,1)S(1)} custom-call(s32[3]{0:T(128)S(1)} %pad_add_fusion.place_ref.refs_0_, f32[16,128]{1,0:T(8,128)S(1)} %bitcast.70, bf16[2048,768]{1,0:T(8,128)(2,1)S(1)} %pad_maximum_fusion.refs_2_, bf16[384,2048]{1,0:T(8,128)(2,1)S(1)} %bitcast.60, ...), custom_call_target="tpu_custom_call" | custom-call | tf_op jit(solution)/shard_map/pallas_call | solution.py:373
  132.7 3.4 %shard_map.121 = bf16[4,2,2,32,1024]{4,3,2,1,0:T(8,128)(2,1)S(1)} custom-call(s32[3]{0:T(128)S(1)} %pad_add_fusion.place_ref.refs_0_, f32[16,128]{1,0:T(8,128)S(1)} %bitcast.71, bf16[2048,768]{1,0:T(8,128)(2,1)S(1)} %pad_maximum_fusion.refs_2_, bf16[384,2048]{1,0:T(8,128)(2,1)S(1)} %bitcast.61, ...), custom_call_target="tpu_custom_call" | custom-call | tf_op jit(solution)/shard_map/pallas_call | solution.py:373
  136.2 3.4 %shard_map.116 = (bf16[2,2,32,1024]{3,2,1,0:T(8,128)(2,1)S(1)}, bf16[2,2,32,1024]{3,2,1,0:T(8,128)(2,1)S(1)}, bf16[2,2,32,1024]{3,2,1,0:T(8,128)(2,1)S(1)}, bf16[2,2,32,1024]{3,2,1,0:T(8,128)(2,1)S(1)}) custom-call(s32[3]{0:T(128)S(1)} %pad_add_fusion.place_ref.refs_0_, f32[16,128]{1,0:T(8,128)S(1)} %bitcast.72, ...), custom_call_target="tpu_custom_call" | custom-call | tf_op jit(solution)/shard_map/pallas_call | solution.py:373
  140.2 3.4 %shard_map.118 = (bf16[2,2,32,1024]{3,2,1,0:T(8,128)(2,1)S(1)}, bf16[2,2,32,1024]{3,2,1,0:T(8,128)(2,1)S(1)}, bf16[2,2,32,1024]{3,2,1,0:T(8,128)(2,1)S(1)}, bf16[2,2,32,1024]{3,2,1,0:T(8,128)(2,1)S(1)}) custom-call(s32[3]{0:T(128)S(1)} %pad_add_fusion.place_ref.refs_0_, f32[16,128]{1,0:T(8,128)S(1)} %bitcast.73, ...), custom_call_target="tpu_custom_call" | custom-call | tf_op jit(solution)/shard_map/pallas_call | solution.py:373
  143.6 0.9 collective-permute-start.43
  144.5 1.3 collective-permute-start.27
  145.8 1.5 collective-permute-start.42
  147.3 3.4 %shard_map.120 = (bf16[2,2,32,1024]{3,2,1,0:T(8,128)(2,1)S(1)}, bf16[2,2,32,1024]{3,2,1,0:T(8,128)(2,1)S(1)}, bf16[2,2,32,1024]{3,2,1,0:T(8,128)(2,1)S(1)}, bf16[2,2,32,1024]{3,2,1,0:T(8,128)(2,1)S(1)}) custom-call(s32[3]{0:T(128)S(1)} %pad_add_fusion.place_ref.refs_0_, f32[16,128]{1,0:T(8,128)S(1)} %bitcast.74, ...), custom_call_target="tpu_custom_call" | custom-call | tf_op jit(solution)/shard_map/pallas_call | solution.py:373
  151.2 3.7 %shard_map.122 = (bf16[2,2,32,1024]{3,2,1,0:T(8,128)(2,1)S(1)}, bf16[2,2,32,1024]{3,2,1,0:T(8,128)(2,1)S(1)}, bf16[2,2,32,1024]{3,2,1,0:T(8,128)(2,1)S(1)}, bf16[2,2,32,1024]{3,2,1,0:T(8,128)(2,1)S(1)}) custom-call(s32[3]{0:T(128)S(1)} %pad_add_fusion.place_ref.refs_0_, f32[16,128]{1,0:T(8,128)S(1)} %bitcast.75, ...), custom_call_target="tpu_custom_call" | custom-call | tf_op jit(solution)/shard_map/pallas_call | solution.py:373
  154.8 1.7 collective-permute-start.57
  157.3 2.9 %collective-permute-done.58 = bf16[2,2,32,1024]{3,2,1,0:T(8,128)(2,1)S(1)} collective-permute-done((bf16[2,2,32,1024]{3,2,1,0:T(8,128)(2,1)S(1)}, bf16[2,2,32,1024]{3,2,1,0:T(8,128)(2,1)S(1)}, u32[]{:S(2)}, u32[]{:S(2)}) %collective-permute-start.58) | collective-permute-done | bytes 262176 | tf_op jit(solution)/shard_map/ppermute | solution.py:144
  160.8 4.7 %collective-permute-done.73 = bf16[2,2,32,1024]{3,2,1,0:T(8,128)(2,1)S(1)} collective-permute-done((bf16[2,2,32,1024]{3,2,1,0:T(8,128)(2,1)S(1)}, bf16[2,2,32,1024]{3,2,1,0:T(8,128)(2,1)S(1)}, u32[]{:S(2)}, u32[]{:S(2)}) %collective-permute-start.73) | collective-permute-done | bytes 262176 | tf_op jit(solution)/shard_map/ppermute | solution.py:144
  166.3 0.9 collective-permute-start.72
  167.3 3.8 %collective-permute-done.29 = bf16[2,2,32,1024]{3,2,1,0:T(8,128)(2,1)S(1)} collective-permute-done((bf16[2,2,32,1024]{3,2,1,0:T(8,128)(2,1)S(1)}, bf16[2,2,32,1024]{3,2,1,0:T(8,128)(2,1)S(1)}, u32[]{:S(2)}, u32[]{:S(2)}) %collective-permute-start.29) | collective-permute-done | bytes 262176 | tf_op jit(solution)/shard_map/ppermute | solution.py:144
  171.7 1.2 collective-permute-start.74
  173.5 1.9 collective-permute-start.45
  175.4 5.1 %collective-permute-done.59 = bf16[2,2,32,1024]{3,2,1,0:T(8,128)(2,1)S(1)} collective-permute-done((bf16[2,2,32,1024]{3,2,1,0:T(8,128)(2,1)S(1)}, bf16[2,2,32,1024]{3,2,1,0:T(8,128)(2,1)S(1)}, u32[]{:S(2)}, u32[]{:S(2)}) %collective-permute-start.59) | collective-permute-done | bytes 262176 | tf_op jit(solution)/shard_map/ppermute | solution.py:144
  180.9 1.8 collective-permute-start.75
  182.9 3.0 %collective-permute-start.46 = (bf16[1,32,1024]{2,1,0:T(8,128)(2,1)S(1)}, bf16[1,32,1024]{2,1,0:T(8,128)(2,1)S(1)}, u32[]{:S(2)}, u32[]{:S(2)}) collective-permute-start(bf16[1,32,1024]{2,1,0:T(8,128)(2,1)S(1)} %fusion.3), channel_id=1, source_target_pairs={{0,16},{8,24},{16,0},{24,8},{1,17},{9,25},{17,1},{25,9},{2,18},{10... | collective-permute-start | bytes 196616 | tf_op jit(solution)/shard_map/ppermute | solution.py:144
  185.9 1.4 collective-permute-done.60
  187.4 1.4 collective-permute-done.75
  188.8 1.6 collective-permute-start.76
  191.3 1.8 collective-permute-done.46
  193.8 1.4 collective-permute-done.76
  (152 shorter events, 29.8 us)
Async XLA Ops:
  0.0 8.0 %collective-permute-start = (bf16[128,256]{1,0:T(8,128)(2,1)}, bf16[128,256]{1,0:T(8,128)(2,1)S(1)}, u32[]{:S(2)}, u32[]{:S(2)}) collective-permute-start(bf16[128,256]{1,0:T(8,128)(2,1)} %bitcast.77), channel_id=1, source_target_pairs={{0,16},{8,24},{16,0},{24,8},{1,17},{9,25},{17,1},{25,9},{2,18},{10... | collective-permute-start | bytes 196616 | tf_op jit(solution)/shard_map/ppermute | solution.py:144
  4.1 21.3 %collective-permute-start.1 = (bf16[128,256]{1,0:T(8,128)(2,1)}, bf16[128,256]{1,0:T(8,128)(2,1)S(1)}, u32[]{:S(2)}, u32[]{:S(2)}) collective-permute-start(bf16[128,256]{1,0:T(8,128)(2,1)} %bitcast.78), channel_id=1, source_target_pairs={{0,8},{8,0},{16,24},{24,16},{1,9},{9,1},{17,25},{25,17},{2,10},{10... | collective-permute-start | bytes 196616 | tf_op jit(solution)/shard_map/ppermute | solution.py:144
  4.1 21.3 %collective-permute-start.4 = (bf16[128,256]{1,0:T(8,128)(2,1)}, bf16[128,256]{1,0:T(8,128)(2,1)S(1)}, u32[]{:S(2)}, u32[]{:S(2)}) collective-permute-start(bf16[128,256]{1,0:T(8,128)(2,1)} %bitcast.82), channel_id=1, source_target_pairs={{0,8},{8,0},{16,24},{24,16},{1,9},{9,1},{17,25},{25,17},{2,10},{10... | collective-permute-start | bytes 196616 | tf_op jit(solution)/shard_map/ppermute | solution.py:144
  8.0 17.5 %collective-permute-start.2 = (bf16[128,256]{1,0:T(8,128)(2,1)S(1)}, bf16[128,256]{1,0:T(8,128)(2,1)S(1)}, u32[]{:S(2)}, u32[]{:S(2)}) collective-permute-start(bf16[128,256]{1,0:T(8,128)(2,1)S(1)} %collective-permute-done.refs_1_), channel_id=1, source_target_pairs={{0,8},{8,0},{16,24},{24,16},{1,9},{9,1},{17,25},{25,17},{2,10},{10... | collective-permute-start | bytes 196616 | tf_op jit(solution)/shard_map/ppermute | solution.py:144
  10.7 14.7 %collective-permute-start.5 = (bf16[128,256]{1,0:T(8,128)(2,1)S(1)}, bf16[128,256]{1,0:T(8,128)(2,1)S(1)}, u32[]{:S(2)}, u32[]{:S(2)}) collective-permute-start(bf16[128,256]{1,0:T(8,128)(2,1)S(1)} %collective-permute-done.3.refs_5_), channel_id=1, source_target_pairs={{0,8},{8,0},{16,24},{24,16},{1,9},{9,1},{17,25},{25,17},{2,10},{10... | collective-permute-start | bytes 196616 | tf_op jit(solution)/shard_map/ppermute | solution.py:144
  15.0 10.5 %all-to-all-start = ((f32[16,1,128]{2,1,0:T(1,128)}), f32[16,1,128]{2,1,0:T(1,128)S(1)}, u32[]{:S(2)}, u32[]{:S(2)}) async-start(f32[16,1,128]{2,1,0:T(1,128)} %bitcast.7), calls=%async_computation | async-start | bytes 16384 | tf_op jit(solution)/shard_map/all_to_all | solution.py:428
  30.0 9.2 %collective-permute-start.10 = (bf16[128,1024]{1,0:T(8,128)(2,1)S(1)}, bf16[128,1024]{1,0:T(8,128)(2,1)S(1)}, u32[]{:S(2)}, u32[]{:S(2)}) collective-permute-start(bf16[128,1024]{1,0:T(8,128)(2,1)S(1)} %shard_map.110.refs_0_), channel_id=1, source_target_pairs={{0,2},{2,0},{4,6},{6,4},{1,3},{3,1},{5,7},{7,5},{8,10},{10,8},{12,... | collective-permute-start | bytes 786440 | tf_op jit(solution)/shard_map/ppermute | solution.py:144
  32.4 9.2 %collective-permute-start.14 = (bf16[128,1024]{1,0:T(8,128)(2,1)S(1)}, bf16[128,1024]{1,0:T(8,128)(2,1)S(1)}, u32[]{:S(2)}, u32[]{:S(2)}) collective-permute-start(bf16[128,1024]{1,0:T(8,128)(2,1)S(1)} %shard_map.111.refs_4_), channel_id=1, source_target_pairs={{0,4},{2,6},{4,0},{6,2},{1,5},{3,7},{5,1},{7,3},{8,12},{10,14},{12... | collective-permute-start | bytes 786440 | tf_op jit(solution)/shard_map/ppermute | solution.py:144
  33.0 14.2 %collective-permute-start.11 = (bf16[128,1024]{1,0:T(8,128)(2,1)S(1)}, bf16[128,1024]{1,0:T(8,128)(2,1)S(1)}, u32[]{:S(2)}, u32[]{:S(2)}) collective-permute-start(bf16[128,1024]{1,0:T(8,128)(2,1)S(1)} %shard_map.110.refs_0_), channel_id=1, source_target_pairs={{0,4},{2,6},{4,0},{6,2},{1,5},{3,7},{5,1},{7,3},{8,12},{10,14},{12... | collective-permute-start | bytes 786440 | tf_op jit(solution)/shard_map/ppermute | solution.py:144
  34.4 13.3 %collective-permute-start.13 = (bf16[128,1024]{1,0:T(8,128)(2,1)S(1)}, bf16[128,1024]{1,0:T(8,128)(2,1)S(1)}, u32[]{:S(2)}, u32[]{:S(2)}) collective-permute-start(bf16[128,1024]{1,0:T(8,128)(2,1)S(1)} %shard_map.111.refs_4_), channel_id=1, source_target_pairs={{0,2},{2,0},{4,6},{6,4},{1,3},{3,1},{5,7},{7,5},{8,10},{10,8},{12,... | collective-permute-start | bytes 786440 | tf_op jit(solution)/shard_map/ppermute | solution.py:144
  39.2 14.3 %collective-permute-start.12 = (bf16[128,1024]{1,0:T(8,128)(2,1)S(1)}, bf16[128,1024]{1,0:T(8,128)(2,1)S(1)}, u32[]{:S(2)}, u32[]{:S(2)}) collective-permute-start(bf16[128,1024]{1,0:T(8,128)(2,1)S(1)} %collective-permute-done.10.refs_1_), channel_id=1, source_target_pairs={{0,4},{2,6},{4,0},{6,2},{1,5},{3,7},{5,1},{7,3},{8,12},{10,14},{12... | collective-permute-start | bytes 786440 | tf_op jit(solution)/shard_map/ppermute | solution.py:144
  41.6 15.1 %collective-permute-start.15 = (bf16[128,1024]{1,0:T(8,128)(2,1)S(1)}, bf16[128,1024]{1,0:T(8,128)(2,1)S(1)}, u32[]{:S(2)}, u32[]{:S(2)}) collective-permute-start(bf16[128,1024]{1,0:T(8,128)(2,1)S(1)} %collective-permute-done.14.refs_6_), channel_id=1, source_target_pairs={{0,2},{2,0},{4,6},{6,4},{1,3},{3,1},{5,7},{7,5},{8,10},{10,8},{12,... | collective-permute-start | bytes 786440 | tf_op jit(solution)/shard_map/ppermute | solution.py:144
  43.1 16.6 %collective-permute-start.7 = (bf16[128,256]{1,0:T(8,128)(2,1)S(1)}, bf16[128,256]{1,0:T(8,128)(2,1)S(1)}, u32[]{:S(2)}, u32[]{:S(2)}) collective-permute-start(bf16[128,256]{1,0:T(8,128)(2,1)S(1)} %get-tuple-element.54), channel_id=1, source_target_pairs={{0,2},{2,0},{4,6},{6,4},{1,3},{3,1},{5,7},{7,5},{8,10},{10,8},{12,... | collective-permute-start | bytes 196616 | tf_op jit(solution)/shard_map/ppermute | solution.py:144
  47.2 12.4 %collective-permute-start.8 = (bf16[128,256]{1,0:T(8,128)(2,1)S(1)}, bf16[128,256]{1,0:T(8,128)(2,1)S(1)}, u32[]{:S(2)}, u32[]{:S(2)}) collective-permute-start(bf16[128,256]{1,0:T(8,128)(2,1)S(1)} %get-tuple-element.55), channel_id=1, source_target_pairs={{0,4},{2,6},{4,0},{6,2},{1,5},{3,7},{5,1},{7,3},{8,12},{10,14},{12... | collective-permute-start | bytes 196616 | tf_op jit(solution)/shard_map/ppermute | solution.py:144
  47.8 11.8 %collective-permute-start.9 = (bf16[128,256]{1,0:T(8,128)(2,1)S(1)}, bf16[128,256]{1,0:T(8,128)(2,1)S(1)}, u32[]{:S(2)}, u32[]{:S(2)}) collective-permute-start(bf16[128,256]{1,0:T(8,128)(2,1)S(1)} %get-tuple-element.56), channel_id=1, source_target_pairs={{0,6},{2,4},{4,2},{6,0},{1,7},{3,5},{5,3},{7,1},{8,14},{10,12},{12... | collective-permute-start | bytes 196616 | tf_op jit(solution)/shard_map/ppermute | solution.py:144
  53.5 11.5 %collective-permute-start.6 = (f32[4,256]{1,0:T(4,128)S(1)}, f32[4,256]{1,0:T(4,128)S(1)}, u32[]{:S(2)}, u32[]{:S(2)}) collective-permute-start(f32[4,256]{1,0:T(4,128)S(1)} %reshape.377.refs_8_), channel_id=1, source_target_pairs={{0,1},{1,0},{2,3},{3,2},{4,5},{5,4},{6,7},{7,6},{8,9},{9,8},{10,11... | collective-permute-start | bytes 12296 | tf_op jit(solution)/shard_map/ppermute | solution.py:144
  65.1 7.0 %collective-permute-start.17 = (bf16[1,4,32,256]{3,2,1,0:T(8,128)(2,1)S(1)}, bf16[1,4,32,256]{3,2,1,0:T(8,128)(2,1)S(1)}, u32[]{:S(2)}, u32[]{:S(2)}) collective-permute-start(bf16[1,4,32,256]{3,2,1,0:T(8,128)(2,1)S(1)} %bitcast.93), channel_id=1, source_target_pairs={{0,16},{8,24},{16,0},{24,8},{1,17},{9,25},{17,1},{25,9},{2,18},{10... | collective-permute-start | bytes 196616 | tf_op jit(solution)/shard_map/ppermute | solution.py:144
  65.9 7.6 %collective-permute-start.32 = (bf16[1,4,32,256]{3,2,1,0:T(8,128)(2,1)S(1)}, bf16[1,4,32,256]{3,2,1,0:T(8,128)(2,1)S(1)}, u32[]{:S(2)}, u32[]{:S(2)}) collective-permute-start(bf16[1,4,32,256]{3,2,1,0:T(8,128)(2,1)S(1)} %bitcast.91), channel_id=1, source_target_pairs={{0,16},{8,24},{16,0},{24,8},{1,17},{9,25},{17,1},{25,9},{2,18},{10... | collective-permute-start | bytes 196616 | tf_op jit(solution)/shard_map/ppermute | solution.py:144
  68.8 11.7 %collective-permute-start.62 = (bf16[1,4,32,256]{3,2,1,0:T(8,128)(2,1)S(1)}, bf16[1,4,32,256]{3,2,1,0:T(8,128)(2,1)S(1)}, u32[]{:S(2)}, u32[]{:S(2)}) collective-permute-start(bf16[1,4,32,256]{3,2,1,0:T(8,128)(2,1)S(1)} %bitcast.87), channel_id=1, source_target_pairs={{0,16},{8,24},{16,0},{24,8},{1,17},{9,25},{17,1},{25,9},{2,18},{10... | collective-permute-start | bytes 196616 | tf_op jit(solution)/shard_map/ppermute | solution.py:144
  74.8 7.3 %collective-permute-start.48 = (bf16[1,2,4,32,256]{4,3,2,1,0:T(8,128)(2,1)S(1)}, bf16[1,2,4,32,256]{4,3,2,1,0:T(8,128)(2,1)S(1)}, u32[]{:S(2)}, u32[]{:S(2)}) collective-permute-start(bf16[1,2,4,32,256]{4,3,2,1,0:T(8,128)(2,1)S(1)} %maximum_bitcast_fusion.2), channel_id=1, source_target_pairs={{0,1},{1,0},{2,3},{3,2},{4,5},{5,4},{6,7},{7,6},{8,9},{9,8},{10,11... | collective-permute-start | bytes 393224 | tf_op jit(solution)/shard_map/ppermute | solution.py:144
  78.5 10.0 %collective-permute-start.19 = (bf16[2,2,4,32,256]{4,3,2,1,0:T(8,128)(2,1)S(1)}, bf16[2,2,4,32,256]{4,3,2,1,0:T(8,128)(2,1)S(1)}, u32[]{:S(2)}, u32[]{:S(2)}) collective-permute-start(bf16[2,2,4,32,256]{4,3,2,1,0:T(8,128)(2,1)S(1)} %pad_maximum_fusion.1.refs_4_), channel_id=1, source_target_pairs={{0,2},{2,0},{4,6},{6,4},{1,3},{3,1},{5,7},{7,5},{8,10},{10,8},{12,... | collective-permute-start | bytes 786440 | tf_op jit(solution)/shard_map/ppermute | solution.py:144
  80.0 9.1 %collective-permute-start.20 = (bf16[2,2,4,32,256]{4,3,2,1,0:T(8,128)(2,1)S(1)}, bf16[2,2,4,32,256]{4,3,2,1,0:T(8,128)(2,1)S(1)}, u32[]{:S(2)}, u32[]{:S(2)}) collective-permute-start(bf16[2,2,4,32,256]{4,3,2,1,0:T(8,128)(2,1)S(1)} %pad_maximum_fusion.1.refs_4_), channel_id=1, source_target_pairs={{0,4},{2,6},{4,0},{6,2},{1,5},{3,7},{5,1},{7,3},{8,12},{10,14},{12... | collective-permute-start | bytes 786440 | tf_op jit(solution)/shard_map/ppermute | solution.py:144
  80.4 9.6 %collective-permute-start.22 = (bf16[2,2,4,32,256]{4,3,2,1,0:T(8,128)(2,1)S(1)}, bf16[2,2,4,32,256]{4,3,2,1,0:T(8,128)(2,1)S(1)}, u32[]{:S(2)}, u32[]{:S(2)}) collective-permute-start(bf16[2,2,4,32,256]{4,3,2,1,0:T(8,128)(2,1)S(1)} %pad_maximum_fusion.1.refs_4_), channel_id=1, source_target_pairs={{0,8},{8,0},{16,24},{24,16},{1,9},{9,1},{17,25},{25,17},{2,10},{10... | collective-permute-start | bytes 786440 | tf_op jit(solution)/shard_map/ppermute | solution.py:144
  80.5 11.5 %collective-permute-start.34 = (bf16[2,2,4,32,256]{4,3,2,1,0:T(8,128)(2,1)S(1)}, bf16[2,2,4,32,256]{4,3,2,1,0:T(8,128)(2,1)S(1)}, u32[]{:S(2)}, u32[]{:S(2)}) collective-permute-start(bf16[2,2,4,32,256]{4,3,2,1,0:T(8,128)(2,1)S(1)} %pad_maximum_fusion.2.refs_4_), channel_id=1, source_target_pairs={{0,4},{2,6},{4,0},{6,2},{1,5},{3,7},{5,1},{7,3},{8,12},{10,14},{12... | collective-permute-start | bytes 786440 | tf_op jit(solution)/shard_map/ppermute | solution.py:144
  87.8 9.2 %collective-permute-start.35 = (bf16[2,2,4,32,256]{4,3,2,1,0:T(8,128)(2,1)S(1)}, bf16[2,2,4,32,256]{4,3,2,1,0:T(8,128)(2,1)S(1)}, u32[]{:S(2)}, u32[]{:S(2)}) collective-permute-start(bf16[2,2,4,32,256]{4,3,2,1,0:T(8,128)(2,1)S(1)} %pad_maximum_fusion.2.refs_4_), channel_id=1, source_target_pairs={{0,2},{2,0},{4,6},{6,4},{1,3},{3,1},{5,7},{7,5},{8,10},{10,8},{12,... | collective-permute-start | bytes 786440 | tf_op jit(solution)/shard_map/ppermute | solution.py:144
  88.5 9.0 %collective-permute-start.37 = (bf16[2,2,4,32,256]{4,3,2,1,0:T(8,128)(2,1)S(1)}, bf16[2,2,4,32,256]{4,3,2,1,0:T(8,128)(2,1)S(1)}, u32[]{:S(2)}, u32[]{:S(2)}) collective-permute-start(bf16[2,2,4,32,256]{4,3,2,1,0:T(8,128)(2,1)S(1)} %pad_maximum_fusion.2.refs_4_), channel_id=1, source_target_pairs={{0,8},{8,0},{16,24},{24,16},{1,9},{9,1},{17,25},{25,17},{2,10},{10... | collective-permute-start | bytes 786440 | tf_op jit(solution)/shard_map/ppermute | solution.py:144
  89.1 13.6 %collective-permute-start.49 = (bf16[2,2,4,32,256]{4,3,2,1,0:T(8,128)(2,1)S(1)}, bf16[2,2,4,32,256]{4,3,2,1,0:T(8,128)(2,1)S(1)}, u32[]{:S(2)}, u32[]{:S(2)}) collective-permute-start(bf16[2,2,4,32,256]{4,3,2,1,0:T(8,128)(2,1)S(1)} %pad_maximum_fusion.3.refs_4_), channel_id=1, source_target_pairs={{0,2},{2,0},{4,6},{6,4},{1,3},{3,1},{5,7},{7,5},{8,10},{10,8},{12,... | collective-permute-start | bytes 786440 | tf_op jit(solution)/shard_map/ppermute | solution.py:144
  90.1 12.6 %collective-permute-start.50 = (bf16[2,2,4,32,256]{4,3,2,1,0:T(8,128)(2,1)S(1)}, bf16[2,2,4,32,256]{4,3,2,1,0:T(8,128)(2,1)S(1)}, u32[]{:S(2)}, u32[]{:S(2)}) collective-permute-start(bf16[2,2,4,32,256]{4,3,2,1,0:T(8,128)(2,1)S(1)} %pad_maximum_fusion.3.refs_4_), channel_id=1, source_target_pairs={{0,4},{2,6},{4,0},{6,2},{1,5},{3,7},{5,1},{7,3},{8,12},{10,14},{12... | collective-permute-start | bytes 786440 | tf_op jit(solution)/shard_map/ppermute | solution.py:144
  92.0 11.1 %collective-permute-start.52 = (bf16[2,2,4,32,256]{4,3,2,1,0:T(8,128)(2,1)S(1)}, bf16[2,2,4,32,256]{4,3,2,1,0:T(8,128)(2,1)S(1)}, u32[]{:S(2)}, u32[]{:S(2)}) collective-permute-start(bf16[2,2,4,32,256]{4,3,2,1,0:T(8,128)(2,1)S(1)} %pad_maximum_fusion.3.refs_4_), channel_id=1, source_target_pairs={{0,8},{8,0},{16,24},{24,16},{1,9},{9,1},{17,25},{25,17},{2,10},{10... | collective-permute-start | bytes 786440 | tf_op jit(solution)/shard_map/ppermute | solution.py:144
  97.0 7.0 %collective-permute-start.64 = (bf16[2,2,4,32,256]{4,3,2,1,0:T(8,128)(2,1)S(1)}, bf16[2,2,4,32,256]{4,3,2,1,0:T(8,128)(2,1)S(1)}, u32[]{:S(2)}, u32[]{:S(2)}) collective-permute-start(bf16[2,2,4,32,256]{4,3,2,1,0:T(8,128)(2,1)S(1)} %pad_maximum_fusion.4.refs_4_), channel_id=1, source_target_pairs={{0,4},{2,6},{4,0},{6,2},{1,5},{3,7},{5,1},{7,3},{8,12},{10,14},{12... | collective-permute-start | bytes 786440 | tf_op jit(solution)/shard_map/ppermute | solution.py:144
  97.5 9.2 %collective-permute-start.65 = (bf16[2,2,4,32,256]{4,3,2,1,0:T(8,128)(2,1)S(1)}, bf16[2,2,4,32,256]{4,3,2,1,0:T(8,128)(2,1)S(1)}, u32[]{:S(2)}, u32[]{:S(2)}) collective-permute-start(bf16[2,2,4,32,256]{4,3,2,1,0:T(8,128)(2,1)S(1)} %pad_maximum_fusion.4.refs_4_), channel_id=1, source_target_pairs={{0,2},{2,0},{4,6},{6,4},{1,3},{3,1},{5,7},{7,5},{8,10},{10,8},{12,... | collective-permute-start | bytes 786440 | tf_op jit(solution)/shard_map/ppermute | solution.py:144
  102.7 8.7 %collective-permute-start.21 = (bf16[2,2,4,32,256]{4,3,2,1,0:T(8,128)(2,1)S(1)}, bf16[2,2,4,32,256]{4,3,2,1,0:T(8,128)(2,1)S(1)}, u32[]{:S(2)}, u32[]{:S(2)}) collective-permute-start(bf16[2,2,4,32,256]{4,3,2,1,0:T(8,128)(2,1)S(1)} %collective-permute-done.19.refs_5_), channel_id=1, source_target_pairs={{0,4},{2,6},{4,0},{6,2},{1,5},{3,7},{5,1},{7,3},{8,12},{10,14},{12... | collective-permute-start | bytes 786440 | tf_op jit(solution)/shard_map/ppermute | solution.py:144
  103.1 8.3 %collective-permute-start.23 = (bf16[2,2,4,32,256]{4,3,2,1,0:T(8,128)(2,1)S(1)}, bf16[2,2,4,32,256]{4,3,2,1,0:T(8,128)(2,1)S(1)}, u32[]{:S(2)}, u32[]{:S(2)}) collective-permute-start(bf16[2,2,4,32,256]{4,3,2,1,0:T(8,128)(2,1)S(1)} %collective-permute-done.19.refs_5_), channel_id=1, source_target_pairs={{0,8},{8,0},{16,24},{24,16},{1,9},{9,1},{17,25},{25,17},{2,10},{10... | collective-permute-start | bytes 786440 | tf_op jit(solution)/shard_map/ppermute | solution.py:144
  104.0 7.8 %collective-permute-start.24 = (bf16[2,2,4,32,256]{4,3,2,1,0:T(8,128)(2,1)S(1)}, bf16[2,2,4,32,256]{4,3,2,1,0:T(8,128)(2,1)S(1)}, u32[]{:S(2)}, u32[]{:S(2)}) collective-permute-start(bf16[2,2,4,32,256]{4,3,2,1,0:T(8,128)(2,1)S(1)} %collective-permute-done.20.refs_6_), channel_id=1, source_target_pairs={{0,8},{8,0},{16,24},{24,16},{1,9},{9,1},{17,25},{25,17},{2,10},{10... | collective-permute-start | bytes 786440 | tf_op jit(solution)/shard_map/ppermute | solution.py:144
  111.4 8.7 %collective-permute-start.51 = (bf16[2,2,4,32,256]{4,3,2,1,0:T(8,128)(2,1)S(1)}, bf16[2,2,4,32,256]{4,3,2,1,0:T(8,128)(2,1)S(1)}, u32[]{:S(2)}, u32[]{:S(2)}) collective-permute-start(bf16[2,2,4,32,256]{4,3,2,1,0:T(8,128)(2,1)S(1)} %collective-permute-done.49.refs_5_), channel_id=1, source_target_pairs={{0,4},{2,6},{4,0},{6,2},{1,5},{3,7},{5,1},{7,3},{8,12},{10,14},{12... | collective-permute-start | bytes 786440 | tf_op jit(solution)/shard_map/ppermute | solution.py:144
  111.8 8.3 %collective-permute-start.25 = (bf16[2,2,4,32,256]{4,3,2,1,0:T(8,128)(2,1)S(1)}, bf16[2,2,4,32,256]{4,3,2,1,0:T(8,128)(2,1)S(1)}, u32[]{:S(2)}, u32[]{:S(2)}) collective-permute-start(bf16[2,2,4,32,256]{4,3,2,1,0:T(8,128)(2,1)S(1)} %collective-permute-done.21.refs_7_), channel_id=1, source_target_pairs={{0,8},{8,0},{16,24},{24,16},{1,9},{9,1},{17,25},{25,17},{2,10},{10... | collective-permute-start | bytes 786440 | tf_op jit(solution)/shard_map/ppermute | solution.py:144
  113.4 10.6 %collective-permute-start.53 = (bf16[2,2,4,32,256]{4,3,2,1,0:T(8,128)(2,1)S(1)}, bf16[2,2,4,32,256]{4,3,2,1,0:T(8,128)(2,1)S(1)}, u32[]{:S(2)}, u32[]{:S(2)}) collective-permute-start(bf16[2,2,4,32,256]{4,3,2,1,0:T(8,128)(2,1)S(1)} %collective-permute-done.49.refs_5_), channel_id=1, source_target_pairs={{0,8},{8,0},{16,24},{24,16},{1,9},{9,1},{17,25},{25,17},{2,10},{10... | collective-permute-start | bytes 786440 | tf_op jit(solution)/shard_map/ppermute | solution.py:144
  113.4 10.7 %collective-permute-start.54 = (bf16[2,2,4,32,256]{4,3,2,1,0:T(8,128)(2,1)S(1)}, bf16[2,2,4,32,256]{4,3,2,1,0:T(8,128)(2,1)S(1)}, u32[]{:S(2)}, u32[]{:S(2)}) collective-permute-start(bf16[2,2,4,32,256]{4,3,2,1,0:T(8,128)(2,1)S(1)} %collective-permute-done.50.refs_6_), channel_id=1, source_target_pairs={{0,8},{8,0},{16,24},{24,16},{1,9},{9,1},{17,25},{25,17},{2,10},{10... | collective-permute-start | bytes 786440 | tf_op jit(solution)/shard_map/ppermute | solution.py:144
  113.9 10.7 %collective-permute-start.66 = (bf16[2,2,4,32,256]{4,3,2,1,0:T(8,128)(2,1)S(1)}, bf16[2,2,4,32,256]{4,3,2,1,0:T(8,128)(2,1)S(1)}, u32[]{:S(2)}, u32[]{:S(2)}) collective-permute-start(bf16[2,2,4,32,256]{4,3,2,1,0:T(8,128)(2,1)S(1)} %collective-permute-done.64.refs_5_), channel_id=1, source_target_pairs={{0,2},{2,0},{4,6},{6,4},{1,3},{3,1},{5,7},{7,5},{8,10},{10,8},{12,... | collective-permute-start | bytes 786440 | tf_op jit(solution)/shard_map/ppermute | solution.py:144
  120.1 8.4 %collective-permute-start.55 = (bf16[2,2,4,32,256]{4,3,2,1,0:T(8,128)(2,1)S(1)}, bf16[2,2,4,32,256]{4,3,2,1,0:T(8,128)(2,1)S(1)}, u32[]{:S(2)}, u32[]{:S(2)}) collective-permute-start(bf16[2,2,4,32,256]{4,3,2,1,0:T(8,128)(2,1)S(1)} %collective-permute-done.51.refs_7_), channel_id=1, source_target_pairs={{0,8},{8,0},{16,24},{24,16},{1,9},{9,1},{17,25},{25,17},{2,10},{10... | collective-permute-start | bytes 786440 | tf_op jit(solution)/shard_map/ppermute | solution.py:144
  124.0 8.2 %collective-permute-start.68 = (bf16[2,2,4,32,256]{4,3,2,1,0:T(8,128)(2,1)S(1)}, bf16[2,2,4,32,256]{4,3,2,1,0:T(8,128)(2,1)S(1)}, u32[]{:S(2)}, u32[]{:S(2)}) collective-permute-start(bf16[2,2,4,32,256]{4,3,2,1,0:T(8,128)(2,1)S(1)} %collective-permute-done.64.refs_5_), channel_id=1, source_target_pairs={{0,8},{8,0},{16,24},{24,16},{1,9},{9,1},{17,25},{25,17},{2,10},{10... | collective-permute-start | bytes 786440 | tf_op jit(solution)/shard_map/ppermute | solution.py:144
  124.1 8.6 %collective-permute-start.69 = (bf16[2,2,4,32,256]{4,3,2,1,0:T(8,128)(2,1)S(1)}, bf16[2,2,4,32,256]{4,3,2,1,0:T(8,128)(2,1)S(1)}, u32[]{:S(2)}, u32[]{:S(2)}) collective-permute-start(bf16[2,2,4,32,256]{4,3,2,1,0:T(8,128)(2,1)S(1)} %collective-permute-done.65.refs_6_), channel_id=1, source_target_pairs={{0,8},{8,0},{16,24},{24,16},{1,9},{9,1},{17,25},{25,17},{2,10},{10... | collective-permute-start | bytes 786440 | tf_op jit(solution)/shard_map/ppermute | solution.py:144
  124.6 8.1 %collective-permute-start.70 = (bf16[2,2,4,32,256]{4,3,2,1,0:T(8,128)(2,1)S(1)}, bf16[2,2,4,32,256]{4,3,2,1,0:T(8,128)(2,1)S(1)}, u32[]{:S(2)}, u32[]{:S(2)}) collective-permute-start(bf16[2,2,4,32,256]{4,3,2,1,0:T(8,128)(2,1)S(1)} %collective-permute-done.66.refs_7_), channel_id=1, source_target_pairs={{0,8},{8,0},{16,24},{24,16},{1,9},{9,1},{17,25},{25,17},{2,10},{10... | collective-permute-start | bytes 786440 | tf_op jit(solution)/shard_map/ppermute | solution.py:144
  124.7 11.6 %collective-permute-start.26 = (bf16[4,2,2,32,1024]{4,3,2,1,0:T(8,128)(2,1)S(1)}, bf16[4,2,2,32,1024]{4,3,2,1,0:T(8,128)(2,1)S(1)}, u32[]{:S(2)}, u32[]{:S(2)}) collective-permute-start(bf16[4,2,2,32,1024]{4,3,2,1,0:T(8,128)(2,1)S(1)} %shard_map.115), channel_id=1, source_target_pairs={{0,8},{8,0},{16,24},{24,16},{1,9},{9,1},{17,25},{25,17},{2,10},{10... | collective-permute-start | bytes 3145736 | tf_op jit(solution)/shard_map/ppermute | solution.py:144
  128.5 11.7 %collective-permute-start.41 = (bf16[4,2,2,32,1024]{4,3,2,1,0:T(8,128)(2,1)S(1)}, bf16[4,2,2,32,1024]{4,3,2,1,0:T(8,128)(2,1)S(1)}, u32[]{:S(2)}, u32[]{:S(2)}) collective-permute-start(bf16[4,2,2,32,1024]{4,3,2,1,0:T(8,128)(2,1)S(1)} %shard_map.117), channel_id=1, source_target_pairs={{0,8},{8,0},{16,24},{24,16},{1,9},{9,1},{17,25},{25,17},{2,10},{10... | collective-permute-start | bytes 3145736 | tf_op jit(solution)/shard_map/ppermute | solution.py:144
  132.2 13.6 %collective-permute-start.56 = (bf16[4,2,2,32,1024]{4,3,2,1,0:T(8,128)(2,1)S(1)}, bf16[4,2,2,32,1024]{4,3,2,1,0:T(8,128)(2,1)S(1)}, u32[]{:S(2)}, u32[]{:S(2)}) collective-permute-start(bf16[4,2,2,32,1024]{4,3,2,1,0:T(8,128)(2,1)S(1)} %shard_map.119), channel_id=1, source_target_pairs={{0,8},{8,0},{16,24},{24,16},{1,9},{9,1},{17,25},{25,17},{2,10},{10... | collective-permute-start | bytes 3145736 | tf_op jit(solution)/shard_map/ppermute | solution.py:144
  136.1 14.6 %collective-permute-start.71 = (bf16[4,2,2,32,1024]{4,3,2,1,0:T(8,128)(2,1)S(1)}, bf16[4,2,2,32,1024]{4,3,2,1,0:T(8,128)(2,1)S(1)}, u32[]{:S(2)}, u32[]{:S(2)}) collective-permute-start(bf16[4,2,2,32,1024]{4,3,2,1,0:T(8,128)(2,1)S(1)} %shard_map.121), channel_id=1, source_target_pairs={{0,8},{8,0},{16,24},{24,16},{1,9},{9,1},{17,25},{25,17},{2,10},{10... | collective-permute-start | bytes 3145736 | tf_op jit(solution)/shard_map/ppermute | solution.py:144
  139.7 15.2 %collective-permute-start.28 = (bf16[2,2,32,1024]{3,2,1,0:T(8,128)(2,1)S(1)}, bf16[2,2,32,1024]{3,2,1,0:T(8,128)(2,1)S(1)}, u32[]{:S(2)}, u32[]{:S(2)}) collective-permute-start(bf16[2,2,32,1024]{3,2,1,0:T(8,128)(2,1)S(1)} %get-tuple-element.69), channel_id=1, source_target_pairs={{0,4},{2,6},{4,0},{6,2},{1,5},{3,7},{5,1},{7,3},{8,12},{10,14},{12... | collective-permute-start | bytes 786440 | tf_op jit(solution)/shard_map/ppermute | solution.py:144
  143.6 13.0 %collective-permute-start.43 = (bf16[2,2,32,1024]{3,2,1,0:T(8,128)(2,1)S(1)}, bf16[2,2,32,1024]{3,2,1,0:T(8,128)(2,1)S(1)}, u32[]{:S(2)}, u32[]{:S(2)}) collective-permute-start(bf16[2,2,32,1024]{3,2,1,0:T(8,128)(2,1)S(1)} %get-tuple-element.74), channel_id=1, source_target_pairs={{0,2},{2,0},{4,6},{6,4},{1,3},{3,1},{5,7},{7,5},{8,10},{10,8},{12,... | collective-permute-start | bytes 786440 | tf_op jit(solution)/shard_map/ppermute | solution.py:144
  144.5 21.8 %collective-permute-start.27 = (bf16[2,2,32,1024]{3,2,1,0:T(8,128)(2,1)S(1)}, bf16[2,2,32,1024]{3,2,1,0:T(8,128)(2,1)S(1)}, u32[]{:S(2)}, u32[]{:S(2)}) collective-permute-start(bf16[2,2,32,1024]{3,2,1,0:T(8,128)(2,1)S(1)} %get-tuple-element.67), channel_id=1, source_target_pairs={{0,4},{2,6},{4,0},{6,2},{1,5},{3,7},{5,1},{7,3},{8,12},{10,14},{12... | collective-permute-start | bytes 786440 | tf_op jit(solution)/shard_map/ppermute | solution.py:144
  145.8 25.9 %collective-permute-start.42 = (bf16[2,2,32,1024]{3,2,1,0:T(8,128)(2,1)S(1)}, bf16[2,2,32,1024]{3,2,1,0:T(8,128)(2,1)S(1)}, u32[]{:S(2)}, u32[]{:S(2)}) collective-permute-start(bf16[2,2,32,1024]{3,2,1,0:T(8,128)(2,1)S(1)} %get-tuple-element.72), channel_id=1, source_target_pairs={{0,2},{2,0},{4,6},{6,4},{1,3},{3,1},{5,7},{7,5},{8,10},{10,8},{12,... | collective-permute-start | bytes 786440 | tf_op jit(solution)/shard_map/ppermute | solution.py:144
  150.7 9.4 %collective-permute-start.58 = (bf16[2,2,32,1024]{3,2,1,0:T(8,128)(2,1)S(1)}, bf16[2,2,32,1024]{3,2,1,0:T(8,128)(2,1)S(1)}, u32[]{:S(2)}, u32[]{:S(2)}) collective-permute-start(bf16[2,2,32,1024]{3,2,1,0:T(8,128)(2,1)S(1)} %get-tuple-element.79), channel_id=1, source_target_pairs={{0,4},{2,6},{4,0},{6,2},{1,5},{3,7},{5,1},{7,3},{8,12},{10,14},{12... | collective-permute-start | bytes 786440 | tf_op jit(solution)/shard_map/ppermute | solution.py:144
  154.8 18.6 %collective-permute-start.57 = (bf16[2,2,32,1024]{3,2,1,0:T(8,128)(2,1)S(1)}, bf16[2,2,32,1024]{3,2,1,0:T(8,128)(2,1)S(1)}, u32[]{:S(2)}, u32[]{:S(2)}) collective-permute-start(bf16[2,2,32,1024]{3,2,1,0:T(8,128)(2,1)S(1)} %get-tuple-element.77), channel_id=1, source_target_pairs={{0,4},{2,6},{4,0},{6,2},{1,5},{3,7},{5,1},{7,3},{8,12},{10,14},{12... | collective-permute-start | bytes 786440 | tf_op jit(solution)/shard_map/ppermute | solution.py:144
  156.6 8.9 %collective-permute-start.73 = (bf16[2,2,32,1024]{3,2,1,0:T(8,128)(2,1)S(1)}, bf16[2,2,32,1024]{3,2,1,0:T(8,128)(2,1)S(1)}, u32[]{:S(2)}, u32[]{:S(2)}) collective-permute-start(bf16[2,2,32,1024]{3,2,1,0:T(8,128)(2,1)S(1)} %get-tuple-element.84), channel_id=1, source_target_pairs={{0,2},{2,0},{4,6},{6,4},{1,3},{3,1},{5,7},{7,5},{8,10},{10,8},{12,... | collective-permute-start | bytes 786440 | tf_op jit(solution)/shard_map/ppermute | solution.py:144
  160.2 10.9 %collective-permute-start.29 = (bf16[2,2,32,1024]{3,2,1,0:T(8,128)(2,1)S(1)}, bf16[2,2,32,1024]{3,2,1,0:T(8,128)(2,1)S(1)}, u32[]{:S(2)}, u32[]{:S(2)}) collective-permute-start(bf16[2,2,32,1024]{3,2,1,0:T(8,128)(2,1)S(1)} %add_convert_fusion.3), channel_id=1, source_target_pairs={{0,2},{2,0},{4,6},{6,4},{1,3},{3,1},{5,7},{7,5},{8,10},{10,8},{12,... | collective-permute-start | bytes 786440 | tf_op jit(solution)/shard_map/ppermute | solution.py:144
  165.5 7.7 %collective-permute-start.44 = (bf16[2,2,32,1024]{3,2,1,0:T(8,128)(2,1)S(1)}, bf16[2,2,32,1024]{3,2,1,0:T(8,128)(2,1)S(1)}, u32[]{:S(2)}, u32[]{:S(2)}) collective-permute-start(bf16[2,2,32,1024]{3,2,1,0:T(8,128)(2,1)S(1)} %add_convert_fusion.2), channel_id=1, source_target_pairs={{0,4},{2,6},{4,0},{6,2},{1,5},{3,7},{5,1},{7,3},{8,12},{10,14},{12... | collective-permute-start | bytes 786440 | tf_op jit(solution)/shard_map/ppermute | solution.py:144
  166.3 14.5 %collective-permute-start.72 = (bf16[2,2,32,1024]{3,2,1,0:T(8,128)(2,1)S(1)}, bf16[2,2,32,1024]{3,2,1,0:T(8,128)(2,1)S(1)}, u32[]{:S(2)}, u32[]{:S(2)}) collective-permute-start(bf16[2,2,32,1024]{3,2,1,0:T(8,128)(2,1)S(1)} %get-tuple-element.82), channel_id=1, source_target_pairs={{0,2},{2,0},{4,6},{6,4},{1,3},{3,1},{5,7},{7,5},{8,10},{10,8},{12,... | collective-permute-start | bytes 786440 | tf_op jit(solution)/shard_map/ppermute | solution.py:144
  171.1 9.4 %collective-permute-start.59 = (bf16[2,2,32,1024]{3,2,1,0:T(8,128)(2,1)S(1)}, bf16[2,2,32,1024]{3,2,1,0:T(8,128)(2,1)S(1)}, u32[]{:S(2)}, u32[]{:S(2)}) collective-permute-start(bf16[2,2,32,1024]{3,2,1,0:T(8,128)(2,1)S(1)} %add_convert_fusion.1), channel_id=1, source_target_pairs={{0,2},{2,0},{4,6},{6,4},{1,3},{3,1},{5,7},{7,5},{8,10},{10,8},{12,... | collective-permute-start | bytes 786440 | tf_op jit(solution)/shard_map/ppermute | solution.py:144
  171.7 9.2 %collective-permute-start.74 = (bf16[2,2,32,1024]{3,2,1,0:T(8,128)(2,1)S(1)}, bf16[2,2,32,1024]{3,2,1,0:T(8,128)(2,1)S(1)}, u32[]{:S(2)}, u32[]{:S(2)}) collective-permute-start(bf16[2,2,32,1024]{3,2,1,0:T(8,128)(2,1)S(1)} %add_convert_fusion), channel_id=1, source_target_pairs={{0,4},{2,6},{4,0},{6,2},{1,5},{3,7},{5,1},{7,3},{8,12},{10,14},{12... | collective-permute-start | bytes 786440 | tf_op jit(solution)/shard_map/ppermute | solution.py:144
  173.2 9.6 %collective-permute-start.30 = (bf16[1,2,32,1024]{3,2,1,0:T(8,128)(2,1)S(1)}, bf16[1,2,32,1024]{3,2,1,0:T(8,128)(2,1)S(1)}, u32[]{:S(2)}, u32[]{:S(2)}) collective-permute-start(bf16[1,2,32,1024]{3,2,1,0:T(8,128)(2,1)S(1)} %add_convert_fusion.7), channel_id=1, source_target_pairs={{0,1},{1,0},{2,3},{3,2},{4,5},{5,4},{6,7},{7,6},{8,9},{9,8},{10,11... | collective-permute-start | bytes 393224 | tf_op jit(solution)/shard_map/ppermute | solution.py:144
  173.5 9.4 %collective-permute-start.45 = (bf16[1,2,32,1024]{3,2,1,0:T(8,128)(2,1)S(1)}, bf16[1,2,32,1024]{3,2,1,0:T(8,128)(2,1)S(1)}, u32[]{:S(2)}, u32[]{:S(2)}) collective-permute-start(bf16[1,2,32,1024]{3,2,1,0:T(8,128)(2,1)S(1)} %add_convert_fusion.6), channel_id=1, source_target_pairs={{0,1},{1,0},{2,3},{3,2},{4,5},{5,4},{6,7},{7,6},{8,9},{9,8},{10,11... | collective-permute-start | bytes 393224 | tf_op jit(solution)/shard_map/ppermute | solution.py:144
  180.9 7.8 %collective-permute-start.75 = (bf16[1,2,32,1024]{3,2,1,0:T(8,128)(2,1)S(1)}, bf16[1,2,32,1024]{3,2,1,0:T(8,128)(2,1)S(1)}, u32[]{:S(2)}, u32[]{:S(2)}) collective-permute-start(bf16[1,2,32,1024]{3,2,1,0:T(8,128)(2,1)S(1)} %add_convert_fusion.4), channel_id=1, source_target_pairs={{0,1},{1,0},{2,3},{3,2},{4,5},{5,4},{6,7},{7,6},{8,9},{9,8},{10,11... | collective-permute-start | bytes 393224 | tf_op jit(solution)/shard_map/ppermute | solution.py:144
  182.8 8.4 %collective-permute-start.31 = (bf16[1,32,1024]{2,1,0:T(8,128)(2,1)S(1)}, bf16[1,32,1024]{2,1,0:T(8,128)(2,1)S(1)}, u32[]{:S(2)}, u32[]{:S(2)}) collective-permute-start(bf16[1,32,1024]{2,1,0:T(8,128)(2,1)S(1)} %fusion.2), channel_id=1, source_target_pairs={{0,16},{8,24},{16,0},{24,8},{1,17},{9,25},{17,1},{25,9},{2,18},{10... | collective-permute-start | bytes 196616 | tf_op jit(solution)/shard_map/ppermute | solution.py:144
  182.9 10.1 %collective-permute-start.46 = (bf16[1,32,1024]{2,1,0:T(8,128)(2,1)S(1)}, bf16[1,32,1024]{2,1,0:T(8,128)(2,1)S(1)}, u32[]{:S(2)}, u32[]{:S(2)}) collective-permute-start(bf16[1,32,1024]{2,1,0:T(8,128)(2,1)S(1)} %fusion.3), channel_id=1, source_target_pairs={{0,16},{8,24},{16,0},{24,8},{1,17},{9,25},{17,1},{25,9},{2,18},{10... | collective-permute-start | bytes 196616 | tf_op jit(solution)/shard_map/ppermute | solution.py:144
  (22 other events, 260.7 us)

commit v4 on v3

--- a/solution.py
+++ b/solution.py
@@ -168,6 +168,24 @@
     return held
 
 
+def exchange_rows(table, steps):
+    lanes = table.shape[1]
+    sizes = {"seq": lax.axis_size("seq"), "expert": lax.axis_size("expert")}
+    table = table.reshape(sizes["seq"], sizes["expert"], lanes)
+    for axis, bit in steps:
+        dim = 0 if axis == "seq" else 1
+        size = sizes[axis]
+        parts = jnp.split(table, size, axis=dim)
+        low = [n for n in range(size) if not n & bit]
+        away = jnp.concatenate([parts[n ^ bit] for n in low], axis=dim)
+        away = swap(away, axis, bit)
+        arrived = jnp.split(away, len(low), axis=dim)
+        for n, part in zip(low, arrived):
+            parts[n ^ bit] = part
+        table = jnp.concatenate(parts, axis=dim)
+    return table.reshape(-1, lanes)
+
+
 def total(terms):
     if len(terms) == 1:
         return terms[0]
@@ -196,8 +214,8 @@
 def expert_kernel(order, near, start_row, *refs):
     groups = len(order)
     refs = list(refs)
-    place_ref, table_ref, w_in_ref, w_out_ref = refs[:4]
-    in_refs, refs = refs[4 : 4 + groups], refs[4 + groups :]
+    table_ref, w_in_ref, w_out_ref = refs[:3]
+    in_refs, refs = refs[3 : 3 + groups], refs[3 + groups :]
     halves, blocks, sessions, rows, piece = in_refs[0].shape
     gain_refs, refs = refs[:halves], refs[halves:]
     proj_ref, received_ref = (None, None) if near else (refs.pop(0), refs.pop(0))
@@ -205,11 +223,16 @@
     half_width = refs[0].shape[-1]
     width = half_width * halves
     hidden_width = w_out_ref.shape[0]
-    me, half_me, seq_me = place_ref[0], place_ref[1], place_ref[2]
+    me, half_me = lax.axis_index("expert"), lax.axis_index("tensor")
     per_half = half_width // piece
     count = groups * rows * blocks
     for k, ref in enumerate(gain_refs):
-        gain_ref[k * per_half : (k + 1) * per_half] = ref[...]
+        for n in range(per_half):
+            for lane in range(0, piece, LANES):
+                line = (n * piece + lane) // LANES
+                gain_ref[k * per_half + n : k * per_half + n + 1, lane : lane + LANES] = ref[
+                    line : line + 1
+                ]
 
     power = jnp.zeros((count, 1), jnp.float32)
     pieces = []
@@ -244,9 +267,8 @@
     scales = []
     for b in range(blocks):
         for r in range(groups):
-            source = lax.bitwise_xor(seq_me, 2 * b + near) * sessions
-            source = source + lax.bitwise_xor(me, order[r])
-            line = table_ref[pl.ds(source, 1), :][:, start_row : start_row + rows]
+            source = (2 * b + near) * sessions + order[r]
+            line = table_ref[source : source + 1, start_row : start_row + rows]
             scales.append(
                 jnp.sum(jnp.where(diagonal, line, 0.0), axis=1, keepdims=True)
             )
@@ -282,7 +304,7 @@
                     refs[r][k, b] = part
 
 
-def attention_kernel(head, order, place_ref, q_ref, *refs):
+def attention_kernel(head, order, q_ref, *refs):
     slots = len(order)
     k_refs, v_refs, out_ref = refs[:slots], refs[slots : 2 * slots], refs[-1]
     rows = q_ref.shape[0]
@@ -291,7 +313,7 @@
     values = jnp.concatenate([ref[:, columns] for ref in v_refs], axis=0)
     down = lax.broadcasted_iota(jnp.int32, (rows, rows), 0)
     across = lax.broadcasted_iota(jnp.int32, (rows, rows), 1)
-    seq_me = place_ref[2]
+    seq_me = lax.axis_index("seq")
     allowed = jnp.concatenate(
         [
             (lax.bitwise_xor(seq_me, place) - seq_me) * rows + across <= down
@@ -303,10 +325,9 @@
     batch = max(1, heads // 2)
     allowed = jnp.concatenate([allowed] * batch, axis=0)
     for first in range(0, heads, batch):
-        start = head * heads + first
         queries = jnp.concatenate(
             [
-                q_ref[:, (start + n) * HEAD_SIZE : (start + n + 1) * HEAD_SIZE]
+                q_ref[:, (first + n) * HEAD_SIZE : (first + n + 1) * HEAD_SIZE]
                 for n in range(batch)
             ],
             axis=0,
@@ -326,41 +347,60 @@
             ]
 
 
-def side_kernel(place_ref, x_ref, ids_ref, weights_ref, table_ref, half_ref, *piece_refs):
-    me, half_me = place_ref[0], place_ref[1]
+def side_kernel(groups, x_ref, q_ref, k_ref, v_ref, ids_ref, weights_ref, *refs):
+    ids, weights, sems = refs[-3:]
+    table_ref, half_ref, k_out, v_out = refs[:4]
+    piece_refs, q_outs = refs[4 : 4 + groups], refs[4 + groups : -3]
+    me, half_me, seq_me = (lax.axis_index(name) for name in ("expert", "tensor", "seq"))
     width, half_width, piece = (ref.shape[1] for ref in (x_ref, half_ref, piece_refs[0]))
-    halves = width // half_width
+    moves = [(ids_ref, ids), (weights_ref, weights)]
+    for r, piece_ref in enumerate(piece_refs):
+        spot = lax.bitwise_xor(me, r) * (width // half_width) + half_me
+        start = pl.multiple_of(spot * piece, piece)
+        moves.append((x_ref.at[:, pl.ds(start, piece)], piece_ref))
+    moves += [(k_ref, k_out), (v_ref, v_out)]
+    depth = q_outs[0].shape[1]
+    for n, out in enumerate(q_outs):
+        moves.append((q_ref.at[:, n * depth : (n + 1) * depth], out))
     start = pl.multiple_of(half_me * half_width, half_width)
-    half_ref[...] = x_ref[:, pl.ds(start, half_width)]
-    for r, piece_ref in enumerate(piece_refs):
-        spot = lax.bitwise_xor(me, r) * halves + half_me
-        piece_ref[...] = x_ref[:, pl.ds(pl.multiple_of(spot * piece, piece), piece)]
-    number = lax.broadcasted_iota(jnp.int32, (x_ref.shape[0], LANES), 1)
-    table = jnp.zeros(number.shape, jnp.float32)
-    for k in range(ids_ref.shape[1]):
-        table += jnp.where(ids_ref[:, k : k + 1] == number, weights_ref[:, k : k + 1], 0.0)
-    table_ref[...] = table.T[: table_ref.shape[0]]
-
-
-def project_kernel(away, place_ref, w_ref, *refs):
+    moves.append((x_ref.at[:, pl.ds(start, half_width)], half_ref))
+    copies = [
+        pltpu.make_async_copy(source, target, sems.at[n])
+        for n, (source, target) in enumerate(moves)
+    ]
+    for copy in copies:
+        copy.start()
+    copies[0].wait()
+    copies[1].wait()
+    for n in range(table_ref.shape[0]):
+        expert = lax.bitwise_xor(seq_me, n // groups) * groups
+        expert = expert + lax.bitwise_xor(me, n % groups)
+        table_ref[n : n + 1] = jnp.sum(
+            jnp.where(ids[...] == expert, weights[...], 0.0), axis=0, keepdims=True
+        )
+    for copy in copies[2:]:
+        copy.wait()
+
+
+def project_kernel(away, w_ref, *refs):
     out_ref, joined_ref = refs[-2:]
     sessions, rows, piece = out_ref.shape
     depth = refs[0].shape[1]
     for n, ref in enumerate(refs[:-2]):
         half, r = divmod(n, sessions)
         joined_ref[r * rows : (r + 1) * rows, half * depth : (half + 1) * depth] = ref[...]
-    start = pl.multiple_of(lax.bitwise_xor(place_ref[1], away) * piece, piece)
+    start = pl.multiple_of(lax.bitwise_xor(lax.axis_index("tensor"), away) * piece, piece)
     result = jnp.dot(
         joined_ref[...], w_ref[:, pl.ds(start, piece)], preferred_element_type=jnp.float32
     )
     out_ref[...] = result.reshape(sessions, rows, piece).astype(out_ref.dtype)
 
 
-def mix_kernel(sessions, place_ref, *refs):
+def mix_kernel(sessions, *refs):
     x_refs, refs = refs[:sessions], refs[sessions:]
     terms, (proj_ref, *chunk_refs) = refs[: -1 - CHUNKS], refs[-1 - CHUNKS :]
     rows = chunk_refs[0].shape[1]
-    me = place_ref[0]
+    me = lax.axis_index("expert")
     for r in range(sessions):
         proj = sum(ref[r].astype(jnp.float32) for ref in terms)
         proj_ref[r] = proj
@@ -369,12 +409,11 @@
             chunk_ref[lax.bitwise_xor(me, r)] = mixed[c * rows : (c + 1) * rows]
 
 
-def local_kernel(kernel, outs, operands, scratch=(), limit=8 << 20):
+def local_kernel(kernel, outs, operands, scratch=(), limit=8 << 20, space=pltpu.VMEM):
     return pl.pallas_call(
         kernel,
         out_shape=outs,
-        in_specs=[pl.BlockSpec(memory_space=pltpu.SMEM)]
-        + [pl.BlockSpec(memory_space=pltpu.VMEM)] * (len(operands) - 1),
+        in_specs=[pl.BlockSpec(memory_space=space)] * len(operands),
         out_specs=[pl.BlockSpec(memory_space=pltpu.VMEM)] * len(outs),
         scratch_shapes=scratch,
         compiler_params=pltpu.CompilerParams(vmem_limit_bytes=limit),
@@ -399,47 +438,53 @@
     seq_count, group_count = lax.axis_size("seq"), lax.axis_size("expert")
     tensor_count = lax.axis_size("tensor")
     experts = seq_count * group_count
-    seq_pos, group_pos = lax.axis_index("seq"), lax.axis_index("expert")
-    tensor_pos = lax.axis_index("tensor")
     seq_bits, group_bits = bits_of(seq_count), bits_of(group_count)
     tensor_bits = bits_of(tensor_count)
     half_width = width // tensor_count
     piece = width // (group_count * tensor_count)
     near, far = seq_bits[:1], seq_bits[1:]
 
-    place = jnp.stack([group_pos, tensor_pos, seq_pos]).astype(jnp.int32)
-
     kv_bits = far + near
     keys = gather_parts(k_rows[0], "seq", kv_bits)
     values = gather_parts(value_rows[0], "seq", kv_bits)
 
-    piece_type = jax.ShapeDtypeStruct((rows_here, piece), x_rows.dtype)
-    table, x_half, *x_slots = local_kernel(
-        side_kernel,
+    kv_heads = k_rows.shape[2] // HEAD_SIZE
+    depth = q_rows.shape[2] // kv_heads
+    kind = x_rows.dtype
+    ids, weights = expert_ids[0].T, gate_weights[0].T
+    shapes = [(experts, rows_here), (rows_here, half_width)]
+    shapes += [k_rows.shape[1:]] * 2 + [(rows_here, piece)] * group_count
+    shapes += [(rows_here, depth)] * kv_heads
+    table, x_half, keys[0], values[0], *rest = local_kernel(
+        functools.partial(side_kernel, group_count),
+        [jax.ShapeDtypeStruct(shape, kind if n else jnp.float32) for n, shape in enumerate(shapes)],
+        [x_rows[0], q_rows[0], k_rows[0], value_rows[0], ids, weights],
         [
-            jax.ShapeDtypeStruct((experts, rows_here), jnp.float32),
-            jax.ShapeDtypeStruct((rows_here, half_width), x_rows.dtype),
-        ]
-        + [piece_type] * group_count,
-        [place, x_rows[0], expert_ids[0], gate_weights[0]],
-    )
+            pltpu.VMEM(ids.shape, ids.dtype),
+            pltpu.VMEM(weights.shape, weights.dtype),
+            pltpu.SemaphoreType.DMA((len(shapes) + 1,)),
+        ],
+        space=pltpu.HBM,
+    )
+    x_slots, queries = rest[:group_count], rest[group_count:]
     for r in range(1, group_count):
         x_slots[r] = swap(x_slots[r], "expert", r)
-    table = lax.all_to_all(table, ("seq", "expert"), split_axis=0, concat_axis=0, tiled=True)
-    gain = norm_gain.reshape(half_width // piece, piece)
-    place, table, gain = lax.optimization_barrier((place, table, gain))
-
-    kv_heads = k_rows.shape[2] // HEAD_SIZE
-    depth = q_rows.shape[2] // kv_heads
+    gain = norm_gain.reshape(half_width // LANES, LANES)
+
     attended = []
     for head in range(kv_heads):
         attended += local_kernel(
             functools.partial(attention_kernel, head, tuple(slot_order(kv_bits))),
             [jax.ShapeDtypeStruct((rows_here, depth), jnp.bfloat16)],
-            [place, q_rows[0], *keys, *values],
+            [queries[head], *keys, *values],
         )
 
-    w_gate, w_up, gain, _ = lax.optimization_barrier((w_gate, w_up, gain, attended[0]))
+    w_gate, w_up, gain, table, _ = lax.optimization_barrier(
+        (w_gate, w_up, gain, table, attended[0])
+    )
+    table = exchange_rows(
+        table, [("seq", bit) for bit in seq_bits] + [("expert", bit) for bit in group_bits]
+    )
     gains = gather_parts(gain, "tensor", tensor_bits)
     w_in = jnp.concatenate([w_gate[0], w_up[0]], axis=1)
 
@@ -456,7 +501,7 @@
         return local_kernel(
             functools.partial(project_kernel, k),
             [jax.ShapeDtypeStruct(shape, kind)],
-            [place, out_weight, *gathered],
+            [out_weight, *gathered],
             [pltpu.VMEM((group_count * rows_here, out_weight.shape[0]), jnp.bfloat16)],
         )[0]
 
@@ -470,9 +515,9 @@
     proj, *by_session = local_kernel(
         functools.partial(mix_kernel, group_count),
         [jax.ShapeDtypeStruct((group_count, rows_here, piece), jnp.float32)] + [part] * CHUNKS,
-        [place, *x_slots, *terms],
-    )
-    w_in, *rest = lax.optimization_barrier((w_in, *gains, *by_session))
+        [*x_slots, *terms],
+    )
+    w_in, table, *rest = lax.optimization_barrier((w_in, table, *gains, *by_session))
     gains, by_session = rest[:tensor_count], rest[tensor_count:]
 
     blocks = seq_count // 2
@@ -490,7 +535,7 @@
 
     def experts_on(c, path, parts, received):
         order = tuple(slot_order(path))
-        operands = [place, table, w_in, w_down[0], *parts, *gains]
+        operands = [table, w_in, w_down[0], *parts, *gains]
         shape = (tensor_count, blocks, rows, half_width)
         if received is None:
             shapes = [jax.ShapeDtypeStruct((group_count, *shape), jnp.bfloat16)]

time: 196 us -> 183 us (0.934)
  waiting for transfers between devices: 89.9 us -> 76.2 us
  starting transfers between devices: 61.9 us -> 70.4 us
  Pallas kernels: 35.6 us -> 27.5 us
    ppermute x77 -> x81, starting transfers between devices: 57.7 us -> 70.4 us  [swap(): return lax.ppermute(value, axis, [(i, i ^ bit) for i in range(count)])]
    ppermute x77 -> x81, waiting for transfers between devices: 84.3 us -> 76.2 us  [swap(): return lax.ppermute(value, axis, [(i, i ^ bit) for i in range(count)])]
    pallas_call x14, Pallas kernels: 35.6 us -> 27.5 us  [local_kernel(): pl.pallas_call(kernel, out_shape=outs, in_specs=[pl.BlockSpec(memory_spac...]
    all_to_all x1 -> x0, waiting for transfers between devices: 5.62 us -> none  [dense_plan(): lax.all_to_all(table, ('seq', 'expert'), split_axis=0, concat_axis=0, til...]
    all_to_all x1 -> x0, starting transfers between devices: 4.15 us -> none  [dense_plan(): lax.all_to_all(table, ('seq', 'expert'), split_axis=0, concat_axis=0, til...]
    unnamed x18 -> x22, local copies, waits for them, and re-layouts: 5.35 us -> 5.58 us
  transfers between devices with their start and end apart: 78 -> 81, of which waited for: 33 -> 29; matrix products, arithmetic and copies ran while one was open for 2% -> 1% of each run, Pallas kernels for 17% -> 14%
where the time goes in v4:
time: 183 us; the launch traced here: 182 us
  waiting for transfers between devices  76.2 us (42%)
  starting transfers between devices  70.4 us (38%)
  Pallas kernels  27.5 us (15%)
  local copies, waits for them, and re-layouts  5.6 us (3%)
  other arithmetic  2.04 us (1%)
    ppermute x81, waiting for transfers between devices, swap(): return lax.ppermute(value, axis, [(i, i ^ bit) for i in range(count)])  76.2 us
    ppermute x81, starting transfers between devices, swap(): return lax.ppermute(value, axis, [(i, i ^ bit) for i in range(count)])  70.4 us
    pallas_call x14, Pallas kernels, local_kernel(): pl.pallas_call(kernel, out_shape=outs, in_specs=[pl.BlockSpec(memory_spac...  27.5 us
    unnamed x22, local copies, waits for them, and re-layouts  5.58 us
  transfers between devices with their start and end apart: 81, of which 29 were waited for; matrix products, arithmetic and copies ran while one was open for 1% of the time, Pallas kernels for 14%

profile of v4, /device:TPU:0, one launch (start us, length us, event | category | flops | bytes accessed | tf_op | source)
XLA Modules:
  0.0 182.2 jit_solution(18077679199930631185)
XLA Ops:
  0.0 4.1 %collective-permute-start = (bf16[128,256]{1,0:T(8,128)(2,1)}, bf16[128,256]{1,0:T(8,128)(2,1)S(1)}, u32[]{:S(2)}, u32[]{:S(2)}) collective-permute-start(bf16[128,256]{1,0:T(8,128)(2,1)} %bitcast.92), channel_id=1, source_target_pairs={{0,16},{8,24},{16,0},{24,8},{1,17},{9,25},{17,1},{25,9},{2,18},{10... | collective-permute-start | bytes 196616 | tf_op jit(solution)/shard_map/ppermute | solution.py:144
  4.6 3.3 %collective-permute-done.refs_1_ = bf16[128,256]{1,0:T(8,128)(2,1)S(1)} collective-permute-done((bf16[128,256]{1,0:T(8,128)(2,1)}, bf16[128,256]{1,0:T(8,128)(2,1)S(1)}, u32[]{:S(2)}, u32[]{:S(2)}) %collective-permute-start) | collective-permute-done | bytes 65568 | tf_op jit(solution)/shard_map/ppermute | solution.py:144
  8.0 2.8 %collective-permute-done.3.refs_5_ = bf16[128,256]{1,0:T(8,128)(2,1)S(1)} collective-permute-done((bf16[128,256]{1,0:T(8,128)(2,1)}, bf16[128,256]{1,0:T(8,128)(2,1)S(1)}, u32[]{:S(2)}, u32[]{:S(2)}) %collective-permute-start.3) | collective-permute-done | bytes 65568 | tf_op jit(solution)/shard_map/ppermute | solution.py:144
  10.7 1.0 copy-done.2
  11.8 1.0 copy-done.3
  16.4 1.2 shard_map.110.refs_0_
  19.0 1.8 collective-permute-start.14
  20.8 1.2 shard_map.111.refs_4_
  22.0 1.6 collective-permute-start.18
  23.6 1.7 collective-permute-start.8
  25.7 1.7 collective-permute-start.15
  27.4 1.0 collective-permute-done.8
  28.3 1.7 collective-permute-start.17
  30.0 1.5 collective-permute-start.16
  32.1 4.7 %collective-permute-done.15.refs_2_ = bf16[128,1024]{1,0:T(8,128)(2,1)S(1)} collective-permute-done((bf16[128,1024]{1,0:T(8,128)(2,1)S(1)}, bf16[128,1024]{1,0:T(8,128)(2,1)S(1)}, u32[]{:S(2)}, u32[]{:S(2)}) %collective-permute-start.15) | collective-permute-done | bytes 262176 | tf_op jit(solution)/shard_map/ppermute | solution.py:144
  36.8 1.5 collective-permute-start.12
  38.4 1.8 collective-permute-start.13
  40.2 2.8 %collective-permute-done.16.refs_3_ = bf16[128,1024]{1,0:T(8,128)(2,1)S(1)} collective-permute-done((bf16[128,1024]{1,0:T(8,128)(2,1)S(1)}, bf16[128,1024]{1,0:T(8,128)(2,1)S(1)}, u32[]{:S(2)}, u32[]{:S(2)}) %collective-permute-start.16) | collective-permute-done | bytes 262176 | tf_op jit(solution)/shard_map/ppermute | solution.py:144
  43.0 2.2 %collective-permute-start.9 = (f32[4,2,128]{2,1,0:T(2,128)S(1)}, f32[4,2,128]{2,1,0:T(2,128)S(1)}, u32[]{:S(2)}, u32[]{:S(2)}) collective-permute-start(f32[4,2,128]{2,1,0:T(2,128)S(1)} %pad_maximum_fusion.10), channel_id=1, source_target_pairs={{0,4},{2,6},{4,0},{6,2},{1,5},{3,7},{5,1},{7,3},{8,12},{10,14},{12... | collective-permute-start | bytes 12296 | tf_op jit(solution)/shard_map/ppermute | solution.py:144
  45.9 3.5 %collective-permute-start.20 = (bf16[4,128,256]{2,1,0:T(8,128)(2,1)S(1)}, bf16[4,128,256]{2,1,0:T(8,128)(2,1)S(1)}, u32[]{:S(2)}, u32[]{:S(2)}) collective-permute-start(bf16[4,128,256]{2,1,0:T(8,128)(2,1)S(1)} %shard_map.112), channel_id=1, source_target_pairs={{0,1},{1,0},{2,3},{3,2},{4,5},{5,4},{6,7},{7,6},{8,9},{9,8},{10,11... | collective-permute-start | bytes 786440 | tf_op jit(solution)/shard_map/ppermute | solution.py:144
  51.0 4.0 %collective-permute-done.20.refs_4_ = bf16[4,128,256]{2,1,0:T(8,128)(2,1)S(1)} collective-permute-done((bf16[4,128,256]{2,1,0:T(8,128)(2,1)S(1)}, bf16[4,128,256]{2,1,0:T(8,128)(2,1)S(1)}, u32[]{:S(2)}, u32[]{:S(2)}) %collective-permute-start.20) | collective-permute-done | bytes 262176 | tf_op jit(solution)/shard_map/ppermute | solution.py:144
  55.1 2.9 %collective-permute-start.36 = (bf16[1,4,32,256]{3,2,1,0:T(8,128)(2,1)S(1)}, bf16[1,4,32,256]{3,2,1,0:T(8,128)(2,1)S(1)}, u32[]{:S(2)}, u32[]{:S(2)}) collective-permute-start(bf16[1,4,32,256]{3,2,1,0:T(8,128)(2,1)S(1)} %bitcast.102), channel_id=1, source_target_pairs={{0,16},{8,24},{16,0},{24,8},{1,17},{9,25},{17,1},{25,9},{2,18},{10... | collective-permute-start | bytes 196616 | tf_op jit(solution)/shard_map/ppermute | solution.py:144
  58.1 2.8 %collective-permute-start.66 = (bf16[1,4,32,256]{3,2,1,0:T(8,128)(2,1)S(1)}, bf16[1,4,32,256]{3,2,1,0:T(8,128)(2,1)S(1)}, u32[]{:S(2)}, u32[]{:S(2)}) collective-permute-start(bf16[1,4,32,256]{3,2,1,0:T(8,128)(2,1)S(1)} %bitcast.98), channel_id=1, source_target_pairs={{0,16},{8,24},{16,0},{24,8},{1,17},{9,25},{17,1},{25,9},{2,18},{10... | collective-permute-start | bytes 196616 | tf_op jit(solution)/shard_map/ppermute | solution.py:144
  60.9 2.5 %collective-permute-start.22 = (bf16[1,2,4,32,256]{4,3,2,1,0:T(8,128)(2,1)S(1)}, bf16[1,2,4,32,256]{4,3,2,1,0:T(8,128)(2,1)S(1)}, u32[]{:S(2)}, u32[]{:S(2)}) collective-permute-start(bf16[1,2,4,32,256]{4,3,2,1,0:T(8,128)(2,1)S(1)} %maximum_bitcast_fusion), channel_id=1, source_target_pairs={{0,1},{1,0},{2,3},{3,2},{4,5},{5,4},{6,7},{7,6},{8,9},{9,8},{10,11... | collective-permute-start | bytes 393224 | tf_op jit(solution)/shard_map/ppermute | solution.py:144
  63.8 2.0 %collective-permute-start.52 = (bf16[1,2,4,32,256]{4,3,2,1,0:T(8,128)(2,1)S(1)}, bf16[1,2,4,32,256]{4,3,2,1,0:T(8,128)(2,1)S(1)}, u32[]{:S(2)}, u32[]{:S(2)}) collective-permute-start(bf16[1,2,4,32,256]{4,3,2,1,0:T(8,128)(2,1)S(1)} %maximum_bitcast_fusion.2), channel_id=1, source_target_pairs={{0,1},{1,0},{2,3},{3,2},{4,5},{5,4},{6,7},{7,6},{8,9},{9,8},{10,11... | collective-permute-start | bytes 393224 | tf_op jit(solution)/shard_map/ppermute | solution.py:144
  65.7 0.9 collective-permute-done.22
  66.7 1.3 collective-permute-start.23
  68.6 1.5 collective-permute-start.38
  70.2 1.1 collective-permute-start.67
  71.3 4.6 %collective-permute-done.67 = bf16[1,2,4,32,256]{4,3,2,1,0:T(8,128)(2,1)S(1)} collective-permute-done((bf16[1,2,4,32,256]{4,3,2,1,0:T(8,128)(2,1)S(1)}, bf16[1,2,4,32,256]{4,3,2,1,0:T(8,128)(2,1)S(1)}, u32[]{:S(2)}, u32[]{:S(2)}) %collective-permute-start.67) | collective-permute-done | bytes 131104 | tf_op jit(solution)/shard_map/ppermute | solution.py:144
  77.0 1.1 collective-permute-start.53
  78.6 1.4 collective-permute-done.38.refs_4_
  80.0 5.0 %collective-permute-done.39.refs_5_ = bf16[2,2,4,32,256]{4,3,2,1,0:T(8,128)(2,1)S(1)} collective-permute-done((bf16[2,2,4,32,256]{4,3,2,1,0:T(8,128)(2,1)S(1)}, bf16[2,2,4,32,256]{4,3,2,1,0:T(8,128)(2,1)S(1)}, u32[]{:S(2)}, u32[]{:S(2)}) %collective-permute-start.39) | collective-permute-done | bytes 262176 | tf_op jit(solution)/shard_map/ppermute | solution.py:144
  86.3 4.3 %collective-permute-done.53.refs_4_ = bf16[2,2,4,32,256]{4,3,2,1,0:T(8,128)(2,1)S(1)} collective-permute-done((bf16[2,2,4,32,256]{4,3,2,1,0:T(8,128)(2,1)S(1)}, bf16[2,2,4,32,256]{4,3,2,1,0:T(8,128)(2,1)S(1)}, u32[]{:S(2)}, u32[]{:S(2)}) %collective-permute-start.53) | collective-permute-done | bytes 262176 | tf_op jit(solution)/shard_map/ppermute | solution.py:144
  92.0 2.6 %collective-permute-done.69.refs_5_ = bf16[2,2,4,32,256]{4,3,2,1,0:T(8,128)(2,1)S(1)} collective-permute-done((bf16[2,2,4,32,256]{4,3,2,1,0:T(8,128)(2,1)S(1)}, bf16[2,2,4,32,256]{4,3,2,1,0:T(8,128)(2,1)S(1)}, u32[]{:S(2)}, u32[]{:S(2)}) %collective-permute-start.69) | collective-permute-done | bytes 262176 | tf_op jit(solution)/shard_map/ppermute | solution.py:144
  95.6 3.8 %collective-permute-done.25.refs_6_ = bf16[2,2,4,32,256]{4,3,2,1,0:T(8,128)(2,1)S(1)} collective-permute-done((bf16[2,2,4,32,256]{4,3,2,1,0:T(8,128)(2,1)S(1)}, bf16[2,2,4,32,256]{4,3,2,1,0:T(8,128)(2,1)S(1)}, u32[]{:S(2)}, u32[]{:S(2)}) %collective-permute-start.25) | collective-permute-done | bytes 262176 | tf_op jit(solution)/shard_map/ppermute | solution.py:144
  100.2 1.2 collective-permute-done.40.refs_6_
  101.9 1.0 collective-permute-start.70
  102.9 5.2 %collective-permute-done.55.refs_6_ = bf16[2,2,4,32,256]{4,3,2,1,0:T(8,128)(2,1)S(1)} collective-permute-done((bf16[2,2,4,32,256]{4,3,2,1,0:T(8,128)(2,1)S(1)}, bf16[2,2,4,32,256]{4,3,2,1,0:T(8,128)(2,1)S(1)}, u32[]{:S(2)}, u32[]{:S(2)}) %collective-permute-start.55) | collective-permute-done | bytes 262176 | tf_op jit(solution)/shard_map/ppermute | solution.py:144
  108.6 2.8 %shard_map.115 = bf16[4,2,2,32,1024]{4,3,2,1,0:T(8,128)(2,1)S(1)} custom-call(f32[16,128]{1,0:T(8,128)S(1)} %bitcast.73, bf16[2048,768]{1,0:T(8,128)(2,1)S(1)} %pad_maximum_fusion.refs_1_, bf16[384,2048]{1,0:T(8,128)(2,1)S(1)} %bitcast.65, bf16[2,2,4,32,256]{4,3,2,1,0:T(8,128)(2,1)S(1)} %collective-permute-done.26.refs_3_, ...), custom_call_target="tpu_custom_call" | custom-call | tf_op jit(solution)/shard_map/pallas_call | solution.py:413
  112.6 3.0 %shard_map.117 = bf16[4,2,2,32,1024]{4,3,2,1,0:T(8,128)(2,1)S(1)} custom-call(f32[16,128]{1,0:T(8,128)S(1)} %bitcast.74, bf16[2048,768]{1,0:T(8,128)(2,1)S(1)} %pad_maximum_fusion.refs_1_, bf16[384,2048]{1,0:T(8,128)(2,1)S(1)} %bitcast.66, bf16[2,2,4,32,256]{4,3,2,1,0:T(8,128)(2,1)S(1)} %collective-permute-done.41.refs_3_, ...), custom_call_target="tpu_custom_call" | custom-call | tf_op jit(solution)/shard_map/pallas_call | solution.py:413
  115.7 2.8 %shard_map.119 = bf16[4,2,2,32,1024]{4,3,2,1,0:T(8,128)(2,1)S(1)} custom-call(f32[16,128]{1,0:T(8,128)S(1)} %bitcast.75, bf16[2048,768]{1,0:T(8,128)(2,1)S(1)} %pad_maximum_fusion.refs_1_, bf16[384,2048]{1,0:T(8,128)(2,1)S(1)} %bitcast.67, bf16[2,2,4,32,256]{4,3,2,1,0:T(8,128)(2,1)S(1)} %collective-permute-done.56.refs_3_, ...), custom_call_target="tpu_custom_call" | custom-call | tf_op jit(solution)/shard_map/pallas_call | solution.py:413
  119.1 2.8 %shard_map.121 = bf16[4,2,2,32,1024]{4,3,2,1,0:T(8,128)(2,1)S(1)} custom-call(f32[16,128]{1,0:T(8,128)S(1)} %bitcast.76, bf16[2048,768]{1,0:T(8,128)(2,1)S(1)} %pad_maximum_fusion.refs_1_, bf16[384,2048]{1,0:T(8,128)(2,1)S(1)} %bitcast.68, bf16[2,2,4,32,256]{4,3,2,1,0:T(8,128)(2,1)S(1)} %collective-permute-done.71.refs_3_, ...), custom_call_target="tpu_custom_call" | custom-call | tf_op jit(solution)/shard_map/pallas_call | solution.py:413
  122.0 2.9 %shard_map.116 = (bf16[2,2,32,1024]{3,2,1,0:T(8,128)(2,1)S(1)}, bf16[2,2,32,1024]{3,2,1,0:T(8,128)(2,1)S(1)}, bf16[2,2,32,1024]{3,2,1,0:T(8,128)(2,1)S(1)}, bf16[2,2,32,1024]{3,2,1,0:T(8,128)(2,1)S(1)}) custom-call(f32[16,128]{1,0:T(8,128)S(1)} %bitcast.77, bf16[2048,768]{1,0:T(8,128)(2,1)S(1)} %pad_maximum_fusion.refs_1_, bf16[384,2048]{1,0:T(8,128)(2,1)S(1)} %bitcast.69, ...), custom_call_target="tpu_custom_call" | custom-call | tf_op jit(solution)/shard_map/pallas_call | solution.py:413
  125.5 2.9 %shard_map.118 = (bf16[2,2,32,1024]{3,2,1,0:T(8,128)(2,1)S(1)}, bf16[2,2,32,1024]{3,2,1,0:T(8,128)(2,1)S(1)}, bf16[2,2,32,1024]{3,2,1,0:T(8,128)(2,1)S(1)}, bf16[2,2,32,1024]{3,2,1,0:T(8,128)(2,1)S(1)}) custom-call(f32[16,128]{1,0:T(8,128)S(1)} %bitcast.78, bf16[2048,768]{1,0:T(8,128)(2,1)S(1)} %pad_maximum_fusion.refs_1_, bf16[384,2048]{1,0:T(8,128)(2,1)S(1)} %bitcast.70, ...), custom_call_target="tpu_custom_call" | custom-call | tf_op jit(solution)/shard_map/pallas_call | solution.py:413
  129.2 1.6 collective-permute-start.31
  130.8 1.2 collective-permute-start.46
  132.0 2.9 %shard_map.120 = (bf16[2,2,32,1024]{3,2,1,0:T(8,128)(2,1)S(1)}, bf16[2,2,32,1024]{3,2,1,0:T(8,128)(2,1)S(1)}, bf16[2,2,32,1024]{3,2,1,0:T(8,128)(2,1)S(1)}, bf16[2,2,32,1024]{3,2,1,0:T(8,128)(2,1)S(1)}) custom-call(f32[16,128]{1,0:T(8,128)S(1)} %bitcast.79, bf16[2048,768]{1,0:T(8,128)(2,1)S(1)} %pad_maximum_fusion.refs_1_, bf16[384,2048]{1,0:T(8,128)(2,1)S(1)} %bitcast.71, ...), custom_call_target="tpu_custom_call" | custom-call | tf_op jit(solution)/shard_map/pallas_call | solution.py:413
  135.5 3.1 %shard_map.122 = (bf16[2,2,32,1024]{3,2,1,0:T(8,128)(2,1)S(1)}, bf16[2,2,32,1024]{3,2,1,0:T(8,128)(2,1)S(1)}, bf16[2,2,32,1024]{3,2,1,0:T(8,128)(2,1)S(1)}, bf16[2,2,32,1024]{3,2,1,0:T(8,128)(2,1)S(1)}) custom-call(f32[16,128]{1,0:T(8,128)S(1)} %bitcast.80, bf16[2048,768]{1,0:T(8,128)(2,1)S(1)} %pad_maximum_fusion.refs_1_, bf16[384,2048]{1,0:T(8,128)(2,1)S(1)} %bitcast.72, ...), custom_call_target="tpu_custom_call" | custom-call | tf_op jit(solution)/shard_map/pallas_call | solution.py:413
  138.6 1.5 collective-permute-start.61
  141.1 4.3 %collective-permute-done.62 = bf16[2,2,32,1024]{3,2,1,0:T(8,128)(2,1)S(1)} collective-permute-done((bf16[2,2,32,1024]{3,2,1,0:T(8,128)(2,1)S(1)}, bf16[2,2,32,1024]{3,2,1,0:T(8,128)(2,1)S(1)}, u32[]{:S(2)}, u32[]{:S(2)}) %collective-permute-start.62) | collective-permute-done | bytes 262176 | tf_op jit(solution)/shard_map/ppermute | solution.py:144
  146.3 2.8 %collective-permute-done.77 = bf16[2,2,32,1024]{3,2,1,0:T(8,128)(2,1)S(1)} collective-permute-done((bf16[2,2,32,1024]{3,2,1,0:T(8,128)(2,1)S(1)}, bf16[2,2,32,1024]{3,2,1,0:T(8,128)(2,1)S(1)}, u32[]{:S(2)}, u32[]{:S(2)}) %collective-permute-start.77) | collective-permute-done | bytes 262176 | tf_op jit(solution)/shard_map/ppermute | solution.py:144
  149.1 1.2 collective-permute-start.48
  151.3 3.4 %collective-permute-done.33 = bf16[2,2,32,1024]{3,2,1,0:T(8,128)(2,1)S(1)} collective-permute-done((bf16[2,2,32,1024]{3,2,1,0:T(8,128)(2,1)S(1)}, bf16[2,2,32,1024]{3,2,1,0:T(8,128)(2,1)S(1)}, u32[]{:S(2)}, u32[]{:S(2)}) %collective-permute-start.33) | collective-permute-done | bytes 262176 | tf_op jit(solution)/shard_map/ppermute | solution.py:144
  155.5 1.5 collective-permute-start.78
  156.9 1.8 collective-permute-start.34
  159.1 5.8 %collective-permute-done.63 = bf16[2,2,32,1024]{3,2,1,0:T(8,128)(2,1)S(1)} collective-permute-done((bf16[2,2,32,1024]{3,2,1,0:T(8,128)(2,1)S(1)}, bf16[2,2,32,1024]{3,2,1,0:T(8,128)(2,1)S(1)}, u32[]{:S(2)}, u32[]{:S(2)}) %collective-permute-start.63) | collective-permute-done | bytes 262176 | tf_op jit(solution)/shard_map/ppermute | solution.py:144
  165.0 1.4 collective-permute-start.64
  167.2 1.4 collective-permute-start.35
  168.6 1.7 collective-permute-start.50
  170.3 2.5 %collective-permute-done.64 = bf16[1,2,32,1024]{3,2,1,0:T(8,128)(2,1)S(1)} collective-permute-done((bf16[1,2,32,1024]{3,2,1,0:T(8,128)(2,1)S(1)}, bf16[1,2,32,1024]{3,2,1,0:T(8,128)(2,1)S(1)}, u32[]{:S(2)}, u32[]{:S(2)}) %collective-permute-start.64) | collective-permute-done | bytes 131104 | tf_op jit(solution)/shard_map/ppermute | solution.py:144
  173.2 2.2 %collective-permute-done.79 = bf16[1,2,32,1024]{3,2,1,0:T(8,128)(2,1)S(1)} collective-permute-done((bf16[1,2,32,1024]{3,2,1,0:T(8,128)(2,1)S(1)}, bf16[1,2,32,1024]{3,2,1,0:T(8,128)(2,1)S(1)}, u32[]{:S(2)}, u32[]{:S(2)}) %collective-permute-start.79) | collective-permute-done | bytes 131104 | tf_op jit(solution)/shard_map/ppermute | solution.py:144
  176.0 2.9 %collective-permute-done.50 = bf16[1,32,1024]{2,1,0:T(8,128)(2,1)S(1)} collective-permute-done((bf16[1,32,1024]{2,1,0:T(8,128)(2,1)S(1)}, bf16[1,32,1024]{2,1,0:T(8,128)(2,1)S(1)}, u32[]{:S(2)}, u32[]{:S(2)}) %collective-permute-start.50) | collective-permute-done | bytes 65568 | tf_op jit(solution)/shard_map/ppermute | solution.py:144
  179.0 1.6 collective-permute-done.65
  (170 shorter events, 28.5 us)
Async XLA Ops:
  0.0 8.0 %collective-permute-start = (bf16[128,256]{1,0:T(8,128)(2,1)}, bf16[128,256]{1,0:T(8,128)(2,1)S(1)}, u32[]{:S(2)}, u32[]{:S(2)}) collective-permute-start(bf16[128,256]{1,0:T(8,128)(2,1)} %bitcast.92), channel_id=1, source_target_pairs={{0,16},{8,24},{16,0},{24,8},{1,17},{9,25},{17,1},{25,9},{2,18},{10... | collective-permute-start | bytes 196616 | tf_op jit(solution)/shard_map/ppermute | solution.py:144
  4.1 6.7 %collective-permute-start.3 = (bf16[128,256]{1,0:T(8,128)(2,1)}, bf16[128,256]{1,0:T(8,128)(2,1)S(1)}, u32[]{:S(2)}, u32[]{:S(2)}) collective-permute-start(bf16[128,256]{1,0:T(8,128)(2,1)} %bitcast.95), channel_id=1, source_target_pairs={{0,16},{8,24},{16,0},{24,8},{1,17},{9,25},{17,1},{25,9},{2,18},{10... | collective-permute-start | bytes 196616 | tf_op jit(solution)/shard_map/ppermute | solution.py:144
  4.1 12.2 %collective-permute-start.1 = (bf16[128,256]{1,0:T(8,128)(2,1)}, bf16[128,256]{1,0:T(8,128)(2,1)S(1)}, u32[]{:S(2)}, u32[]{:S(2)}) collective-permute-start(bf16[128,256]{1,0:T(8,128)(2,1)} %bitcast.93), channel_id=1, source_target_pairs={{0,8},{8,0},{16,24},{24,16},{1,9},{9,1},{17,25},{25,17},{2,10},{10... | collective-permute-start | bytes 196616 | tf_op jit(solution)/shard_map/ppermute | solution.py:144
  4.1 12.2 %collective-permute-start.4 = (bf16[128,256]{1,0:T(8,128)(2,1)}, bf16[128,256]{1,0:T(8,128)(2,1)S(1)}, u32[]{:S(2)}, u32[]{:S(2)}) collective-permute-start(bf16[128,256]{1,0:T(8,128)(2,1)} %bitcast.96), channel_id=1, source_target_pairs={{0,8},{8,0},{16,24},{24,16},{1,9},{9,1},{17,25},{25,17},{2,10},{10... | collective-permute-start | bytes 196616 | tf_op jit(solution)/shard_map/ppermute | solution.py:144
  8.0 8.3 %collective-permute-start.2 = (bf16[128,256]{1,0:T(8,128)(2,1)S(1)}, bf16[128,256]{1,0:T(8,128)(2,1)S(1)}, u32[]{:S(2)}, u32[]{:S(2)}) collective-permute-start(bf16[128,256]{1,0:T(8,128)(2,1)S(1)} %collective-permute-done.refs_1_), channel_id=1, source_target_pairs={{0,8},{8,0},{16,24},{24,16},{1,9},{9,1},{17,25},{25,17},{2,10},{10... | collective-permute-start | bytes 196616 | tf_op jit(solution)/shard_map/ppermute | solution.py:144
  19.0 11.0 %collective-permute-start.14 = (bf16[128,1024]{1,0:T(8,128)(2,1)S(1)}, bf16[128,1024]{1,0:T(8,128)(2,1)S(1)}, u32[]{:S(2)}, u32[]{:S(2)}) collective-permute-start(bf16[128,1024]{1,0:T(8,128)(2,1)S(1)} %shard_map.110.refs_0_), channel_id=1, source_target_pairs={{0,2},{2,0},{4,6},{6,4},{1,3},{3,1},{5,7},{7,5},{8,10},{10,8},{12,... | collective-permute-start | bytes 786440 | tf_op jit(solution)/shard_map/ppermute | solution.py:144
  22.0 9.6 %collective-permute-start.18 = (bf16[128,1024]{1,0:T(8,128)(2,1)S(1)}, bf16[128,1024]{1,0:T(8,128)(2,1)S(1)}, u32[]{:S(2)}, u32[]{:S(2)}) collective-permute-start(bf16[128,1024]{1,0:T(8,128)(2,1)S(1)} %shard_map.111.refs_4_), channel_id=1, source_target_pairs={{0,4},{2,6},{4,0},{6,2},{1,5},{3,7},{5,1},{7,3},{8,12},{10,14},{12... | collective-permute-start | bytes 786440 | tf_op jit(solution)/shard_map/ppermute | solution.py:144
  25.3 25.6 %collective-permute-start.11 = (bf16[128,256]{1,0:T(8,128)(2,1)S(1)}, bf16[128,256]{1,0:T(8,128)(2,1)S(1)}, u32[]{:S(2)}, u32[]{:S(2)}) collective-permute-start(bf16[128,256]{1,0:T(8,128)(2,1)S(1)} %get-tuple-element.58), channel_id=1, source_target_pairs={{0,2},{2,0},{4,6},{6,4},{1,3},{3,1},{5,7},{7,5},{8,10},{10,8},{12,... | collective-permute-start | bytes 196616 | tf_op jit(solution)/shard_map/ppermute | solution.py:144
  25.7 11.1 %collective-permute-start.15 = (bf16[128,1024]{1,0:T(8,128)(2,1)S(1)}, bf16[128,1024]{1,0:T(8,128)(2,1)S(1)}, u32[]{:S(2)}, u32[]{:S(2)}) collective-permute-start(bf16[128,1024]{1,0:T(8,128)(2,1)S(1)} %shard_map.110.refs_0_), channel_id=1, source_target_pairs={{0,4},{2,6},{4,0},{6,2},{1,5},{3,7},{5,1},{7,3},{8,12},{10,14},{12... | collective-permute-start | bytes 786440 | tf_op jit(solution)/shard_map/ppermute | solution.py:144
  28.3 10.0 %collective-permute-start.17 = (bf16[128,1024]{1,0:T(8,128)(2,1)S(1)}, bf16[128,1024]{1,0:T(8,128)(2,1)S(1)}, u32[]{:S(2)}, u32[]{:S(2)}) collective-permute-start(bf16[128,1024]{1,0:T(8,128)(2,1)S(1)} %shard_map.111.refs_4_), channel_id=1, source_target_pairs={{0,2},{2,0},{4,6},{6,4},{1,3},{3,1},{5,7},{7,5},{8,10},{10,8},{12,... | collective-permute-start | bytes 786440 | tf_op jit(solution)/shard_map/ppermute | solution.py:144
  30.0 12.9 %collective-permute-start.16 = (bf16[128,1024]{1,0:T(8,128)(2,1)S(1)}, bf16[128,1024]{1,0:T(8,128)(2,1)S(1)}, u32[]{:S(2)}, u32[]{:S(2)}) collective-permute-start(bf16[128,1024]{1,0:T(8,128)(2,1)S(1)} %collective-permute-done.14.refs_1_), channel_id=1, source_target_pairs={{0,4},{2,6},{4,0},{6,2},{1,5},{3,7},{5,1},{7,3},{8,12},{10,14},{12... | collective-permute-start | bytes 786440 | tf_op jit(solution)/shard_map/ppermute | solution.py:144
  31.6 13.6 %collective-permute-start.19 = (bf16[128,1024]{1,0:T(8,128)(2,1)S(1)}, bf16[128,1024]{1,0:T(8,128)(2,1)S(1)}, u32[]{:S(2)}, u32[]{:S(2)}) collective-permute-start(bf16[128,1024]{1,0:T(8,128)(2,1)S(1)} %collective-permute-done.18.refs_6_), channel_id=1, source_target_pairs={{0,2},{2,0},{4,6},{6,4},{1,3},{3,1},{5,7},{7,5},{8,10},{10,8},{12,... | collective-permute-start | bytes 786440 | tf_op jit(solution)/shard_map/ppermute | solution.py:144
  36.8 14.1 %collective-permute-start.12 = (bf16[128,256]{1,0:T(8,128)(2,1)S(1)}, bf16[128,256]{1,0:T(8,128)(2,1)S(1)}, u32[]{:S(2)}, u32[]{:S(2)}) collective-permute-start(bf16[128,256]{1,0:T(8,128)(2,1)S(1)} %get-tuple-element.59), channel_id=1, source_target_pairs={{0,4},{2,6},{4,0},{6,2},{1,5},{3,7},{5,1},{7,3},{8,12},{10,14},{12... | collective-permute-start | bytes 196616 | tf_op jit(solution)/shard_map/ppermute | solution.py:144
  38.4 12.6 %collective-permute-start.13 = (bf16[128,256]{1,0:T(8,128)(2,1)S(1)}, bf16[128,256]{1,0:T(8,128)(2,1)S(1)}, u32[]{:S(2)}, u32[]{:S(2)}) collective-permute-start(bf16[128,256]{1,0:T(8,128)(2,1)S(1)} %get-tuple-element.60), channel_id=1, source_target_pairs={{0,6},{2,4},{4,2},{6,0},{1,7},{3,5},{5,3},{7,1},{8,14},{10,12},{12... | collective-permute-start | bytes 196616 | tf_op jit(solution)/shard_map/ppermute | solution.py:144
  45.9 9.0 %collective-permute-start.20 = (bf16[4,128,256]{2,1,0:T(8,128)(2,1)S(1)}, bf16[4,128,256]{2,1,0:T(8,128)(2,1)S(1)}, u32[]{:S(2)}, u32[]{:S(2)}) collective-permute-start(bf16[4,128,256]{2,1,0:T(8,128)(2,1)S(1)} %shard_map.112), channel_id=1, source_target_pairs={{0,1},{1,0},{2,3},{3,2},{4,5},{5,4},{6,7},{7,6},{8,9},{9,8},{10,11... | collective-permute-start | bytes 786440 | tf_op jit(solution)/shard_map/ppermute | solution.py:144
  55.1 8.4 %collective-permute-start.36 = (bf16[1,4,32,256]{3,2,1,0:T(8,128)(2,1)S(1)}, bf16[1,4,32,256]{3,2,1,0:T(8,128)(2,1)S(1)}, u32[]{:S(2)}, u32[]{:S(2)}) collective-permute-start(bf16[1,4,32,256]{3,2,1,0:T(8,128)(2,1)S(1)} %bitcast.102), channel_id=1, source_target_pairs={{0,16},{8,24},{16,0},{24,8},{1,17},{9,25},{17,1},{25,9},{2,18},{10... | collective-permute-start | bytes 196616 | tf_op jit(solution)/shard_map/ppermute | solution.py:144
  58.1 10.5 %collective-permute-start.66 = (bf16[1,4,32,256]{3,2,1,0:T(8,128)(2,1)S(1)}, bf16[1,4,32,256]{3,2,1,0:T(8,128)(2,1)S(1)}, u32[]{:S(2)}, u32[]{:S(2)}) collective-permute-start(bf16[1,4,32,256]{3,2,1,0:T(8,128)(2,1)S(1)} %bitcast.98), channel_id=1, source_target_pairs={{0,16},{8,24},{16,0},{24,8},{1,17},{9,25},{17,1},{25,9},{2,18},{10... | collective-permute-start | bytes 196616 | tf_op jit(solution)/shard_map/ppermute | solution.py:144
  66.7 10.0 %collective-permute-start.23 = (bf16[2,2,4,32,256]{4,3,2,1,0:T(8,128)(2,1)S(1)}, bf16[2,2,4,32,256]{4,3,2,1,0:T(8,128)(2,1)S(1)}, u32[]{:S(2)}, u32[]{:S(2)}) collective-permute-start(bf16[2,2,4,32,256]{4,3,2,1,0:T(8,128)(2,1)S(1)} %pad_maximum_fusion.1.refs_3_), channel_id=1, source_target_pairs={{0,2},{2,0},{4,6},{6,4},{1,3},{3,1},{5,7},{7,5},{8,10},{10,8},{12,... | collective-permute-start | bytes 786440 | tf_op jit(solution)/shard_map/ppermute | solution.py:144
  68.0 9.0 %collective-permute-start.24 = (bf16[2,2,4,32,256]{4,3,2,1,0:T(8,128)(2,1)S(1)}, bf16[2,2,4,32,256]{4,3,2,1,0:T(8,128)(2,1)S(1)}, u32[]{:S(2)}, u32[]{:S(2)}) collective-permute-start(bf16[2,2,4,32,256]{4,3,2,1,0:T(8,128)(2,1)S(1)} %pad_maximum_fusion.1.refs_3_), channel_id=1, source_target_pairs={{0,4},{2,6},{4,0},{6,2},{1,5},{3,7},{5,1},{7,3},{8,12},{10,14},{12... | collective-permute-start | bytes 786440 | tf_op jit(solution)/shard_map/ppermute | solution.py:144
  68.5 9.5 %collective-permute-start.26 = (bf16[2,2,4,32,256]{4,3,2,1,0:T(8,128)(2,1)S(1)}, bf16[2,2,4,32,256]{4,3,2,1,0:T(8,128)(2,1)S(1)}, u32[]{:S(2)}, u32[]{:S(2)}) collective-permute-start(bf16[2,2,4,32,256]{4,3,2,1,0:T(8,128)(2,1)S(1)} %pad_maximum_fusion.1.refs_3_), channel_id=1, source_target_pairs={{0,8},{8,0},{16,24},{24,16},{1,9},{9,1},{17,25},{25,17},{2,10},{10... | collective-permute-start | bytes 786440 | tf_op jit(solution)/shard_map/ppermute | solution.py:144
  68.6 11.4 %collective-permute-start.38 = (bf16[2,2,4,32,256]{4,3,2,1,0:T(8,128)(2,1)S(1)}, bf16[2,2,4,32,256]{4,3,2,1,0:T(8,128)(2,1)S(1)}, u32[]{:S(2)}, u32[]{:S(2)}) collective-permute-start(bf16[2,2,4,32,256]{4,3,2,1,0:T(8,128)(2,1)S(1)} %pad_maximum_fusion.2.refs_3_), channel_id=1, source_target_pairs={{0,4},{2,6},{4,0},{6,2},{1,5},{3,7},{5,1},{7,3},{8,12},{10,14},{12... | collective-permute-start | bytes 786440 | tf_op jit(solution)/shard_map/ppermute | solution.py:144
  75.8 9.2 %collective-permute-start.39 = (bf16[2,2,4,32,256]{4,3,2,1,0:T(8,128)(2,1)S(1)}, bf16[2,2,4,32,256]{4,3,2,1,0:T(8,128)(2,1)S(1)}, u32[]{:S(2)}, u32[]{:S(2)}) collective-permute-start(bf16[2,2,4,32,256]{4,3,2,1,0:T(8,128)(2,1)S(1)} %pad_maximum_fusion.2.refs_3_), channel_id=1, source_target_pairs={{0,2},{2,0},{4,6},{6,4},{1,3},{3,1},{5,7},{7,5},{8,10},{10,8},{12,... | collective-permute-start | bytes 786440 | tf_op jit(solution)/shard_map/ppermute | solution.py:144
  76.7 8.8 %collective-permute-start.41 = (bf16[2,2,4,32,256]{4,3,2,1,0:T(8,128)(2,1)S(1)}, bf16[2,2,4,32,256]{4,3,2,1,0:T(8,128)(2,1)S(1)}, u32[]{:S(2)}, u32[]{:S(2)}) collective-permute-start(bf16[2,2,4,32,256]{4,3,2,1,0:T(8,128)(2,1)S(1)} %pad_maximum_fusion.2.refs_3_), channel_id=1, source_target_pairs={{0,8},{8,0},{16,24},{24,16},{1,9},{9,1},{17,25},{25,17},{2,10},{10... | collective-permute-start | bytes 786440 | tf_op jit(solution)/shard_map/ppermute | solution.py:144
  77.0 13.7 %collective-permute-start.53 = (bf16[2,2,4,32,256]{4,3,2,1,0:T(8,128)(2,1)S(1)}, bf16[2,2,4,32,256]{4,3,2,1,0:T(8,128)(2,1)S(1)}, u32[]{:S(2)}, u32[]{:S(2)}) collective-permute-start(bf16[2,2,4,32,256]{4,3,2,1,0:T(8,128)(2,1)S(1)} %pad_maximum_fusion.3.refs_3_), channel_id=1, source_target_pairs={{0,2},{2,0},{4,6},{6,4},{1,3},{3,1},{5,7},{7,5},{8,10},{10,8},{12,... | collective-permute-start | bytes 786440 | tf_op jit(solution)/shard_map/ppermute | solution.py:144
  78.1 12.6 %collective-permute-start.54 = (bf16[2,2,4,32,256]{4,3,2,1,0:T(8,128)(2,1)S(1)}, bf16[2,2,4,32,256]{4,3,2,1,0:T(8,128)(2,1)S(1)}, u32[]{:S(2)}, u32[]{:S(2)}) collective-permute-start(bf16[2,2,4,32,256]{4,3,2,1,0:T(8,128)(2,1)S(1)} %pad_maximum_fusion.3.refs_3_), channel_id=1, source_target_pairs={{0,4},{2,6},{4,0},{6,2},{1,5},{3,7},{5,1},{7,3},{8,12},{10,14},{12... | collective-permute-start | bytes 786440 | tf_op jit(solution)/shard_map/ppermute | solution.py:144
  80.0 11.2 %collective-permute-start.56 = (bf16[2,2,4,32,256]{4,3,2,1,0:T(8,128)(2,1)S(1)}, bf16[2,2,4,32,256]{4,3,2,1,0:T(8,128)(2,1)S(1)}, u32[]{:S(2)}, u32[]{:S(2)}) collective-permute-start(bf16[2,2,4,32,256]{4,3,2,1,0:T(8,128)(2,1)S(1)} %pad_maximum_fusion.3.refs_3_), channel_id=1, source_target_pairs={{0,8},{8,0},{16,24},{24,16},{1,9},{9,1},{17,25},{25,17},{2,10},{10... | collective-permute-start | bytes 786440 | tf_op jit(solution)/shard_map/ppermute | solution.py:144
  85.0 7.0 %collective-permute-start.68 = (bf16[2,2,4,32,256]{4,3,2,1,0:T(8,128)(2,1)S(1)}, bf16[2,2,4,32,256]{4,3,2,1,0:T(8,128)(2,1)S(1)}, u32[]{:S(2)}, u32[]{:S(2)}) collective-permute-start(bf16[2,2,4,32,256]{4,3,2,1,0:T(8,128)(2,1)S(1)} %pad_maximum_fusion.4.refs_3_), channel_id=1, source_target_pairs={{0,4},{2,6},{4,0},{6,2},{1,5},{3,7},{5,1},{7,3},{8,12},{10,14},{12... | collective-permute-start | bytes 786440 | tf_op jit(solution)/shard_map/ppermute | solution.py:144
  85.6 9.1 %collective-permute-start.69 = (bf16[2,2,4,32,256]{4,3,2,1,0:T(8,128)(2,1)S(1)}, bf16[2,2,4,32,256]{4,3,2,1,0:T(8,128)(2,1)S(1)}, u32[]{:S(2)}, u32[]{:S(2)}) collective-permute-start(bf16[2,2,4,32,256]{4,3,2,1,0:T(8,128)(2,1)S(1)} %pad_maximum_fusion.4.refs_3_), channel_id=1, source_target_pairs={{0,2},{2,0},{4,6},{6,4},{1,3},{3,1},{5,7},{7,5},{8,10},{10,8},{12,... | collective-permute-start | bytes 786440 | tf_op jit(solution)/shard_map/ppermute | solution.py:144
  90.6 8.7 %collective-permute-start.25 = (bf16[2,2,4,32,256]{4,3,2,1,0:T(8,128)(2,1)S(1)}, bf16[2,2,4,32,256]{4,3,2,1,0:T(8,128)(2,1)S(1)}, u32[]{:S(2)}, u32[]{:S(2)}) collective-permute-start(bf16[2,2,4,32,256]{4,3,2,1,0:T(8,128)(2,1)S(1)} %collective-permute-done.23.refs_4_), channel_id=1, source_target_pairs={{0,4},{2,6},{4,0},{6,2},{1,5},{3,7},{5,1},{7,3},{8,12},{10,14},{12... | collective-permute-start | bytes 786440 | tf_op jit(solution)/shard_map/ppermute | solution.py:144
  91.2 8.2 %collective-permute-start.27 = (bf16[2,2,4,32,256]{4,3,2,1,0:T(8,128)(2,1)S(1)}, bf16[2,2,4,32,256]{4,3,2,1,0:T(8,128)(2,1)S(1)}, u32[]{:S(2)}, u32[]{:S(2)}) collective-permute-start(bf16[2,2,4,32,256]{4,3,2,1,0:T(8,128)(2,1)S(1)} %collective-permute-done.23.refs_4_), channel_id=1, source_target_pairs={{0,8},{8,0},{16,24},{24,16},{1,9},{9,1},{17,25},{25,17},{2,10},{10... | collective-permute-start | bytes 786440 | tf_op jit(solution)/shard_map/ppermute | solution.py:144
  92.0 7.9 %collective-permute-start.28 = (bf16[2,2,4,32,256]{4,3,2,1,0:T(8,128)(2,1)S(1)}, bf16[2,2,4,32,256]{4,3,2,1,0:T(8,128)(2,1)S(1)}, u32[]{:S(2)}, u32[]{:S(2)}) collective-permute-start(bf16[2,2,4,32,256]{4,3,2,1,0:T(8,128)(2,1)S(1)} %collective-permute-done.24.refs_5_), channel_id=1, source_target_pairs={{0,8},{8,0},{16,24},{24,16},{1,9},{9,1},{17,25},{25,17},{2,10},{10... | collective-permute-start | bytes 786440 | tf_op jit(solution)/shard_map/ppermute | solution.py:144
  94.7 6.7 %collective-permute-start.40 = (bf16[2,2,4,32,256]{4,3,2,1,0:T(8,128)(2,1)S(1)}, bf16[2,2,4,32,256]{4,3,2,1,0:T(8,128)(2,1)S(1)}, u32[]{:S(2)}, u32[]{:S(2)}) collective-permute-start(bf16[2,2,4,32,256]{4,3,2,1,0:T(8,128)(2,1)S(1)} %collective-permute-done.38.refs_4_), channel_id=1, source_target_pairs={{0,2},{2,0},{4,6},{6,4},{1,3},{3,1},{5,7},{7,5},{8,10},{10,8},{12,... | collective-permute-start | bytes 786440 | tf_op jit(solution)/shard_map/ppermute | solution.py:144
  99.4 8.7 %collective-permute-start.55 = (bf16[2,2,4,32,256]{4,3,2,1,0:T(8,128)(2,1)S(1)}, bf16[2,2,4,32,256]{4,3,2,1,0:T(8,128)(2,1)S(1)}, u32[]{:S(2)}, u32[]{:S(2)}) collective-permute-start(bf16[2,2,4,32,256]{4,3,2,1,0:T(8,128)(2,1)S(1)} %collective-permute-done.53.refs_4_), channel_id=1, source_target_pairs={{0,4},{2,6},{4,0},{6,2},{1,5},{3,7},{5,1},{7,3},{8,12},{10,14},{12... | collective-permute-start | bytes 786440 | tf_op jit(solution)/shard_map/ppermute | solution.py:144
  99.9 8.2 %collective-permute-start.29 = (bf16[2,2,4,32,256]{4,3,2,1,0:T(8,128)(2,1)S(1)}, bf16[2,2,4,32,256]{4,3,2,1,0:T(8,128)(2,1)S(1)}, u32[]{:S(2)}, u32[]{:S(2)}) collective-permute-start(bf16[2,2,4,32,256]{4,3,2,1,0:T(8,128)(2,1)S(1)} %collective-permute-done.25.refs_6_), channel_id=1, source_target_pairs={{0,8},{8,0},{16,24},{24,16},{1,9},{9,1},{17,25},{25,17},{2,10},{10... | collective-permute-start | bytes 786440 | tf_op jit(solution)/shard_map/ppermute | solution.py:144
  101.4 10.1 %collective-permute-start.57 = (bf16[2,2,4,32,256]{4,3,2,1,0:T(8,128)(2,1)S(1)}, bf16[2,2,4,32,256]{4,3,2,1,0:T(8,128)(2,1)S(1)}, u32[]{:S(2)}, u32[]{:S(2)}) collective-permute-start(bf16[2,2,4,32,256]{4,3,2,1,0:T(8,128)(2,1)S(1)} %collective-permute-done.53.refs_4_), channel_id=1, source_target_pairs={{0,8},{8,0},{16,24},{24,16},{1,9},{9,1},{17,25},{25,17},{2,10},{10... | collective-permute-start | bytes 786440 | tf_op jit(solution)/shard_map/ppermute | solution.py:144
  101.4 10.2 %collective-permute-start.58 = (bf16[2,2,4,32,256]{4,3,2,1,0:T(8,128)(2,1)S(1)}, bf16[2,2,4,32,256]{4,3,2,1,0:T(8,128)(2,1)S(1)}, u32[]{:S(2)}, u32[]{:S(2)}) collective-permute-start(bf16[2,2,4,32,256]{4,3,2,1,0:T(8,128)(2,1)S(1)} %collective-permute-done.54.refs_5_), channel_id=1, source_target_pairs={{0,8},{8,0},{16,24},{24,16},{1,9},{9,1},{17,25},{25,17},{2,10},{10... | collective-permute-start | bytes 786440 | tf_op jit(solution)/shard_map/ppermute | solution.py:144
  101.9 10.1 %collective-permute-start.70 = (bf16[2,2,4,32,256]{4,3,2,1,0:T(8,128)(2,1)S(1)}, bf16[2,2,4,32,256]{4,3,2,1,0:T(8,128)(2,1)S(1)}, u32[]{:S(2)}, u32[]{:S(2)}) collective-permute-start(bf16[2,2,4,32,256]{4,3,2,1,0:T(8,128)(2,1)S(1)} %collective-permute-done.68.refs_4_), channel_id=1, source_target_pairs={{0,2},{2,0},{4,6},{6,4},{1,3},{3,1},{5,7},{7,5},{8,10},{10,8},{12,... | collective-permute-start | bytes 786440 | tf_op jit(solution)/shard_map/ppermute | solution.py:144
  108.1 7.5 %collective-permute-start.59 = (bf16[2,2,4,32,256]{4,3,2,1,0:T(8,128)(2,1)S(1)}, bf16[2,2,4,32,256]{4,3,2,1,0:T(8,128)(2,1)S(1)}, u32[]{:S(2)}, u32[]{:S(2)}) collective-permute-start(bf16[2,2,4,32,256]{4,3,2,1,0:T(8,128)(2,1)S(1)} %collective-permute-done.55.refs_6_), channel_id=1, source_target_pairs={{0,8},{8,0},{16,24},{24,16},{1,9},{9,1},{17,25},{25,17},{2,10},{10... | collective-permute-start | bytes 786440 | tf_op jit(solution)/shard_map/ppermute | solution.py:144
  111.5 7.1 %collective-permute-start.72 = (bf16[2,2,4,32,256]{4,3,2,1,0:T(8,128)(2,1)S(1)}, bf16[2,2,4,32,256]{4,3,2,1,0:T(8,128)(2,1)S(1)}, u32[]{:S(2)}, u32[]{:S(2)}) collective-permute-start(bf16[2,2,4,32,256]{4,3,2,1,0:T(8,128)(2,1)S(1)} %collective-permute-done.68.refs_4_), channel_id=1, source_target_pairs={{0,8},{8,0},{16,24},{24,16},{1,9},{9,1},{17,25},{25,17},{2,10},{10... | collective-permute-start | bytes 786440 | tf_op jit(solution)/shard_map/ppermute | solution.py:144
  111.6 7.5 %collective-permute-start.73 = (bf16[2,2,4,32,256]{4,3,2,1,0:T(8,128)(2,1)S(1)}, bf16[2,2,4,32,256]{4,3,2,1,0:T(8,128)(2,1)S(1)}, u32[]{:S(2)}, u32[]{:S(2)}) collective-permute-start(bf16[2,2,4,32,256]{4,3,2,1,0:T(8,128)(2,1)S(1)} %collective-permute-done.69.refs_5_), channel_id=1, source_target_pairs={{0,8},{8,0},{16,24},{24,16},{1,9},{9,1},{17,25},{25,17},{2,10},{10... | collective-permute-start | bytes 786440 | tf_op jit(solution)/shard_map/ppermute | solution.py:144
  112.0 7.0 %collective-permute-start.74 = (bf16[2,2,4,32,256]{4,3,2,1,0:T(8,128)(2,1)S(1)}, bf16[2,2,4,32,256]{4,3,2,1,0:T(8,128)(2,1)S(1)}, u32[]{:S(2)}, u32[]{:S(2)}) collective-permute-start(bf16[2,2,4,32,256]{4,3,2,1,0:T(8,128)(2,1)S(1)} %collective-permute-done.70.refs_6_), channel_id=1, source_target_pairs={{0,8},{8,0},{16,24},{24,16},{1,9},{9,1},{17,25},{25,17},{2,10},{10... | collective-permute-start | bytes 786440 | tf_op jit(solution)/shard_map/ppermute | solution.py:144
  112.1 9.9 %collective-permute-start.30 = (bf16[4,2,2,32,1024]{4,3,2,1,0:T(8,128)(2,1)S(1)}, bf16[4,2,2,32,1024]{4,3,2,1,0:T(8,128)(2,1)S(1)}, u32[]{:S(2)}, u32[]{:S(2)}) collective-permute-start(bf16[4,2,2,32,1024]{4,3,2,1,0:T(8,128)(2,1)S(1)} %shard_map.115), channel_id=1, source_target_pairs={{0,8},{8,0},{16,24},{24,16},{1,9},{9,1},{17,25},{25,17},{2,10},{10... | collective-permute-start | bytes 3145736 | tf_op jit(solution)/shard_map/ppermute | solution.py:144
  115.6 10.0 %collective-permute-start.45 = (bf16[4,2,2,32,1024]{4,3,2,1,0:T(8,128)(2,1)S(1)}, bf16[4,2,2,32,1024]{4,3,2,1,0:T(8,128)(2,1)S(1)}, u32[]{:S(2)}, u32[]{:S(2)}) collective-permute-start(bf16[4,2,2,32,1024]{4,3,2,1,0:T(8,128)(2,1)S(1)} %shard_map.117), channel_id=1, source_target_pairs={{0,8},{8,0},{16,24},{24,16},{1,9},{9,1},{17,25},{25,17},{2,10},{10... | collective-permute-start | bytes 3145736 | tf_op jit(solution)/shard_map/ppermute | solution.py:144
  118.6 12.2 %collective-permute-start.60 = (bf16[4,2,2,32,1024]{4,3,2,1,0:T(8,128)(2,1)S(1)}, bf16[4,2,2,32,1024]{4,3,2,1,0:T(8,128)(2,1)S(1)}, u32[]{:S(2)}, u32[]{:S(2)}) collective-permute-start(bf16[4,2,2,32,1024]{4,3,2,1,0:T(8,128)(2,1)S(1)} %shard_map.119), channel_id=1, source_target_pairs={{0,8},{8,0},{16,24},{24,16},{1,9},{9,1},{17,25},{25,17},{2,10},{10... | collective-permute-start | bytes 3145736 | tf_op jit(solution)/shard_map/ppermute | solution.py:144
  121.9 12.9 %collective-permute-start.75 = (bf16[4,2,2,32,1024]{4,3,2,1,0:T(8,128)(2,1)S(1)}, bf16[4,2,2,32,1024]{4,3,2,1,0:T(8,128)(2,1)S(1)}, u32[]{:S(2)}, u32[]{:S(2)}) collective-permute-start(bf16[4,2,2,32,1024]{4,3,2,1,0:T(8,128)(2,1)S(1)} %shard_map.121), channel_id=1, source_target_pairs={{0,8},{8,0},{16,24},{24,16},{1,9},{9,1},{17,25},{25,17},{2,10},{10... | collective-permute-start | bytes 3145736 | tf_op jit(solution)/shard_map/ppermute | solution.py:144
  124.9 13.6 %collective-permute-start.32 = (bf16[2,2,32,1024]{3,2,1,0:T(8,128)(2,1)S(1)}, bf16[2,2,32,1024]{3,2,1,0:T(8,128)(2,1)S(1)}, u32[]{:S(2)}, u32[]{:S(2)}) collective-permute-start(bf16[2,2,32,1024]{3,2,1,0:T(8,128)(2,1)S(1)} %get-tuple-element.75), channel_id=1, source_target_pairs={{0,4},{2,6},{4,0},{6,2},{1,5},{3,7},{5,1},{7,3},{8,12},{10,14},{12... | collective-permute-start | bytes 786440 | tf_op jit(solution)/shard_map/ppermute | solution.py:144
  128.4 11.8 %collective-permute-start.47 = (bf16[2,2,32,1024]{3,2,1,0:T(8,128)(2,1)S(1)}, bf16[2,2,32,1024]{3,2,1,0:T(8,128)(2,1)S(1)}, u32[]{:S(2)}, u32[]{:S(2)}) collective-permute-start(bf16[2,2,32,1024]{3,2,1,0:T(8,128)(2,1)S(1)} %get-tuple-element.80), channel_id=1, source_target_pairs={{0,2},{2,0},{4,6},{6,4},{1,3},{3,1},{5,7},{7,5},{8,10},{10,8},{12,... | collective-permute-start | bytes 786440 | tf_op jit(solution)/shard_map/ppermute | solution.py:144
  129.2 21.2 %collective-permute-start.31 = (bf16[2,2,32,1024]{3,2,1,0:T(8,128)(2,1)S(1)}, bf16[2,2,32,1024]{3,2,1,0:T(8,128)(2,1)S(1)}, u32[]{:S(2)}, u32[]{:S(2)}) collective-permute-start(bf16[2,2,32,1024]{3,2,1,0:T(8,128)(2,1)S(1)} %get-tuple-element.73), channel_id=1, source_target_pairs={{0,4},{2,6},{4,0},{6,2},{1,5},{3,7},{5,1},{7,3},{8,12},{10,14},{12... | collective-permute-start | bytes 786440 | tf_op jit(solution)/shard_map/ppermute | solution.py:144
  130.8 24.7 %collective-permute-start.46 = (bf16[2,2,32,1024]{3,2,1,0:T(8,128)(2,1)S(1)}, bf16[2,2,32,1024]{3,2,1,0:T(8,128)(2,1)S(1)}, u32[]{:S(2)}, u32[]{:S(2)}) collective-permute-start(bf16[2,2,32,1024]{3,2,1,0:T(8,128)(2,1)S(1)} %get-tuple-element.78), channel_id=1, source_target_pairs={{0,2},{2,0},{4,6},{6,4},{1,3},{3,1},{5,7},{7,5},{8,10},{10,8},{12,... | collective-permute-start | bytes 786440 | tf_op jit(solution)/shard_map/ppermute | solution.py:144
  134.8 10.5 %collective-permute-start.62 = (bf16[2,2,32,1024]{3,2,1,0:T(8,128)(2,1)S(1)}, bf16[2,2,32,1024]{3,2,1,0:T(8,128)(2,1)S(1)}, u32[]{:S(2)}, u32[]{:S(2)}) collective-permute-start(bf16[2,2,32,1024]{3,2,1,0:T(8,128)(2,1)S(1)} %get-tuple-element.85), channel_id=1, source_target_pairs={{0,4},{2,6},{4,0},{6,2},{1,5},{3,7},{5,1},{7,3},{8,12},{10,14},{12... | collective-permute-start | bytes 786440 | tf_op jit(solution)/shard_map/ppermute | solution.py:144
  138.6 20.2 %collective-permute-start.61 = (bf16[2,2,32,1024]{3,2,1,0:T(8,128)(2,1)S(1)}, bf16[2,2,32,1024]{3,2,1,0:T(8,128)(2,1)S(1)}, u32[]{:S(2)}, u32[]{:S(2)}) collective-permute-start(bf16[2,2,32,1024]{3,2,1,0:T(8,128)(2,1)S(1)} %get-tuple-element.83), channel_id=1, source_target_pairs={{0,4},{2,6},{4,0},{6,2},{1,5},{3,7},{5,1},{7,3},{8,12},{10,14},{12... | collective-permute-start | bytes 786440 | tf_op jit(solution)/shard_map/ppermute | solution.py:144
  140.2 8.9 %collective-permute-start.77 = (bf16[2,2,32,1024]{3,2,1,0:T(8,128)(2,1)S(1)}, bf16[2,2,32,1024]{3,2,1,0:T(8,128)(2,1)S(1)}, u32[]{:S(2)}, u32[]{:S(2)}) collective-permute-start(bf16[2,2,32,1024]{3,2,1,0:T(8,128)(2,1)S(1)} %get-tuple-element.90), channel_id=1, source_target_pairs={{0,2},{2,0},{4,6},{6,4},{1,3},{3,1},{5,7},{7,5},{8,10},{10,8},{12,... | collective-permute-start | bytes 786440 | tf_op jit(solution)/shard_map/ppermute | solution.py:144
  145.4 9.3 %collective-permute-start.33 = (bf16[2,2,32,1024]{3,2,1,0:T(8,128)(2,1)S(1)}, bf16[2,2,32,1024]{3,2,1,0:T(8,128)(2,1)S(1)}, u32[]{:S(2)}, u32[]{:S(2)}) collective-permute-start(bf16[2,2,32,1024]{3,2,1,0:T(8,128)(2,1)S(1)} %add_convert_fusion.3), channel_id=1, source_target_pairs={{0,2},{2,0},{4,6},{6,4},{1,3},{3,1},{5,7},{7,5},{8,10},{10,8},{12,... | collective-permute-start | bytes 786440 | tf_op jit(solution)/shard_map/ppermute | solution.py:144
  149.1 7.8 %collective-permute-start.48 = (bf16[2,2,32,1024]{3,2,1,0:T(8,128)(2,1)S(1)}, bf16[2,2,32,1024]{3,2,1,0:T(8,128)(2,1)S(1)}, u32[]{:S(2)}, u32[]{:S(2)}) collective-permute-start(bf16[2,2,32,1024]{3,2,1,0:T(8,128)(2,1)S(1)} %add_convert_fusion.2), channel_id=1, source_target_pairs={{0,4},{2,6},{4,0},{6,2},{1,5},{3,7},{5,1},{7,3},{8,12},{10,14},{12... | collective-permute-start | bytes 786440 | tf_op jit(solution)/shard_map/ppermute | solution.py:144
  150.4 15.9 %collective-permute-start.76 = (bf16[2,2,32,1024]{3,2,1,0:T(8,128)(2,1)S(1)}, bf16[2,2,32,1024]{3,2,1,0:T(8,128)(2,1)S(1)}, u32[]{:S(2)}, u32[]{:S(2)}) collective-permute-start(bf16[2,2,32,1024]{3,2,1,0:T(8,128)(2,1)S(1)} %get-tuple-element.88), channel_id=1, source_target_pairs={{0,2},{2,0},{4,6},{6,4},{1,3},{3,1},{5,7},{7,5},{8,10},{10,8},{12,... | collective-permute-start | bytes 786440 | tf_op jit(solution)/shard_map/ppermute | solution.py:144
  154.7 10.2 %collective-permute-start.63 = (bf16[2,2,32,1024]{3,2,1,0:T(8,128)(2,1)S(1)}, bf16[2,2,32,1024]{3,2,1,0:T(8,128)(2,1)S(1)}, u32[]{:S(2)}, u32[]{:S(2)}) collective-permute-start(bf16[2,2,32,1024]{3,2,1,0:T(8,128)(2,1)S(1)} %add_convert_fusion.1), channel_id=1, source_target_pairs={{0,2},{2,0},{4,6},{6,4},{1,3},{3,1},{5,7},{7,5},{8,10},{10,8},{12,... | collective-permute-start | bytes 786440 | tf_op jit(solution)/shard_map/ppermute | solution.py:144
  155.5 10.9 %collective-permute-start.78 = (bf16[2,2,32,1024]{3,2,1,0:T(8,128)(2,1)S(1)}, bf16[2,2,32,1024]{3,2,1,0:T(8,128)(2,1)S(1)}, u32[]{:S(2)}, u32[]{:S(2)}) collective-permute-start(bf16[2,2,32,1024]{3,2,1,0:T(8,128)(2,1)S(1)} %add_convert_fusion), channel_id=1, source_target_pairs={{0,4},{2,6},{4,0},{6,2},{1,5},{3,7},{5,1},{7,3},{8,12},{10,14},{12... | collective-permute-start | bytes 786440 | tf_op jit(solution)/shard_map/ppermute | solution.py:144
  156.9 10.3 %collective-permute-start.34 = (bf16[1,2,32,1024]{3,2,1,0:T(8,128)(2,1)S(1)}, bf16[1,2,32,1024]{3,2,1,0:T(8,128)(2,1)S(1)}, u32[]{:S(2)}, u32[]{:S(2)}) collective-permute-start(bf16[1,2,32,1024]{3,2,1,0:T(8,128)(2,1)S(1)} %add_convert_fusion.7), channel_id=1, source_target_pairs={{0,1},{1,0},{2,3},{3,2},{4,5},{5,4},{6,7},{7,6},{8,9},{9,8},{10,11... | collective-permute-start | bytes 393224 | tf_op jit(solution)/shard_map/ppermute | solution.py:144
  158.7 9.9 %collective-permute-start.49 = (bf16[1,2,32,1024]{3,2,1,0:T(8,128)(2,1)S(1)}, bf16[1,2,32,1024]{3,2,1,0:T(8,128)(2,1)S(1)}, u32[]{:S(2)}, u32[]{:S(2)}) collective-permute-start(bf16[1,2,32,1024]{3,2,1,0:T(8,128)(2,1)S(1)} %add_convert_fusion.6), channel_id=1, source_target_pairs={{0,1},{1,0},{2,3},{3,2},{4,5},{5,4},{6,7},{7,6},{8,9},{9,8},{10,11... | collective-permute-start | bytes 393224 | tf_op jit(solution)/shard_map/ppermute | solution.py:144
  165.0 7.9 %collective-permute-start.64 = (bf16[1,2,32,1024]{3,2,1,0:T(8,128)(2,1)S(1)}, bf16[1,2,32,1024]{3,2,1,0:T(8,128)(2,1)S(1)}, u32[]{:S(2)}, u32[]{:S(2)}) collective-permute-start(bf16[1,2,32,1024]{3,2,1,0:T(8,128)(2,1)S(1)} %add_convert_fusion.5), channel_id=1, source_target_pairs={{0,1},{1,0},{2,3},{3,2},{4,5},{5,4},{6,7},{7,6},{8,9},{9,8},{10,11... | collective-permute-start | bytes 393224 | tf_op jit(solution)/shard_map/ppermute | solution.py:144
  166.4 9.0 %collective-permute-start.79 = (bf16[1,2,32,1024]{3,2,1,0:T(8,128)(2,1)S(1)}, bf16[1,2,32,1024]{3,2,1,0:T(8,128)(2,1)S(1)}, u32[]{:S(2)}, u32[]{:S(2)}) collective-permute-start(bf16[1,2,32,1024]{3,2,1,0:T(8,128)(2,1)S(1)} %add_convert_fusion.4), channel_id=1, source_target_pairs={{0,1},{1,0},{2,3},{3,2},{4,5},{5,4},{6,7},{7,6},{8,9},{9,8},{10,11... | collective-permute-start | bytes 393224 | tf_op jit(solution)/shard_map/ppermute | solution.py:144
  167.2 8.8 %collective-permute-start.35 = (bf16[1,32,1024]{2,1,0:T(8,128)(2,1)S(1)}, bf16[1,32,1024]{2,1,0:T(8,128)(2,1)S(1)}, u32[]{:S(2)}, u32[]{:S(2)}) collective-permute-start(bf16[1,32,1024]{2,1,0:T(8,128)(2,1)S(1)} %fusion.2), channel_id=1, source_target_pairs={{0,16},{8,24},{16,0},{24,8},{1,17},{9,25},{17,1},{25,9},{2,18},{10... | collective-permute-start | bytes 196616 | tf_op jit(solution)/shard_map/ppermute | solution.py:144
  168.6 10.3 %collective-permute-start.50 = (bf16[1,32,1024]{2,1,0:T(8,128)(2,1)S(1)}, bf16[1,32,1024]{2,1,0:T(8,128)(2,1)S(1)}, u32[]{:S(2)}, u32[]{:S(2)}) collective-permute-start(bf16[1,32,1024]{2,1,0:T(8,128)(2,1)S(1)} %fusion.3), channel_id=1, source_target_pairs={{0,16},{8,24},{16,0},{24,8},{1,17},{9,25},{17,1},{25,9},{2,18},{10... | collective-permute-start | bytes 196616 | tf_op jit(solution)/shard_map/ppermute | solution.py:144
  172.9 7.8 %collective-permute-start.65 = (bf16[1,32,1024]{2,1,0:T(8,128)(2,1)S(1)}, bf16[1,32,1024]{2,1,0:T(8,128)(2,1)S(1)}, u32[]{:S(2)}, u32[]{:S(2)}) collective-permute-start(bf16[1,32,1024]{2,1,0:T(8,128)(2,1)S(1)} %fusion.4), channel_id=1, source_target_pairs={{0,16},{8,24},{16,0},{24,8},{1,17},{9,25},{17,1},{25,9},{2,18},{10... | collective-permute-start | bytes 196616 | tf_op jit(solution)/shard_map/ppermute | solution.py:144
  (28 other events, 260.4 us)

commit v5 on v4

--- a/solution.py
+++ b/solution.py
@@ -396,17 +396,21 @@
     out_ref[...] = result.reshape(sessions, rows, piece).astype(out_ref.dtype)
 
 
-def mix_kernel(sessions, *refs):
+def mix_kernel(groups, *refs):
+    sessions = sum(len(slots) for slots in groups)
     x_refs, refs = refs[:sessions], refs[sessions:]
     terms, (proj_ref, *chunk_refs) = refs[: -1 - CHUNKS], refs[-1 - CHUNKS :]
+    each = len(terms) // len(groups)
     rows = chunk_refs[0].shape[1]
     me = lax.axis_index("expert")
-    for r in range(sessions):
-        proj = sum(ref[r].astype(jnp.float32) for ref in terms)
-        proj_ref[r] = proj
-        mixed = (x_refs[r][...].astype(jnp.float32) + proj).astype(jnp.bfloat16)
-        for c, chunk_ref in enumerate(chunk_refs):
-            chunk_ref[lax.bitwise_xor(me, r)] = mixed[c * rows : (c + 1) * rows]
+    for g, slots in enumerate(groups):
+        for n, r in enumerate(slots):
+            here = terms[g * each : (g + 1) * each]
+            proj = sum(ref[n].astype(jnp.float32) for ref in here)
+            proj_ref[r] = proj
+            mixed = (x_refs[r][...].astype(jnp.float32) + proj).astype(jnp.bfloat16)
+            for c, chunk_ref in enumerate(chunk_refs):
+                chunk_ref[lax.bitwise_xor(me, r)] = mixed[c * rows : (c + 1) * rows]
 
 
 def local_kernel(kernel, outs, operands, scratch=(), limit=8 << 20, space=pltpu.VMEM):
@@ -458,7 +462,10 @@
     table, x_half, keys[0], values[0], *rest = local_kernel(
         functools.partial(side_kernel, group_count),
         [jax.ShapeDtypeStruct(shape, kind if n else jnp.float32) for n, shape in enumerate(shapes)],
-        [x_rows[0], q_rows[0], k_rows[0], value_rows[0], ids, weights],
+        [
+            pltpu.with_memory_space_constraint(value, pltpu.HBM)
+            for value in (x_rows[0], q_rows[0], k_rows[0], value_rows[0], ids, weights)
+        ],
         [
             pltpu.VMEM(ids.shape, ids.dtype),
             pltpu.VMEM(weights.shape, weights.dtype),
@@ -494,26 +501,30 @@
         path = paths[n % len(paths)]
         held = gather_parts(rows_of, "expert", path)
         order = slot_order(path)
-        gathered += [held[order.index(r)] for r in range(group_count)]
-
-    def projected(k, kind):
-        shape = (group_count, rows_here, piece)
+        gathered.append([held[order.index(r)] for r in range(group_count)])
+
+    direct = [r for r in range(group_count) if not r & (r - 1)]
+    groups = [direct, [r for r in range(group_count) if r not in direct]]
+
+    def projected(k, g, kind):
+        slots = groups[g]
         return local_kernel(
             functools.partial(project_kernel, k),
-            [jax.ShapeDtypeStruct(shape, kind)],
-            [out_weight, *gathered],
-            [pltpu.VMEM((group_count * rows_here, out_weight.shape[0]), jnp.bfloat16)],
+            [jax.ShapeDtypeStruct((len(slots), rows_here, piece), kind)],
+            [out_weight] + [held[r] for held in gathered for r in slots],
+            [pltpu.VMEM((len(slots) * rows_here, out_weight.shape[0]), jnp.bfloat16)],
         )[0]
 
     terms = []
-    for k in range(1, tensor_count):
-        away = projected(k, jnp.bfloat16)
-        terms.append(swap(away, "tensor", k))
-    terms.append(projected(0, jnp.float32))
+    for g in range(len(groups)):
+        for k in range(1, tensor_count):
+            away = projected(k, g, jnp.bfloat16)
+            terms.append(swap(away, "tensor", k))
+        terms.append(projected(0, g, jnp.float32))
     rows = rows_here // CHUNKS
     part = jax.ShapeDtypeStruct((group_count, rows, piece), jnp.bfloat16)
     proj, *by_session = local_kernel(
-        functools.partial(mix_kernel, group_count),
+        functools.partial(mix_kernel, groups),
         [jax.ShapeDtypeStruct((group_count, rows_here, piece), jnp.float32)] + [part] * CHUNKS,
         [*x_slots, *terms],
     )
@@ -573,7 +584,7 @@
     experts = counts[0] * counts[1]
     capacity = max(2, 3 * rows_here * TOPK // (2 * experts))
     dense = experts * rows_here <= 2 * experts * capacity
-    regular = all(count > 1 and count & (count - 1) == 0 for count in counts)
+    regular = counts[1] > 2 and all(count > 1 and count & (count - 1) == 0 for count in counts)
     fits = experts <= LANES and rows_here % (16 * CHUNKS) == 0
     if dense and regular and fits:
         return dense_plan(*arrays)

time: 183 us -> 182 us (level)
  local copies, waits for them, and re-layouts: 5.6 us -> 0.05 us
  waiting for transfers between devices: 76.2 us -> 79.9 us
    unnamed x22 -> x10, local copies, waits for them, and re-layouts: 5.58 us -> 0.03 us
    ppermute x81 -> x82, waiting for transfers between devices: 76.2 us -> 79.9 us  [swap(): return lax.ppermute(value, axis, [(i, i ^ bit) for i in range(count)])]
    pallas_call x14 -> x16, Pallas kernels: 27.5 us -> 28.9 us  [local_kernel(): pl.pallas_call(kernel, out_shape=outs, in_specs=[pl.BlockSpec(memory_spac...]
    ppermute x81 -> x82, starting transfers between devices: 70.4 us -> 70.5 us  [swap(): return lax.ppermute(value, axis, [(i, i ^ bit) for i in range(count)])]
  transfers between devices with their start and end apart: 81 -> 82, of which waited for: 29 -> 27; matrix products, arithmetic and copies ran while one was open for 1% -> 1% of each run, Pallas kernels for 14% -> 15%
where the time goes in v5:
time: 182 us
  waiting for transfers between devices  79.9 us (44%)
  starting transfers between devices  70.5 us (39%)
  Pallas kernels  28.9 us (16%)
  other arithmetic  2.04 us (1%)
    ppermute x82, waiting for transfers between devices, swap(): return lax.ppermute(value, axis, [(i, i ^ bit) for i in range(count)])  79.9 us
    ppermute x82, starting transfers between devices, swap(): return lax.ppermute(value, axis, [(i, i ^ bit) for i in range(count)])  70.5 us
    pallas_call x16, Pallas kernels, local_kernel(): pl.pallas_call(kernel, out_shape=outs, in_specs=[pl.BlockSpec(memory_spac...  28.9 us
  transfers between devices with their start and end apart: 82, of which 27 were waited for; matrix products, arithmetic and copies ran while one was open for 1% of the time, Pallas kernels for 15%

profile of v5, /device:TPU:0, one launch (start us, length us, event | category | flops | bytes accessed | tf_op | source)
XLA Modules:
  0.0 181.8 jit_solution(9841230731838846298)
XLA Ops:
  0.0 4.1 %collective-permute-start = (bf16[128,256]{1,0:T(8,128)(2,1)}, bf16[128,256]{1,0:T(8,128)(2,1)S(1)}, u32[]{:S(2)}, u32[]{:S(2)}) collective-permute-start(bf16[128,256]{1,0:T(8,128)(2,1)} %bitcast.102), channel_id=1, source_target_pairs={{0,16},{8,24},{16,0},{24,8},{1,17},{9,25},{17,1},{25,9},{2,18},{10... | collective-permute-start | bytes 196616 | tf_op jit(solution)/shard_map/ppermute | solution.py:144
  4.6 3.3 %collective-permute-done.refs_1_ = bf16[128,256]{1,0:T(8,128)(2,1)S(1)} collective-permute-done((bf16[128,256]{1,0:T(8,128)(2,1)}, bf16[128,256]{1,0:T(8,128)(2,1)S(1)}, u32[]{:S(2)}, u32[]{:S(2)}) %collective-permute-start) | collective-permute-done | bytes 65568 | tf_op jit(solution)/shard_map/ppermute | solution.py:144
  8.0 2.8 %collective-permute-done.3.refs_5_ = bf16[128,256]{1,0:T(8,128)(2,1)S(1)} collective-permute-done((bf16[128,256]{1,0:T(8,128)(2,1)}, bf16[128,256]{1,0:T(8,128)(2,1)S(1)}, u32[]{:S(2)}, u32[]{:S(2)}) %collective-permute-start.3) | collective-permute-done | bytes 65568 | tf_op jit(solution)/shard_map/ppermute | solution.py:144
  10.7 1.4 shard_map.109
  12.2 1.2 shard_map.110.refs_0_
  14.9 4.5 %collective-permute-done.7 = f32[2,4,128]{2,1,0:T(4,128)S(1)} collective-permute-done((f32[2,4,128]{2,1,0:T(4,128)S(1)}, f32[2,4,128]{2,1,0:T(4,128)S(1)}, u32[]{:S(2)}, u32[]{:S(2)}) %collective-permute-start.7) | collective-permute-done | bytes 4128 | tf_op jit(solution)/shard_map/ppermute | solution.py:144
  19.4 1.8 collective-permute-start.8
  21.5 1.7 collective-permute-start.14
  23.2 1.5 collective-permute-start.15
  24.7 1.2 shard_map.111.refs_3_
  26.9 4.9 %collective-permute-done.14.refs_1_ = bf16[128,1024]{1,0:T(8,128)(2,1)S(1)} collective-permute-done((bf16[128,1024]{1,0:T(8,128)(2,1)S(1)}, bf16[128,1024]{1,0:T(8,128)(2,1)S(1)}, u32[]{:S(2)}, u32[]{:S(2)}) %collective-permute-start.14) | collective-permute-done | bytes 262176 | tf_op jit(solution)/shard_map/ppermute | solution.py:144
  31.8 1.5 collective-permute-start.9
  33.3 2.2 %collective-permute-done.17.refs_5_ = bf16[128,1024]{1,0:T(8,128)(2,1)S(1)} collective-permute-done((bf16[128,1024]{1,0:T(8,128)(2,1)S(1)}, bf16[128,1024]{1,0:T(8,128)(2,1)S(1)}, u32[]{:S(2)}, u32[]{:S(2)}) %collective-permute-start.17) | collective-permute-done | bytes 262176 | tf_op jit(solution)/shard_map/ppermute | solution.py:144
  36.0 1.2 collective-permute-start.18
  37.2 1.5 collective-permute-start.19
  40.0 3.9 %collective-permute-done.19.refs_0_ = bf16[128,1024]{1,0:T(8,128)(2,1)S(1)} collective-permute-done((bf16[128,1024]{1,0:T(8,128)(2,1)S(1)}, bf16[128,1024]{1,0:T(8,128)(2,1)S(1)}, u32[]{:S(2)}, u32[]{:S(2)}) %collective-permute-start.19) | collective-permute-done | bytes 262176 | tf_op jit(solution)/shard_map/ppermute | solution.py:144
  43.8 1.5 collective-permute-start.12
  47.5 1.4 collective-permute-start.21
  50.7 1.5 collective-permute-done.21.refs_6_
  52.3 2.1 %collective-permute-start.22 = (bf16[1,4,32,256]{3,2,1,0:T(8,128)(2,1)S(1)}, bf16[1,4,32,256]{3,2,1,0:T(8,128)(2,1)S(1)}, u32[]{:S(2)}, u32[]{:S(2)}) collective-permute-start(bf16[1,4,32,256]{3,2,1,0:T(8,128)(2,1)S(1)} %bitcast.96), channel_id=1, source_target_pairs={{0,16},{8,24},{16,0},{24,8},{1,17},{9,25},{17,1},{25,9},{2,18},{10... | collective-permute-start | bytes 196616 | tf_op jit(solution)/shard_map/ppermute | solution.py:144
  55.3 2.0 %collective-permute-start.52 = (bf16[1,4,32,256]{3,2,1,0:T(8,128)(2,1)S(1)}, bf16[1,4,32,256]{3,2,1,0:T(8,128)(2,1)S(1)}, u32[]{:S(2)}, u32[]{:S(2)}) collective-permute-start(bf16[1,4,32,256]{3,2,1,0:T(8,128)(2,1)S(1)} %bitcast.92), channel_id=1, source_target_pairs={{0,16},{8,24},{16,0},{24,8},{1,17},{9,25},{17,1},{25,9},{2,18},{10... | collective-permute-start | bytes 196616 | tf_op jit(solution)/shard_map/ppermute | solution.py:144
  58.2 1.7 collective-permute-start.23
  59.9 2.3 %collective-permute-start.38 = (bf16[1,2,4,32,256]{4,3,2,1,0:T(8,128)(2,1)S(1)}, bf16[1,2,4,32,256]{4,3,2,1,0:T(8,128)(2,1)S(1)}, u32[]{:S(2)}, u32[]{:S(2)}) collective-permute-start(bf16[1,2,4,32,256]{4,3,2,1,0:T(8,128)(2,1)S(1)} %maximum_bitcast_fusion.1), channel_id=1, source_target_pairs={{0,1},{1,0},{2,3},{3,2},{4,5},{5,4},{6,7},{7,6},{8,9},{9,8},{10,11... | collective-permute-start | bytes 393224 | tf_op jit(solution)/shard_map/ppermute | solution.py:144
  62.3 1.4 collective-permute-start.53
  64.9 3.1 %collective-permute-start.25 = (bf16[2,2,4,32,256]{4,3,2,1,0:T(8,128)(2,1)S(1)}, bf16[2,2,4,32,256]{4,3,2,1,0:T(8,128)(2,1)S(1)}, u32[]{:S(2)}, u32[]{:S(2)}) collective-permute-start(bf16[2,2,4,32,256]{4,3,2,1,0:T(8,128)(2,1)S(1)} %pad_maximum_fusion.1.refs_3_), channel_id=1, source_target_pairs={{0,4},{2,6},{4,0},{6,2},{1,5},{3,7},{5,1},{7,3},{8,12},{10,14},{12... | collective-permute-start | bytes 786440 | tf_op jit(solution)/shard_map/ppermute | solution.py:144
  69.1 5.0 %collective-permute-done.68 = bf16[1,2,4,32,256]{4,3,2,1,0:T(8,128)(2,1)S(1)} collective-permute-done((bf16[1,2,4,32,256]{4,3,2,1,0:T(8,128)(2,1)S(1)}, bf16[1,2,4,32,256]{4,3,2,1,0:T(8,128)(2,1)S(1)}, u32[]{:S(2)}, u32[]{:S(2)}) %collective-permute-start.68) | collective-permute-done | bytes 131104 | tf_op jit(solution)/shard_map/ppermute | solution.py:144
  75.2 1.1 collective-permute-start.54
  76.3 1.7 collective-permute-start.55
  78.1 5.2 %collective-permute-done.40.refs_5_ = bf16[2,2,4,32,256]{4,3,2,1,0:T(8,128)(2,1)S(1)} collective-permute-done((bf16[2,2,4,32,256]{4,3,2,1,0:T(8,128)(2,1)S(1)}, bf16[2,2,4,32,256]{4,3,2,1,0:T(8,128)(2,1)S(1)}, u32[]{:S(2)}, u32[]{:S(2)}) %collective-permute-start.40) | collective-permute-done | bytes 262176 | tf_op jit(solution)/shard_map/ppermute | solution.py:144
  83.3 1.7 collective-permute-start.69
  85.1 3.8 %collective-permute-done.54.refs_4_ = bf16[2,2,4,32,256]{4,3,2,1,0:T(8,128)(2,1)S(1)} collective-permute-done((bf16[2,2,4,32,256]{4,3,2,1,0:T(8,128)(2,1)S(1)}, bf16[2,2,4,32,256]{4,3,2,1,0:T(8,128)(2,1)S(1)}, u32[]{:S(2)}, u32[]{:S(2)}) %collective-permute-start.54) | collective-permute-done | bytes 262176 | tf_op jit(solution)/shard_map/ppermute | solution.py:144
  88.9 1.7 collective-permute-start.26
  91.1 2.0 %collective-permute-done.70.refs_5_ = bf16[2,2,4,32,256]{4,3,2,1,0:T(8,128)(2,1)S(1)} collective-permute-done((bf16[2,2,4,32,256]{4,3,2,1,0:T(8,128)(2,1)S(1)}, bf16[2,2,4,32,256]{4,3,2,1,0:T(8,128)(2,1)S(1)}, u32[]{:S(2)}, u32[]{:S(2)}) %collective-permute-start.70) | collective-permute-done | bytes 262176 | tf_op jit(solution)/shard_map/ppermute | solution.py:144
  93.9 3.7 %collective-permute-done.26.refs_6_ = bf16[2,2,4,32,256]{4,3,2,1,0:T(8,128)(2,1)S(1)} collective-permute-done((bf16[2,2,4,32,256]{4,3,2,1,0:T(8,128)(2,1)S(1)}, bf16[2,2,4,32,256]{4,3,2,1,0:T(8,128)(2,1)S(1)}, u32[]{:S(2)}, u32[]{:S(2)}) %collective-permute-start.26) | collective-permute-done | bytes 262176 | tf_op jit(solution)/shard_map/ppermute | solution.py:144
  97.6 1.7 collective-permute-start.56
  101.2 5.2 %collective-permute-done.56.refs_6_ = bf16[2,2,4,32,256]{4,3,2,1,0:T(8,128)(2,1)S(1)} collective-permute-done((bf16[2,2,4,32,256]{4,3,2,1,0:T(8,128)(2,1)S(1)}, bf16[2,2,4,32,256]{4,3,2,1,0:T(8,128)(2,1)S(1)}, u32[]{:S(2)}, u32[]{:S(2)}) %collective-permute-start.56) | collective-permute-done | bytes 262176 | tf_op jit(solution)/shard_map/ppermute | solution.py:144
  106.9 2.8 %shard_map.117 = bf16[4,2,2,32,1024]{4,3,2,1,0:T(8,128)(2,1)S(1)} custom-call(f32[16,128]{1,0:T(8,128)S(1)} %bitcast.73, bf16[2048,768]{1,0:T(8,128)(2,1)S(1)} %pad_maximum_fusion.refs_1_, bf16[384,2048]{1,0:T(8,128)(2,1)S(1)} %bitcast.65, bf16[2,2,4,32,256]{4,3,2,1,0:T(8,128)(2,1)S(1)} %collective-permute-done.27.refs_3_, ...), custom_call_target="tpu_custom_call" | custom-call | tf_op jit(solution)/shard_map/pallas_call | solution.py:417
  110.8 3.0 %shard_map.119 = bf16[4,2,2,32,1024]{4,3,2,1,0:T(8,128)(2,1)S(1)} custom-call(f32[16,128]{1,0:T(8,128)S(1)} %bitcast.74, bf16[2048,768]{1,0:T(8,128)(2,1)S(1)} %pad_maximum_fusion.refs_1_, bf16[384,2048]{1,0:T(8,128)(2,1)S(1)} %bitcast.66, bf16[2,2,4,32,256]{4,3,2,1,0:T(8,128)(2,1)S(1)} %collective-permute-done.42.refs_3_, ...), custom_call_target="tpu_custom_call" | custom-call | tf_op jit(solution)/shard_map/pallas_call | solution.py:417
  114.0 2.8 %shard_map.121 = bf16[4,2,2,32,1024]{4,3,2,1,0:T(8,128)(2,1)S(1)} custom-call(f32[16,128]{1,0:T(8,128)S(1)} %bitcast.75, bf16[2048,768]{1,0:T(8,128)(2,1)S(1)} %pad_maximum_fusion.refs_1_, bf16[384,2048]{1,0:T(8,128)(2,1)S(1)} %bitcast.67, bf16[2,2,4,32,256]{4,3,2,1,0:T(8,128)(2,1)S(1)} %collective-permute-done.57.refs_3_, ...), custom_call_target="tpu_custom_call" | custom-call | tf_op jit(solution)/shard_map/pallas_call | solution.py:417
  117.3 2.8 %shard_map.123 = bf16[4,2,2,32,1024]{4,3,2,1,0:T(8,128)(2,1)S(1)} custom-call(f32[16,128]{1,0:T(8,128)S(1)} %bitcast.76, bf16[2048,768]{1,0:T(8,128)(2,1)S(1)} %pad_maximum_fusion.refs_1_, bf16[384,2048]{1,0:T(8,128)(2,1)S(1)} %bitcast.68, bf16[2,2,4,32,256]{4,3,2,1,0:T(8,128)(2,1)S(1)} %collective-permute-done.72.refs_3_, ...), custom_call_target="tpu_custom_call" | custom-call | tf_op jit(solution)/shard_map/pallas_call | solution.py:417
  120.3 2.9 %shard_map.118 = (bf16[2,2,32,1024]{3,2,1,0:T(8,128)(2,1)S(1)}, bf16[2,2,32,1024]{3,2,1,0:T(8,128)(2,1)S(1)}, bf16[2,2,32,1024]{3,2,1,0:T(8,128)(2,1)S(1)}, bf16[2,2,32,1024]{3,2,1,0:T(8,128)(2,1)S(1)}) custom-call(f32[16,128]{1,0:T(8,128)S(1)} %bitcast.77, bf16[2048,768]{1,0:T(8,128)(2,1)S(1)} %pad_maximum_fusion.refs_1_, bf16[384,2048]{1,0:T(8,128)(2,1)S(1)} %bitcast.69, ...), custom_call_target="tpu_custom_call" | custom-call | tf_op jit(solution)/shard_map/pallas_call | solution.py:417
  123.2 1.8 collective-permute-start.33
  125.0 2.9 %shard_map.120 = (bf16[2,2,32,1024]{3,2,1,0:T(8,128)(2,1)S(1)}, bf16[2,2,32,1024]{3,2,1,0:T(8,128)(2,1)S(1)}, bf16[2,2,32,1024]{3,2,1,0:T(8,128)(2,1)S(1)}, bf16[2,2,32,1024]{3,2,1,0:T(8,128)(2,1)S(1)}) custom-call(f32[16,128]{1,0:T(8,128)S(1)} %bitcast.78, bf16[2048,768]{1,0:T(8,128)(2,1)S(1)} %pad_maximum_fusion.refs_1_, bf16[384,2048]{1,0:T(8,128)(2,1)S(1)} %bitcast.70, ...), custom_call_target="tpu_custom_call" | custom-call | tf_op jit(solution)/shard_map/pallas_call | solution.py:417
  128.0 1.2 collective-permute-start.32
  129.2 1.0 collective-permute-start.47
  130.2 3.1 %shard_map.122 = (bf16[2,2,32,1024]{3,2,1,0:T(8,128)(2,1)S(1)}, bf16[2,2,32,1024]{3,2,1,0:T(8,128)(2,1)S(1)}, bf16[2,2,32,1024]{3,2,1,0:T(8,128)(2,1)S(1)}, bf16[2,2,32,1024]{3,2,1,0:T(8,128)(2,1)S(1)}) custom-call(f32[16,128]{1,0:T(8,128)S(1)} %bitcast.79, bf16[2048,768]{1,0:T(8,128)(2,1)S(1)} %pad_maximum_fusion.refs_1_, bf16[384,2048]{1,0:T(8,128)(2,1)S(1)} %bitcast.71, ...), custom_call_target="tpu_custom_call" | custom-call | tf_op jit(solution)/shard_map/pallas_call | solution.py:417
  133.3 1.8 collective-permute-start.63
  135.1 2.9 %shard_map.124 = (bf16[2,2,32,1024]{3,2,1,0:T(8,128)(2,1)S(1)}, bf16[2,2,32,1024]{3,2,1,0:T(8,128)(2,1)S(1)}, bf16[2,2,32,1024]{3,2,1,0:T(8,128)(2,1)S(1)}, bf16[2,2,32,1024]{3,2,1,0:T(8,128)(2,1)S(1)}) custom-call(f32[16,128]{1,0:T(8,128)S(1)} %bitcast.80, bf16[2048,768]{1,0:T(8,128)(2,1)S(1)} %pad_maximum_fusion.refs_1_, bf16[384,2048]{1,0:T(8,128)(2,1)S(1)} %bitcast.72, ...), custom_call_target="tpu_custom_call" | custom-call | tf_op jit(solution)/shard_map/pallas_call | solution.py:417
  138.4 1.1 collective-permute-start.78
  139.5 4.1 %collective-permute-done.63 = bf16[2,2,32,1024]{3,2,1,0:T(8,128)(2,1)S(1)} collective-permute-done((bf16[2,2,32,1024]{3,2,1,0:T(8,128)(2,1)S(1)}, bf16[2,2,32,1024]{3,2,1,0:T(8,128)(2,1)S(1)}, u32[]{:S(2)}, u32[]{:S(2)}) %collective-permute-start.63) | collective-permute-done | bytes 262176 | tf_op jit(solution)/shard_map/ppermute | solution.py:144
  143.6 1.1 collective-permute-start.34
  144.8 3.5 %collective-permute-done.78 = bf16[2,2,32,1024]{3,2,1,0:T(8,128)(2,1)S(1)} collective-permute-done((bf16[2,2,32,1024]{3,2,1,0:T(8,128)(2,1)S(1)}, bf16[2,2,32,1024]{3,2,1,0:T(8,128)(2,1)S(1)}, u32[]{:S(2)}, u32[]{:S(2)}) %collective-permute-start.78) | collective-permute-done | bytes 262176 | tf_op jit(solution)/shard_map/ppermute | solution.py:144
  148.7 1.0 collective-permute-start.77
  149.7 4.2 %collective-permute-done.34 = bf16[2,2,32,1024]{3,2,1,0:T(8,128)(2,1)S(1)} collective-permute-done((bf16[2,2,32,1024]{3,2,1,0:T(8,128)(2,1)S(1)}, bf16[2,2,32,1024]{3,2,1,0:T(8,128)(2,1)S(1)}, u32[]{:S(2)}, u32[]{:S(2)}) %collective-permute-start.34) | collective-permute-done | bytes 262176 | tf_op jit(solution)/shard_map/ppermute | solution.py:144
  154.3 1.0 collective-permute-start.79
  155.3 1.2 collective-permute-start.35
  157.5 6.8 %collective-permute-done.64 = bf16[2,2,32,1024]{3,2,1,0:T(8,128)(2,1)S(1)} collective-permute-done((bf16[2,2,32,1024]{3,2,1,0:T(8,128)(2,1)S(1)}, bf16[2,2,32,1024]{3,2,1,0:T(8,128)(2,1)S(1)}, u32[]{:S(2)}, u32[]{:S(2)}) %collective-permute-start.64) | collective-permute-done | bytes 262176 | tf_op jit(solution)/shard_map/ppermute | solution.py:144
  164.8 1.8 collective-permute-start.80
  166.7 1.2 collective-permute-start.36
  168.0 1.8 collective-permute-start.51
  169.8 2.9 %collective-permute-done.65 = bf16[1,2,32,1024]{3,2,1,0:T(8,128)(2,1)S(1)} collective-permute-done((bf16[1,2,32,1024]{3,2,1,0:T(8,128)(2,1)S(1)}, bf16[1,2,32,1024]{3,2,1,0:T(8,128)(2,1)S(1)}, u32[]{:S(2)}, u32[]{:S(2)}) %collective-permute-start.65) | collective-permute-done | bytes 131104 | tf_op jit(solution)/shard_map/ppermute | solution.py:144
  173.1 1.9 %collective-permute-done.80 = bf16[1,2,32,1024]{3,2,1,0:T(8,128)(2,1)S(1)} collective-permute-done((bf16[1,2,32,1024]{3,2,1,0:T(8,128)(2,1)S(1)}, bf16[1,2,32,1024]{3,2,1,0:T(8,128)(2,1)S(1)}, u32[]{:S(2)}, u32[]{:S(2)}) %collective-permute-start.80) | collective-permute-done | bytes 131104 | tf_op jit(solution)/shard_map/ppermute | solution.py:144
  175.9 2.8 %collective-permute-done.51 = bf16[1,32,1024]{2,1,0:T(8,128)(2,1)S(1)} collective-permute-done((bf16[1,32,1024]{2,1,0:T(8,128)(2,1)S(1)}, bf16[1,32,1024]{2,1,0:T(8,128)(2,1)S(1)}, u32[]{:S(2)}, u32[]{:S(2)}) %collective-permute-start.51) | collective-permute-done | bytes 65568 | tf_op jit(solution)/shard_map/ppermute | solution.py:144
  179.7 1.4 collective-permute-done.81
  (162 shorter events, 26.1 us)
Async XLA Ops:
  0.0 8.0 %collective-permute-start = (bf16[128,256]{1,0:T(8,128)(2,1)}, bf16[128,256]{1,0:T(8,128)(2,1)S(1)}, u32[]{:S(2)}, u32[]{:S(2)}) collective-permute-start(bf16[128,256]{1,0:T(8,128)(2,1)} %bitcast.102), channel_id=1, source_target_pairs={{0,16},{8,24},{16,0},{24,8},{1,17},{9,25},{17,1},{25,9},{2,18},{10... | collective-permute-start | bytes 196616 | tf_op jit(solution)/shard_map/ppermute | solution.py:144
  4.1 6.7 %collective-permute-start.3 = (bf16[128,256]{1,0:T(8,128)(2,1)}, bf16[128,256]{1,0:T(8,128)(2,1)S(1)}, u32[]{:S(2)}, u32[]{:S(2)}) collective-permute-start(bf16[128,256]{1,0:T(8,128)(2,1)} %bitcast.105), channel_id=1, source_target_pairs={{0,16},{8,24},{16,0},{24,8},{1,17},{9,25},{17,1},{25,9},{2,18},{10... | collective-permute-start | bytes 196616 | tf_op jit(solution)/shard_map/ppermute | solution.py:144
  4.1 8.1 %collective-permute-start.1 = (bf16[128,256]{1,0:T(8,128)(2,1)}, bf16[128,256]{1,0:T(8,128)(2,1)S(1)}, u32[]{:S(2)}, u32[]{:S(2)}) collective-permute-start(bf16[128,256]{1,0:T(8,128)(2,1)} %bitcast.103), channel_id=1, source_target_pairs={{0,8},{8,0},{16,24},{24,16},{1,9},{9,1},{17,25},{25,17},{2,10},{10... | collective-permute-start | bytes 196616 | tf_op jit(solution)/shard_map/ppermute | solution.py:144
  4.1 8.1 %collective-permute-start.4 = (bf16[128,256]{1,0:T(8,128)(2,1)}, bf16[128,256]{1,0:T(8,128)(2,1)S(1)}, u32[]{:S(2)}, u32[]{:S(2)}) collective-permute-start(bf16[128,256]{1,0:T(8,128)(2,1)} %bitcast.106), channel_id=1, source_target_pairs={{0,8},{8,0},{16,24},{24,16},{1,9},{9,1},{17,25},{25,17},{2,10},{10... | collective-permute-start | bytes 196616 | tf_op jit(solution)/shard_map/ppermute | solution.py:144
  19.4 7.1 %collective-permute-start.8 = (f32[4,2,128]{2,1,0:T(2,128)S(1)}, f32[4,2,128]{2,1,0:T(2,128)S(1)}, u32[]{:S(2)}, u32[]{:S(2)}) collective-permute-start(f32[4,2,128]{2,1,0:T(2,128)S(1)} %pad_maximum_fusion.9), channel_id=1, source_target_pairs={{0,2},{2,0},{4,6},{6,4},{1,3},{3,1},{5,7},{7,5},{8,10},{10,8},{12,... | collective-permute-start | bytes 12296 | tf_op jit(solution)/shard_map/ppermute | solution.py:144
  21.2 25.5 %collective-permute-start.11 = (bf16[128,256]{1,0:T(8,128)(2,1)S(1)}, bf16[128,256]{1,0:T(8,128)(2,1)S(1)}, u32[]{:S(2)}, u32[]{:S(2)}) collective-permute-start(bf16[128,256]{1,0:T(8,128)(2,1)S(1)} %get-tuple-element.58), channel_id=1, source_target_pairs={{0,2},{2,0},{4,6},{6,4},{1,3},{3,1},{5,7},{7,5},{8,10},{10,8},{12,... | collective-permute-start | bytes 196616 | tf_op jit(solution)/shard_map/ppermute | solution.py:144
  21.5 10.3 %collective-permute-start.14 = (bf16[128,1024]{1,0:T(8,128)(2,1)S(1)}, bf16[128,1024]{1,0:T(8,128)(2,1)S(1)}, u32[]{:S(2)}, u32[]{:S(2)}) collective-permute-start(bf16[128,1024]{1,0:T(8,128)(2,1)S(1)} %shard_map.110.refs_0_), channel_id=1, source_target_pairs={{0,2},{2,0},{4,6},{6,4},{1,3},{3,1},{5,7},{7,5},{8,10},{10,8},{12,... | collective-permute-start | bytes 786440 | tf_op jit(solution)/shard_map/ppermute | solution.py:144
  23.2 12.2 %collective-permute-start.15 = (bf16[128,1024]{1,0:T(8,128)(2,1)S(1)}, bf16[128,1024]{1,0:T(8,128)(2,1)S(1)}, u32[]{:S(2)}, u32[]{:S(2)}) collective-permute-start(bf16[128,1024]{1,0:T(8,128)(2,1)S(1)} %shard_map.110.refs_0_), channel_id=1, source_target_pairs={{0,4},{2,6},{4,0},{6,2},{1,5},{3,7},{5,1},{7,3},{8,12},{10,14},{12... | collective-permute-start | bytes 786440 | tf_op jit(solution)/shard_map/ppermute | solution.py:144
  25.9 9.5 %collective-permute-start.17 = (bf16[128,1024]{1,0:T(8,128)(2,1)S(1)}, bf16[128,1024]{1,0:T(8,128)(2,1)S(1)}, u32[]{:S(2)}, u32[]{:S(2)}) collective-permute-start(bf16[128,1024]{1,0:T(8,128)(2,1)S(1)} %shard_map.111.refs_3_), channel_id=1, source_target_pairs={{0,4},{2,6},{4,0},{6,2},{1,5},{3,7},{5,1},{7,3},{8,12},{10,14},{12... | collective-permute-start | bytes 786440 | tf_op jit(solution)/shard_map/ppermute | solution.py:144
  26.5 8.9 %collective-permute-start.16 = (bf16[128,1024]{1,0:T(8,128)(2,1)S(1)}, bf16[128,1024]{1,0:T(8,128)(2,1)S(1)}, u32[]{:S(2)}, u32[]{:S(2)}) collective-permute-start(bf16[128,1024]{1,0:T(8,128)(2,1)S(1)} %shard_map.111.refs_3_), channel_id=1, source_target_pairs={{0,2},{2,0},{4,6},{6,4},{1,3},{3,1},{5,7},{7,5},{8,10},{10,8},{12,... | collective-permute-start | bytes 786440 | tf_op jit(solution)/shard_map/ppermute | solution.py:144
  31.8 15.7 %collective-permute-start.9 = (f32[4,2,128]{2,1,0:T(2,128)S(1)}, f32[4,2,128]{2,1,0:T(2,128)S(1)}, u32[]{:S(2)}, u32[]{:S(2)}) collective-permute-start(f32[4,2,128]{2,1,0:T(2,128)S(1)} %pad_maximum_fusion.10), channel_id=1, source_target_pairs={{0,4},{2,6},{4,0},{6,2},{1,5},{3,7},{5,1},{7,3},{8,12},{10,14},{12... | collective-permute-start | bytes 12296 | tf_op jit(solution)/shard_map/ppermute | solution.py:144
  36.0 14.7 %collective-permute-start.18 = (bf16[3,128,256]{2,1,0:T(8,128)(2,1)S(1)}, bf16[3,128,256]{2,1,0:T(8,128)(2,1)S(1)}, u32[]{:S(2)}, u32[]{:S(2)}) collective-permute-start(bf16[3,128,256]{2,1,0:T(8,128)(2,1)S(1)} %shard_map.112), channel_id=1, source_target_pairs={{0,1},{1,0},{2,3},{3,2},{4,5},{5,4},{6,7},{7,6},{8,9},{9,8},{10,11... | collective-permute-start | bytes 589832 | tf_op jit(solution)/shard_map/ppermute | solution.py:144
  37.2 6.6 %collective-permute-start.19 = (bf16[128,1024]{1,0:T(8,128)(2,1)S(1)}, bf16[128,1024]{1,0:T(8,128)(2,1)S(1)}, u32[]{:S(2)}, u32[]{:S(2)}) collective-permute-start(bf16[128,1024]{1,0:T(8,128)(2,1)S(1)} %collective-permute-done.14.refs_1_), channel_id=1, source_target_pairs={{0,4},{2,6},{4,0},{6,2},{1,5},{3,7},{5,1},{7,3},{8,12},{10,14},{12... | collective-permute-start | bytes 786440 | tf_op jit(solution)/shard_map/ppermute | solution.py:144
  38.7 6.8 %collective-permute-start.20 = (bf16[128,1024]{1,0:T(8,128)(2,1)S(1)}, bf16[128,1024]{1,0:T(8,128)(2,1)S(1)}, u32[]{:S(2)}, u32[]{:S(2)}) collective-permute-start(bf16[128,1024]{1,0:T(8,128)(2,1)S(1)} %collective-permute-done.17.refs_5_), channel_id=1, source_target_pairs={{0,2},{2,0},{4,6},{6,4},{1,3},{3,1},{5,7},{7,5},{8,10},{10,8},{12,... | collective-permute-start | bytes 786440 | tf_op jit(solution)/shard_map/ppermute | solution.py:144
  55.3 7.0 %collective-permute-start.52 = (bf16[1,4,32,256]{3,2,1,0:T(8,128)(2,1)S(1)}, bf16[1,4,32,256]{3,2,1,0:T(8,128)(2,1)S(1)}, u32[]{:S(2)}, u32[]{:S(2)}) collective-permute-start(bf16[1,4,32,256]{3,2,1,0:T(8,128)(2,1)S(1)} %bitcast.92), channel_id=1, source_target_pairs={{0,16},{8,24},{16,0},{24,8},{1,17},{9,25},{17,1},{25,9},{2,18},{10... | collective-permute-start | bytes 196616 | tf_op jit(solution)/shard_map/ppermute | solution.py:144
  57.3 10.7 %collective-permute-start.67 = (bf16[1,4,32,256]{3,2,1,0:T(8,128)(2,1)S(1)}, bf16[1,4,32,256]{3,2,1,0:T(8,128)(2,1)S(1)}, u32[]{:S(2)}, u32[]{:S(2)}) collective-permute-start(bf16[1,4,32,256]{3,2,1,0:T(8,128)(2,1)S(1)} %bitcast.90), channel_id=1, source_target_pairs={{0,16},{8,24},{16,0},{24,8},{1,17},{9,25},{17,1},{25,9},{2,18},{10... | collective-permute-start | bytes 196616 | tf_op jit(solution)/shard_map/ppermute | solution.py:144
  59.9 8.1 %collective-permute-start.38 = (bf16[1,2,4,32,256]{4,3,2,1,0:T(8,128)(2,1)S(1)}, bf16[1,2,4,32,256]{4,3,2,1,0:T(8,128)(2,1)S(1)}, u32[]{:S(2)}, u32[]{:S(2)}) collective-permute-start(bf16[1,2,4,32,256]{4,3,2,1,0:T(8,128)(2,1)S(1)} %maximum_bitcast_fusion.1), channel_id=1, source_target_pairs={{0,1},{1,0},{2,3},{3,2},{4,5},{5,4},{6,7},{7,6},{8,9},{9,8},{10,11... | collective-permute-start | bytes 393224 | tf_op jit(solution)/shard_map/ppermute | solution.py:144
  64.5 10.7 %collective-permute-start.24 = (bf16[2,2,4,32,256]{4,3,2,1,0:T(8,128)(2,1)S(1)}, bf16[2,2,4,32,256]{4,3,2,1,0:T(8,128)(2,1)S(1)}, u32[]{:S(2)}, u32[]{:S(2)}) collective-permute-start(bf16[2,2,4,32,256]{4,3,2,1,0:T(8,128)(2,1)S(1)} %pad_maximum_fusion.1.refs_3_), channel_id=1, source_target_pairs={{0,2},{2,0},{4,6},{6,4},{1,3},{3,1},{5,7},{7,5},{8,10},{10,8},{12,... | collective-permute-start | bytes 786440 | tf_op jit(solution)/shard_map/ppermute | solution.py:144
  64.9 10.3 %collective-permute-start.25 = (bf16[2,2,4,32,256]{4,3,2,1,0:T(8,128)(2,1)S(1)}, bf16[2,2,4,32,256]{4,3,2,1,0:T(8,128)(2,1)S(1)}, u32[]{:S(2)}, u32[]{:S(2)}) collective-permute-start(bf16[2,2,4,32,256]{4,3,2,1,0:T(8,128)(2,1)S(1)} %pad_maximum_fusion.1.refs_3_), channel_id=1, source_target_pairs={{0,4},{2,6},{4,0},{6,2},{1,5},{3,7},{5,1},{7,3},{8,12},{10,14},{12... | collective-permute-start | bytes 786440 | tf_op jit(solution)/shard_map/ppermute | solution.py:144
  68.0 8.4 %collective-permute-start.27 = (bf16[2,2,4,32,256]{4,3,2,1,0:T(8,128)(2,1)S(1)}, bf16[2,2,4,32,256]{4,3,2,1,0:T(8,128)(2,1)S(1)}, u32[]{:S(2)}, u32[]{:S(2)}) collective-permute-start(bf16[2,2,4,32,256]{4,3,2,1,0:T(8,128)(2,1)S(1)} %pad_maximum_fusion.1.refs_3_), channel_id=1, source_target_pairs={{0,8},{8,0},{16,24},{24,16},{1,9},{9,1},{17,25},{25,17},{2,10},{10... | collective-permute-start | bytes 786440 | tf_op jit(solution)/shard_map/ppermute | solution.py:144
  68.0 10.0 %collective-permute-start.39 = (bf16[2,2,4,32,256]{4,3,2,1,0:T(8,128)(2,1)S(1)}, bf16[2,2,4,32,256]{4,3,2,1,0:T(8,128)(2,1)S(1)}, u32[]{:S(2)}, u32[]{:S(2)}) collective-permute-start(bf16[2,2,4,32,256]{4,3,2,1,0:T(8,128)(2,1)S(1)} %pad_maximum_fusion.2.refs_3_), channel_id=1, source_target_pairs={{0,4},{2,6},{4,0},{6,2},{1,5},{3,7},{5,1},{7,3},{8,12},{10,14},{12... | collective-permute-start | bytes 786440 | tf_op jit(solution)/shard_map/ppermute | solution.py:144
  74.1 9.2 %collective-permute-start.40 = (bf16[2,2,4,32,256]{4,3,2,1,0:T(8,128)(2,1)S(1)}, bf16[2,2,4,32,256]{4,3,2,1,0:T(8,128)(2,1)S(1)}, u32[]{:S(2)}, u32[]{:S(2)}) collective-permute-start(bf16[2,2,4,32,256]{4,3,2,1,0:T(8,128)(2,1)S(1)} %pad_maximum_fusion.2.refs_3_), channel_id=1, source_target_pairs={{0,2},{2,0},{4,6},{6,4},{1,3},{3,1},{5,7},{7,5},{8,10},{10,8},{12,... | collective-permute-start | bytes 786440 | tf_op jit(solution)/shard_map/ppermute | solution.py:144
  75.1 9.9 %collective-permute-start.42 = (bf16[2,2,4,32,256]{4,3,2,1,0:T(8,128)(2,1)S(1)}, bf16[2,2,4,32,256]{4,3,2,1,0:T(8,128)(2,1)S(1)}, u32[]{:S(2)}, u32[]{:S(2)}) collective-permute-start(bf16[2,2,4,32,256]{4,3,2,1,0:T(8,128)(2,1)S(1)} %pad_maximum_fusion.2.refs_3_), channel_id=1, source_target_pairs={{0,8},{8,0},{16,24},{24,16},{1,9},{9,1},{17,25},{25,17},{2,10},{10... | collective-permute-start | bytes 786440 | tf_op jit(solution)/shard_map/ppermute | solution.py:144
  75.2 13.7 %collective-permute-start.54 = (bf16[2,2,4,32,256]{4,3,2,1,0:T(8,128)(2,1)S(1)}, bf16[2,2,4,32,256]{4,3,2,1,0:T(8,128)(2,1)S(1)}, u32[]{:S(2)}, u32[]{:S(2)}) collective-permute-start(bf16[2,2,4,32,256]{4,3,2,1,0:T(8,128)(2,1)S(1)} %pad_maximum_fusion.3.refs_3_), channel_id=1, source_target_pairs={{0,2},{2,0},{4,6},{6,4},{1,3},{3,1},{5,7},{7,5},{8,10},{10,8},{12,... | collective-permute-start | bytes 786440 | tf_op jit(solution)/shard_map/ppermute | solution.py:144
  76.3 12.6 %collective-permute-start.55 = (bf16[2,2,4,32,256]{4,3,2,1,0:T(8,128)(2,1)S(1)}, bf16[2,2,4,32,256]{4,3,2,1,0:T(8,128)(2,1)S(1)}, u32[]{:S(2)}, u32[]{:S(2)}) collective-permute-start(bf16[2,2,4,32,256]{4,3,2,1,0:T(8,128)(2,1)S(1)} %pad_maximum_fusion.3.refs_3_), channel_id=1, source_target_pairs={{0,4},{2,6},{4,0},{6,2},{1,5},{3,7},{5,1},{7,3},{8,12},{10,14},{12... | collective-permute-start | bytes 786440 | tf_op jit(solution)/shard_map/ppermute | solution.py:144
  78.1 12.6 %collective-permute-start.57 = (bf16[2,2,4,32,256]{4,3,2,1,0:T(8,128)(2,1)S(1)}, bf16[2,2,4,32,256]{4,3,2,1,0:T(8,128)(2,1)S(1)}, u32[]{:S(2)}, u32[]{:S(2)}) collective-permute-start(bf16[2,2,4,32,256]{4,3,2,1,0:T(8,128)(2,1)S(1)} %pad_maximum_fusion.3.refs_3_), channel_id=1, source_target_pairs={{0,8},{8,0},{16,24},{24,16},{1,9},{9,1},{17,25},{25,17},{2,10},{10... | collective-permute-start | bytes 786440 | tf_op jit(solution)/shard_map/ppermute | solution.py:144
  83.3 7.6 %collective-permute-start.69 = (bf16[2,2,4,32,256]{4,3,2,1,0:T(8,128)(2,1)S(1)}, bf16[2,2,4,32,256]{4,3,2,1,0:T(8,128)(2,1)S(1)}, u32[]{:S(2)}, u32[]{:S(2)}) collective-permute-start(bf16[2,2,4,32,256]{4,3,2,1,0:T(8,128)(2,1)S(1)} %pad_maximum_fusion.4.refs_3_), channel_id=1, source_target_pairs={{0,4},{2,6},{4,0},{6,2},{1,5},{3,7},{5,1},{7,3},{8,12},{10,14},{12... | collective-permute-start | bytes 786440 | tf_op jit(solution)/shard_map/ppermute | solution.py:144
  85.0 8.2 %collective-permute-start.70 = (bf16[2,2,4,32,256]{4,3,2,1,0:T(8,128)(2,1)S(1)}, bf16[2,2,4,32,256]{4,3,2,1,0:T(8,128)(2,1)S(1)}, u32[]{:S(2)}, u32[]{:S(2)}) collective-permute-start(bf16[2,2,4,32,256]{4,3,2,1,0:T(8,128)(2,1)S(1)} %pad_maximum_fusion.4.refs_3_), channel_id=1, source_target_pairs={{0,2},{2,0},{4,6},{6,4},{1,3},{3,1},{5,7},{7,5},{8,10},{10,8},{12,... | collective-permute-start | bytes 786440 | tf_op jit(solution)/shard_map/ppermute | solution.py:144
  88.9 8.7 %collective-permute-start.26 = (bf16[2,2,4,32,256]{4,3,2,1,0:T(8,128)(2,1)S(1)}, bf16[2,2,4,32,256]{4,3,2,1,0:T(8,128)(2,1)S(1)}, u32[]{:S(2)}, u32[]{:S(2)}) collective-permute-start(bf16[2,2,4,32,256]{4,3,2,1,0:T(8,128)(2,1)S(1)} %collective-permute-done.24.refs_4_), channel_id=1, source_target_pairs={{0,4},{2,6},{4,0},{6,2},{1,5},{3,7},{5,1},{7,3},{8,12},{10,14},{12... | collective-permute-start | bytes 786440 | tf_op jit(solution)/shard_map/ppermute | solution.py:144
  90.6 7.0 %collective-permute-start.28 = (bf16[2,2,4,32,256]{4,3,2,1,0:T(8,128)(2,1)S(1)}, bf16[2,2,4,32,256]{4,3,2,1,0:T(8,128)(2,1)S(1)}, u32[]{:S(2)}, u32[]{:S(2)}) collective-permute-start(bf16[2,2,4,32,256]{4,3,2,1,0:T(8,128)(2,1)S(1)} %collective-permute-done.24.refs_4_), channel_id=1, source_target_pairs={{0,8},{8,0},{16,24},{24,16},{1,9},{9,1},{17,25},{25,17},{2,10},{10... | collective-permute-start | bytes 786440 | tf_op jit(solution)/shard_map/ppermute | solution.py:144
  90.9 8.5 %collective-permute-start.29 = (bf16[2,2,4,32,256]{4,3,2,1,0:T(8,128)(2,1)S(1)}, bf16[2,2,4,32,256]{4,3,2,1,0:T(8,128)(2,1)S(1)}, u32[]{:S(2)}, u32[]{:S(2)}) collective-permute-start(bf16[2,2,4,32,256]{4,3,2,1,0:T(8,128)(2,1)S(1)} %collective-permute-done.25.refs_5_), channel_id=1, source_target_pairs={{0,8},{8,0},{16,24},{24,16},{1,9},{9,1},{17,25},{25,17},{2,10},{10... | collective-permute-start | bytes 786440 | tf_op jit(solution)/shard_map/ppermute | solution.py:144
  93.2 7.0 %collective-permute-start.41 = (bf16[2,2,4,32,256]{4,3,2,1,0:T(8,128)(2,1)S(1)}, bf16[2,2,4,32,256]{4,3,2,1,0:T(8,128)(2,1)S(1)}, u32[]{:S(2)}, u32[]{:S(2)}) collective-permute-start(bf16[2,2,4,32,256]{4,3,2,1,0:T(8,128)(2,1)S(1)} %collective-permute-done.39.refs_4_), channel_id=1, source_target_pairs={{0,2},{2,0},{4,6},{6,4},{1,3},{3,1},{5,7},{7,5},{8,10},{10,8},{12,... | collective-permute-start | bytes 786440 | tf_op jit(solution)/shard_map/ppermute | solution.py:144
  97.6 8.7 %collective-permute-start.56 = (bf16[2,2,4,32,256]{4,3,2,1,0:T(8,128)(2,1)S(1)}, bf16[2,2,4,32,256]{4,3,2,1,0:T(8,128)(2,1)S(1)}, u32[]{:S(2)}, u32[]{:S(2)}) collective-permute-start(bf16[2,2,4,32,256]{4,3,2,1,0:T(8,128)(2,1)S(1)} %collective-permute-done.54.refs_4_), channel_id=1, source_target_pairs={{0,4},{2,6},{4,0},{6,2},{1,5},{3,7},{5,1},{7,3},{8,12},{10,14},{12... | collective-permute-start | bytes 786440 | tf_op jit(solution)/shard_map/ppermute | solution.py:144
  99.4 7.0 %collective-permute-start.30 = (bf16[2,2,4,32,256]{4,3,2,1,0:T(8,128)(2,1)S(1)}, bf16[2,2,4,32,256]{4,3,2,1,0:T(8,128)(2,1)S(1)}, u32[]{:S(2)}, u32[]{:S(2)}) collective-permute-start(bf16[2,2,4,32,256]{4,3,2,1,0:T(8,128)(2,1)S(1)} %collective-permute-done.26.refs_6_), channel_id=1, source_target_pairs={{0,8},{8,0},{16,24},{24,16},{1,9},{9,1},{17,25},{25,17},{2,10},{10... | collective-permute-start | bytes 786440 | tf_op jit(solution)/shard_map/ppermute | solution.py:144
  100.2 9.5 %collective-permute-start.58 = (bf16[2,2,4,32,256]{4,3,2,1,0:T(8,128)(2,1)S(1)}, bf16[2,2,4,32,256]{4,3,2,1,0:T(8,128)(2,1)S(1)}, u32[]{:S(2)}, u32[]{:S(2)}) collective-permute-start(bf16[2,2,4,32,256]{4,3,2,1,0:T(8,128)(2,1)S(1)} %collective-permute-done.54.refs_4_), channel_id=1, source_target_pairs={{0,8},{8,0},{16,24},{24,16},{1,9},{9,1},{17,25},{25,17},{2,10},{10... | collective-permute-start | bytes 786440 | tf_op jit(solution)/shard_map/ppermute | solution.py:144
  100.2 9.6 %collective-permute-start.59 = (bf16[2,2,4,32,256]{4,3,2,1,0:T(8,128)(2,1)S(1)}, bf16[2,2,4,32,256]{4,3,2,1,0:T(8,128)(2,1)S(1)}, u32[]{:S(2)}, u32[]{:S(2)}) collective-permute-start(bf16[2,2,4,32,256]{4,3,2,1,0:T(8,128)(2,1)S(1)} %collective-permute-done.55.refs_5_), channel_id=1, source_target_pairs={{0,8},{8,0},{16,24},{24,16},{1,9},{9,1},{17,25},{25,17},{2,10},{10... | collective-permute-start | bytes 786440 | tf_op jit(solution)/shard_map/ppermute | solution.py:144
  100.7 9.6 %collective-permute-start.71 = (bf16[2,2,4,32,256]{4,3,2,1,0:T(8,128)(2,1)S(1)}, bf16[2,2,4,32,256]{4,3,2,1,0:T(8,128)(2,1)S(1)}, u32[]{:S(2)}, u32[]{:S(2)}) collective-permute-start(bf16[2,2,4,32,256]{4,3,2,1,0:T(8,128)(2,1)S(1)} %collective-permute-done.69.refs_4_), channel_id=1, source_target_pairs={{0,2},{2,0},{4,6},{6,4},{1,3},{3,1},{5,7},{7,5},{8,10},{10,8},{12,... | collective-permute-start | bytes 786440 | tf_op jit(solution)/shard_map/ppermute | solution.py:144
  106.4 7.5 %collective-permute-start.60 = (bf16[2,2,4,32,256]{4,3,2,1,0:T(8,128)(2,1)S(1)}, bf16[2,2,4,32,256]{4,3,2,1,0:T(8,128)(2,1)S(1)}, u32[]{:S(2)}, u32[]{:S(2)}) collective-permute-start(bf16[2,2,4,32,256]{4,3,2,1,0:T(8,128)(2,1)S(1)} %collective-permute-done.56.refs_6_), channel_id=1, source_target_pairs={{0,8},{8,0},{16,24},{24,16},{1,9},{9,1},{17,25},{25,17},{2,10},{10... | collective-permute-start | bytes 786440 | tf_op jit(solution)/shard_map/ppermute | solution.py:144
  109.7 7.1 %collective-permute-start.73 = (bf16[2,2,4,32,256]{4,3,2,1,0:T(8,128)(2,1)S(1)}, bf16[2,2,4,32,256]{4,3,2,1,0:T(8,128)(2,1)S(1)}, u32[]{:S(2)}, u32[]{:S(2)}) collective-permute-start(bf16[2,2,4,32,256]{4,3,2,1,0:T(8,128)(2,1)S(1)} %collective-permute-done.69.refs_4_), channel_id=1, source_target_pairs={{0,8},{8,0},{16,24},{24,16},{1,9},{9,1},{17,25},{25,17},{2,10},{10... | collective-permute-start | bytes 786440 | tf_op jit(solution)/shard_map/ppermute | solution.py:144
  109.8 7.5 %collective-permute-start.74 = (bf16[2,2,4,32,256]{4,3,2,1,0:T(8,128)(2,1)S(1)}, bf16[2,2,4,32,256]{4,3,2,1,0:T(8,128)(2,1)S(1)}, u32[]{:S(2)}, u32[]{:S(2)}) collective-permute-start(bf16[2,2,4,32,256]{4,3,2,1,0:T(8,128)(2,1)S(1)} %collective-permute-done.70.refs_5_), channel_id=1, source_target_pairs={{0,8},{8,0},{16,24},{24,16},{1,9},{9,1},{17,25},{25,17},{2,10},{10... | collective-permute-start | bytes 786440 | tf_op jit(solution)/shard_map/ppermute | solution.py:144
  110.3 7.0 %collective-permute-start.75 = (bf16[2,2,4,32,256]{4,3,2,1,0:T(8,128)(2,1)S(1)}, bf16[2,2,4,32,256]{4,3,2,1,0:T(8,128)(2,1)S(1)}, u32[]{:S(2)}, u32[]{:S(2)}) collective-permute-start(bf16[2,2,4,32,256]{4,3,2,1,0:T(8,128)(2,1)S(1)} %collective-permute-done.71.refs_6_), channel_id=1, source_target_pairs={{0,8},{8,0},{16,24},{24,16},{1,9},{9,1},{17,25},{25,17},{2,10},{10... | collective-permute-start | bytes 786440 | tf_op jit(solution)/shard_map/ppermute | solution.py:144
  110.4 9.9 %collective-permute-start.31 = (bf16[4,2,2,32,1024]{4,3,2,1,0:T(8,128)(2,1)S(1)}, bf16[4,2,2,32,1024]{4,3,2,1,0:T(8,128)(2,1)S(1)}, u32[]{:S(2)}, u32[]{:S(2)}) collective-permute-start(bf16[4,2,2,32,1024]{4,3,2,1,0:T(8,128)(2,1)S(1)} %shard_map.117), channel_id=1, source_target_pairs={{0,8},{8,0},{16,24},{24,16},{1,9},{9,1},{17,25},{25,17},{2,10},{10... | collective-permute-start | bytes 3145736 | tf_op jit(solution)/shard_map/ppermute | solution.py:144
  113.8 11.1 %collective-permute-start.46 = (bf16[4,2,2,32,1024]{4,3,2,1,0:T(8,128)(2,1)S(1)}, bf16[4,2,2,32,1024]{4,3,2,1,0:T(8,128)(2,1)S(1)}, u32[]{:S(2)}, u32[]{:S(2)}) collective-permute-start(bf16[4,2,2,32,1024]{4,3,2,1,0:T(8,128)(2,1)S(1)} %shard_map.119), channel_id=1, source_target_pairs={{0,8},{8,0},{16,24},{24,16},{1,9},{9,1},{17,25},{25,17},{2,10},{10... | collective-permute-start | bytes 3145736 | tf_op jit(solution)/shard_map/ppermute | solution.py:144
  116.8 12.4 %collective-permute-start.61 = (bf16[4,2,2,32,1024]{4,3,2,1,0:T(8,128)(2,1)S(1)}, bf16[4,2,2,32,1024]{4,3,2,1,0:T(8,128)(2,1)S(1)}, u32[]{:S(2)}, u32[]{:S(2)}) collective-permute-start(bf16[4,2,2,32,1024]{4,3,2,1,0:T(8,128)(2,1)S(1)} %shard_map.121), channel_id=1, source_target_pairs={{0,8},{8,0},{16,24},{24,16},{1,9},{9,1},{17,25},{25,17},{2,10},{10... | collective-permute-start | bytes 3145736 | tf_op jit(solution)/shard_map/ppermute | solution.py:144
  120.2 13.1 %collective-permute-start.76 = (bf16[4,2,2,32,1024]{4,3,2,1,0:T(8,128)(2,1)S(1)}, bf16[4,2,2,32,1024]{4,3,2,1,0:T(8,128)(2,1)S(1)}, u32[]{:S(2)}, u32[]{:S(2)}) collective-permute-start(bf16[4,2,2,32,1024]{4,3,2,1,0:T(8,128)(2,1)S(1)} %shard_map.123), channel_id=1, source_target_pairs={{0,8},{8,0},{16,24},{24,16},{1,9},{9,1},{17,25},{25,17},{2,10},{10... | collective-permute-start | bytes 3145736 | tf_op jit(solution)/shard_map/ppermute | solution.py:144
  123.2 14.8 %collective-permute-start.33 = (bf16[2,2,32,1024]{3,2,1,0:T(8,128)(2,1)S(1)}, bf16[2,2,32,1024]{3,2,1,0:T(8,128)(2,1)S(1)}, u32[]{:S(2)}, u32[]{:S(2)}) collective-permute-start(bf16[2,2,32,1024]{3,2,1,0:T(8,128)(2,1)S(1)} %get-tuple-element.75), channel_id=1, source_target_pairs={{0,4},{2,6},{4,0},{6,2},{1,5},{3,7},{5,1},{7,3},{8,12},{10,14},{12... | collective-permute-start | bytes 786440 | tf_op jit(solution)/shard_map/ppermute | solution.py:144
  127.8 10.6 %collective-permute-start.48 = (bf16[2,2,32,1024]{3,2,1,0:T(8,128)(2,1)S(1)}, bf16[2,2,32,1024]{3,2,1,0:T(8,128)(2,1)S(1)}, u32[]{:S(2)}, u32[]{:S(2)}) collective-permute-start(bf16[2,2,32,1024]{3,2,1,0:T(8,128)(2,1)S(1)} %get-tuple-element.80), channel_id=1, source_target_pairs={{0,2},{2,0},{4,6},{6,4},{1,3},{3,1},{5,7},{7,5},{8,10},{10,8},{12,... | collective-permute-start | bytes 786440 | tf_op jit(solution)/shard_map/ppermute | solution.py:144
  128.0 20.7 %collective-permute-start.32 = (bf16[2,2,32,1024]{3,2,1,0:T(8,128)(2,1)S(1)}, bf16[2,2,32,1024]{3,2,1,0:T(8,128)(2,1)S(1)}, u32[]{:S(2)}, u32[]{:S(2)}) collective-permute-start(bf16[2,2,32,1024]{3,2,1,0:T(8,128)(2,1)S(1)} %get-tuple-element.73), channel_id=1, source_target_pairs={{0,4},{2,6},{4,0},{6,2},{1,5},{3,7},{5,1},{7,3},{8,12},{10,14},{12... | collective-permute-start | bytes 786440 | tf_op jit(solution)/shard_map/ppermute | solution.py:144
  129.2 25.1 %collective-permute-start.47 = (bf16[2,2,32,1024]{3,2,1,0:T(8,128)(2,1)S(1)}, bf16[2,2,32,1024]{3,2,1,0:T(8,128)(2,1)S(1)}, u32[]{:S(2)}, u32[]{:S(2)}) collective-permute-start(bf16[2,2,32,1024]{3,2,1,0:T(8,128)(2,1)S(1)} %get-tuple-element.78), channel_id=1, source_target_pairs={{0,2},{2,0},{4,6},{6,4},{1,3},{3,1},{5,7},{7,5},{8,10},{10,8},{12,... | collective-permute-start | bytes 786440 | tf_op jit(solution)/shard_map/ppermute | solution.py:144
  133.3 10.3 %collective-permute-start.63 = (bf16[2,2,32,1024]{3,2,1,0:T(8,128)(2,1)S(1)}, bf16[2,2,32,1024]{3,2,1,0:T(8,128)(2,1)S(1)}, u32[]{:S(2)}, u32[]{:S(2)}) collective-permute-start(bf16[2,2,32,1024]{3,2,1,0:T(8,128)(2,1)S(1)} %get-tuple-element.85), channel_id=1, source_target_pairs={{0,4},{2,6},{4,0},{6,2},{1,5},{3,7},{5,1},{7,3},{8,12},{10,14},{12... | collective-permute-start | bytes 786440 | tf_op jit(solution)/shard_map/ppermute | solution.py:144
  138.0 18.6 %collective-permute-start.62 = (bf16[2,2,32,1024]{3,2,1,0:T(8,128)(2,1)S(1)}, bf16[2,2,32,1024]{3,2,1,0:T(8,128)(2,1)S(1)}, u32[]{:S(2)}, u32[]{:S(2)}) collective-permute-start(bf16[2,2,32,1024]{3,2,1,0:T(8,128)(2,1)S(1)} %get-tuple-element.83), channel_id=1, source_target_pairs={{0,4},{2,6},{4,0},{6,2},{1,5},{3,7},{5,1},{7,3},{8,12},{10,14},{12... | collective-permute-start | bytes 786440 | tf_op jit(solution)/shard_map/ppermute | solution.py:144
  138.4 9.9 %collective-permute-start.78 = (bf16[2,2,32,1024]{3,2,1,0:T(8,128)(2,1)S(1)}, bf16[2,2,32,1024]{3,2,1,0:T(8,128)(2,1)S(1)}, u32[]{:S(2)}, u32[]{:S(2)}) collective-permute-start(bf16[2,2,32,1024]{3,2,1,0:T(8,128)(2,1)S(1)} %get-tuple-element.90), channel_id=1, source_target_pairs={{0,2},{2,0},{4,6},{6,4},{1,3},{3,1},{5,7},{7,5},{8,10},{10,8},{12,... | collective-permute-start | bytes 786440 | tf_op jit(solution)/shard_map/ppermute | solution.py:144
  143.6 10.3 %collective-permute-start.34 = (bf16[2,2,32,1024]{3,2,1,0:T(8,128)(2,1)S(1)}, bf16[2,2,32,1024]{3,2,1,0:T(8,128)(2,1)S(1)}, u32[]{:S(2)}, u32[]{:S(2)}) collective-permute-start(bf16[2,2,32,1024]{3,2,1,0:T(8,128)(2,1)S(1)} %add_convert_fusion.3), channel_id=1, source_target_pairs={{0,2},{2,0},{4,6},{6,4},{1,3},{3,1},{5,7},{7,5},{8,10},{10,8},{12,... | collective-permute-start | bytes 786440 | tf_op jit(solution)/shard_map/ppermute | solution.py:144
  148.3 7.0 %collective-permute-start.49 = (bf16[2,2,32,1024]{3,2,1,0:T(8,128)(2,1)S(1)}, bf16[2,2,32,1024]{3,2,1,0:T(8,128)(2,1)S(1)}, u32[]{:S(2)}, u32[]{:S(2)}) collective-permute-start(bf16[2,2,32,1024]{3,2,1,0:T(8,128)(2,1)S(1)} %add_convert_fusion.2), channel_id=1, source_target_pairs={{0,4},{2,6},{4,0},{6,2},{1,5},{3,7},{5,1},{7,3},{8,12},{10,14},{12... | collective-permute-start | bytes 786440 | tf_op jit(solution)/shard_map/ppermute | solution.py:144
  148.7 16.0 %collective-permute-start.77 = (bf16[2,2,32,1024]{3,2,1,0:T(8,128)(2,1)S(1)}, bf16[2,2,32,1024]{3,2,1,0:T(8,128)(2,1)S(1)}, u32[]{:S(2)}, u32[]{:S(2)}) collective-permute-start(bf16[2,2,32,1024]{3,2,1,0:T(8,128)(2,1)S(1)} %get-tuple-element.88), channel_id=1, source_target_pairs={{0,2},{2,0},{4,6},{6,4},{1,3},{3,1},{5,7},{7,5},{8,10},{10,8},{12,... | collective-permute-start | bytes 786440 | tf_op jit(solution)/shard_map/ppermute | solution.py:144
  153.9 10.4 %collective-permute-start.64 = (bf16[2,2,32,1024]{3,2,1,0:T(8,128)(2,1)S(1)}, bf16[2,2,32,1024]{3,2,1,0:T(8,128)(2,1)S(1)}, u32[]{:S(2)}, u32[]{:S(2)}) collective-permute-start(bf16[2,2,32,1024]{3,2,1,0:T(8,128)(2,1)S(1)} %add_convert_fusion.1), channel_id=1, source_target_pairs={{0,2},{2,0},{4,6},{6,4},{1,3},{3,1},{5,7},{7,5},{8,10},{10,8},{12,... | collective-permute-start | bytes 786440 | tf_op jit(solution)/shard_map/ppermute | solution.py:144
  154.3 10.4 %collective-permute-start.79 = (bf16[2,2,32,1024]{3,2,1,0:T(8,128)(2,1)S(1)}, bf16[2,2,32,1024]{3,2,1,0:T(8,128)(2,1)S(1)}, u32[]{:S(2)}, u32[]{:S(2)}) collective-permute-start(bf16[2,2,32,1024]{3,2,1,0:T(8,128)(2,1)S(1)} %add_convert_fusion), channel_id=1, source_target_pairs={{0,4},{2,6},{4,0},{6,2},{1,5},{3,7},{5,1},{7,3},{8,12},{10,14},{12... | collective-permute-start | bytes 786440 | tf_op jit(solution)/shard_map/ppermute | solution.py:144
  155.3 11.3 %collective-permute-start.35 = (bf16[1,2,32,1024]{3,2,1,0:T(8,128)(2,1)S(1)}, bf16[1,2,32,1024]{3,2,1,0:T(8,128)(2,1)S(1)}, u32[]{:S(2)}, u32[]{:S(2)}) collective-permute-start(bf16[1,2,32,1024]{3,2,1,0:T(8,128)(2,1)S(1)} %add_convert_fusion.7), channel_id=1, source_target_pairs={{0,1},{1,0},{2,3},{3,2},{4,5},{5,4},{6,7},{7,6},{8,9},{9,8},{10,11... | collective-permute-start | bytes 393224 | tf_op jit(solution)/shard_map/ppermute | solution.py:144
  156.6 11.3 %collective-permute-start.50 = (bf16[1,2,32,1024]{3,2,1,0:T(8,128)(2,1)S(1)}, bf16[1,2,32,1024]{3,2,1,0:T(8,128)(2,1)S(1)}, u32[]{:S(2)}, u32[]{:S(2)}) collective-permute-start(bf16[1,2,32,1024]{3,2,1,0:T(8,128)(2,1)S(1)} %add_convert_fusion.6), channel_id=1, source_target_pairs={{0,1},{1,0},{2,3},{3,2},{4,5},{5,4},{6,7},{7,6},{8,9},{9,8},{10,11... | collective-permute-start | bytes 393224 | tf_op jit(solution)/shard_map/ppermute | solution.py:144
  164.4 8.3 %collective-permute-start.65 = (bf16[1,2,32,1024]{3,2,1,0:T(8,128)(2,1)S(1)}, bf16[1,2,32,1024]{3,2,1,0:T(8,128)(2,1)S(1)}, u32[]{:S(2)}, u32[]{:S(2)}) collective-permute-start(bf16[1,2,32,1024]{3,2,1,0:T(8,128)(2,1)S(1)} %add_convert_fusion.5), channel_id=1, source_target_pairs={{0,1},{1,0},{2,3},{3,2},{4,5},{5,4},{6,7},{7,6},{8,9},{9,8},{10,11... | collective-permute-start | bytes 393224 | tf_op jit(solution)/shard_map/ppermute | solution.py:144
  164.8 10.2 %collective-permute-start.80 = (bf16[1,2,32,1024]{3,2,1,0:T(8,128)(2,1)S(1)}, bf16[1,2,32,1024]{3,2,1,0:T(8,128)(2,1)S(1)}, u32[]{:S(2)}, u32[]{:S(2)}) collective-permute-start(bf16[1,2,32,1024]{3,2,1,0:T(8,128)(2,1)S(1)} %add_convert_fusion.4), channel_id=1, source_target_pairs={{0,1},{1,0},{2,3},{3,2},{4,5},{5,4},{6,7},{7,6},{8,9},{9,8},{10,11... | collective-permute-start | bytes 393224 | tf_op jit(solution)/shard_map/ppermute | solution.py:144
  166.7 9.2 %collective-permute-start.36 = (bf16[1,32,1024]{2,1,0:T(8,128)(2,1)S(1)}, bf16[1,32,1024]{2,1,0:T(8,128)(2,1)S(1)}, u32[]{:S(2)}, u32[]{:S(2)}) collective-permute-start(bf16[1,32,1024]{2,1,0:T(8,128)(2,1)S(1)} %fusion.2), channel_id=1, source_target_pairs={{0,16},{8,24},{16,0},{24,8},{1,17},{9,25},{17,1},{25,9},{2,18},{10... | collective-permute-start | bytes 196616 | tf_op jit(solution)/shard_map/ppermute | solution.py:144
  168.0 10.7 %collective-permute-start.51 = (bf16[1,32,1024]{2,1,0:T(8,128)(2,1)S(1)}, bf16[1,32,1024]{2,1,0:T(8,128)(2,1)S(1)}, u32[]{:S(2)}, u32[]{:S(2)}) collective-permute-start(bf16[1,32,1024]{2,1,0:T(8,128)(2,1)S(1)} %fusion.3), channel_id=1, source_target_pairs={{0,16},{8,24},{16,0},{24,8},{1,17},{9,25},{17,1},{25,9},{2,18},{10... | collective-permute-start | bytes 196616 | tf_op jit(solution)/shard_map/ppermute | solution.py:144
  172.7 6.9 %collective-permute-start.66 = (bf16[1,32,1024]{2,1,0:T(8,128)(2,1)S(1)}, bf16[1,32,1024]{2,1,0:T(8,128)(2,1)S(1)}, u32[]{:S(2)}, u32[]{:S(2)}) collective-permute-start(bf16[1,32,1024]{2,1,0:T(8,128)(2,1)S(1)} %fusion.4), channel_id=1, source_target_pairs={{0,16},{8,24},{16,0},{24,8},{1,17},{9,25},{17,1},{25,9},{2,18},{10... | collective-permute-start | bytes 196616 | tf_op jit(solution)/shard_map/ppermute | solution.py:144
  (23 other events, 241.9 us)
